TPU v7x, 32 devices: a whole 2x2x4 slice. The times are simulated.
32 devices in a mesh: band: 2 (over y), member: 16 (over z, x, core).
Axes of the slice: x: 2, y: 2, z: 4, core: 2. Of those that a mesh axis runs over, the one named last changes fastest.
Arguments:
- ensemble: bfloat16 [128, 4, 64, 1024], P('member', None, 'band'), may hold values from -6 to 6
- variance: float32 [4, 64, 1024], P(None, 'band'), may hold values from 0.25 to 4
- obs_index: int32 [16, 8192], P('member', 'band'), may hold values from 0 to 131071
- obs_value: float32 [16, 8192], P('member', 'band'), may hold values from -8 to 8
- obs_error: float32 [16, 8192], P('member', 'band'), may hold values from 0.5 to 2
- root_ranks: int32 [2], replicated, may hold values from 0 to 15
Outputs:
- increment: float32 [4, 64, 1024], P(None, 'band')
Inputs may be any that keep to these rules, and one draw needn't show every extreme that they name: `obs_index`: the position level * 32 * 1024 + row within the band * 1024 + longitude; columns b * 4096 to (b + 1) * 4096 - 1 belong to band b; positions may repeat.
All inputs are finite; a program needn't handle non-finite values.
Results may differ from a plain program's by a relative error of at most 0.0024.
Values may be sent and summed in bfloat16 or wider, within the bound.
No kernel may reach another device: no remote copies, remote signals or barrier semaphores. Data moves between devices by JAX's collectives and lax.ppermute only.
A program may use at most 64 MiB of HBM per device.

v0:
```python
import jax
import jax.numpy as jnp
from jax import lax
from jax.sharding import PartitionSpec as P

HALF = 8
ITERS = 2


huber_edge = 1.5
ensemble_share = 0.75
static_share = 0.25


def with_halo(x, sides, width):
    for axis, dim in sides:
        count, length = (lax.axis_size(axis), x.shape[dim])
        up = [(i, (i + 1) % count) for i in range(count - 1)]
        down = [(j, i) for i, j in up]
        last = lax.slice_in_dim(x, length - width, length, axis=dim)
        initial = lax.slice_in_dim(x, 0, width, axis=dim)
        before = lax.ppermute(last, axis, up)
        after = lax.ppermute(initial, axis, down)
        x = jnp.concatenate([before, x, after], axis=dim)
    return x


def spread_2(value, axis, source):
    kept = jnp.where(lax.axis_index(axis) == source, value, 0).astype(value.dtype)
    return lax.psum(kept, axis)


def tap_matrix(distance, radius):
    offsets = jnp.arange(-radius, radius + 1).astype(jnp.float32)
    raw = jnp.exp(-0.5 * (offsets / (0.5 * radius)) ** 2)
    norm_value = jnp.sqrt(jnp.sum(raw * raw))
    scaled = distance.astype(jnp.float32) / (0.5 * radius)
    entry = jnp.exp(-0.5 * scaled**2) / norm_value
    return jnp.where(jnp.abs(distance) <= radius, entry, 0.0).astype(jnp.bfloat16)


def lon_operator(lon_cols, radius):
    source = jnp.arange(lon_cols)[:, None]
    target = jnp.arange(lon_cols)[None, :]
    offset = (target - source) % lon_cols
    circular = jnp.minimum(offset, lon_cols - offset)
    return tap_matrix(circular, radius)


def lat_operator(out_rows, radius):
    target = jnp.arange(out_rows)[:, None]
    source = jnp.arange(out_rows + 2 * radius)[None, :]
    return tap_matrix(source - radius - target, radius)


def apply_rows(matrix, padded):
    return jnp.einsum("ij,bjk->bik", matrix, padded, preferred_element_type=jnp.float32)


def smooth_rows(block, matrix):
    padded = with_halo(block, (("band", 1),), HALF)
    return apply_rows(matrix, padded)


def make_gradient(field, positions, values, errors):
    departure = values - field.reshape(-1)[positions]
    weight = huber_edge / jnp.maximum(jnp.abs(departure / errors), huber_edge)
    flat = (
        jnp.zeros((field.size,), jnp.float32)
        .at[positions]
        .add(weight * departure / (errors * errors))
    )
    return (weight, flat.reshape(field.shape))


def local(ensemble, variance, obs_index, obs_value, obs_error, root_ranks):
    members_here, levels, lat_rows, lon_cols = ensemble.shape
    stacked_rows = members_here * levels
    member_pos = lax.axis_index("member")
    members = members_here * lax.axis_size("member")
    lon_matrix = lon_operator(lon_cols, HALF)
    lat_matrix = lat_operator(lat_rows, HALF)
    positions = obs_index[0]
    values = obs_value[0]
    errors = obs_error[0]
    field = jnp.zeros((levels, lat_rows, lon_cols), jnp.float32)
    for iteration in range(ITERS):
        block = root_ranks[iteration]
        use_places = spread_2(positions, "member", block)
        use_values, use_errors = (
            spread_2(values, "member", block),
            spread_2(errors, "member", block),
        )
        weight, gradient = make_gradient(field, use_places, use_values, use_errors)
        mixed = (ensemble.astype(jnp.float32) * gradient[None]).astype(jnp.bfloat16)
        mixed = mixed.reshape(stacked_rows, lat_rows, lon_cols)
        first = jnp.dot(mixed, lon_matrix, preferred_element_type=jnp.float32).astype(jnp.bfloat16)
        first = smooth_rows(first, lat_matrix).astype(jnp.bfloat16)
        second = jnp.dot(first, lon_matrix, preferred_element_type=jnp.float32).astype(jnp.bfloat16)
        second = smooth_rows(second, lat_matrix)
        second = second.reshape(members_here, levels, lat_rows, lon_cols)
        spread = jnp.sum(ensemble.astype(jnp.float32) * second, axis=0)
        summed = lax.psum(spread, "member")
        direction = ensemble_share * summed / (members - 1) + static_share * variance * gradient
        reached = direction.reshape(-1)[use_places]
        curve_local = jnp.sum(weight * reached * reached / (use_errors * use_errors))
        is_root = (member_pos == block).astype(jnp.float32)
        curve = lax.psum(is_root * curve_local, ("band", "member"))
        along, back = lax.psum((jnp.sum(gradient * direction), jnp.sum(field * gradient)), "band")
        field = field + (along - back) / (along + curve) * direction
    return field


def solution(mesh):
    in_specs = (
        P("member", None, "band", None),
        P(None, "band", None),
        P("member", "band"),
        P("member", "band"),
        P("member", "band"),
        P(),
    )
    out_specs = P(None, "band", None)
    return jax.shard_map(local, mesh=mesh, in_specs=in_specs, out_specs=out_specs, check_vma=False)
```

profile of v0, /device:TPU:0, one launch (start us, length us, event | category | flops | bytes accessed | tf_op | source)
XLA Modules:
  0.0 615.6 jit_solution(10129226375615687975)
XLA Ops:
  6.5 1.3 fusion.168
  9.2 1.4 broadcast_select_fusion
  10.7 0.7 broadcast_select_fusion.2
  11.4 63.0 %all-reduce = (s32[4096]{0:T(1024)S(1)}, s32[4096]{0:T(1024)S(1)}) all-reduce(s32[4096]{0:T(1024)S(1)} %bitcast.67, s32[4096]{0:T(1024)S(1)} %bitcast.66), channel_id=1, replica_groups=mesh['band'=2,'member'=16] {'member'}, use_global_device_ids=true, to_apply=%region_0.1 | all-reduce | flops 8192 | bytes 65536 | tf_op jit(solution)/shard_map/psum | solution.py:30
  74.4 0.7 multiply_reduce_fusion.4
  75.8 23.0 %gather_fusion = f32[4096]{0:T(1024)S(1)} fusion(f32[131072]{0:T(1024)S(1)} %broadcast.64, s32[4096]{0:T(1024)S(1)} %get-tuple-element.43), kind=kCustom, calls=%fused_computation | custom fusion | bytes 49152 | tf_op jit(solution)/shard_map/gather | solution.py:66
  98.9 1.8 all-reduce.12.cloned.1.call-done
  100.7 0.8 multiply_divide_fusion.1
  101.5 22.0 %scatter_custom_fusion = f32[131072]{0:T(1024)S(1)} fusion(s32[4096]{0:T(1024)S(1)} %get-tuple-element.42, f32[4096]{0:T(1024)S(1)} %multiply_divide_fusion.1, f32[]{:T(128)} %constant.20.clone.1), kind=kCustom, calls=%fused_computation.83 | custom fusion | flops 4096 | bytes 524292 | tf_op jit(solution)/shard_map/scatter-add | solution.py:71
  123.5 0.1 reshape.52
  123.6 0.6 fusion.1
  124.2 5.5 fusion.57
  129.8 0.1 fusion.167
  129.9 1.3 copy-done.2
  131.1 3.4 collective-permute-start
  134.6 1.3 collective-permute-start.1
  135.9 10.0 %collective-permute-done = bf16[32,8,1024]{2,1,0:T(8,128)(2,1)S(1)} collective-permute-done((bf16[32,8,1024]{2,1,0:T(8,128)(2,1)S(1)}, bf16[32,8,1024]{2,1,0:T(8,128)(2,1)S(1)}, u32[]{:S(2)}, u32[]{:S(2)}) %collective-permute-start) | collective-permute-done | bytes 524320 | tf_op jit(solution)/shard_map/ppermute | solution.py:22
  145.8 4.3 collective-permute-done.1
  150.1 7.5 %fusion.63 = bf16[32,32,1024]{2,1,0:T(8,128)(2,1)} fusion(f32[]{:T(128)S(6)} %sqrt.4, bf16[32,8,1024]{2,1,0:T(8,128)(2,1)} %collective-permute-done.1, bf16[32,32,1024]{2,1,0:T(8,128)(2,1)} %copy-done.2, bf16[32,8,1024]{2,1,0:T(8,128)(2,1)S(1)} %collective-permute-done, s32[48]{0:T(128)S(1)} %iota_add_fusion), kind=kOutput, calls=%fused_computation.71 | convolution fusion | flops 2283813888 | bytes 5243076 | tf_op jit(solution)/shard_map/dot_general | solution.py:99
  157.6 1.3 fusion.166
  158.9 1.4 collective-permute-start.2
  160.3 1.3 collective-permute-start.3
  161.6 9.0 %collective-permute-done.2 = bf16[32,8,1024]{2,1,0:T(8,128)(2,1)S(1)} collective-permute-done((bf16[32,8,1024]{2,1,0:T(8,128)(2,1)S(1)}, bf16[32,8,1024]{2,1,0:T(8,128)(2,1)S(1)}, u32[]{:S(2)}, u32[]{:S(2)}) %collective-permute-start.2) | collective-permute-done | bytes 524320 | tf_op jit(solution)/shard_map/ppermute | solution.py:22
  170.6 4.1 collective-permute-done.3
  174.8 2.3 fusion.14
  177.1 1.5 fusion.2
  178.6 0.2 all-reduce.10.cloned.1.call-start
  178.8 88.8 %all-reduce.8.cloned.1.call-done = f32[4,32,1024]{2,1,0:T(8,128)} async-done(((f32[4,32,1024]{2,1,0:T(8,128)}), f32[4,32,1024]{2,1,0:T(8,128)}) %all-reduce.8.cloned.1.call-update) | async-done | bytes 524304 | tf_op jit(solution)/shard_map/psum | solution.py:103
  267.6 2.0 multiply_reduce_fusion.3
  269.6 0.1 copy.7
  269.7 23.0 %gather_fusion.1 = f32[4096]{0:T(1024)S(1)} fusion(f32[131072]{0:T(1024)S(1)} %bitcast.56, s32[4096]{0:T(1024)S(1)} %get-tuple-element.43), kind=kCustom, calls=%fused_computation.1 | custom fusion | bytes 49152 | tf_op jit(solution)/shard_map/gather | solution.py:105
  292.8 0.6 fusion.88
  293.9 1.8 multiply_reduce_fusion.2
  295.7 40.6 %psum.104 = f32[]{:T(128)} all-reduce(f32[]{:T(128)S(6)} %mul.123), channel_id=1, replica_groups=mesh['band'=2,'member'=16] {'band','member'}, use_global_device_ids=true, to_apply=%region_12.13 | all-reduce | flops 1 | bytes 8 | tf_op jit(solution)/shard_map/psum | solution.py:108
  336.3 6.1 all-reduce.3
  345.0 0.1 copy.8
  345.1 23.0 %gather_fusion.2 = f32[4096]{0:T(1024)S(1)} fusion(f32[131072]{0:T(1024)S(1)} %bitcast.57, s32[4096]{0:T(1024)S(1)} %get-tuple-element.28), kind=kCustom, calls=%fused_computation.2 | custom fusion | bytes 49152 | tf_op jit(solution)/shard_map/gather | solution.py:66
  368.2 22.7 %scatter_custom_fusion.1 = f32[131072]{0:T(1024)} fusion(s32[4096]{0:T(1024)S(1)} %get-tuple-element.29, f32[4096]{0:T(1024)S(1)} %multiply_divide_fusion, f32[]{:T(128)} %constant.20.clone.1), kind=kCustom, calls=%fused_computation.81 | custom fusion | flops 4096 | bytes 524292 | tf_op jit(solution)/shard_map/scatter-add | solution.py:71
  390.8 1.1 reshape.57
  392.0 0.6 fusion.3
  392.6 5.5 fusion.60
  398.2 1.3 copy-done.3
  399.5 0.1 fusion.165
  399.6 4.0 collective-permute-start.4
  403.6 1.3 collective-permute-start.5
  404.9 7.9 %collective-permute-done.4 = bf16[32,8,1024]{2,1,0:T(8,128)(2,1)S(1)} collective-permute-done((bf16[32,8,1024]{2,1,0:T(8,128)(2,1)S(1)}, bf16[32,8,1024]{2,1,0:T(8,128)(2,1)S(1)}, u32[]{:S(2)}, u32[]{:S(2)}) %collective-permute-start.4) | collective-permute-done | bytes 524320 | tf_op jit(solution)/shard_map/ppermute | solution.py:22
  412.8 0.8 copy-done.8
  413.6 3.5 collective-permute-done.5
  417.0 7.6 %fusion.68 = bf16[32,32,1024]{2,1,0:T(8,128)(2,1)} fusion(f32[]{:T(128)S(6)} %sqrt.4, bf16[32,8,1024]{2,1,0:T(8,128)(2,1)} %collective-permute-done.5, bf16[32,32,1024]{2,1,0:T(8,128)(2,1)} %copy-done.3, bf16[32,8,1024]{2,1,0:T(8,128)(2,1)} %copy-done.8, s32[48]{0:T(128)S(1)} %iota_add_fusion), kind=kOutput, calls=%fused_computation.72 | convolution fusion | flops 2283813888 | bytes 5243076 | tf_op jit(solution)/shard_map/dot_general | solution.py:99
  424.6 1.3 fusion.164
  425.9 1.4 collective-permute-start.6
  427.3 1.5 collective-permute-start.7
  428.8 6.8 %collective-permute-done.6 = bf16[32,8,1024]{2,1,0:T(8,128)(2,1)S(1)} collective-permute-done((bf16[32,8,1024]{2,1,0:T(8,128)(2,1)S(1)}, bf16[32,8,1024]{2,1,0:T(8,128)(2,1)S(1)}, u32[]{:S(2)}, u32[]{:S(2)}) %collective-permute-start.6) | collective-permute-done | bytes 524320 | tf_op jit(solution)/shard_map/ppermute | solution.py:22
  435.6 4.1 collective-permute-done.7
  439.7 2.3 fusion.26
  442.0 1.5 fusion.4
  443.5 88.7 %all-reduce.10.cloned.1.call-done = f32[4,32,1024]{2,1,0:T(8,128)} async-done(((f32[4,32,1024]{2,1,0:T(8,128)}), f32[4,32,1024]{2,1,0:T(8,128)}) %all-reduce.10.cloned.1.call-update) | async-done | bytes 524304 | tf_op jit(solution)/shard_map/psum | solution.py:103
  532.2 2.0 multiply_reduce_fusion
  534.3 0.1 copy.9
  534.4 23.0 %gather_fusion.3 = f32[4096]{0:T(1024)S(1)} fusion(f32[131072]{0:T(1024)S(1)} %bitcast.58, s32[4096]{0:T(1024)S(1)} %get-tuple-element.28), kind=kCustom, calls=%fused_computation.3 | custom fusion | bytes 49152 | tf_op jit(solution)/shard_map/gather | solution.py:105
  557.4 0.7 fusion.87
  558.8 40.7 %psum.111 = f32[]{:T(128)} all-reduce(f32[]{:T(128)S(6)} %mul.136), channel_id=1, replica_groups=mesh['band'=2,'member'=16] {'band','member'}, use_global_device_ids=true, to_apply=%region_24.25 | all-reduce | flops 1 | bytes 8 | tf_op jit(solution)/shard_map/psum | solution.py:108
  599.5 6.1 all-reduce.2
  608.2 0.9 multiply_add_fusion
  (25 shorter events, 0.2 us)
Async XLA Ops:
  6.5 94.2 %all-reduce.12.cloned.1.call-start = ((), (), s32[]{:S(2)}) async-start(), calls=%async_computation.2 | async-start | bytes 131072 | tf_op jit(solution)/shard_map/psum | solution.py:30
  10.6 257.0 %all-reduce.8.cloned.1.call-start = ((), (), s32[]{:S(2)}) async-start(), calls=%async_computation | async-start | bytes 1048576 | tf_op jit(solution)/shard_map/psum | solution.py:103
  75.8 47.8 %copy-start = (bf16[8,4,32,1024]{3,2,1,0:T(8,128)(2,1)S(1)}, bf16[8,4,32,1024]{3,2,1,0:T(8,128)(2,1)}, u32[]{:S(2)}) copy-start(bf16[8,4,32,1024]{3,2,1,0:T(8,128)(2,1)} %param.6) | copy-start | bytes 6291460
  123.5 6.3 %copy-start.1 = (f32[131072]{0:T(1024)}, f32[131072]{0:T(1024)S(1)}, u32[]{:S(2)}) copy-start(f32[131072]{0:T(1024)S(1)} %scatter_custom_fusion) | copy-start | bytes 1572868
  129.8 1.4 copy-start.2
  131.1 14.7 %collective-permute-start = (bf16[32,8,1024]{2,1,0:T(8,128)(2,1)S(1)}, bf16[32,8,1024]{2,1,0:T(8,128)(2,1)S(1)}, u32[]{:S(2)}, u32[]{:S(2)}) collective-permute-start(bf16[32,8,1024]{2,1,0:T(8,128)(2,1)S(1)} %get-tuple-element.26), channel_id=1, source_target_pairs={{0,16},{1,17},{2,18},{3,19},{4,20},{5,21},{6,22},{7,23},{8,24},{9,... | collective-permute-start | bytes 1572872 | tf_op jit(solution)/shard_map/ppermute | solution.py:22
  134.6 15.5 %collective-permute-start.1 = (bf16[32,8,1024]{2,1,0:T(8,128)(2,1)S(1)}, bf16[32,8,1024]{2,1,0:T(8,128)(2,1)}, u32[]{:S(2)}, u32[]{:S(2)}) collective-permute-start(bf16[32,8,1024]{2,1,0:T(8,128)(2,1)S(1)} %get-tuple-element.27), channel_id=1, source_target_pairs={{16,0},{17,1},{18,2},{19,3},{20,4},{21,5},{22,6},{23,7},{24,8},{25... | collective-permute-start | bytes 1572872 | tf_op jit(solution)/shard_map/ppermute | solution.py:23
  158.9 11.7 %collective-permute-start.2 = (bf16[32,8,1024]{2,1,0:T(8,128)(2,1)S(1)}, bf16[32,8,1024]{2,1,0:T(8,128)(2,1)S(1)}, u32[]{:S(2)}, u32[]{:S(2)}) collective-permute-start(bf16[32,8,1024]{2,1,0:T(8,128)(2,1)S(1)} %get-tuple-element.24), channel_id=1, source_target_pairs={{0,16},{1,17},{2,18},{3,19},{4,20},{5,21},{6,22},{7,23},{8,24},{9,... | collective-permute-start | bytes 1572872 | tf_op jit(solution)/shard_map/ppermute | solution.py:22
  160.3 14.5 %collective-permute-start.3 = (bf16[32,8,1024]{2,1,0:T(8,128)(2,1)S(1)}, bf16[32,8,1024]{2,1,0:T(8,128)(2,1)S(1)}, u32[]{:S(2)}, u32[]{:S(2)}) collective-permute-start(bf16[32,8,1024]{2,1,0:T(8,128)(2,1)S(1)} %get-tuple-element.25), channel_id=1, source_target_pairs={{16,0},{17,1},{18,2},{19,3},{20,4},{21,5},{22,6},{23,7},{24,8},{25... | collective-permute-start | bytes 1572872 | tf_op jit(solution)/shard_map/ppermute | solution.py:23
  178.6 353.6 %all-reduce.10.cloned.1.call-start = ((), (), s32[]{:S(2)}) async-start(), calls=%async_computation.1 | async-start | bytes 1048576 | tf_op jit(solution)/shard_map/psum | solution.py:103
  269.7 23.1 %copy-start.6 = (f32[4096]{0:T(1024)S(1)}, f32[4096]{0:T(1024)}, u32[]{:S(2)}) copy-start(f32[4096]{0:T(1024)} %get-tuple-element.9) | copy-start | bytes 49156
  269.7 23.1 %copy-start.7 = (f32[4096]{0:T(1024)S(1)}, f32[4096]{0:T(1024)}, u32[]{:S(2)}) copy-start(f32[4096]{0:T(1024)} %get-tuple-element.10) | copy-start | bytes 49156
  345.1 23.1 %copy-start.4 = (f32[4096]{0:T(1024)S(1)}, f32[4096]{0:T(1024)}, u32[]{:S(2)}) copy-start(f32[4096]{0:T(1024)} %get-tuple-element.11) | copy-start | bytes 49156
  345.1 23.1 %copy-start.5 = (f32[4096]{0:T(1024)S(1)}, f32[4096]{0:T(1024)}, u32[]{:S(2)}) copy-start(f32[4096]{0:T(1024)} %get-tuple-element.12) | copy-start | bytes 49156
  398.2 1.4 copy-start.3
  399.6 13.2 %collective-permute-start.4 = (bf16[32,8,1024]{2,1,0:T(8,128)(2,1)S(1)}, bf16[32,8,1024]{2,1,0:T(8,128)(2,1)S(1)}, u32[]{:S(2)}, u32[]{:S(2)}) collective-permute-start(bf16[32,8,1024]{2,1,0:T(8,128)(2,1)S(1)} %get-tuple-element.22), channel_id=1, source_target_pairs={{0,16},{1,17},{2,18},{3,19},{4,20},{5,21},{6,22},{7,23},{8,24},{9,... | collective-permute-start | bytes 1572872 | tf_op jit(solution)/shard_map/ppermute | solution.py:22
  403.6 13.4 %collective-permute-start.5 = (bf16[32,8,1024]{2,1,0:T(8,128)(2,1)S(1)}, bf16[32,8,1024]{2,1,0:T(8,128)(2,1)}, u32[]{:S(2)}, u32[]{:S(2)}) collective-permute-start(bf16[32,8,1024]{2,1,0:T(8,128)(2,1)S(1)} %get-tuple-element.23), channel_id=1, source_target_pairs={{16,0},{17,1},{18,2},{19,3},{20,4},{21,5},{22,6},{23,7},{24,8},{25... | collective-permute-start | bytes 1572872 | tf_op jit(solution)/shard_map/ppermute | solution.py:23
  412.8 0.8 copy-start.8
  425.9 9.7 %collective-permute-start.6 = (bf16[32,8,1024]{2,1,0:T(8,128)(2,1)S(1)}, bf16[32,8,1024]{2,1,0:T(8,128)(2,1)S(1)}, u32[]{:S(2)}, u32[]{:S(2)}) collective-permute-start(bf16[32,8,1024]{2,1,0:T(8,128)(2,1)S(1)} %get-tuple-element.20), channel_id=1, source_target_pairs={{0,16},{1,17},{2,18},{3,19},{4,20},{5,21},{6,22},{7,23},{8,24},{9,... | collective-permute-start | bytes 1572872 | tf_op jit(solution)/shard_map/ppermute | solution.py:22
  427.3 12.4 %collective-permute-start.7 = (bf16[32,8,1024]{2,1,0:T(8,128)(2,1)S(1)}, bf16[32,8,1024]{2,1,0:T(8,128)(2,1)S(1)}, u32[]{:S(2)}, u32[]{:S(2)}) collective-permute-start(bf16[32,8,1024]{2,1,0:T(8,128)(2,1)S(1)} %get-tuple-element.21), channel_id=1, source_target_pairs={{16,0},{17,1},{18,2},{19,3},{20,4},{21,5},{22,6},{23,7},{24,8},{25... | collective-permute-start | bytes 1572872 | tf_op jit(solution)/shard_map/ppermute | solution.py:23
Sparse Core Ops, SparseCore 0:
  11.2 89.4 all-reduce.11
  178.7 88.8 all-reduce.7
  443.7 88.5 all-reduce.9
where the time goes:
time: 617 us; the launch traced here: 616 us
  waiting for transfers between devices  229 us (37%)
  blocking collectives  156 us (25%)
  local copies, waits for them, and re-layouts  101 us (16%)
  other arithmetic  60.5 us (10%)
  matrix products  30.9 us (5%)
  between operations  21.9 us (4%)
  starting transfers between devices  15.8 us (3%)
    psum x2, waiting for transfers between devices, local(): summed = lax.psum(spread, 'member')  178 us
    psum x2, blocking collectives, local(): curve = lax.psum(is_root * curve_local, ('band', 'member'))  81.3 us
    psum x1, blocking collectives, spread_2(): return lax.psum(kept, axis)  63 us
    gather x2, local copies, waits for them, and re-layouts, make_gradient(): departure = values - field.reshape(-1)[positions]  46.1 us
    gather x2, local copies, waits for them, and re-layouts, local(): reached = direction.reshape(-1)[use_places]  46.1 us
    scatter-add x2, other arithmetic, make_gradient(): flat = jnp.zeros((field.size,), jnp.float32).at[positions].add(weight * d...  44.7 us
    ppermute x4, waiting for transfers between devices, with_halo(): before = lax.ppermute(last, axis, up)  33.7 us
    ppermute x4, waiting for transfers between devices, with_halo(): after = lax.ppermute(initial, axis, down)  16 us
  transfers between devices with their start and end apart: 11, of which 11 were waited for; matrix products, arithmetic and copies ran while one was open for 4% of the time, Pallas kernels for 0%

commit v1 on v0

v1 whole, which is shorter than its diff:
```python
import functools

import jax
import jax.numpy as jnp
from jax import lax
from jax.experimental import pallas as pl
from jax.experimental.pallas import tpu as pltpu
from jax.sharding import PartitionSpec as P

HALF = 8
ITERS = 2
REACH = 2 * HALF

huber_edge = 1.5
ensemble_share = 0.75
static_share = 0.25

LANES = 256
F32 = jnp.float32
BF16 = jnp.bfloat16


def tap_matrix(distance, radius):
    offsets = jnp.arange(-radius, radius + 1).astype(F32)
    raw = jnp.exp(-0.5 * (offsets / (0.5 * radius)) ** 2)
    norm_value = jnp.sqrt(jnp.sum(raw * raw))
    scaled = distance.astype(F32) / (0.5 * radius)
    entry = jnp.exp(-0.5 * scaled**2) / norm_value
    return jnp.where(jnp.abs(distance) <= radius, entry, 0.0).astype(BF16)


def lon_tile(radius):
    source = jnp.arange(2 * LANES)[:, None] - LANES // 2
    target = jnp.arange(LANES)[None, :]
    return tap_matrix(source - target, radius)


def lat_block(out_level, out_row, in_level, in_row, rows_total, radius):
    distance = in_row[None, :] - out_row[:, None]
    entry = tap_matrix(distance, radius)
    inside = (out_row >= 0) & (out_row < rows_total)
    keep = (out_level[:, None] == in_level[None, :]) & inside[:, None]
    return jnp.where(keep, entry, 0).astype(BF16)


def split_bf16(x):
    hi = x.astype(BF16)
    lo = (x - hi.astype(F32)).astype(BF16)
    return hi, lo


def onehot(index, count):
    rows = lax.broadcasted_iota(jnp.int32, (count, index.shape[1]), 0)
    return jnp.where(rows == index, 1.0, 0.0).astype(BF16)


def scatter_kernel(lon, rows, sources, *refs):
    start_ref, own_idx, own_coef = refs[:3]
    ext = refs[3:3 + 2 * sources]
    own_out, ext_out, own_acc, ext_acc = refs[3 + 2 * sources:]
    blocks = lon // LANES
    chunks = own_idx.shape[0]
    row_bits = lon

    def add(idx, coef, seg, acc):
        lane = idx % LANES
        hi, lo = split_bf16(coef)
        spot = lax.broadcasted_iota(jnp.int32, (LANES, idx.shape[1]), 0) == lane
        side = jnp.concatenate(
            [
                jnp.where(spot, hi.astype(F32), 0.0).astype(BF16),
                jnp.where(spot, lo.astype(F32), 0.0).astype(BF16),
            ],
            axis=0,
        )
        hot = onehot(seg, acc.shape[0])
        acc[...] += lax.dot_general(
            hot, side, (((1,), (1,)), ((), ())), preferred_element_type=F32
        )

    own_acc[...] = jnp.zeros_like(own_acc)
    ext_acc[...] = jnp.zeros_like(ext_acc)
    own_rows = own_out.shape[0]
    ext_rows = ext_out.shape[0] // sources
    for c in range(chunks):
        idx = own_idx[c:c + 1, :].astype(jnp.int32)
        blk = (idx % lon) // LANES
        add(idx, own_coef[c:c + 1, :], blk * own_rows + idx // row_bits, own_acc)
        for s in range(sources):
            idx = ext[2 * s][c:c + 1, :].astype(jnp.int32)
            blk = (idx % lon) // LANES
            level = idx // (row_bits * rows)
            row = (idx // row_bits) % rows - start_ref[s]
            inside = (row >= 0) & (row < REACH)
            seg = blk * ext_rows + level * REACH + row
            seg = jnp.where(inside, seg, -1)
            add(idx, ext[2 * s + 1][c:c + 1, :], seg, ext_acc.at[s])
    for b in range(blocks):
        lanes = slice(b * LANES, (b + 1) * LANES)
        part = own_acc[b * own_rows:(b + 1) * own_rows, :]
        own_out[:, lanes] = part[:, :LANES] + part[:, LANES:]
        for s in range(sources):
            part = ext_acc[s, b * ext_rows:(b + 1) * ext_rows, :]
            ext_out[s * ext_rows:(s + 1) * ext_rows, lanes] = part[:, :LANES] + part[:, LANES:]


def scatter_obs(levels, rows, lon, starts, own, ext):
    sources = len(ext)
    blocks = lon // LANES
    own_rows, ext_rows = levels * rows, levels * REACH
    vm = pl.BlockSpec(memory_space=pltpu.VMEM)
    args = [starts, *own]
    for pair in ext:
        args += list(pair)
    return pl.pallas_call(
        functools.partial(scatter_kernel, lon, rows, sources),
        out_shape=(
            jax.ShapeDtypeStruct((own_rows, lon), F32),
            jax.ShapeDtypeStruct((sources * ext_rows, lon), F32),
        ),
        in_specs=[pl.BlockSpec(memory_space=pltpu.SMEM)] + [vm] * (len(args) - 1),
        out_specs=(vm, vm),
        scratch_shapes=[
            pltpu.VMEM((blocks * own_rows, 2 * LANES), F32),
            pltpu.VMEM((sources, blocks * ext_rows, 2 * LANES), F32),
        ],
        name="scatter_obs",
    )(*args)


def lon_pass(x, tile):
    lon = x.shape[1]
    half = LANES // 2
    parts = []
    for j in range(lon // LANES):
        lo, hi = j * LANES - half, (j + 1) * LANES + half
        if lo < 0:
            window = jnp.concatenate([x[:, lon + lo:], x[:, :hi]], axis=1)
        elif hi > lon:
            window = jnp.concatenate([x[:, lo:], x[:, :hi - lon]], axis=1)
        else:
            window = x[:, lo:hi]
        parts.append(jnp.dot(window, tile, preferred_element_type=F32).astype(BF16))
    return jnp.concatenate(parts, axis=1)


def filter_kernel(share, own_ref, ext_ref, grad_ref, gext_ref, var_ref, static_ref,
                  tile_ref, lat1_ref, lat2_ref, out_ref):
    step = pl.program_id(0)
    own = own_ref[0].astype(F32)
    ext = ext_ref[0].astype(F32)
    mixed = jnp.concatenate(
        [(own * grad_ref[...]).astype(BF16), (ext * gext_ref[...]).astype(BF16)], axis=0
    )
    tile = tile_ref[...]
    first = lon_pass(mixed, tile)
    first = jnp.dot(lat1_ref[...], first, preferred_element_type=F32).astype(BF16)
    second = lon_pass(first, tile)
    second = jnp.dot(lat2_ref[...], second, preferred_element_type=F32)
    product = own * second * share

    @pl.when(step == 0)
    def _():
        out_ref[...] = static_ref[0] * var_ref[...] * grad_ref[...] + product

    @pl.when(step > 0)
    def _():
        out_ref[...] += product


def filter_members(share, own, ext, grad, gext, variance, static, tile, lat1, lat2):
    members, rows, lon = own.shape
    whole = lambda a: pl.BlockSpec(a.shape, lambda i: (0,) * a.ndim)
    return pl.pallas_call(
        functools.partial(filter_kernel, share),
        grid=(members,),
        out_shape=jax.ShapeDtypeStruct((rows, lon), F32),
        in_specs=[
            pl.BlockSpec((1,) + own.shape[1:], lambda i: (i, 0, 0)),
            pl.BlockSpec((1,) + ext.shape[1:], lambda i: (i, 0, 0)),
            whole(grad), whole(gext), whole(variance),
            pl.BlockSpec(memory_space=pltpu.SMEM),
            whole(tile), whole(lat1), whole(lat2),
        ],
        out_specs=pl.BlockSpec((rows, lon), lambda i: (0, 0)),
        name="filter_members",
    )(own, ext, grad, gext, variance, static, tile, lat1, lat2)


def gather_kernel(lon, precise, field_ref, *refs):
    count = len(precise)
    idx_refs, out_ref, table = refs[:count], refs[count], refs[count + 1]
    rows = field_ref.shape[0]
    blocks = lon // LANES
    for b in range(blocks):
        part = field_ref[:, b * LANES:(b + 1) * LANES]
        turned = jnp.transpose(part)
        hi, lo = split_bf16(turned)
        table[:LANES, b * rows:(b + 1) * rows] = hi
        table[LANES:, b * rows:(b + 1) * rows] = lo
    chunks = idx_refs[0].shape[0]
    for n, (idx_ref, exact) in enumerate(zip(idx_refs, precise)):
        source = table[...] if exact else table[:LANES, :]
        for c in range(chunks):
            idx = idx_ref[c:c + 1, :].astype(jnp.int32)
            blk = (idx % lon) // LANES
            hot = onehot(blk * rows + idx // lon, blocks * rows)
            found = jnp.dot(source, hot, preferred_element_type=F32)
            if exact:
                found = found[:LANES] + found[LANES:]
            spot = lax.broadcasted_iota(jnp.int32, found.shape, 0) == idx % LANES
            value = jnp.sum(jnp.where(spot, found, 0.0), axis=0, keepdims=True)
            out_ref[n * chunks + c:n * chunks + c + 1, :] = value


def gather_places(field, idx_list, precise):
    rows, lon = field.shape
    chunks = idx_list[0].shape[0]
    vm = pl.BlockSpec(memory_space=pltpu.VMEM)
    return pl.pallas_call(
        functools.partial(gather_kernel, lon, tuple(precise)),
        out_shape=jax.ShapeDtypeStruct((len(idx_list) * chunks, lon), F32),
        in_specs=[vm] * (1 + len(idx_list)),
        out_specs=vm,
        scratch_shapes=[pltpu.VMEM((2 * LANES, (lon // LANES) * rows), BF16)],
        name="gather_places",
    )(field, *idx_list)


def partner(count, bit):
    return [(j, j ^ bit) for j in range(count)]


def member_bits(count):
    bits, d = [], 1
    while d < count:
        bits.append(d)
        d *= 2
    assert d == count
    return bits


def sum_members(x, count):
    for bit in member_bits(count):
        x = x + lax.ppermute(x, "member", partner(count, bit))
    return x


def reduce_with_tail(x, tail, count, position):
    rows = x.shape[0]
    for bit in member_bits(count):
        half = rows // 2
        upper = (position // bit) % 2 == 1
        low, high = x[:half], x[half:]
        message = jnp.concatenate([jnp.where(upper, low, high), tail], axis=0)
        message = lax.ppermute(message, "member", partner(count, bit))
        x = jnp.where(upper, high, low) + message[:half]
        tail = tail + message[half:]
        rows = half
    return x, tail


def gather_rows(x, count, position):
    for bit in reversed(member_bits(count)):
        other = lax.ppermute(x, "member", partner(count, bit))
        upper = (position // bit) % 2 == 1
        x = jnp.concatenate([jnp.where(upper, other, x), jnp.where(upper, x, other)], axis=0)
    return x


def from_bands(x, count):
    if count == 2:
        return [lax.ppermute(x, "band", [(0, 1), (1, 0)])]
    up = [(i, i + 1) for i in range(count - 1)]
    down = [(j, i) for i, j in up]
    return [lax.ppermute(x, "band", up), lax.ppermute(x, "band", down)]


def band_halo(ens, count, position):
    rows = ens.shape[2]
    first, last = ens[:, :, :REACH], ens[:, :, rows - REACH:]
    if count == 2:
        edge = jnp.where(position == 0, last, first)
        return [lax.ppermute(edge, "band", [(0, 1), (1, 0)])]
    up = [(i, i + 1) for i in range(count - 1)]
    down = [(j, i) for i, j in up]
    return [lax.ppermute(last, "band", up), lax.ppermute(first, "band", down)]


def local(ensemble, variance, obs_index, obs_value, obs_error, root_ranks):
    members_here, levels, lat_rows, lon = ensemble.shape
    n_member, n_band = lax.axis_size("member"), lax.axis_size("band")
    member_pos, band_pos = lax.axis_index("member"), lax.axis_index("band")
    members = members_here * n_member
    total_rows = lat_rows * n_band
    shape = (obs_index.shape[1] // lon, lon)
    chunks = shape[0]

    if n_band == 2:
        starts = jnp.where(band_pos == 0, 0, lat_rows - REACH).reshape(1)
        near = [jnp.where(band_pos == 0, lat_rows, lat_rows - REACH)]
        near_inner = [jnp.where(band_pos == 0, lat_rows, lat_rows - HALF)]
    else:
        starts = jnp.array([lat_rows - REACH, 0])
        base = band_pos * lat_rows
        near = [base - REACH, base + lat_rows]
        near_inner = [base - HALF, base + lat_rows]
    starts = starts.astype(jnp.int32)

    level_of = jnp.arange(levels)
    def row_list(start, width):
        level = jnp.repeat(level_of, width)
        row = jnp.tile(jnp.arange(width), levels) + start
        return level, row
    own_rows = row_list(band_pos * lat_rows, lat_rows)
    outer = [own_rows] + [row_list(s, REACH) for s in near]
    inner = [own_rows] + [row_list(s, HALF) for s in near_inner]
    join = lambda parts: tuple(jnp.concatenate(p) for p in zip(*parts))
    outer, inner = join(outer), join(inner)
    lat1 = lat_block(*inner, *outer, total_rows, HALF)
    lat2 = lat_block(*own_rows, *inner, total_rows, HALF)
    tile = lon_tile(HALF)

    index = obs_index[0].reshape(shape).astype(F32)
    values = obs_value[0].reshape(shape)
    errors = obs_error[0].reshape(shape)
    weight = huber_edge / jnp.maximum(jnp.abs(values / errors), huber_edge)
    share_0 = weight / (errors * errors)
    block_0 = jnp.concatenate([index, share_0 * values, share_0], axis=0)
    block_1 = jnp.concatenate([index, values, errors], axis=0)
    message = jnp.concatenate(
        [
            jnp.where(member_pos == root_ranks[0], block_0, 0.0),
            jnp.where(member_pos == root_ranks[1], block_1, 0.0),
        ],
        axis=0,
    )
    halo = band_halo(ensemble, n_band, band_pos)
    message = sum_members(message, n_member)
    pieces = lambda a: [a[k * chunks:(k + 1) * chunks] for k in range(6)]
    index_0, coef_0, share_0, index_1, value_1, error_1 = pieces(message)
    near_parts = [pieces(a) for a in from_bands(message, n_band)]

    own = ensemble.reshape(members_here, levels * lat_rows, lon)
    ext = jnp.concatenate([h.reshape(members_here, levels * REACH, lon) for h in halo], axis=1)
    variance = variance.reshape(levels * lat_rows, lon)
    static = jnp.where(member_pos == 0, static_share, 0.0).reshape(1).astype(F32)
    share = ensemble_share / (members - 1)

    def direction_part(own_obs, ext_obs):
        grad, gext = scatter_obs(levels, lat_rows, lon, starts, own_obs, ext_obs)
        return filter_members(share, own, ext, grad, gext, variance, static, tile, lat1, lat2)

    part = direction_part((index_0, coef_0), [(p[0], p[1]) for p in near_parts])
    reached = gather_places(part, [index_0, index_1], [True, True])
    slice_0, reached = reduce_with_tail(part, reached, n_member, member_pos)
    reached_0, reached_1 = reached[:chunks], reached[chunks:]
    along = jnp.sum(coef_0 * reached_0)
    curve = jnp.sum(share_0 * reached_0 * reached_0)

    def band_sum(pair, extra):
        sums = jnp.broadcast_to(pair[:, None], (2, lon))
        text = jnp.concatenate([sums] + extra, axis=0)
        if n_band == 2:
            other = from_bands(text, n_band)
            return pair + other[0][:2, 0], [o[2:] for o in other]
        other = from_bands(text, n_band) if extra else []
        return lax.psum(pair, "band"), [o[2:] for o in other]

    (along, curve), near_reached = band_sum(jnp.stack([along, curve]), [reached_1])
    scale_0 = along / (along + curve)

    def weigh(at_place, value, error):
        departure = value - at_place
        weight = huber_edge / jnp.maximum(jnp.abs(departure / error), huber_edge)
        share = weight / (error * error)
        return share * departure, share

    field_1 = scale_0 * reached_1
    coef_1, share_1 = weigh(field_1, value_1, error_1)
    ext_obs = [
        (p[3], weigh(scale_0 * r, p[4], jnp.where(p[5] > 0, p[5], 1.0))[0])
        for p, r in zip(near_parts, near_reached)
    ]
    part = direction_part((index_1, coef_1), ext_obs)
    reached = gather_places(part, [index_1], [True])
    slice_1, reached = reduce_with_tail(part, reached, n_member, member_pos)
    along = jnp.sum(coef_1 * (reached - field_1))
    curve_along = jnp.sum(coef_1 * reached) + jnp.sum(share_1 * reached * reached)
    (along, curve_along), _ = band_sum(jnp.stack([along, curve_along]), [])
    scale_1 = along / curve_along
    out = scale_0 * slice_0 + scale_1 * slice_1
    out = gather_rows(out, n_member, member_pos)
    return out.reshape(levels, lat_rows, lon)


def solution(mesh):
    in_specs = (
        P("member", None, "band", None),
        P(None, "band", None),
        P("member", "band"),
        P("member", "band"),
        P("member", "band"),
        P(),
    )
    out_specs = P(None, "band", None)
    return jax.shard_map(local, mesh=mesh, in_specs=in_specs, out_specs=out_specs, check_vma=False)
```

time: 617 us -> 164 us (0.27)
  waiting for transfers between devices: 229 us -> 57.9 us
  blocking collectives: 156 us -> 0 us
  local copies, waits for them, and re-layouts: 101 us -> 5.37 us
  Pallas kernels: 0 us -> 44.5 us
  other arithmetic: 60.5 us -> 18.1 us
  matrix products: 30.9 us -> 0 us
  between operations: 21.9 us -> 6.95 us
  starting transfers between devices: 15.8 us -> 30.5 us
    psum x3 -> x0, waiting for transfers between devices: 179 us -> none  [the longest x2 178 us: local(): summed = lax.psum(spread, 'member')]
    psum x5 -> x0, blocking collectives: 156 us -> none  [the longest x2 81.3 us: local(): curve = lax.psum(is_root * curve_local, ('band', 'member'))]
    gather x4 -> x0, local copies, waits for them, and re-layouts: 92.1 us -> none  [the longest x2 46.1 us: make_gradient(): departure = values - field.reshape(-1)[positions]]
    scatter-add x2 -> x0, other arithmetic: 44.7 us -> none  [make_gradient(): flat = jnp.zeros((field.size,), jnp.float32).at[positions].add(weight * d...]
    pallas_call x0 -> x6, Pallas kernels: none -> 44.5 us  [the longest x2 21.7 us: filter_members(): pl.pallas_call(functools.partial(filter_kernel, share), grid=(members,),...]
    dot_general x6 -> x0, matrix products: 30.9 us -> none  [the longest x2 15.2 us: local(): jnp.dot(first, lon_matrix, preferred_element_type=jnp.float32)]
    ppermute x8 -> x20, starting transfers between devices: 15.5 us -> 30.5 us  [the longest x8 13.4 us: reduce_with_tail(): message = lax.ppermute(message, 'member', partner(count, bit))]
    reduce_sum x7 -> x2, other arithmetic: 10 us -> 1.3 us  [the longest x1 0.69 us: local(): along = jnp.sum(coef_1 * (reached - field_1))]
  transfers between devices with their start and end apart: 11 -> 20, of which waited for: 11 -> 18; matrix products, arithmetic and copies ran while one was open for 4% -> 5% of each run, Pallas kernels for 0% -> 4%
where the time goes in v1:
time: 164 us; the launch traced here: 163 us
  waiting for transfers between devices  57.9 us (35%)
  Pallas kernels  44.5 us (27%)
  starting transfers between devices  30.5 us (19%)
  other arithmetic  18.1 us (11%)
  between operations  6.95 us (4%)
  local copies, waits for them, and re-layouts  5.37 us (3%)
    ppermute x8, waiting for transfers between devices, reduce_with_tail(): message = lax.ppermute(message, 'member', partner(count, bit))  22.5 us
    pallas_call x2, Pallas kernels, filter_members(): pl.pallas_call(functools.partial(filter_kernel, share), grid=(members,),...  21.7 us
    ppermute x3, waiting for transfers between devices, from_bands(): return [lax.ppermute(x, 'band', [(0, 1), (1, 0)])]  17.9 us
    ppermute x8, starting transfers between devices, reduce_with_tail(): message = lax.ppermute(message, 'member', partner(count, bit))  13.4 us
    pallas_call x2, Pallas kernels, scatter_obs(): pl.pallas_call(functools.partial(scatter_kernel, lon, rows, sources), out...  11.8 us
    pallas_call x2, Pallas kernels, gather_places(): pl.pallas_call(functools.partial(gather_kernel, lon, tuple(precise)), out...  11 us
    ppermute x4, waiting for transfers between devices, gather_rows(): other = lax.ppermute(x, 'member', partner(count, bit))  9.36 us
    ppermute x4, waiting for transfers between devices, sum_members(): x = x + lax.ppermute(x, 'member', partner(count, bit))  8.1 us
  transfers between devices with their start and end apart: 20, of which 18 were waited for; matrix products, arithmetic and copies ran while one was open for 5% of the time, Pallas kernels for 4%

profile of v1, /device:TPU:0, one launch (start us, length us, event | category | flops | bytes accessed | tf_op | source)
XLA Modules:
  0.0 163.3 jit_solution(8027365543771101980)
XLA Ops:
  0.0 1.7 %slice_select_fusion = bf16[8,4,16,1024]{3,2,1,0:T(8,128)(2,1)S(1)} fusion(bf16[8,4,32,1024]{3,2,1,0:T(8,128)(2,1)} %param.6, pred[]{:T(512)S(6)} %eq.80), kind=kLoop, calls=%fused_computation | loop fusion | flops 524288 | bytes 3145729 | tf_op jit(solution)/shard_map/jit(_where)/select_n | solution.py:283
  1.7 3.1 %collective-permute-start.4 = (bf16[8,4,16,1024]{3,2,1,0:T(8,128)(2,1)S(1)}, bf16[8,4,16,1024]{3,2,1,0:T(8,128)(2,1)S(1)}, u32[]{:S(2)}, u32[]{:S(2)}) collective-permute-start(bf16[8,4,16,1024]{3,2,1,0:T(8,128)(2,1)S(1)} %slice_select_fusion), channel_id=1, source_target_pairs={{0,16},{16,0},{1,17},{17,1},{2,18},{18,2},{3,19},{19,3},{4,20},{20... | collective-permute-start | bytes 3145736 | tf_op jit(solution)/shard_map/ppermute | solution.py:284
  5.4 0.7 reduce.13
  6.1 0.7 reduce.12
  6.8 0.7 fusion.33
  9.0 0.6 multiply_reduce_fusion.3
  10.9 1.0 select_convert_fusion.tile_ref
  12.0 1.6 collective-permute-start.1
  13.5 0.8 and_select_fusion.lat1_ref
  14.3 2.9 %collective-permute-done.1 = f32[24,1024]{1,0:T(8,128)S(1)} collective-permute-done((f32[24,1024]{1,0:T(8,128)S(1)}, f32[24,1024]{1,0:T(8,128)S(1)}, u32[]{:S(2)}, u32[]{:S(2)}) %collective-permute-start.1) | collective-permute-done | bytes 98336 | tf_op jit(solution)/shard_map/ppermute | solution.py:245
  17.2 1.6 %collective-permute-start.2 = (f32[24,1024]{1,0:T(8,128)S(1)}, f32[24,1024]{1,0:T(8,128)S(1)}, u32[]{:S(2)}, u32[]{:S(2)}) collective-permute-start(f32[24,1024]{1,0:T(8,128)S(1)} %add.156), channel_id=1, source_target_pairs={{0,4},{1,5},{2,6},{3,7},{4,0},{5,1},{6,2},{7,3},{8,12},{9,13},{10,... | collective-permute-start | bytes 294920 | tf_op jit(solution)/shard_map/ppermute | solution.py:245
  18.9 3.0 %collective-permute-done.2 = f32[24,1024]{1,0:T(8,128)S(1)} collective-permute-done((f32[24,1024]{1,0:T(8,128)S(1)}, f32[24,1024]{1,0:T(8,128)S(1)}, u32[]{:S(2)}, u32[]{:S(2)}) %collective-permute-start.2) | collective-permute-done | bytes 98336 | tf_op jit(solution)/shard_map/ppermute | solution.py:245
  21.9 2.7 %collective-permute-start.3 = (f32[24,1024]{1,0:T(8,128)S(1)}, f32[24,1024]{1,0:T(8,128)S(1)}, u32[]{:S(2)}, u32[]{:S(2)}) collective-permute-start(f32[24,1024]{1,0:T(8,128)S(1)} %add.157), channel_id=1, source_target_pairs={{0,8},{1,9},{2,10},{3,11},{4,12},{5,13},{6,14},{7,15},{8,0},{9,1},... | collective-permute-start | bytes 294920 | tf_op jit(solution)/shard_map/ppermute | solution.py:245
  24.6 0.8 and_select_fusion.1.lat2_ref
  25.4 2.2 %collective-permute-done.3 = f32[24,1024]{1,0:T(8,128)S(1)} collective-permute-done((f32[24,1024]{1,0:T(8,128)S(1)}, f32[24,1024]{1,0:T(8,128)S(1)}, u32[]{:S(2)}, u32[]{:S(2)}) %collective-permute-start.3) | collective-permute-done | bytes 98336 | tf_op jit(solution)/shard_map/ppermute | solution.py:245
  28.0 0.6 fusion.30
  28.6 3.6 %collective-permute-done.5 = f32[24,1024]{1,0:T(8,128)S(1)} collective-permute-done((f32[24,1024]{1,0:T(8,128)S(1)}, f32[24,1024]{1,0:T(8,128)S(1)}, u32[]{:S(2)}, u32[]{:S(2)}) %collective-permute-start.5) | collective-permute-done | bytes 98336 | tf_op jit(solution)/shard_map/ppermute | solution.py:273
  32.2 0.6 fusion.29
  32.8 5.9 %scatter_obs.2 = (f32[128,1024]{1,0:T(8,128)}, f32[64,1024]{1,0:T(8,128)}) custom-call(s32[1]{0:T(128)} %bitcast.4.refs_0_, f32[4,1024]{1,0:T(4,128)} %get-tuple-element.34.refs_1_.refs_0_, f32[4,1024]{1,0:T(4,128)} %get-tuple-element.32.refs_2_, f32[4,1024]{1,0:T(4,128)} %get-tuple-element.31.refs_3_, f32[4,1024]{1,0:T(4,128)} %get-tuple-element.30.refs_4_), custom_call_target="tpu_custom_call" | custom-call | tf_op jit(solution)/shard_map/scatter_obs/pallas_call | solution.py:115
  38.7 1.0 copy-done.2
  39.7 10.9 %filter_members.2.field_ref = f32[128,1024]{1,0:T(8,128)} custom-call(bf16[8,128,1024]{2,1,0:T(8,128)(2,1)} %bitcast.19, bf16[8,64,1024]{2,1,0:T(8,128)(2,1)} %bitcast.21, f32[128,1024]{1,0:T(8,128)} %get-tuple-element.9.grad_ref, f32[64,1024]{1,0:T(8,128)} %get-tuple-element.10.gext_ref, f32[128,1024]{1,0:T(8,128)} %bitcast.23, f32[1]{0:T(128)} %bitcast.6.static_ref, ...), custom_call_target="tpu_custom_call" | custom-call | tf_op jit(solution)/shard_map/filter_members/pallas_call | solution.py:174
  50.6 6.7 %gather_places.2 = f32[8,1024]{1,0:T(8,128)} custom-call(f32[128,1024]{1,0:T(8,128)} %filter_members.2.field_ref, f32[4,1024]{1,0:T(4,128)} %get-tuple-element.34.refs_1_.refs_0_, f32[4,1024]{1,0:T(4,128)} %get-tuple-element.33.refs_1_.refs_0_), custom_call_target="tpu_custom_call" | custom-call | tf_op jit(solution)/shard_map/gather_places/pallas_call | solution.py:220
  57.3 1.1 slice_select_fusion.2
  58.4 0.8 pad_maximum_fusion.1
  59.3 1.5 collective-permute-done.6
  60.9 1.5 collective-permute-start.7
  62.5 4.8 %collective-permute-done.7 = f32[40,1024]{1,0:T(8,128)S(1)} collective-permute-done((f32[40,1024]{1,0:T(8,128)S(1)}, f32[40,1024]{1,0:T(8,128)S(1)}, u32[]{:S(2)}, u32[]{:S(2)}) %collective-permute-start.7) | collective-permute-done | bytes 163872 | tf_op jit(solution)/shard_map/ppermute | solution.py:256
  67.3 1.8 %collective-permute-start.8 = (f32[24,1024]{1,0:T(8,128)S(1)}, f32[24,1024]{1,0:T(8,128)S(1)}, u32[]{:S(2)}, u32[]{:S(2)}) collective-permute-start(f32[24,1024]{1,0:T(8,128)S(1)} %pad_maximum_fusion.8), channel_id=1, source_target_pairs={{0,4},{1,5},{2,6},{3,7},{4,0},{5,1},{6,2},{7,3},{8,12},{9,13},{10,... | collective-permute-start | bytes 294920 | tf_op jit(solution)/shard_map/ppermute | solution.py:256
  69.1 2.9 %collective-permute-done.8 = f32[24,1024]{1,0:T(8,128)S(1)} collective-permute-done((f32[24,1024]{1,0:T(8,128)S(1)}, f32[24,1024]{1,0:T(8,128)S(1)}, u32[]{:S(2)}, u32[]{:S(2)}) %collective-permute-start.8) | collective-permute-done | bytes 98336 | tf_op jit(solution)/shard_map/ppermute | solution.py:256
  72.0 3.1 %collective-permute-start.9 = (f32[16,1024]{1,0:T(8,128)S(1)}, f32[16,1024]{1,0:T(8,128)S(1)}, u32[]{:S(2)}, u32[]{:S(2)}) collective-permute-start(f32[16,1024]{1,0:T(8,128)S(1)} %pad_maximum_fusion.12), channel_id=1, source_target_pairs={{0,8},{1,9},{2,10},{3,11},{4,12},{5,13},{6,14},{7,15},{8,0},{9,1},... | collective-permute-start | bytes 196616 | tf_op jit(solution)/shard_map/ppermute | solution.py:256
  75.2 2.2 %collective-permute-done.9 = f32[16,1024]{1,0:T(8,128)S(1)} collective-permute-done((f32[16,1024]{1,0:T(8,128)S(1)}, f32[16,1024]{1,0:T(8,128)S(1)}, u32[]{:S(2)}, u32[]{:S(2)}) %collective-permute-start.9) | collective-permute-done | bytes 65568 | tf_op jit(solution)/shard_map/ppermute | solution.py:256
  77.4 0.6 multiply_reduce_fusion.2
  78.0 1.3 pad_maximum_fusion.16
  79.9 3.4 %collective-permute-done.10 = f32[6,1024]{1,0:T(8,128)S(1)} collective-permute-done((f32[6,1024]{1,0:T(8,128)S(1)}, f32[6,1024]{1,0:T(8,128)S(1)}, u32[]{:S(2)}, u32[]{:S(2)}) %collective-permute-start.10) | collective-permute-done | bytes 24608 | tf_op jit(solution)/shard_map/ppermute | solution.py:273
  83.4 1.3 fusion.34
  84.7 0.6 fusion.32
  87.1 0.6 fusion.26
  87.7 0.6 divide_multiply_fusion
  88.4 5.9 %scatter_obs.3 = (f32[128,1024]{1,0:T(8,128)}, f32[64,1024]{1,0:T(8,128)}) custom-call(s32[1]{0:T(128)} %bitcast.4.refs_0_, f32[4,1024]{1,0:T(4,128)} %get-tuple-element.33.refs_1_.refs_0_, f32[4,1024]{1,0:T(4,128)} %get-tuple-element.18.refs_2_, f32[4,1024]{1,0:T(4,128)} %get-tuple-element.29.refs_3_, f32[4,1024]{1,0:T(4,128)} %get-tuple-element.28.refs_4_), custom_call_target="tpu_custom_call" | custom-call | tf_op jit(solution)/shard_map/scatter_obs/pallas_call | solution.py:115
  94.3 10.9 %filter_members.3.field_ref = f32[128,1024]{1,0:T(8,128)} custom-call(bf16[8,128,1024]{2,1,0:T(8,128)(2,1)} %bitcast.20, bf16[8,64,1024]{2,1,0:T(8,128)(2,1)} %bitcast.22, f32[128,1024]{1,0:T(8,128)} %get-tuple-element.11.grad_ref, f32[64,1024]{1,0:T(8,128)} %get-tuple-element.12.gext_ref, f32[128,1024]{1,0:T(8,128)} %bitcast.24, f32[1]{0:T(128)} %bitcast.6.static_ref, ...), custom_call_target="tpu_custom_call" | custom-call | tf_op jit(solution)/shard_map/filter_members/pallas_call | solution.py:174
  105.2 4.3 %gather_places.3 = f32[4,1024]{1,0:T(4,128)} custom-call(f32[128,1024]{1,0:T(8,128)} %filter_members.3.field_ref, f32[4,1024]{1,0:T(4,128)} %get-tuple-element.33.refs_1_.refs_0_), custom_call_target="tpu_custom_call" | custom-call | tf_op jit(solution)/shard_map/gather_places/pallas_call | solution.py:220
  109.5 1.1 slice_select_fusion.1
  110.5 0.7 pad_maximum_fusion.2
  111.4 1.6 collective-permute-done.11
  113.1 1.6 collective-permute-start.12
  114.7 4.7 %collective-permute-done.12 = f32[36,1024]{1,0:T(8,128)S(1)} collective-permute-done((f32[36,1024]{1,0:T(8,128)S(1)}, f32[36,1024]{1,0:T(8,128)S(1)}, u32[]{:S(2)}, u32[]{:S(2)}) %collective-permute-start.12) | collective-permute-done | bytes 147488 | tf_op jit(solution)/shard_map/ppermute | solution.py:256
  119.4 2.1 %collective-permute-start.13 = (f32[20,1024]{1,0:T(8,128)S(1)}, f32[20,1024]{1,0:T(8,128)S(1)}, u32[]{:S(2)}, u32[]{:S(2)}) collective-permute-start(f32[20,1024]{1,0:T(8,128)S(1)} %pad_maximum_fusion.9), channel_id=1, source_target_pairs={{0,4},{1,5},{2,6},{3,7},{4,0},{5,1},{6,2},{7,3},{8,12},{9,13},{10,... | collective-permute-start | bytes 245768 | tf_op jit(solution)/shard_map/ppermute | solution.py:256
  121.6 2.6 %collective-permute-done.13 = f32[20,1024]{1,0:T(8,128)S(1)} collective-permute-done((f32[20,1024]{1,0:T(8,128)S(1)}, f32[20,1024]{1,0:T(8,128)S(1)}, u32[]{:S(2)}, u32[]{:S(2)}) %collective-permute-start.13) | collective-permute-done | bytes 81952 | tf_op jit(solution)/shard_map/ppermute | solution.py:256
  124.2 3.1 %collective-permute-start.14 = (f32[12,1024]{1,0:T(8,128)S(1)}, f32[12,1024]{1,0:T(8,128)S(1)}, u32[]{:S(2)}, u32[]{:S(2)}) collective-permute-start(f32[12,1024]{1,0:T(8,128)S(1)} %pad_maximum_fusion.13), channel_id=1, source_target_pairs={{0,8},{1,9},{2,10},{3,11},{4,12},{5,13},{6,14},{7,15},{8,0},{9,1},... | collective-permute-start | bytes 147464 | tf_op jit(solution)/shard_map/ppermute | solution.py:256
  127.3 2.2 %collective-permute-done.14 = f32[12,1024]{1,0:T(8,128)S(1)} collective-permute-done((f32[12,1024]{1,0:T(8,128)S(1)}, f32[12,1024]{1,0:T(8,128)S(1)}, u32[]{:S(2)}, u32[]{:S(2)}) %collective-permute-start.14) | collective-permute-done | bytes 49184 | tf_op jit(solution)/shard_map/ppermute | solution.py:256
  129.6 0.7 multiply_reduce_fusion.1
  131.5 0.7 pad_maximum_fusion.17
  132.3 0.6 collective-permute-start.15
  132.9 10.9 %collective-permute-done.15 = f32[2,1024]{0,1:T(8,128)S(1)} collective-permute-done((f32[2,1024]{0,1:T(8,128)S(1)}, f32[2,1024]{0,1:T(8,128)S(1)}, u32[]{:S(2)}, u32[]{:S(2)}) %collective-permute-start.15) | collective-permute-done | bytes 8224 | tf_op jit(solution)/shard_map/ppermute | solution.py:273
  143.7 0.7 fusion.27
  144.5 0.6 fusion.31
  146.5 2.7 %collective-permute-start.16 = (f32[8,1024]{1,0:T(8,128)S(1)}, f32[8,1024]{1,0:T(8,128)S(1)}, u32[]{:S(2)}, u32[]{:S(2)}) collective-permute-start(f32[8,1024]{1,0:T(8,128)S(1)} %fusion.21), channel_id=1, source_target_pairs={{0,8},{1,9},{2,10},{3,11},{4,12},{5,13},{6,14},{7,15},{8,0},{9,1},... | collective-permute-start | bytes 98312 | tf_op jit(solution)/shard_map/ppermute | solution.py:265
  149.2 2.1 %collective-permute-done.16 = f32[8,1024]{1,0:T(8,128)S(1)} collective-permute-done((f32[8,1024]{1,0:T(8,128)S(1)}, f32[8,1024]{1,0:T(8,128)S(1)}, u32[]{:S(2)}, u32[]{:S(2)}) %collective-permute-start.16) | collective-permute-done | bytes 32800 | tf_op jit(solution)/shard_map/ppermute | solution.py:265
  151.4 2.1 %collective-permute-start.17 = (f32[16,1024]{1,0:T(8,128)S(1)}, f32[16,1024]{1,0:T(8,128)S(1)}, u32[]{:S(2)}, u32[]{:S(2)}) collective-permute-start(f32[16,1024]{1,0:T(8,128)S(1)} %pad_maximum_fusion.14), channel_id=1, source_target_pairs={{0,4},{1,5},{2,6},{3,7},{4,0},{5,1},{6,2},{7,3},{8,12},{9,13},{10,... | collective-permute-start | bytes 196616 | tf_op jit(solution)/shard_map/ppermute | solution.py:265
  153.5 2.2 %collective-permute-done.17 = f32[16,1024]{1,0:T(8,128)S(1)} collective-permute-done((f32[16,1024]{1,0:T(8,128)S(1)}, f32[16,1024]{1,0:T(8,128)S(1)}, u32[]{:S(2)}, u32[]{:S(2)}) %collective-permute-start.17) | collective-permute-done | bytes 65568 | tf_op jit(solution)/shard_map/ppermute | solution.py:265
  155.8 1.6 collective-permute-start.18
  157.3 3.5 %collective-permute-done.18 = f32[32,1024]{1,0:T(8,128)S(1)} collective-permute-done((f32[32,1024]{1,0:T(8,128)S(1)}, f32[32,1024]{1,0:T(8,128)S(1)}, u32[]{:S(2)}, u32[]{:S(2)}) %collective-permute-start.18) | collective-permute-done | bytes 131104 | tf_op jit(solution)/shard_map/ppermute | solution.py:265
  160.9 1.5 collective-permute-done.19
  162.5 0.8 pad_maximum_fusion
  (97 shorter events, 3.3 us)
Async XLA Ops:
  0.0 4.8 %copy-start.6 = (s32[1,4096]{1,0:T(1,128)S(1)}, s32[1,4096]{1,0:T(1,128)}, u32[]{:S(2)}) copy-start(s32[1,4096]{1,0:T(1,128)} %param.8) | copy-start | bytes 49156
  0.0 5.4 %copy-start.7 = (f32[1,4096]{1,0:T(1,128)S(1)}, f32[1,4096]{1,0:T(1,128)}, u32[]{:S(2)}) copy-start(f32[1,4096]{1,0:T(1,128)} %param.9) | copy-start | bytes 49156
  0.0 6.1 %copy-start.8 = (f32[1,4096]{1,0:T(1,128)S(1)}, f32[1,4096]{1,0:T(1,128)}, u32[]{:S(2)}) copy-start(f32[1,4096]{1,0:T(1,128)} %param.10) | copy-start | bytes 49156
  0.0 6.8 %copy-start.9 = (s32[2]{0:T(128)S(1)}, s32[2]{0:T(128)}, u32[]{:S(2)}) copy-start(s32[2]{0:T(128)} %param.11) | copy-start | bytes 28
  1.7 37.0 %collective-permute-start.4 = (bf16[8,4,16,1024]{3,2,1,0:T(8,128)(2,1)S(1)}, bf16[8,4,16,1024]{3,2,1,0:T(8,128)(2,1)S(1)}, u32[]{:S(2)}, u32[]{:S(2)}) collective-permute-start(bf16[8,4,16,1024]{3,2,1,0:T(8,128)(2,1)S(1)} %slice_select_fusion), channel_id=1, source_target_pairs={{0,16},{16,0},{1,17},{17,1},{2,18},{18,2},{3,19},{19,3},{4,20},{20... | collective-permute-start | bytes 3145736 | tf_op jit(solution)/shard_map/ppermute | solution.py:284
  8.9 3.0 %collective-permute-start = (f32[24,1024]{1,0:T(8,128)S(1)}, f32[24,1024]{1,0:T(8,128)S(1)}, u32[]{:S(2)}, u32[]{:S(2)}) collective-permute-start(f32[24,1024]{1,0:T(8,128)S(1)} %pad_maximum_fusion.7), channel_id=1, source_target_pairs={{0,1},{1,0},{2,3},{3,2},{4,5},{5,4},{6,7},{7,6},{8,9},{9,8},{10,11... | collective-permute-start | bytes 294920 | tf_op jit(solution)/shard_map/ppermute | solution.py:245
  12.0 5.3 %collective-permute-start.1 = (f32[24,1024]{1,0:T(8,128)S(1)}, f32[24,1024]{1,0:T(8,128)S(1)}, u32[]{:S(2)}, u32[]{:S(2)}) collective-permute-start(f32[24,1024]{1,0:T(8,128)S(1)} %fusion.35), channel_id=1, source_target_pairs={{0,2},{1,3},{2,0},{3,1},{4,6},{5,7},{6,4},{7,5},{8,10},{9,11},{10,... | collective-permute-start | bytes 294920 | tf_op jit(solution)/shard_map/ppermute | solution.py:245
  17.2 4.7 %collective-permute-start.2 = (f32[24,1024]{1,0:T(8,128)S(1)}, f32[24,1024]{1,0:T(8,128)S(1)}, u32[]{:S(2)}, u32[]{:S(2)}) collective-permute-start(f32[24,1024]{1,0:T(8,128)S(1)} %add.156), channel_id=1, source_target_pairs={{0,4},{1,5},{2,6},{3,7},{4,0},{5,1},{6,2},{7,3},{8,12},{9,13},{10,... | collective-permute-start | bytes 294920 | tf_op jit(solution)/shard_map/ppermute | solution.py:245
  21.9 5.6 %collective-permute-start.3 = (f32[24,1024]{1,0:T(8,128)S(1)}, f32[24,1024]{1,0:T(8,128)S(1)}, u32[]{:S(2)}, u32[]{:S(2)}) collective-permute-start(f32[24,1024]{1,0:T(8,128)S(1)} %add.157), channel_id=1, source_target_pairs={{0,8},{1,9},{2,10},{3,11},{4,12},{5,13},{6,14},{7,15},{8,0},{9,1},... | collective-permute-start | bytes 294920 | tf_op jit(solution)/shard_map/ppermute | solution.py:245
  27.5 4.7 %collective-permute-start.5 = (f32[24,1024]{1,0:T(8,128)S(1)}, f32[24,1024]{1,0:T(8,128)S(1)}, u32[]{:S(2)}, u32[]{:S(2)}) collective-permute-start(f32[24,1024]{1,0:T(8,128)S(1)} %add.158), channel_id=1, source_target_pairs={{0,16},{16,0},{1,17},{17,1},{2,18},{18,2},{3,19},{19,3},{4,20},{20... | collective-permute-start | bytes 294920 | tf_op jit(solution)/shard_map/ppermute | solution.py:273
  38.7 1.0 copy-start.2
  50.6 10.2 %copy-start = (f32[128,1024]{1,0:T(8,128)S(1)}, f32[128,1024]{1,0:T(8,128)}, u32[]{:S(2)}) copy-start(f32[128,1024]{1,0:T(8,128)} %filter_members.2.field_ref) | copy-start | bytes 1572868
  57.3 3.6 %copy-start.3 = (f32[8,1024]{1,0:T(8,128)S(1)}, f32[8,1024]{1,0:T(8,128)}, u32[]{:S(2)}) copy-start(f32[8,1024]{1,0:T(8,128)} %gather_places.2) | copy-start | bytes 98308
  59.1 1.6 %collective-permute-start.6 = (f32[72,1024]{1,0:T(8,128)S(1)}, f32[72,1024]{1,0:T(8,128)S(1)}, u32[]{:S(2)}, u32[]{:S(2)}) collective-permute-start(f32[72,1024]{1,0:T(8,128)S(1)} %pad_maximum_fusion.1), channel_id=1, source_target_pairs={{0,1},{1,0},{2,3},{3,2},{4,5},{5,4},{6,7},{7,6},{8,9},{9,8},{10,11... | collective-permute-start | bytes 884744 | tf_op jit(solution)/shard_map/ppermute | solution.py:256
  60.9 6.3 %collective-permute-start.7 = (f32[40,1024]{1,0:T(8,128)S(1)}, f32[40,1024]{1,0:T(8,128)S(1)}, u32[]{:S(2)}, u32[]{:S(2)}) collective-permute-start(f32[40,1024]{1,0:T(8,128)S(1)} %pad_maximum_fusion.4), channel_id=1, source_target_pairs={{0,2},{1,3},{2,0},{3,1},{4,6},{5,7},{6,4},{7,5},{8,10},{9,11},{10,... | collective-permute-start | bytes 491528 | tf_op jit(solution)/shard_map/ppermute | solution.py:256
  67.3 4.7 %collective-permute-start.8 = (f32[24,1024]{1,0:T(8,128)S(1)}, f32[24,1024]{1,0:T(8,128)S(1)}, u32[]{:S(2)}, u32[]{:S(2)}) collective-permute-start(f32[24,1024]{1,0:T(8,128)S(1)} %pad_maximum_fusion.8), channel_id=1, source_target_pairs={{0,4},{1,5},{2,6},{3,7},{4,0},{5,1},{6,2},{7,3},{8,12},{9,13},{10,... | collective-permute-start | bytes 294920 | tf_op jit(solution)/shard_map/ppermute | solution.py:256
  72.0 5.4 %collective-permute-start.9 = (f32[16,1024]{1,0:T(8,128)S(1)}, f32[16,1024]{1,0:T(8,128)S(1)}, u32[]{:S(2)}, u32[]{:S(2)}) collective-permute-start(f32[16,1024]{1,0:T(8,128)S(1)} %pad_maximum_fusion.12), channel_id=1, source_target_pairs={{0,8},{1,9},{2,10},{3,11},{4,12},{5,13},{6,14},{7,15},{8,0},{9,1},... | collective-permute-start | bytes 196616 | tf_op jit(solution)/shard_map/ppermute | solution.py:256
  79.4 3.9 %collective-permute-start.10 = (f32[6,1024]{1,0:T(8,128)S(1)}, f32[6,1024]{1,0:T(8,128)S(1)}, u32[]{:S(2)}, u32[]{:S(2)}) collective-permute-start(f32[6,1024]{1,0:T(8,128)S(1)} %pad_maximum_fusion.15), channel_id=1, source_target_pairs={{0,16},{16,0},{1,17},{17,1},{2,18},{18,2},{3,19},{19,3},{4,20},{20... | collective-permute-start | bytes 73736 | tf_op jit(solution)/shard_map/ppermute | solution.py:273
  105.2 7.8 %copy-start.1 = (f32[128,1024]{1,0:T(8,128)S(1)}, f32[128,1024]{1,0:T(8,128)}, u32[]{:S(2)}) copy-start(f32[128,1024]{1,0:T(8,128)} %filter_members.3.field_ref) | copy-start | bytes 1572868
  109.4 3.6 %copy-start.4 = (f32[4,1024]{1,0:T(4,128)S(1)}, f32[4,1024]{1,0:T(4,128)}, u32[]{:S(2)}) copy-start(f32[4,1024]{1,0:T(4,128)} %gather_places.3) | copy-start | bytes 49156
  110.5 19.1 %copy-start.5 = (f32[4,1024]{1,0:T(4,128)S(1)}, f32[4,1024]{1,0:T(4,128)}, u32[]{:S(2)}) copy-start(f32[4,1024]{1,0:T(4,128)} %get-tuple-element.18.refs_2_) | copy-start | bytes 49156
  111.3 1.6 %collective-permute-start.11 = (f32[68,1024]{1,0:T(8,128)S(1)}, f32[68,1024]{1,0:T(8,128)S(1)}, u32[]{:S(2)}, u32[]{:S(2)}) collective-permute-start(f32[68,1024]{1,0:T(8,128)S(1)} %pad_maximum_fusion.2), channel_id=1, source_target_pairs={{0,1},{1,0},{2,3},{3,2},{4,5},{5,4},{6,7},{7,6},{8,9},{9,8},{10,11... | collective-permute-start | bytes 835592 | tf_op jit(solution)/shard_map/ppermute | solution.py:256
  113.1 6.3 %collective-permute-start.12 = (f32[36,1024]{1,0:T(8,128)S(1)}, f32[36,1024]{1,0:T(8,128)S(1)}, u32[]{:S(2)}, u32[]{:S(2)}) collective-permute-start(f32[36,1024]{1,0:T(8,128)S(1)} %pad_maximum_fusion.5), channel_id=1, source_target_pairs={{0,2},{1,3},{2,0},{3,1},{4,6},{5,7},{6,4},{7,5},{8,10},{9,11},{10,... | collective-permute-start | bytes 442376 | tf_op jit(solution)/shard_map/ppermute | solution.py:256
  119.4 4.7 %collective-permute-start.13 = (f32[20,1024]{1,0:T(8,128)S(1)}, f32[20,1024]{1,0:T(8,128)S(1)}, u32[]{:S(2)}, u32[]{:S(2)}) collective-permute-start(f32[20,1024]{1,0:T(8,128)S(1)} %pad_maximum_fusion.9), channel_id=1, source_target_pairs={{0,4},{1,5},{2,6},{3,7},{4,0},{5,1},{6,2},{7,3},{8,12},{9,13},{10,... | collective-permute-start | bytes 245768 | tf_op jit(solution)/shard_map/ppermute | solution.py:256
  124.2 5.4 %collective-permute-start.14 = (f32[12,1024]{1,0:T(8,128)S(1)}, f32[12,1024]{1,0:T(8,128)S(1)}, u32[]{:S(2)}, u32[]{:S(2)}) collective-permute-start(f32[12,1024]{1,0:T(8,128)S(1)} %pad_maximum_fusion.13), channel_id=1, source_target_pairs={{0,8},{1,9},{2,10},{3,11},{4,12},{5,13},{6,14},{7,15},{8,0},{9,1},... | collective-permute-start | bytes 147464 | tf_op jit(solution)/shard_map/ppermute | solution.py:256
  132.3 11.4 %collective-permute-start.15 = (f32[2,1024]{0,1:T(8,128)S(1)}, f32[2,1024]{0,1:T(8,128)S(1)}, u32[]{:S(2)}, u32[]{:S(2)}) collective-permute-start(f32[2,1024]{0,1:T(8,128)S(1)} %broadcast_in_dim.76), channel_id=1, source_target_pairs={{0,16},{16,0},{1,17},{17,1},{2,18},{18,2},{3,19},{19,3},{4,20},{20... | collective-permute-start | bytes 24584 | tf_op jit(solution)/shard_map/ppermute | solution.py:273
  146.5 4.9 %collective-permute-start.16 = (f32[8,1024]{1,0:T(8,128)S(1)}, f32[8,1024]{1,0:T(8,128)S(1)}, u32[]{:S(2)}, u32[]{:S(2)}) collective-permute-start(f32[8,1024]{1,0:T(8,128)S(1)} %fusion.21), channel_id=1, source_target_pairs={{0,8},{1,9},{2,10},{3,11},{4,12},{5,13},{6,14},{7,15},{8,0},{9,1},... | collective-permute-start | bytes 98312 | tf_op jit(solution)/shard_map/ppermute | solution.py:265
  151.4 4.4 %collective-permute-start.17 = (f32[16,1024]{1,0:T(8,128)S(1)}, f32[16,1024]{1,0:T(8,128)S(1)}, u32[]{:S(2)}, u32[]{:S(2)}) collective-permute-start(f32[16,1024]{1,0:T(8,128)S(1)} %pad_maximum_fusion.14), channel_id=1, source_target_pairs={{0,4},{1,5},{2,6},{3,7},{4,0},{5,1},{6,2},{7,3},{8,12},{9,13},{10,... | collective-permute-start | bytes 196616 | tf_op jit(solution)/shard_map/ppermute | solution.py:265
  155.8 5.0 %collective-permute-start.18 = (f32[32,1024]{1,0:T(8,128)S(1)}, f32[32,1024]{1,0:T(8,128)S(1)}, u32[]{:S(2)}, u32[]{:S(2)}) collective-permute-start(f32[32,1024]{1,0:T(8,128)S(1)} %pad_maximum_fusion.6), channel_id=1, source_target_pairs={{0,2},{1,3},{2,0},{3,1},{4,6},{5,7},{6,4},{7,5},{8,10},{9,11},{10,... | collective-permute-start | bytes 393224 | tf_op jit(solution)/shard_map/ppermute | solution.py:265
  160.8 1.6 collective-permute-start.19

commit v2 on v1

v2 whole, which is shorter than its diff:
```python
import functools

import jax
import jax.numpy as jnp
from jax import lax
from jax.experimental import pallas as pl
from jax.experimental.pallas import tpu as pltpu
from jax.sharding import PartitionSpec as P

HALF = 8
ITERS = 2
REACH = 2 * HALF

huber_edge = 1.5
ensemble_share = 0.75
static_share = 0.25

LANES = 256
F32 = jnp.float32
BF16 = jnp.bfloat16


def tap_matrix(distance, radius):
    offsets = jnp.arange(-radius, radius + 1).astype(F32)
    raw = jnp.exp(-0.5 * (offsets / (0.5 * radius)) ** 2)
    norm_value = jnp.sqrt(jnp.sum(raw * raw))
    scaled = distance.astype(F32) / (0.5 * radius)
    entry = jnp.exp(-0.5 * scaled**2) / norm_value
    return jnp.where(jnp.abs(distance) <= radius, entry, 0.0).astype(BF16)


def lon_tile(radius):
    source = jnp.arange(2 * LANES)[:, None] - LANES // 2
    target = jnp.arange(LANES)[None, :]
    return tap_matrix(source - target, radius)


def lat_block(out_level, out_row, in_level, in_row, rows_total, radius):
    distance = in_row[None, :] - out_row[:, None]
    entry = tap_matrix(distance, radius)
    inside = (out_row >= 0) & (out_row < rows_total)
    keep = (out_level[:, None] == in_level[None, :]) & inside[:, None]
    return jnp.where(keep, entry, 0).astype(BF16)


def split_bf16(x):
    hi = x.astype(BF16)
    lo = (x - hi.astype(F32)).astype(BF16)
    return hi, lo


def onehot(index, count):
    rows = lax.broadcasted_iota(jnp.int32, (count, index.shape[1]), 0)
    return jnp.where(rows == index, 1.0, 0.0).astype(BF16)


def vmem():
    return pl.BlockSpec(memory_space=pltpu.VMEM)


def smem():
    return pl.BlockSpec(memory_space=pltpu.SMEM)


def weigh(at_place, value, error):
    departure = value - at_place
    weight = huber_edge / jnp.maximum(jnp.abs(departure / error), huber_edge)
    share = weight / (error * error)
    return share * departure, share


def prepare_kernel(roots, idx_ref, value_ref, error_ref, out_ref):
    chunks, lon = out_ref.shape[0] // 6, out_ref.shape[1]
    position = lax.axis_index("member")
    first, second = position == roots[0], position == roots[1]
    for c in range(chunks):
        lanes = slice(c * lon, (c + 1) * lon)
        idx = idx_ref[:, lanes].astype(F32)
        value, error = value_ref[:, lanes], error_ref[:, lanes]
        coef, share = weigh(0.0, value, error)
        for k, x in enumerate((idx, coef, share)):
            out_ref[k * chunks + c:k * chunks + c + 1, :] = jnp.where(first, x, 0.0)
        for k, x in enumerate((idx, value, error)):
            k += 3
            out_ref[k * chunks + c:k * chunks + c + 1, :] = jnp.where(second, x, 0.0)


def prepare(roots, index, value, error, lon):
    return pl.pallas_call(
        prepare_kernel,
        out_shape=jax.ShapeDtypeStruct((6 * (index.shape[1] // lon), lon), F32),
        in_specs=[smem(), vmem(), vmem(), vmem()],
        out_specs=vmem(),
        name="prepare",
    )(roots, index, value, error)


def add_onehot(idx, coef, seg, acc):
    lane = idx % LANES
    hi, lo = split_bf16(coef)
    spot = lax.broadcasted_iota(jnp.int32, (LANES, idx.shape[1]), 0) == lane
    side = jnp.concatenate(
        [
            jnp.where(spot, hi.astype(F32), 0.0).astype(BF16),
            jnp.where(spot, lo.astype(F32), 0.0).astype(BF16),
        ],
        axis=0,
    )
    hot = onehot(seg, acc.shape[0])
    acc[...] += lax.dot_general(
        hot, side, (((1,), (1,)), ((), ())), preferred_element_type=F32
    )


def total_of(totals, row):
    value = totals[0][row:row + 1, :1]
    for t in totals[1:]:
        value = value + t[row:row + 1, :1]
    return value


def scale_of(totals, chunks):
    along = total_of(totals, chunks)
    return along / (along + total_of(totals, chunks + 1))


def coefficients(second, message, chunks, text, totals, c):
    row = lambda ref, k: ref[k * chunks + c:k * chunks + c + 1, :]
    if not second:
        return row(message, 0), row(message, 1)
    at_place = scale_of(totals, chunks) * row(text, 0)
    error = row(message, 5)
    coef, _ = weigh(at_place, row(message, 4), jnp.where(error > 0, error, 1.0))
    return row(message, 3), coef


def scatter_kernel(second, rows, lon, near, *refs):
    refs = list(refs)
    start_ref = refs.pop(0) if near is not None else None
    out_ref, acc = refs[-2:]
    message = refs[0]
    text, totals = (refs[1], refs[2:-2]) if second else (None, None)
    chunks = message.shape[0] // 6
    width = out_ref.shape[0]
    acc[...] = jnp.zeros_like(acc)
    for c in range(chunks):
        place, coef = coefficients(second, message, chunks, text, totals, c)
        idx = place.astype(jnp.int32)
        blk = (idx % lon) // LANES
        if near is None:
            seg = blk * width + idx // lon
        else:
            row = (idx // lon) % rows - start_ref[near]
            inside = (row >= 0) & (row < REACH)
            seg = blk * width + (idx // (lon * rows)) * REACH + row
            seg = jnp.where(inside, seg, -1)
        add_onehot(idx, coef, seg, acc)
    for b in range(lon // LANES):
        part = acc[b * width:(b + 1) * width, :]
        out_ref[:, b * LANES:(b + 1) * LANES] = part[:, :LANES] + part[:, LANES:]


def scatter_obs(levels, rows, lon, message, text, totals, near=None, starts=None):
    second = text is not None
    width = levels * (rows if near is None else REACH)
    args = [message] + ([text, *totals] if second else [])
    specs = [vmem()] * len(args)
    if near is not None:
        args, specs = [starts] + args, [smem()] + specs
    return pl.pallas_call(
        functools.partial(scatter_kernel, second, rows, lon, near),
        out_shape=jax.ShapeDtypeStruct((width, lon), F32),
        in_specs=specs,
        out_specs=vmem(),
        scratch_shapes=[pltpu.VMEM(((lon // LANES) * width, 2 * LANES), F32)],
        name="scatter_own" if near is None else "scatter_near",
    )(*args)


def lon_pass(x, tile):
    lon = x.shape[1]
    half = LANES // 2
    parts = []
    for j in range(lon // LANES):
        lo, hi = j * LANES - half, (j + 1) * LANES + half
        if lo < 0:
            window = jnp.concatenate([x[:, lon + lo:], x[:, :hi]], axis=1)
        elif hi > lon:
            window = jnp.concatenate([x[:, lo:], x[:, :hi - lon]], axis=1)
        else:
            window = x[:, lo:hi]
        parts.append(jnp.dot(window, tile, preferred_element_type=F32).astype(BF16))
    return jnp.concatenate(parts, axis=1)


def filter_kernel(share, own_ref, ext_ref, grad_ref, gext_ref, var_ref,
                  tile_ref, lat1_ref, lat2_ref, keep_ref, send_ref, acc_ref):
    step = pl.program_id(0)
    position = lax.axis_index("member")
    own = own_ref[0].astype(F32)
    ext = ext_ref[0].astype(F32)
    mixed = jnp.concatenate(
        [(own * grad_ref[...]).astype(BF16), (ext * gext_ref[...]).astype(BF16)], axis=0
    )
    tile = tile_ref[...]
    first = lon_pass(mixed, tile)
    first = jnp.dot(lat1_ref[...], first, preferred_element_type=F32).astype(BF16)
    second = lon_pass(first, tile)
    second = jnp.dot(lat2_ref[...], second, preferred_element_type=F32)
    product = own * second

    @pl.when(step == 0)
    def _():
        acc_ref[...] = product

    @pl.when(step > 0)
    def _():
        acc_ref[...] += product

    @pl.when(step == pl.num_programs(0) - 1)
    def _():
        half = keep_ref.shape[0]
        static = jnp.where(position == 0, static_share, 0.0)
        bit = position % 2
        for ref, start in ((keep_ref, bit * half), (send_ref, (1 - bit) * half)):
            rows = pl.ds(pl.multiple_of(start, half), half)
            ref[...] = share * acc_ref[rows, :] + static * var_ref[rows, :] * grad_ref[rows, :]


def filter_members(share, own, ext, grad, gext, variance, tile, lat1, lat2):
    members, rows, lon = own.shape
    whole = lambda a: pl.BlockSpec(a.shape, lambda i: (0,) * a.ndim)
    half = jax.ShapeDtypeStruct((rows // 2, lon), F32)
    return pl.pallas_call(
        functools.partial(filter_kernel, share),
        grid=(members,),
        out_shape=(half, half),
        in_specs=[
            pl.BlockSpec((1,) + own.shape[1:], lambda i: (i, 0, 0)),
            pl.BlockSpec((1,) + ext.shape[1:], lambda i: (i, 0, 0)),
            whole(grad), whole(gext), whole(variance),
            whole(tile), whole(lat1), whole(lat2),
        ],
        out_specs=(whole(half), whole(half)),
        scratch_shapes=[pltpu.VMEM((rows, lon), F32)],
        name="filter_members",
    )(own, ext, grad, gext, variance, tile, lat1, lat2)


def gather_kernel(which, keep_ref, got_ref, message, next_ref, send_ref):
    position = lax.axis_index("member")
    rows, lon = keep_ref.shape
    chunks = message.shape[0] // 6
    start = (position % 2) * rows
    field = keep_ref[...] + got_ref[...]
    low, high = field[:rows // 2], field[rows // 2:]
    upper = (position // 2) % 2 == 1
    next_ref[...] = jnp.where(upper, high, low)
    send_ref[:rows // 2, :] = jnp.where(upper, low, high)
    blocks = lon // LANES
    stacked = jnp.concatenate(
        [field[:, b * LANES:(b + 1) * LANES] for b in range(blocks)], axis=0
    )
    table = jnp.concatenate(split_bf16(jnp.transpose(stacked)), axis=0)
    for n, place in enumerate(which):
        for c in range(chunks):
            at = place * chunks + c
            idx = message[at:at + 1, :].astype(jnp.int32)
            blk = (idx % lon) // LANES
            row = idx // lon - start
            inside = (row >= 0) & (row < rows)
            hot = onehot(jnp.where(inside, blk * rows + row, -1), blocks * rows)
            found = jnp.dot(table, hot, preferred_element_type=F32)
            found = found[:LANES] + found[LANES:]
            spot = lax.broadcasted_iota(jnp.int32, found.shape, 0) == idx % LANES
            value = jnp.sum(jnp.where(spot, found, 0.0), axis=0, keepdims=True)
            at = rows // 2 + n * chunks + c
            send_ref[at:at + 1, :] = value


def gather_places(which, keep, got, message):
    rows, lon = keep.shape
    tail = len(which) * (message.shape[0] // 6)
    return pl.pallas_call(
        functools.partial(gather_kernel, which),
        out_shape=(
            jax.ShapeDtypeStruct((rows // 2, lon), F32),
            jax.ShapeDtypeStruct((rows // 2 + tail, lon), F32),
        ),
        in_specs=[vmem()] * 3,
        out_specs=(vmem(), vmem()),
        name="gather_places",
    )(keep, got, message)


def sums_kernel(second, *refs):
    tail, message, out_ref = refs[0], refs[1], refs[-1]
    chunks = message.shape[0] // 6
    lon = message.shape[1]
    part = lambda ref, k: ref[k * chunks:(k + 1) * chunks, :]
    total = lambda x: jnp.sum(jnp.sum(x, axis=0, keepdims=True), axis=1, keepdims=True)
    out_ref[...] = jnp.zeros_like(out_ref)
    reached = part(tail, 0)
    if second:
        text, totals = refs[2], refs[3:-1]
        at_place = scale_of(totals, chunks) * part(text, 0)
        coef, share = weigh(at_place, part(message, 4), part(message, 5))
        along = total(coef * (reached - at_place))
        curve = total(coef * at_place) + total(share * reached * reached)
    else:
        out_ref[:chunks, :] = part(tail, 1)
        along = total(part(message, 1) * reached)
        curve = total(part(message, 2) * reached * reached)
    out_ref[chunks:chunks + 1, :] = jnp.broadcast_to(along, (1, out_ref.shape[1]))
    out_ref[chunks + 1:chunks + 2, :] = jnp.broadcast_to(curve, (1, out_ref.shape[1]))


def sums(tail, message, text=None, totals=()):
    chunks, lon = message.shape[0] // 6, message.shape[1]
    second = text is not None
    args = [tail, message] + ([text, *totals] if second else [])
    rows = -(-(chunks + 2) // 8) * 8
    return pl.pallas_call(
        functools.partial(sums_kernel, second),
        out_shape=jax.ShapeDtypeStruct((rows, LANES // 2 if second else lon), F32),
        in_specs=[vmem()] * len(args),
        out_specs=vmem(),
        name="sums",
    )(*args)


def combine_kernel(chunks, count, *refs):
    pair, out_ref = refs[0], refs[-1]
    first, second = refs[1:1 + count], refs[1 + count:-1]
    scale_0 = scale_of(first, chunks)
    scale_1 = scale_of(second, chunks)
    out_ref[...] = scale_0 * pair[0] + scale_1 * pair[1]


def combine(pair, first, second, chunks):
    args = [pair, *first, *second]
    return pl.pallas_call(
        functools.partial(combine_kernel, chunks, len(first)),
        out_shape=jax.ShapeDtypeStruct(pair.shape[1:], F32),
        in_specs=[vmem()] * len(args),
        out_specs=vmem(),
        name="combine",
    )(*args)


def partner(count, bit):
    return [(j, j ^ bit) for j in range(count)]


def member_bits(count):
    bits, d = [], 1
    while d < count:
        bits.append(d)
        d *= 2
    assert d == count
    return bits


def swap(x, bit, count):
    return lax.ppermute(x, "member", partner(count, bit))


def reduce_with_tail(keep, send, bits, count, position):
    rows = keep.shape[0]
    for n, bit in enumerate(bits):
        got = swap(send, bit, count)
        x = keep + got[:rows]
        tail = send[rows:] + got[rows:]
        if n + 1 < len(bits):
            rows //= 2
            upper = (position // bits[n + 1]) % 2 == 1
            keep = jnp.where(upper, x[rows:], x[:rows])
            send = jnp.concatenate([jnp.where(upper, x[:rows], x[rows:]), tail], axis=0)
    return x, tail


def gather_rows(x, bit, count, position):
    other = swap(x, bit, count)
    upper = (position // bit) % 2 == 1
    axis = x.ndim - 2
    return jnp.concatenate([jnp.where(upper, other, x), jnp.where(upper, x, other)], axis=axis)


def from_bands(x, count):
    if count == 2:
        return [lax.ppermute(x, "band", [(0, 1), (1, 0)])]
    up = [(i, i + 1) for i in range(count - 1)]
    down = [(j, i) for i, j in up]
    return [lax.ppermute(x, "band", up), lax.ppermute(x, "band", down)]


def band_halo(ens, count, position):
    rows = ens.shape[2]
    first, last = ens[:, :, :REACH], ens[:, :, rows - REACH:]
    if count == 2:
        edge = jnp.where(position == 0, last, first)
        return [lax.ppermute(edge, "band", [(0, 1), (1, 0)])]
    up = [(i, i + 1) for i in range(count - 1)]
    down = [(j, i) for i, j in up]
    return [lax.ppermute(last, "band", up), lax.ppermute(first, "band", down)]


def local(ensemble, variance, obs_index, obs_value, obs_error, root_ranks):
    members_here, levels, lat_rows, lon = ensemble.shape
    n_member, n_band = lax.axis_size("member"), lax.axis_size("band")
    member_pos, band_pos = lax.axis_index("member"), lax.axis_index("band")
    members = members_here * n_member
    total_rows = lat_rows * n_band
    chunks = obs_index.shape[1] // lon
    bits = member_bits(n_member)

    if n_band == 2:
        starts = jnp.where(band_pos == 0, 0, lat_rows - REACH).reshape(1)
        near = [jnp.where(band_pos == 0, lat_rows, lat_rows - REACH)]
        near_inner = [jnp.where(band_pos == 0, lat_rows, lat_rows - HALF)]
    else:
        starts = jnp.array([lat_rows - REACH, 0])
        base = band_pos * lat_rows
        near = [base - REACH, base + lat_rows]
        near_inner = [base - HALF, base + lat_rows]
    starts = starts.astype(jnp.int32)

    level_of = jnp.arange(levels)
    def row_list(start, width):
        level = jnp.repeat(level_of, width)
        row = jnp.tile(jnp.arange(width), levels) + start
        return level, row
    own_rows = row_list(band_pos * lat_rows, lat_rows)
    outer = [own_rows] + [row_list(s, REACH) for s in near]
    inner = [own_rows] + [row_list(s, HALF) for s in near_inner]
    join = lambda parts: tuple(jnp.concatenate(p) for p in zip(*parts))
    outer, inner = join(outer), join(inner)
    lat1 = lat_block(*inner, *outer, total_rows, HALF)
    lat2 = lat_block(*own_rows, *inner, total_rows, HALF)
    tile = lon_tile(HALF)

    message = prepare(root_ranks, obs_index, obs_value, obs_error, lon)
    message = message + swap(message, bits[0], n_member)
    ensemble, message = lax.optimization_barrier((ensemble, message))
    halo = band_halo(ensemble, n_band, band_pos)
    for bit in bits[1:]:
        message = message + swap(message, bit, n_member)
    around = from_bands(message, n_band)

    own = ensemble.reshape(members_here, levels * lat_rows, lon)
    ext = jnp.concatenate([h.reshape(members_here, levels * REACH, lon) for h in halo], axis=1)
    variance = variance.reshape(levels * lat_rows, lon)
    share = ensemble_share / (members - 1)

    def direction_parts(text=None, totals=(), texts=()):
        scatter = functools.partial(scatter_obs, levels, lat_rows, lon)
        grad = scatter(message, text, totals)
        gext = [
            scatter(a, texts[s] if texts else None, totals, s, starts)
            for s, a in enumerate(around)
        ]
        gext = jnp.concatenate(gext, axis=0)
        keep, send = filter_members(share, own, ext, grad, gext, variance, tile, lat1, lat2)
        got = swap(send, bits[0], n_member)
        which = (3,) if texts else (0, 3)
        keep, send = gather_places(which, keep, got, message)
        piece, tail = reduce_with_tail(keep, send, bits[1:], n_member, member_pos)
        return piece, tail + swap(tail, bits[0], n_member)

    def band_totals(text):
        texts = from_bands(text, n_band)
        if n_band == 2:
            return [text, *texts], texts
        return [lax.psum(text, "band")], texts

    piece_0, tail = direction_parts()
    text = sums(tail, message)
    totals_0, texts = band_totals(text)

    piece_1, tail = direction_parts(text, totals_0, texts)
    totals_1, _ = band_totals(sums(tail, message, text, totals_0))
    pair = gather_rows(jnp.stack([piece_0, piece_1]), bits[-1], n_member, member_pos)
    out = combine(pair, totals_0, totals_1, chunks)
    for bit in reversed(bits[:-1]):
        out = gather_rows(out, bit, n_member, member_pos)
    return out.reshape(levels, lat_rows, lon)


def solution(mesh):
    in_specs = (
        P("member", None, "band", None),
        P(None, "band", None),
        P("member", "band"),
        P("member", "band"),
        P("member", "band"),
        P(),
    )
    out_specs = P(None, "band", None)
    return jax.shard_map(local, mesh=mesh, in_specs=in_specs, out_specs=out_specs, check_vma=False)
```

time: 164 us -> 152 us (0.927)
  waiting for transfers between devices: 57.9 us -> 48.5 us
  Pallas kernels: 44.5 us -> 51.6 us
  between operations: 6.95 us -> 0.93 us
  other arithmetic: 18.1 us -> 13 us
  starting transfers between devices: 30.5 us -> 32.7 us
    ppermute x3, waiting for transfers between devices: 17.9 us -> 6.47 us  [from_bands(): return [lax.ppermute(x, 'band', [(0, 1), (1, 0)])]]
    pallas_call x4 -> x10, Pallas kernels: 22.8 us -> 30.1 us  [the longest x4 16.2 us: scatter_obs(): pl.pallas_call(functools.partial(scatter_kernel, second, rows, lon, near)...]
    add x20 -> x15, other arithmetic: 2.3 us -> 5.6 us  [the longest x4 1.87 us: reduce_with_tail(): x = keep + got[:rows]]
    unnamed x23 -> x16, local copies, waits for them, and re-layouts: 1.55 us -> 4.25 us
    select_n x9 -> x4, other arithmetic: 2.24 us -> 0.03 us  [reduce_with_tail(): send = jnp.concatenate([jnp.where(upper, x[:rows], x[rows:]), tail], axis=0)]
    ppermute x3, starting transfers between devices: 1.55 us -> 3.58 us  [from_bands(): return [lax.ppermute(x, 'band', [(0, 1), (1, 0)])]]
    slice x4 -> x0, local copies, waits for them, and re-layouts: 2.02 us -> none  [the longest x2 1.25 us: local(): pieces = lambda a: [a[k * chunks:(k + 1) * chunks] for k in range(6)]]
    ppermute x16 -> x18, waiting for transfers between devices: 40 us -> 42 us  [swap(): return lax.ppermute(x, 'member', partner(count, bit))]
  transfers between devices with their start and end apart: 20 -> 22, of which waited for: 18 -> 20; matrix products, arithmetic and copies ran while one was open for 5% -> 3% of each run, Pallas kernels for 4% -> 6%
where the time goes in v2:
time: 152 us
  Pallas kernels  51.6 us (34%)
  waiting for transfers between devices  48.5 us (32%)
  starting transfers between devices  32.7 us (22%)
  other arithmetic  13 us (9%)
  local copies, waits for them, and re-layouts  4.78 us (3%)
    ppermute x18, waiting for transfers between devices, swap(): return lax.ppermute(x, 'member', partner(count, bit))  42 us
    ppermute x18, starting transfers between devices, swap(): return lax.ppermute(x, 'member', partner(count, bit))  26.2 us
    pallas_call x2, Pallas kernels, filter_members(): pl.pallas_call(functools.partial(filter_kernel, share), grid=(members,),...  21.6 us
    pallas_call x4, Pallas kernels, scatter_obs(): pl.pallas_call(functools.partial(scatter_kernel, second, rows, lon, near)...  16.2 us
    pallas_call x2, Pallas kernels, gather_places(): pl.pallas_call(functools.partial(gather_kernel, which), out_shape=(jax.Sh...  7.5 us
    ppermute x3, waiting for transfers between devices, from_bands(): return [lax.ppermute(x, 'band', [(0, 1), (1, 0)])]  6.47 us
    unnamed x16, local copies, waits for them, and re-layouts  4.25 us
    ppermute x3, starting transfers between devices, from_bands(): return [lax.ppermute(x, 'band', [(0, 1), (1, 0)])]  3.58 us
  transfers between devices with their start and end apart: 22, of which 20 were waited for; matrix products, arithmetic and copies ran while one was open for 3% of the time, Pallas kernels for 6%

profile of v2, /device:TPU:0, one launch (start us, length us, event | category | flops | bytes accessed | tf_op | source)
XLA Modules:
  0.0 151.6 jit_solution(11787407202857014860)
XLA Ops:
  0.0 1.5 prepare.1
  2.4 0.7 collective-permute-done
  3.1 0.9 add.130
  4.0 1.7 %slice_select_fusion = bf16[8,4,16,1024]{3,2,1,0:T(8,128)(2,1)S(1)} fusion(bf16[8,4,32,1024]{3,2,1,0:T(8,128)(2,1)} %param.6, pred[]{:T(512)S(6)} %eq.61), kind=kLoop, calls=%fused_computation | loop fusion | flops 524288 | bytes 3145729 | tf_op jit(solution)/shard_map/jit(_where)/select_n | solution.py:401
  5.7 2.9 %collective-permute-start.1 = (bf16[8,4,16,1024]{3,2,1,0:T(8,128)(2,1)S(1)}, bf16[8,4,16,1024]{3,2,1,0:T(8,128)(2,1)S(1)}, u32[]{:S(2)}, u32[]{:S(2)}) collective-permute-start(bf16[8,4,16,1024]{3,2,1,0:T(8,128)(2,1)S(1)} %slice_select_fusion), channel_id=1, source_target_pairs={{0,16},{16,0},{1,17},{17,1},{2,18},{18,2},{3,19},{19,3},{4,20},{20... | collective-permute-start | bytes 3145736 | tf_op jit(solution)/shard_map/ppermute | solution.py:402
  10.1 1.0 select_convert_fusion.tile_ref
  11.1 1.5 collective-permute-start.2
  12.6 3.1 %collective-permute-done.2 = f32[24,1024]{1,0:T(8,128)S(1)} collective-permute-done((f32[24,1024]{1,0:T(8,128)S(1)}, f32[24,1024]{1,0:T(8,128)S(1)}, u32[]{:S(2)}, u32[]{:S(2)}) %collective-permute-start.2) | collective-permute-done | bytes 98336 | tf_op jit(solution)/shard_map/ppermute | solution.py:365
  15.7 1.6 %collective-permute-start.3 = (f32[24,1024]{1,0:T(8,128)S(1)}, f32[24,1024]{1,0:T(8,128)S(1)}, u32[]{:S(2)}, u32[]{:S(2)}) collective-permute-start(f32[24,1024]{1,0:T(8,128)S(1)} %add.131), channel_id=1, source_target_pairs={{0,4},{1,5},{2,6},{3,7},{4,0},{5,1},{6,2},{7,3},{8,12},{9,13},{10,... | collective-permute-start | bytes 294920 | tf_op jit(solution)/shard_map/ppermute | solution.py:365
  17.4 0.8 and_select_fusion.lat1_ref
  18.2 2.2 %collective-permute-done.3 = f32[24,1024]{1,0:T(8,128)S(1)} collective-permute-done((f32[24,1024]{1,0:T(8,128)S(1)}, f32[24,1024]{1,0:T(8,128)S(1)}, u32[]{:S(2)}, u32[]{:S(2)}) %collective-permute-start.3) | collective-permute-done | bytes 98336 | tf_op jit(solution)/shard_map/ppermute | solution.py:365
  20.4 2.7 %collective-permute-start.4 = (f32[24,1024]{1,0:T(8,128)S(1)}, f32[24,1024]{1,0:T(8,128)S(1)}, u32[]{:S(2)}, u32[]{:S(2)}) collective-permute-start(f32[24,1024]{1,0:T(8,128)S(1)} %add.132), channel_id=1, source_target_pairs={{0,8},{1,9},{2,10},{3,11},{4,12},{5,13},{6,14},{7,15},{8,0},{9,1},... | collective-permute-start | bytes 294920 | tf_op jit(solution)/shard_map/ppermute | solution.py:365
  23.1 2.9 %collective-permute-done.4 = f32[24,1024]{1,0:T(8,128)S(1)} collective-permute-done((f32[24,1024]{1,0:T(8,128)S(1)}, f32[24,1024]{1,0:T(8,128)S(1)}, u32[]{:S(2)}, u32[]{:S(2)}) %collective-permute-start.4) | collective-permute-done | bytes 98336 | tf_op jit(solution)/shard_map/ppermute | solution.py:365
  26.4 0.8 and_select_fusion.1.lat2_ref
  27.2 4.6 %scatter_own.2.grad_ref = f32[128,1024]{1,0:T(8,128)} custom-call(f32[24,1024]{1,0:T(8,128)} %copy-done), custom_call_target="tpu_custom_call" | custom-call | tf_op jit(solution)/shard_map/scatter_own/pallas_call | solution.py:170
  31.7 2.5 %collective-permute-done.5.refs_1_ = f32[24,1024]{1,0:T(8,128)S(1)} collective-permute-done((f32[24,1024]{1,0:T(8,128)S(1)}, f32[24,1024]{1,0:T(8,128)S(1)}, u32[]{:S(2)}, u32[]{:S(2)}) %collective-permute-start.5) | collective-permute-done | bytes 98336 | tf_op jit(solution)/shard_map/ppermute | solution.py:391
  34.2 0.7 copy-done.3
  34.9 3.4 %scatter_near.2.gext_ref = f32[64,1024]{1,0:T(8,128)} custom-call(s32[1]{0:T(128)} %bitcast.2.refs_0_, f32[24,1024]{1,0:T(8,128)} %copy-done.3), custom_call_target="tpu_custom_call" | custom-call | tf_op jit(solution)/shard_map/scatter_near/pallas_call | solution.py:170
  38.3 1.0 copy-done.1
  39.3 10.8 %filter_members.2 = (f32[64,1024]{1,0:T(8,128)}, f32[64,1024]{1,0:T(8,128)}) custom-call(bf16[8,128,1024]{2,1,0:T(8,128)(2,1)} %bitcast.9, bf16[8,64,1024]{2,1,0:T(8,128)(2,1)} %bitcast.11, f32[128,1024]{1,0:T(8,128)} %scatter_own.2.grad_ref, f32[64,1024]{1,0:T(8,128)} %scatter_near.2.gext_ref, f32[128,1024]{1,0:T(8,128)} %bitcast.13, ...), custom_call_target="tpu_custom_call" | custom-call | tf_op jit(solution)/shard_map/filter_members/pallas_call | solution.py:234
  50.1 1.7 %collective-permute-done.6.got_ref = f32[64,1024]{1,0:T(8,128)S(1)} collective-permute-done((f32[64,1024]{1,0:T(8,128)}, f32[64,1024]{1,0:T(8,128)S(1)}, u32[]{:S(2)}, u32[]{:S(2)}) %collective-permute-start.6) | collective-permute-done | bytes 262176 | tf_op jit(solution)/shard_map/ppermute | solution.py:365
  51.8 0.7 copy-done.4
  52.5 4.4 %gather_places.2 = (f32[32,1024]{1,0:T(8,128)}, f32[40,1024]{1,0:T(8,128)}) custom-call(f32[64,1024]{1,0:T(8,128)} %get-tuple-element.17.keep_ref, f32[64,1024]{1,0:T(8,128)} %copy-done.4, f32[24,1024]{1,0:T(8,128)} %copy-done), custom_call_target="tpu_custom_call" | custom-call | tf_op jit(solution)/shard_map/gather_places/pallas_call | solution.py:284
  56.9 1.7 %collective-permute-start.7 = (f32[40,1024]{1,0:T(8,128)}, f32[40,1024]{1,0:T(8,128)S(1)}, u32[]{:S(2)}, u32[]{:S(2)}) collective-permute-start(f32[40,1024]{1,0:T(8,128)} %get-tuple-element.20), channel_id=1, source_target_pairs={{0,2},{1,3},{2,0},{3,1},{4,6},{5,7},{6,4},{7,5},{8,10},{9,11},{10,... | collective-permute-start | bytes 491528 | tf_op jit(solution)/shard_map/ppermute | solution.py:365
  58.6 4.7 %collective-permute-done.7 = f32[40,1024]{1,0:T(8,128)S(1)} collective-permute-done((f32[40,1024]{1,0:T(8,128)}, f32[40,1024]{1,0:T(8,128)S(1)}, u32[]{:S(2)}, u32[]{:S(2)}) %collective-permute-start.7) | collective-permute-done | bytes 163872 | tf_op jit(solution)/shard_map/ppermute | solution.py:365
  63.3 0.9 slice_add_fusion.1
  64.3 0.8 slice_add_fusion.8
  65.1 1.9 %collective-permute-start.8 = (f32[24,1024]{1,0:T(8,128)S(1)}, f32[24,1024]{1,0:T(8,128)S(1)}, u32[]{:S(2)}, u32[]{:S(2)}) collective-permute-start(f32[24,1024]{1,0:T(8,128)S(1)} %pad_maximum_fusion.4), channel_id=1, source_target_pairs={{0,4},{1,5},{2,6},{3,7},{4,0},{5,1},{6,2},{7,3},{8,12},{9,13},{10,... | collective-permute-start | bytes 294920 | tf_op jit(solution)/shard_map/ppermute | solution.py:365
  66.9 2.8 %collective-permute-done.8 = f32[24,1024]{1,0:T(8,128)S(1)} collective-permute-done((f32[24,1024]{1,0:T(8,128)S(1)}, f32[24,1024]{1,0:T(8,128)S(1)}, u32[]{:S(2)}, u32[]{:S(2)}) %collective-permute-start.8) | collective-permute-done | bytes 98336 | tf_op jit(solution)/shard_map/ppermute | solution.py:365
  69.8 2.9 %collective-permute-start.9 = (f32[16,1024]{1,0:T(8,128)S(1)}, f32[16,1024]{1,0:T(8,128)S(1)}, u32[]{:S(2)}, u32[]{:S(2)}) collective-permute-start(f32[16,1024]{1,0:T(8,128)S(1)} %pad_maximum_fusion.6), channel_id=1, source_target_pairs={{0,8},{1,9},{2,10},{3,11},{4,12},{5,13},{6,14},{7,15},{8,0},{9,1},... | collective-permute-start | bytes 196616 | tf_op jit(solution)/shard_map/ppermute | solution.py:365
  72.7 2.3 %collective-permute-done.9 = f32[16,1024]{1,0:T(8,128)S(1)} collective-permute-done((f32[16,1024]{1,0:T(8,128)S(1)}, f32[16,1024]{1,0:T(8,128)S(1)}, u32[]{:S(2)}, u32[]{:S(2)}) %collective-permute-start.9) | collective-permute-done | bytes 65568 | tf_op jit(solution)/shard_map/ppermute | solution.py:365
  75.1 1.2 collective-permute-done.10
  76.3 0.6 add.150.refs_0_
  76.9 1.6 %sums.2.refs_1_.refs_2_.refs_3_ = f32[8,1024]{1,0:T(8,128)} custom-call(f32[8,1024]{1,0:T(8,128)} %add.150.refs_0_, f32[24,1024]{1,0:T(8,128)} %copy-done), custom_call_target="tpu_custom_call" | custom-call | tf_op jit(solution)/shard_map/sums/pallas_call | solution.py:323
  78.6 1.7 %collective-permute-start.11 = (f32[8,1024]{1,0:T(8,128)}, f32[8,1024]{1,0:T(8,128)S(1)}, u32[]{:S(2)}, u32[]{:S(2)}) collective-permute-start(f32[8,1024]{1,0:T(8,128)} %sums.2.refs_1_.refs_2_.refs_3_), channel_id=1, source_target_pairs={{0,16},{16,0},{1,17},{17,1},{2,18},{18,2},{3,19},{19,3},{4,20},{20... | collective-permute-start | bytes 98312 | tf_op jit(solution)/shard_map/ppermute | solution.py:391
  80.3 2.4 %collective-permute-done.11.refs_3_.refs_2_.refs_4_ = f32[8,1024]{1,0:T(8,128)S(1)} collective-permute-done((f32[8,1024]{1,0:T(8,128)}, f32[8,1024]{1,0:T(8,128)S(1)}, u32[]{:S(2)}, u32[]{:S(2)}) %collective-permute-start.11) | collective-permute-done | bytes 32800 | tf_op jit(solution)/shard_map/ppermute | solution.py:391
  83.3 4.7 %scatter_own.3.grad_ref = f32[128,1024]{1,0:T(8,128)} custom-call(f32[24,1024]{1,0:T(8,128)} %copy-done, f32[8,1024]{1,0:T(8,128)} %sums.2.refs_1_.refs_2_.refs_3_, f32[8,1024]{1,0:T(8,128)} %sums.2.refs_1_.refs_2_.refs_3_, f32[8,1024]{1,0:T(8,128)} %copy-done.2), custom_call_target="tpu_custom_call" | custom-call | tf_op jit(solution)/shard_map/scatter_own/pallas_call | solution.py:170
  88.0 3.5 %scatter_near.3.gext_ref = f32[64,1024]{1,0:T(8,128)} custom-call(s32[1]{0:T(128)} %bitcast.2.refs_0_, f32[24,1024]{1,0:T(8,128)} %copy-done.3, f32[8,1024]{1,0:T(8,128)} %copy-done.2, f32[8,1024]{1,0:T(8,128)} %sums.2.refs_1_.refs_2_.refs_3_, f32[8,1024]{1,0:T(8,128)} %copy-done.2), custom_call_target="tpu_custom_call" | custom-call | tf_op jit(solution)/shard_map/scatter_near/pallas_call | solution.py:170
  91.5 10.8 %filter_members.3 = (f32[64,1024]{1,0:T(8,128)}, f32[64,1024]{1,0:T(8,128)}) custom-call(bf16[8,128,1024]{2,1,0:T(8,128)(2,1)} %bitcast.10, bf16[8,64,1024]{2,1,0:T(8,128)(2,1)} %bitcast.12, f32[128,1024]{1,0:T(8,128)} %scatter_own.3.grad_ref, f32[64,1024]{1,0:T(8,128)} %scatter_near.3.gext_ref, f32[128,1024]{1,0:T(8,128)} %bitcast.14, ...), custom_call_target="tpu_custom_call" | custom-call | tf_op jit(solution)/shard_map/filter_members/pallas_call | solution.py:234
  102.2 1.7 %collective-permute-done.12.got_ref = f32[64,1024]{1,0:T(8,128)S(1)} collective-permute-done((f32[64,1024]{1,0:T(8,128)}, f32[64,1024]{1,0:T(8,128)S(1)}, u32[]{:S(2)}, u32[]{:S(2)}) %collective-permute-start.12) | collective-permute-done | bytes 262176 | tf_op jit(solution)/shard_map/ppermute | solution.py:365
  104.0 0.7 copy-done.5
  104.7 3.1 %gather_places.3 = (f32[32,1024]{1,0:T(8,128)}, f32[36,1024]{1,0:T(8,128)}) custom-call(f32[64,1024]{1,0:T(8,128)} %get-tuple-element.21.keep_ref, f32[64,1024]{1,0:T(8,128)} %copy-done.5, f32[24,1024]{1,0:T(8,128)} %copy-done), custom_call_target="tpu_custom_call" | custom-call | tf_op jit(solution)/shard_map/gather_places/pallas_call | solution.py:284
  107.8 1.7 %collective-permute-start.13 = (f32[36,1024]{1,0:T(8,128)}, f32[36,1024]{1,0:T(8,128)S(1)}, u32[]{:S(2)}, u32[]{:S(2)}) collective-permute-start(f32[36,1024]{1,0:T(8,128)} %get-tuple-element.24), channel_id=1, source_target_pairs={{0,2},{1,3},{2,0},{3,1},{4,6},{5,7},{6,4},{7,5},{8,10},{9,11},{10,... | collective-permute-start | bytes 442376 | tf_op jit(solution)/shard_map/ppermute | solution.py:365
  109.5 4.7 %collective-permute-done.13 = f32[36,1024]{1,0:T(8,128)S(1)} collective-permute-done((f32[36,1024]{1,0:T(8,128)}, f32[36,1024]{1,0:T(8,128)S(1)}, u32[]{:S(2)}, u32[]{:S(2)}) %collective-permute-start.13) | collective-permute-done | bytes 147488 | tf_op jit(solution)/shard_map/ppermute | solution.py:365
  114.3 0.9 slice_add_fusion
  115.2 0.8 slice_add_fusion.11
  116.0 1.9 %collective-permute-start.14 = (f32[20,1024]{1,0:T(8,128)S(1)}, f32[20,1024]{1,0:T(8,128)S(1)}, u32[]{:S(2)}, u32[]{:S(2)}) collective-permute-start(f32[20,1024]{1,0:T(8,128)S(1)} %pad_maximum_fusion.5), channel_id=1, source_target_pairs={{0,4},{1,5},{2,6},{3,7},{4,0},{5,1},{6,2},{7,3},{8,12},{9,13},{10,... | collective-permute-start | bytes 245768 | tf_op jit(solution)/shard_map/ppermute | solution.py:365
  117.9 2.8 %collective-permute-done.14 = f32[20,1024]{1,0:T(8,128)S(1)} collective-permute-done((f32[20,1024]{1,0:T(8,128)S(1)}, f32[20,1024]{1,0:T(8,128)S(1)}, u32[]{:S(2)}, u32[]{:S(2)}) %collective-permute-start.14) | collective-permute-done | bytes 81952 | tf_op jit(solution)/shard_map/ppermute | solution.py:365
  120.7 3.0 %collective-permute-start.15 = (f32[12,1024]{1,0:T(8,128)S(1)}, f32[12,1024]{1,0:T(8,128)S(1)}, u32[]{:S(2)}, u32[]{:S(2)}) collective-permute-start(f32[12,1024]{1,0:T(8,128)S(1)} %pad_maximum_fusion.7), channel_id=1, source_target_pairs={{0,8},{1,9},{2,10},{3,11},{4,12},{5,13},{6,14},{7,15},{8,0},{9,1},... | collective-permute-start | bytes 147464 | tf_op jit(solution)/shard_map/ppermute | solution.py:365
  123.8 2.2 %collective-permute-done.15 = f32[12,1024]{1,0:T(8,128)S(1)} collective-permute-done((f32[12,1024]{1,0:T(8,128)S(1)}, f32[12,1024]{1,0:T(8,128)S(1)}, u32[]{:S(2)}, u32[]{:S(2)}) %collective-permute-start.15) | collective-permute-done | bytes 49184 | tf_op jit(solution)/shard_map/ppermute | solution.py:365
  126.0 3.0 %collective-permute-start.16 = (f32[2,8,1024]{2,1,0:T(8,128)S(1)}, f32[2,8,1024]{2,1,0:T(8,128)S(1)}, u32[]{:S(2)}, u32[]{:S(2)}) collective-permute-start(f32[2,8,1024]{2,1,0:T(8,128)S(1)} %pad_maximum_fusion.8), channel_id=1, source_target_pairs={{0,8},{1,9},{2,10},{3,11},{4,12},{5,13},{6,14},{7,15},{8,0},{9,1},... | collective-permute-start | bytes 196616 | tf_op jit(solution)/shard_map/ppermute | solution.py:365
  129.0 1.2 collective-permute-done.17
  130.8 1.7 %sums.3.refs_3_ = f32[8,128]{1,0:T(8,128)} custom-call(f32[4,1024]{1,0:T(4,128)} %add.157.refs_0_, f32[24,1024]{1,0:T(8,128)} %copy-done, f32[8,1024]{1,0:T(8,128)} %sums.2.refs_1_.refs_2_.refs_3_, f32[8,1024]{1,0:T(8,128)} %sums.2.refs_1_.refs_2_.refs_3_, f32[8,1024]{1,0:T(8,128)} %copy-done.2), custom_call_target="tpu_custom_call" | custom-call | tf_op jit(solution)/shard_map/sums/pallas_call | solution.py:323
  132.5 1.5 %collective-permute-start.18 = (f32[8,128]{1,0:T(8,128)}, f32[8,128]{1,0:T(8,128)S(1)}, u32[]{:S(2)}, u32[]{:S(2)}) collective-permute-start(f32[8,128]{1,0:T(8,128)} %sums.3.refs_3_), channel_id=1, source_target_pairs={{0,16},{16,0},{1,17},{17,1},{2,18},{18,2},{3,19},{19,3},{4,20},{20... | collective-permute-start | bytes 12296 | tf_op jit(solution)/shard_map/ppermute | solution.py:391
  134.1 0.7 pad_maximum_fusion.2.refs_0_
  134.7 1.6 %collective-permute-done.18.refs_4_ = f32[8,128]{1,0:T(8,128)S(1)} collective-permute-done((f32[8,128]{1,0:T(8,128)}, f32[8,128]{1,0:T(8,128)S(1)}, u32[]{:S(2)}, u32[]{:S(2)}) %collective-permute-start.18) | collective-permute-done | bytes 4128 | tf_op jit(solution)/shard_map/ppermute | solution.py:391
  136.9 1.6 %combine.1 = f32[16,1024]{1,0:T(8,128)} custom-call(f32[2,16,1024]{2,1,0:T(8,128)} %pad_maximum_fusion.2.refs_0_, f32[8,1024]{1,0:T(8,128)} %sums.2.refs_1_.refs_2_.refs_3_, f32[8,1024]{1,0:T(8,128)} %copy-done.2, f32[8,128]{1,0:T(8,128)} %sums.3.refs_3_, f32[8,128]{1,0:T(8,128)} %copy-done.6), custom_call_target="tpu_custom_call" | custom-call | tf_op jit(solution)/shard_map/combine/pallas_call | solution.py:342
  138.5 2.2 %collective-permute-start.19 = (f32[16,1024]{1,0:T(8,128)}, f32[16,1024]{1,0:T(8,128)S(1)}, u32[]{:S(2)}, u32[]{:S(2)}) collective-permute-start(f32[16,1024]{1,0:T(8,128)} %combine.1), channel_id=1, source_target_pairs={{0,4},{1,5},{2,6},{3,7},{4,0},{5,1},{6,2},{7,3},{8,12},{9,13},{10,... | collective-permute-start | bytes 196616 | tf_op jit(solution)/shard_map/ppermute | solution.py:365
  140.7 2.5 %collective-permute-done.19 = f32[16,1024]{1,0:T(8,128)S(1)} collective-permute-done((f32[16,1024]{1,0:T(8,128)}, f32[16,1024]{1,0:T(8,128)S(1)}, u32[]{:S(2)}, u32[]{:S(2)}) %collective-permute-start.19) | collective-permute-done | bytes 65568 | tf_op jit(solution)/shard_map/ppermute | solution.py:365
  143.2 0.9 broadcast_select_fusion.7
  144.0 1.5 %collective-permute-start.20 = (f32[32,1024]{1,0:T(8,128)S(1)}, f32[32,1024]{1,0:T(8,128)S(1)}, u32[]{:S(2)}, u32[]{:S(2)}) collective-permute-start(f32[32,1024]{1,0:T(8,128)S(1)} %pad_maximum_fusion.3), channel_id=1, source_target_pairs={{0,2},{1,3},{2,0},{3,1},{4,6},{5,7},{6,4},{7,5},{8,10},{9,11},{10,... | collective-permute-start | bytes 393224 | tf_op jit(solution)/shard_map/ppermute | solution.py:365
  145.6 3.5 %collective-permute-done.20 = f32[32,1024]{1,0:T(8,128)S(1)} collective-permute-done((f32[32,1024]{1,0:T(8,128)S(1)}, f32[32,1024]{1,0:T(8,128)S(1)}, u32[]{:S(2)}, u32[]{:S(2)}) %collective-permute-start.20) | collective-permute-done | bytes 131104 | tf_op jit(solution)/shard_map/ppermute | solution.py:365
  149.2 1.5 collective-permute-done.21
  150.8 0.8 pad_maximum_fusion
  (66 shorter events, 4.3 us)
Async XLA Ops:
  1.5 1.6 %collective-permute-start = (f32[24,1024]{1,0:T(8,128)}, f32[24,1024]{1,0:T(8,128)S(1)}, u32[]{:S(2)}, u32[]{:S(2)}) collective-permute-start(f32[24,1024]{1,0:T(8,128)} %prepare.1), channel_id=1, source_target_pairs={{0,1},{1,0},{2,3},{3,2},{4,5},{5,4},{6,7},{7,6},{8,9},{9,8},{10,11... | collective-permute-start | bytes 294920 | tf_op jit(solution)/shard_map/ppermute | solution.py:365
  5.7 32.6 %collective-permute-start.1 = (bf16[8,4,16,1024]{3,2,1,0:T(8,128)(2,1)S(1)}, bf16[8,4,16,1024]{3,2,1,0:T(8,128)(2,1)S(1)}, u32[]{:S(2)}, u32[]{:S(2)}) collective-permute-start(bf16[8,4,16,1024]{3,2,1,0:T(8,128)(2,1)S(1)} %slice_select_fusion), channel_id=1, source_target_pairs={{0,16},{16,0},{1,17},{17,1},{2,18},{18,2},{3,19},{19,3},{4,20},{20... | collective-permute-start | bytes 3145736 | tf_op jit(solution)/shard_map/ppermute | solution.py:402
  11.1 4.6 %collective-permute-start.2 = (f32[24,1024]{1,0:T(8,128)S(1)}, f32[24,1024]{1,0:T(8,128)S(1)}, u32[]{:S(2)}, u32[]{:S(2)}) collective-permute-start(f32[24,1024]{1,0:T(8,128)S(1)} %add.130), channel_id=1, source_target_pairs={{0,2},{1,3},{2,0},{3,1},{4,6},{5,7},{6,4},{7,5},{8,10},{9,11},{10,... | collective-permute-start | bytes 294920 | tf_op jit(solution)/shard_map/ppermute | solution.py:365
  15.7 4.7 %collective-permute-start.3 = (f32[24,1024]{1,0:T(8,128)S(1)}, f32[24,1024]{1,0:T(8,128)S(1)}, u32[]{:S(2)}, u32[]{:S(2)}) collective-permute-start(f32[24,1024]{1,0:T(8,128)S(1)} %add.131), channel_id=1, source_target_pairs={{0,4},{1,5},{2,6},{3,7},{4,0},{5,1},{6,2},{7,3},{8,12},{9,13},{10,... | collective-permute-start | bytes 294920 | tf_op jit(solution)/shard_map/ppermute | solution.py:365
  20.4 5.6 %collective-permute-start.4 = (f32[24,1024]{1,0:T(8,128)S(1)}, f32[24,1024]{1,0:T(8,128)S(1)}, u32[]{:S(2)}, u32[]{:S(2)}) collective-permute-start(f32[24,1024]{1,0:T(8,128)S(1)} %add.132), channel_id=1, source_target_pairs={{0,8},{1,9},{2,10},{3,11},{4,12},{5,13},{6,14},{7,15},{8,0},{9,1},... | collective-permute-start | bytes 294920 | tf_op jit(solution)/shard_map/ppermute | solution.py:365
  26.1 1.1 copy-start
  26.1 8.1 %collective-permute-start.5 = (f32[24,1024]{1,0:T(8,128)S(1)}, f32[24,1024]{1,0:T(8,128)S(1)}, u32[]{:S(2)}, u32[]{:S(2)}) collective-permute-start(f32[24,1024]{1,0:T(8,128)S(1)} %add.133.refs_0_.message.refs_1_), channel_id=1, source_target_pairs={{0,16},{16,0},{1,17},{17,1},{2,18},{18,2},{3,19},{19,3},{4,20},{20... | collective-permute-start | bytes 294920 | tf_op jit(solution)/shard_map/ppermute | solution.py:391
  34.2 0.7 copy-start.3
  38.3 1.0 copy-start.1
  50.1 1.7 %collective-permute-start.6 = (f32[64,1024]{1,0:T(8,128)}, f32[64,1024]{1,0:T(8,128)S(1)}, u32[]{:S(2)}, u32[]{:S(2)}) collective-permute-start(f32[64,1024]{1,0:T(8,128)} %get-tuple-element.18), channel_id=1, source_target_pairs={{0,1},{1,0},{2,3},{3,2},{4,5},{5,4},{6,7},{7,6},{8,9},{9,8},{10,11... | collective-permute-start | bytes 786440 | tf_op jit(solution)/shard_map/ppermute | solution.py:365
  51.8 0.7 copy-start.4
  56.9 6.5 %collective-permute-start.7 = (f32[40,1024]{1,0:T(8,128)}, f32[40,1024]{1,0:T(8,128)S(1)}, u32[]{:S(2)}, u32[]{:S(2)}) collective-permute-start(f32[40,1024]{1,0:T(8,128)} %get-tuple-element.20), channel_id=1, source_target_pairs={{0,2},{1,3},{2,0},{3,1},{4,6},{5,7},{6,4},{7,5},{8,10},{9,11},{10,... | collective-permute-start | bytes 491528 | tf_op jit(solution)/shard_map/ppermute | solution.py:365
  65.1 4.7 %collective-permute-start.8 = (f32[24,1024]{1,0:T(8,128)S(1)}, f32[24,1024]{1,0:T(8,128)S(1)}, u32[]{:S(2)}, u32[]{:S(2)}) collective-permute-start(f32[24,1024]{1,0:T(8,128)S(1)} %pad_maximum_fusion.4), channel_id=1, source_target_pairs={{0,4},{1,5},{2,6},{3,7},{4,0},{5,1},{6,2},{7,3},{8,12},{9,13},{10,... | collective-permute-start | bytes 294920 | tf_op jit(solution)/shard_map/ppermute | solution.py:365
  69.8 5.2 %collective-permute-start.9 = (f32[16,1024]{1,0:T(8,128)S(1)}, f32[16,1024]{1,0:T(8,128)S(1)}, u32[]{:S(2)}, u32[]{:S(2)}) collective-permute-start(f32[16,1024]{1,0:T(8,128)S(1)} %pad_maximum_fusion.6), channel_id=1, source_target_pairs={{0,8},{1,9},{2,10},{3,11},{4,12},{5,13},{6,14},{7,15},{8,0},{9,1},... | collective-permute-start | bytes 196616 | tf_op jit(solution)/shard_map/ppermute | solution.py:365
  75.0 1.3 collective-permute-start.10
  78.6 4.1 %collective-permute-start.11 = (f32[8,1024]{1,0:T(8,128)}, f32[8,1024]{1,0:T(8,128)S(1)}, u32[]{:S(2)}, u32[]{:S(2)}) collective-permute-start(f32[8,1024]{1,0:T(8,128)} %sums.2.refs_1_.refs_2_.refs_3_), channel_id=1, source_target_pairs={{0,16},{16,0},{1,17},{17,1},{2,18},{18,2},{3,19},{19,3},{4,20},{20... | collective-permute-start | bytes 98312 | tf_op jit(solution)/shard_map/ppermute | solution.py:391
  82.7 0.6 copy-start.2
  102.2 1.7 %collective-permute-start.12 = (f32[64,1024]{1,0:T(8,128)}, f32[64,1024]{1,0:T(8,128)S(1)}, u32[]{:S(2)}, u32[]{:S(2)}) collective-permute-start(f32[64,1024]{1,0:T(8,128)} %get-tuple-element.22), channel_id=1, source_target_pairs={{0,1},{1,0},{2,3},{3,2},{4,5},{5,4},{6,7},{7,6},{8,9},{9,8},{10,11... | collective-permute-start | bytes 786440 | tf_op jit(solution)/shard_map/ppermute | solution.py:365
  104.0 0.7 copy-start.5
  107.8 6.5 %collective-permute-start.13 = (f32[36,1024]{1,0:T(8,128)}, f32[36,1024]{1,0:T(8,128)S(1)}, u32[]{:S(2)}, u32[]{:S(2)}) collective-permute-start(f32[36,1024]{1,0:T(8,128)} %get-tuple-element.24), channel_id=1, source_target_pairs={{0,2},{1,3},{2,0},{3,1},{4,6},{5,7},{6,4},{7,5},{8,10},{9,11},{10,... | collective-permute-start | bytes 442376 | tf_op jit(solution)/shard_map/ppermute | solution.py:365
  116.0 4.7 %collective-permute-start.14 = (f32[20,1024]{1,0:T(8,128)S(1)}, f32[20,1024]{1,0:T(8,128)S(1)}, u32[]{:S(2)}, u32[]{:S(2)}) collective-permute-start(f32[20,1024]{1,0:T(8,128)S(1)} %pad_maximum_fusion.5), channel_id=1, source_target_pairs={{0,4},{1,5},{2,6},{3,7},{4,0},{5,1},{6,2},{7,3},{8,12},{9,13},{10,... | collective-permute-start | bytes 245768 | tf_op jit(solution)/shard_map/ppermute | solution.py:365
  120.7 5.3 %collective-permute-start.15 = (f32[12,1024]{1,0:T(8,128)S(1)}, f32[12,1024]{1,0:T(8,128)S(1)}, u32[]{:S(2)}, u32[]{:S(2)}) collective-permute-start(f32[12,1024]{1,0:T(8,128)S(1)} %pad_maximum_fusion.7), channel_id=1, source_target_pairs={{0,8},{1,9},{2,10},{3,11},{4,12},{5,13},{6,14},{7,15},{8,0},{9,1},... | collective-permute-start | bytes 147464 | tf_op jit(solution)/shard_map/ppermute | solution.py:365
  126.0 8.0 %collective-permute-start.16 = (f32[2,8,1024]{2,1,0:T(8,128)S(1)}, f32[2,8,1024]{2,1,0:T(8,128)S(1)}, u32[]{:S(2)}, u32[]{:S(2)}) collective-permute-start(f32[2,8,1024]{2,1,0:T(8,128)S(1)} %pad_maximum_fusion.8), channel_id=1, source_target_pairs={{0,8},{1,9},{2,10},{3,11},{4,12},{5,13},{6,14},{7,15},{8,0},{9,1},... | collective-permute-start | bytes 196616 | tf_op jit(solution)/shard_map/ppermute | solution.py:365
  129.0 1.2 collective-permute-start.17
  132.5 3.8 %collective-permute-start.18 = (f32[8,128]{1,0:T(8,128)}, f32[8,128]{1,0:T(8,128)S(1)}, u32[]{:S(2)}, u32[]{:S(2)}) collective-permute-start(f32[8,128]{1,0:T(8,128)} %sums.3.refs_3_), channel_id=1, source_target_pairs={{0,16},{16,0},{1,17},{17,1},{2,18},{18,2},{3,19},{19,3},{4,20},{20... | collective-permute-start | bytes 12296 | tf_op jit(solution)/shard_map/ppermute | solution.py:391
  136.3 0.6 copy-start.6
  138.5 4.6 %collective-permute-start.19 = (f32[16,1024]{1,0:T(8,128)}, f32[16,1024]{1,0:T(8,128)S(1)}, u32[]{:S(2)}, u32[]{:S(2)}) collective-permute-start(f32[16,1024]{1,0:T(8,128)} %combine.1), channel_id=1, source_target_pairs={{0,4},{1,5},{2,6},{3,7},{4,0},{5,1},{6,2},{7,3},{8,12},{9,13},{10,... | collective-permute-start | bytes 196616 | tf_op jit(solution)/shard_map/ppermute | solution.py:365
  144.0 5.0 %collective-permute-start.20 = (f32[32,1024]{1,0:T(8,128)S(1)}, f32[32,1024]{1,0:T(8,128)S(1)}, u32[]{:S(2)}, u32[]{:S(2)}) collective-permute-start(f32[32,1024]{1,0:T(8,128)S(1)} %pad_maximum_fusion.3), channel_id=1, source_target_pairs={{0,2},{1,3},{2,0},{3,1},{4,6},{5,7},{6,4},{7,5},{8,10},{9,11},{10,... | collective-permute-start | bytes 393224 | tf_op jit(solution)/shard_map/ppermute | solution.py:365
  149.1 1.6 %collective-permute-start.21 = (f32[64,1024]{1,0:T(8,128)S(1)}, f32[64,1024]{1,0:T(8,128)S(1)}, u32[]{:S(2)}, u32[]{:S(2)}) collective-permute-start(f32[64,1024]{1,0:T(8,128)S(1)} %pad_maximum_fusion.1), channel_id=1, source_target_pairs={{0,1},{1,0},{2,3},{3,2},{4,5},{5,4},{6,7},{7,6},{8,9},{9,8},{10,11... | collective-permute-start | bytes 786440 | tf_op jit(solution)/shard_map/ppermute | solution.py:365

commit v3 on v2

--- a/solution.py
+++ b/solution.py
@@ -2,6 +2,7 @@
 
 import jax
 import jax.numpy as jnp
+import numpy as np
 from jax import lax
 from jax.experimental import pallas as pl
 from jax.experimental.pallas import tpu as pltpu
@@ -16,31 +17,53 @@
 static_share = 0.25
 
 LANES = 256
+GRANT = 20 << 20
 F32 = jnp.float32
 BF16 = jnp.bfloat16
 
 
 def tap_matrix(distance, radius):
-    offsets = jnp.arange(-radius, radius + 1).astype(F32)
-    raw = jnp.exp(-0.5 * (offsets / (0.5 * radius)) ** 2)
-    norm_value = jnp.sqrt(jnp.sum(raw * raw))
-    scaled = distance.astype(F32) / (0.5 * radius)
-    entry = jnp.exp(-0.5 * scaled**2) / norm_value
-    return jnp.where(jnp.abs(distance) <= radius, entry, 0.0).astype(BF16)
+    offsets = np.arange(-radius, radius + 1).astype(np.float32)
+    raw = np.exp(np.float32(-0.5) * (offsets / np.float32(0.5 * radius)) ** 2)
+    taps = raw / np.sqrt(np.sum(raw * raw))
+    entry = taps[np.clip(distance, -radius, radius) + radius]
+    return np.where(np.abs(distance) <= radius, entry, 0.0).astype(np.float32)
 
 
 def lon_tile(radius):
-    source = jnp.arange(2 * LANES)[:, None] - LANES // 2
-    target = jnp.arange(LANES)[None, :]
+    source = np.arange(2 * LANES)[:, None] - LANES // 2
+    target = np.arange(LANES)[None, :]
     return tap_matrix(source - target, radius)
 
 
 def lat_block(out_level, out_row, in_level, in_row, rows_total, radius):
-    distance = in_row[None, :] - out_row[:, None]
-    entry = tap_matrix(distance, radius)
+    entry = tap_matrix(in_row[None, :] - out_row[:, None], radius)
     inside = (out_row >= 0) & (out_row < rows_total)
     keep = (out_level[:, None] == in_level[None, :]) & inside[:, None]
-    return jnp.where(keep, entry, 0).astype(BF16)
+    return np.where(keep, entry, 0.0)
+
+
+def lat_operators(levels, rows, bands, radius):
+    reach = 2 * radius
+    first, second = [], []
+    for band in range(bands):
+        base = band * rows
+        if bands == 2:
+            sides = [(base + rows, base + rows) if band == 0 else (base - reach, base - radius)]
+        else:
+            sides = [(base - reach, base - radius), (base + rows, base + rows)]
+
+        def row_list(start, width):
+            level = np.repeat(np.arange(levels), width)
+            return level, np.tile(np.arange(width), levels) + start
+
+        own = row_list(base, rows)
+        join = lambda parts: tuple(np.concatenate(p) for p in zip(*parts))
+        outer = join([own] + [row_list(s[0], reach) for s in sides])
+        inner = join([own] + [row_list(s[1], radius) for s in sides])
+        first.append(lat_block(*inner, *outer, rows * bands, radius))
+        second.append(lat_block(*own, *inner, rows * bands, radius))
+    return np.stack(first), np.stack(second)
 
 
 def split_bf16(x):
@@ -49,9 +72,23 @@
     return hi, lo
 
 
-def onehot(index, count):
-    rows = lax.broadcasted_iota(jnp.int32, (count, index.shape[1]), 0)
-    return jnp.where(rows == index, 1.0, 0.0).astype(BF16)
+def counter(count, width):
+    column = lax.broadcasted_iota(jnp.int32, (count, LANES // 2), 0).astype(F32).astype(BF16)
+    return jnp.concatenate([column] * (width // (LANES // 2)), axis=1)
+
+
+def onehot(blk, row, rows, blocks):
+    count = counter(rows, row.shape[1])
+    one, zero = jnp.ones((), BF16), jnp.zeros((), BF16)
+    parts = []
+    for b in range(blocks):
+        here = jnp.where(blk == b, row, -1).astype(F32).astype(BF16)
+        parts.append(jnp.where(count == here, one, zero))
+    return jnp.concatenate(parts, axis=0)
+
+
+def limit():
+    return pltpu.CompilerParams(vmem_limit_bytes=GRANT)
 
 
 def vmem():
@@ -91,22 +128,17 @@
         out_shape=jax.ShapeDtypeStruct((6 * (index.shape[1] // lon), lon), F32),
         in_specs=[smem(), vmem(), vmem(), vmem()],
         out_specs=vmem(),
+        compiler_params=limit(),
         name="prepare",
     )(roots, index, value, error)
 
 
-def add_onehot(idx, coef, seg, acc):
-    lane = idx % LANES
-    hi, lo = split_bf16(coef)
-    spot = lax.broadcasted_iota(jnp.int32, (LANES, idx.shape[1]), 0) == lane
-    side = jnp.concatenate(
-        [
-            jnp.where(spot, hi.astype(F32), 0.0).astype(BF16),
-            jnp.where(spot, lo.astype(F32), 0.0).astype(BF16),
-        ],
-        axis=0,
-    )
-    hot = onehot(seg, acc.shape[0])
+def add_onehot(idx, coef, blk, row, acc, blocks):
+    lane = (idx % LANES).astype(F32).astype(BF16)
+    spot = counter(LANES, idx.shape[1]) == lane
+    zero = jnp.zeros((), BF16)
+    side = jnp.concatenate([jnp.where(spot, x, zero) for x in split_bf16(coef)], axis=0)
+    hot = onehot(blk, row, acc.shape[0] // blocks, blocks)
     acc[...] += lax.dot_general(
         hot, side, (((1,), (1,)), ((), ())), preferred_element_type=F32
     )
@@ -148,13 +180,12 @@
         idx = place.astype(jnp.int32)
         blk = (idx % lon) // LANES
         if near is None:
-            seg = blk * width + idx // lon
+            row = idx // lon
         else:
             row = (idx // lon) % rows - start_ref[near]
             inside = (row >= 0) & (row < REACH)
-            seg = blk * width + (idx // (lon * rows)) * REACH + row
-            seg = jnp.where(inside, seg, -1)
-        add_onehot(idx, coef, seg, acc)
+            row = jnp.where(inside, (idx // (lon * rows)) * REACH + row, -1)
+        add_onehot(idx, coef, blk, row, acc, lon // LANES)
     for b in range(lon // LANES):
         part = acc[b * width:(b + 1) * width, :]
         out_ref[:, b * LANES:(b + 1) * LANES] = part[:, :LANES] + part[:, LANES:]
@@ -173,12 +204,13 @@
         in_specs=specs,
         out_specs=vmem(),
         scratch_shapes=[pltpu.VMEM(((lon // LANES) * width, 2 * LANES), F32)],
+        compiler_params=limit(),
         name="scatter_own" if near is None else "scatter_near",
     )(*args)
 
 
 def lon_pass(x, tile):
-    lon = x.shape[1]
+    rows, lon = x.shape
     half = LANES // 2
     parts = []
     for j in range(lon // LANES):
@@ -189,8 +221,10 @@
             window = jnp.concatenate([x[:, lo:], x[:, :hi - lon]], axis=1)
         else:
             window = x[:, lo:hi]
-        parts.append(jnp.dot(window, tile, preferred_element_type=F32).astype(BF16))
-    return jnp.concatenate(parts, axis=1)
+        parts.append(window)
+    stacked = jnp.concatenate(parts, axis=0)
+    y = jnp.dot(stacked, tile, preferred_element_type=F32).astype(BF16)
+    return jnp.concatenate([y[j * rows:(j + 1) * rows] for j in range(lon // LANES)], axis=1)
 
 
 def filter_kernel(share, own_ref, ext_ref, grad_ref, gext_ref, var_ref,
@@ -204,9 +238,10 @@
     )
     tile = tile_ref[...]
     first = lon_pass(mixed, tile)
-    first = jnp.dot(lat1_ref[...], first, preferred_element_type=F32).astype(BF16)
+    band = lax.axis_index("band")
+    first = jnp.dot(lat1_ref[band], first, preferred_element_type=F32).astype(BF16)
     second = lon_pass(first, tile)
-    second = jnp.dot(lat2_ref[...], second, preferred_element_type=F32)
+    second = jnp.dot(lat2_ref[band], second, preferred_element_type=F32)
     product = own * second
 
     @pl.when(step == 0)
@@ -243,6 +278,7 @@
         ],
         out_specs=(whole(half), whole(half)),
         scratch_shapes=[pltpu.VMEM((rows, lon), F32)],
+        compiler_params=limit(),
         name="filter_members",
     )(own, ext, grad, gext, variance, tile, lat1, lat2)
 
@@ -269,7 +305,7 @@
             blk = (idx % lon) // LANES
             row = idx // lon - start
             inside = (row >= 0) & (row < rows)
-            hot = onehot(jnp.where(inside, blk * rows + row, -1), blocks * rows)
+            hot = onehot(blk, jnp.where(inside, row, -1), rows, blocks)
             found = jnp.dot(table, hot, preferred_element_type=F32)
             found = found[:LANES] + found[LANES:]
             spot = lax.broadcasted_iota(jnp.int32, found.shape, 0) == idx % LANES
@@ -289,12 +325,14 @@
         ),
         in_specs=[vmem()] * 3,
         out_specs=(vmem(), vmem()),
+        compiler_params=limit(),
         name="gather_places",
     )(keep, got, message)
 
 
 def sums_kernel(second, *refs):
-    tail, message, out_ref = refs[0], refs[1], refs[-1]
+    tail = refs[0][...] + refs[1][...]
+    message, out_ref = refs[2], refs[-1]
     chunks = message.shape[0] // 6
     lon = message.shape[1]
     part = lambda ref, k: ref[k * chunks:(k + 1) * chunks, :]
@@ -302,7 +340,7 @@
     out_ref[...] = jnp.zeros_like(out_ref)
     reached = part(tail, 0)
     if second:
-        text, totals = refs[2], refs[3:-1]
+        text, totals = refs[3], refs[4:-1]
         at_place = scale_of(totals, chunks) * part(text, 0)
         coef, share = weigh(at_place, part(message, 4), part(message, 5))
         along = total(coef * (reached - at_place))
@@ -315,16 +353,17 @@
     out_ref[chunks + 1:chunks + 2, :] = jnp.broadcast_to(curve, (1, out_ref.shape[1]))
 
 
-def sums(tail, message, text=None, totals=()):
+def sums(tails, message, text=None, totals=()):
     chunks, lon = message.shape[0] // 6, message.shape[1]
     second = text is not None
-    args = [tail, message] + ([text, *totals] if second else [])
+    args = [*tails, message] + ([text, *totals] if second else [])
     rows = -(-(chunks + 2) // 8) * 8
     return pl.pallas_call(
         functools.partial(sums_kernel, second),
         out_shape=jax.ShapeDtypeStruct((rows, LANES // 2 if second else lon), F32),
         in_specs=[vmem()] * len(args),
         out_specs=vmem(),
+        compiler_params=limit(),
         name="sums",
     )(*args)
 
@@ -344,6 +383,7 @@
         out_shape=jax.ShapeDtypeStruct(pair.shape[1:], F32),
         in_specs=[vmem()] * len(args),
         out_specs=vmem(),
+        compiler_params=limit(),
         name="combine",
     )(*args)
 
@@ -410,34 +450,16 @@
     n_member, n_band = lax.axis_size("member"), lax.axis_size("band")
     member_pos, band_pos = lax.axis_index("member"), lax.axis_index("band")
     members = members_here * n_member
-    total_rows = lat_rows * n_band
     chunks = obs_index.shape[1] // lon
     bits = member_bits(n_member)
 
     if n_band == 2:
         starts = jnp.where(band_pos == 0, 0, lat_rows - REACH).reshape(1)
-        near = [jnp.where(band_pos == 0, lat_rows, lat_rows - REACH)]
-        near_inner = [jnp.where(band_pos == 0, lat_rows, lat_rows - HALF)]
     else:
         starts = jnp.array([lat_rows - REACH, 0])
-        base = band_pos * lat_rows
-        near = [base - REACH, base + lat_rows]
-        near_inner = [base - HALF, base + lat_rows]
     starts = starts.astype(jnp.int32)
-
-    level_of = jnp.arange(levels)
-    def row_list(start, width):
-        level = jnp.repeat(level_of, width)
-        row = jnp.tile(jnp.arange(width), levels) + start
-        return level, row
-    own_rows = row_list(band_pos * lat_rows, lat_rows)
-    outer = [own_rows] + [row_list(s, REACH) for s in near]
-    inner = [own_rows] + [row_list(s, HALF) for s in near_inner]
-    join = lambda parts: tuple(jnp.concatenate(p) for p in zip(*parts))
-    outer, inner = join(outer), join(inner)
-    lat1 = lat_block(*inner, *outer, total_rows, HALF)
-    lat2 = lat_block(*own_rows, *inner, total_rows, HALF)
-    tile = lon_tile(HALF)
+    lat1, lat2 = (jnp.asarray(m, BF16) for m in lat_operators(levels, lat_rows, n_band, HALF))
+    tile = jnp.asarray(lon_tile(HALF), BF16)
 
     message = prepare(root_ranks, obs_index, obs_value, obs_error, lon)
     message = message + swap(message, bits[0], n_member)
@@ -465,7 +487,7 @@
         which = (3,) if texts else (0, 3)
         keep, send = gather_places(which, keep, got, message)
         piece, tail = reduce_with_tail(keep, send, bits[1:], n_member, member_pos)
-        return piece, tail + swap(tail, bits[0], n_member)
+        return piece, (tail, swap(tail, bits[0], n_member))
 
     def band_totals(text):
         texts = from_bands(text, n_band)

time: 152 us -> 140 us (0.921)
  Pallas kernels: 51.6 us -> 36.1 us
  waiting for transfers between devices: 48.5 us -> 55.1 us
  other arithmetic: 13 us -> 8.07 us
  local copies, waits for them, and re-layouts: 4.78 us -> 7 us
    pallas_call x4, Pallas kernels: 16.2 us -> 9.31 us  [scatter_obs(): pl.pallas_call(functools.partial(scatter_kernel, second, rows, lon, near)...]
    ppermute x3, waiting for transfers between devices: 6.47 us -> 12.5 us  [from_bands(): return [lax.ppermute(x, 'band', [(0, 1), (1, 0)])]]
    pallas_call x2, Pallas kernels: 3.32 us -> 0.3 us  [sums(): pl.pallas_call(functools.partial(sums_kernel, second), out_shape=jax.Shap...]
    pallas_call x2, Pallas kernels: 7.5 us -> 4.57 us  [gather_places(): pl.pallas_call(functools.partial(gather_kernel, which), out_shape=(jax.Sh...]
    unnamed x16 -> x28, local copies, waits for them, and re-layouts: 4.25 us -> 7 us
    select_n x2 -> x0, other arithmetic: 1.57 us -> none  [lat_block(): return jnp.where(keep, entry, 0).astype(BF16)]
    pallas_call x1, Pallas kernels: 1.63 us -> 0.09 us  [combine(): pl.pallas_call(functools.partial(combine_kernel, chunks, len(first)), out...]
  transfers between devices with their start and end apart: 22 -> 22, of which waited for: 20 -> 20; matrix products, arithmetic and copies ran while one was open for 3% -> 0% of each run, Pallas kernels for 6% -> 3%
where the time goes in v3:
time: 140 us
  waiting for transfers between devices  55.1 us (39%)
  Pallas kernels  36.1 us (26%)
  starting transfers between devices  32.9 us (24%)
  other arithmetic  8.07 us (6%)
  local copies, waits for them, and re-layouts  7 us (5%)
    ppermute x18, waiting for transfers between devices, swap(): return lax.ppermute(x, 'member', partner(count, bit))  42.6 us
    ppermute x18, starting transfers between devices, swap(): return lax.ppermute(x, 'member', partner(count, bit))  26.5 us
    pallas_call x2, Pallas kernels, filter_members(): pl.pallas_call(functools.partial(filter_kernel, share), grid=(members,),...  21.3 us
    ppermute x3, waiting for transfers between devices, from_bands(): return [lax.ppermute(x, 'band', [(0, 1), (1, 0)])]  12.5 us
    pallas_call x4, Pallas kernels, scatter_obs(): pl.pallas_call(functools.partial(scatter_kernel, second, rows, lon, near)...  9.31 us
    unnamed x28, local copies, waits for them, and re-layouts  7 us
    pallas_call x2, Pallas kernels, gather_places(): pl.pallas_call(functools.partial(gather_kernel, which), out_shape=(jax.Sh...  4.57 us
    ppermute x3, starting transfers between devices, from_bands(): return [lax.ppermute(x, 'band', [(0, 1), (1, 0)])]  3.56 us
  transfers between devices with their start and end apart: 22, of which 20 were waited for; matrix products, arithmetic and copies ran while one was open for 0% of the time, Pallas kernels for 3%

profile of v3, /device:TPU:0, one launch (start us, length us, event | category | flops | bytes accessed | tf_op | source)
XLA Modules:
  0.0 139.5 jit_solution(10559921071727765106)
XLA Ops:
  0.0 0.7 copy-done.9
  0.7 0.7 copy-done.10
  1.4 0.7 copy-done.11
  2.2 0.7 copy-done.12
  2.8 0.6 prepare.1
  3.4 0.6 collective-permute-start
  3.9 0.9 collective-permute-done
  4.9 2.8 %slice_select_fusion = bf16[8,4,16,1024]{3,2,1,0:T(8,128)(2,1)} fusion(bf16[8,4,32,1024]{3,2,1,0:T(8,128)(2,1)} %param.9, pred[]{:T(512)S(6)} %eq.33), kind=kLoop, calls=%fused_computation | loop fusion | flops 524288 | bytes 3145729 | tf_op jit(solution)/shard_map/jit(_where)/select_n | solution.py:441
  7.7 2.9 %collective-permute-start.1 = (bf16[8,4,16,1024]{3,2,1,0:T(8,128)(2,1)}, bf16[8,4,16,1024]{3,2,1,0:T(8,128)(2,1)S(1)}, u32[]{:S(2)}, u32[]{:S(2)}) collective-permute-start(bf16[8,4,16,1024]{3,2,1,0:T(8,128)(2,1)} %slice_select_fusion), channel_id=1, source_target_pairs={{0,16},{16,0},{1,17},{17,1},{2,18},{18,2},{3,19},{19,3},{4,20},{20... | collective-permute-start | bytes 3145736 | tf_op jit(solution)/shard_map/ppermute | solution.py:442
  10.6 1.5 %collective-permute-start.2 = (f32[24,1024]{1,0:T(8,128)S(1)}, f32[24,1024]{1,0:T(8,128)S(1)}, u32[]{:S(2)}, u32[]{:S(2)}) collective-permute-start(f32[24,1024]{1,0:T(8,128)S(1)} %add.73), channel_id=1, source_target_pairs={{0,2},{1,3},{2,0},{3,1},{4,6},{5,7},{6,4},{7,5},{8,10},{9,11},{10,... | collective-permute-start | bytes 294920 | tf_op jit(solution)/shard_map/ppermute | solution.py:405
  12.1 3.1 %collective-permute-done.2 = f32[24,1024]{1,0:T(8,128)S(1)} collective-permute-done((f32[24,1024]{1,0:T(8,128)S(1)}, f32[24,1024]{1,0:T(8,128)S(1)}, u32[]{:S(2)}, u32[]{:S(2)}) %collective-permute-start.2) | collective-permute-done | bytes 98336 | tf_op jit(solution)/shard_map/ppermute | solution.py:405
  15.2 1.6 %collective-permute-start.3 = (f32[24,1024]{1,0:T(8,128)S(1)}, f32[24,1024]{1,0:T(8,128)S(1)}, u32[]{:S(2)}, u32[]{:S(2)}) collective-permute-start(f32[24,1024]{1,0:T(8,128)S(1)} %add.74), channel_id=1, source_target_pairs={{0,4},{1,5},{2,6},{3,7},{4,0},{5,1},{6,2},{7,3},{8,12},{9,13},{10,... | collective-permute-start | bytes 294920 | tf_op jit(solution)/shard_map/ppermute | solution.py:405
  16.9 3.0 %collective-permute-done.3 = f32[24,1024]{1,0:T(8,128)S(1)} collective-permute-done((f32[24,1024]{1,0:T(8,128)S(1)}, f32[24,1024]{1,0:T(8,128)S(1)}, u32[]{:S(2)}, u32[]{:S(2)}) %collective-permute-start.3) | collective-permute-done | bytes 98336 | tf_op jit(solution)/shard_map/ppermute | solution.py:405
  19.9 2.7 %collective-permute-start.4 = (f32[24,1024]{1,0:T(8,128)S(1)}, f32[24,1024]{1,0:T(8,128)S(1)}, u32[]{:S(2)}, u32[]{:S(2)}) collective-permute-start(f32[24,1024]{1,0:T(8,128)S(1)} %add.75), channel_id=1, source_target_pairs={{0,8},{1,9},{2,10},{3,11},{4,12},{5,13},{6,14},{7,15},{8,0},{9,1},... | collective-permute-start | bytes 294920 | tf_op jit(solution)/shard_map/ppermute | solution.py:405
  22.6 2.9 %collective-permute-done.4 = f32[24,1024]{1,0:T(8,128)S(1)} collective-permute-done((f32[24,1024]{1,0:T(8,128)S(1)}, f32[24,1024]{1,0:T(8,128)S(1)}, u32[]{:S(2)}, u32[]{:S(2)}) %collective-permute-start.4) | collective-permute-done | bytes 98336 | tf_op jit(solution)/shard_map/ppermute | solution.py:405
  25.5 0.3 collective-permute-start.5
  25.8 2.4 %scatter_own.2.grad_ref = f32[128,1024]{1,0:T(8,128)S(1)} custom-call(f32[24,1024]{1,0:T(8,128)S(1)} %add.76.refs_0_.message.refs_2_), custom_call_target="tpu_custom_call" | custom-call | tf_op jit(solution)/shard_map/scatter_own/pallas_call | solution.py:201
  28.2 8.3 %collective-permute-done.5.refs_1_ = f32[24,1024]{1,0:T(8,128)} collective-permute-done((f32[24,1024]{1,0:T(8,128)S(1)}, f32[24,1024]{1,0:T(8,128)}, u32[]{:S(2)}, u32[]{:S(2)}) %collective-permute-start.5) | collective-permute-done | bytes 98336 | tf_op jit(solution)/shard_map/ppermute | solution.py:431
  36.5 2.2 %scatter_near.2.gext_ref = f32[64,1024]{1,0:T(8,128)S(1)} custom-call(s32[1]{0:T(128)} %bitcast.2.refs_0_, f32[24,1024]{1,0:T(8,128)} %collective-permute-done.5.refs_1_), custom_call_target="tpu_custom_call" | custom-call | tf_op jit(solution)/shard_map/scatter_near/pallas_call | solution.py:201
  38.7 1.0 copy-done.1
  39.8 0.9 copy-done.4
  40.7 0.9 copy-done.6
  41.6 10.6 %filter_members.2 = (f32[64,1024]{1,0:T(8,128)S(1)}, f32[64,1024]{1,0:T(8,128)S(1)}) custom-call(bf16[8,128,1024]{2,1,0:T(8,128)(2,1)S(1)} %bitcast.9, bf16[8,64,1024]{2,1,0:T(8,128)(2,1)S(1)} %bitcast.11, f32[128,1024]{1,0:T(8,128)S(1)} %scatter_own.2.grad_ref, f32[64,1024]{1,0:T(8,128)S(1)} %scatter_near.2.gext_ref, f32[128,1024]{1,0:T(8,128)S(1)} %bitcast.13, ...), custom_call_target="tpu_custom_call" | custom-call | tf_op jit(solution)/shard_map/filter_members/pallas_call | solution.py:269
  52.3 1.5 %collective-permute-done.6.got_ref = f32[64,1024]{1,0:T(8,128)S(1)} collective-permute-done((f32[64,1024]{1,0:T(8,128)S(1)}, f32[64,1024]{1,0:T(8,128)S(1)}, u32[]{:S(2)}, u32[]{:S(2)}) %collective-permute-start.6) | collective-permute-done | bytes 262176 | tf_op jit(solution)/shard_map/ppermute | solution.py:405
  53.8 3.2 %gather_places.2 = (f32[32,1024]{1,0:T(8,128)S(1)}, f32[40,1024]{1,0:T(8,128)}) custom-call(f32[64,1024]{1,0:T(8,128)S(1)} %get-tuple-element.17.keep_ref, f32[64,1024]{1,0:T(8,128)S(1)} %collective-permute-done.6.got_ref, f32[24,1024]{1,0:T(8,128)S(1)} %add.76.refs_0_.message.refs_2_), custom_call_target="tpu_custom_call" | custom-call | tf_op jit(solution)/shard_map/gather_places/pallas_call | solution.py:320
  57.0 0.7 copy-done.8
  57.7 1.7 %collective-permute-start.7 = (f32[40,1024]{1,0:T(8,128)}, f32[40,1024]{1,0:T(8,128)}, u32[]{:S(2)}, u32[]{:S(2)}) collective-permute-start(f32[40,1024]{1,0:T(8,128)} %get-tuple-element.20), channel_id=1, source_target_pairs={{0,2},{1,3},{2,0},{3,1},{4,6},{5,7},{6,4},{7,5},{8,10},{9,11},{10,... | collective-permute-start | bytes 491528 | tf_op jit(solution)/shard_map/ppermute | solution.py:405
  59.4 4.8 %collective-permute-done.7 = f32[40,1024]{1,0:T(8,128)} collective-permute-done((f32[40,1024]{1,0:T(8,128)}, f32[40,1024]{1,0:T(8,128)}, u32[]{:S(2)}, u32[]{:S(2)}) %collective-permute-start.7) | collective-permute-done | bytes 163872 | tf_op jit(solution)/shard_map/ppermute | solution.py:405
  64.2 1.0 slice_add_fusion.1
  65.2 0.7 copy-done.13
  65.9 0.8 slice_add_fusion.8
  66.7 0.6 pad_maximum_fusion.4
  67.3 1.8 %collective-permute-start.8 = (f32[24,1024]{1,0:T(8,128)}, f32[24,1024]{1,0:T(8,128)}, u32[]{:S(2)}, u32[]{:S(2)}) collective-permute-start(f32[24,1024]{1,0:T(8,128)} %pad_maximum_fusion.4), channel_id=1, source_target_pairs={{0,4},{1,5},{2,6},{3,7},{4,0},{5,1},{6,2},{7,3},{8,12},{9,13},{10,... | collective-permute-start | bytes 294920 | tf_op jit(solution)/shard_map/ppermute | solution.py:405
  69.2 3.1 %collective-permute-done.8 = f32[24,1024]{1,0:T(8,128)} collective-permute-done((f32[24,1024]{1,0:T(8,128)}, f32[24,1024]{1,0:T(8,128)}, u32[]{:S(2)}, u32[]{:S(2)}) %collective-permute-start.8) | collective-permute-done | bytes 98336 | tf_op jit(solution)/shard_map/ppermute | solution.py:405
  72.3 0.9 slice_add_fusion.3
  73.2 0.8 slice_add_fusion.7
  74.0 2.9 %collective-permute-start.9 = (f32[16,1024]{1,0:T(8,128)S(1)}, f32[16,1024]{1,0:T(8,128)S(1)}, u32[]{:S(2)}, u32[]{:S(2)}) collective-permute-start(f32[16,1024]{1,0:T(8,128)S(1)} %pad_maximum_fusion.6), channel_id=1, source_target_pairs={{0,8},{1,9},{2,10},{3,11},{4,12},{5,13},{6,14},{7,15},{8,0},{9,1},... | collective-permute-start | bytes 196616 | tf_op jit(solution)/shard_map/ppermute | solution.py:405
  76.9 2.3 %collective-permute-done.9 = f32[16,1024]{1,0:T(8,128)S(1)} collective-permute-done((f32[16,1024]{1,0:T(8,128)S(1)}, f32[16,1024]{1,0:T(8,128)S(1)}, u32[]{:S(2)}, u32[]{:S(2)}) %collective-permute-start.9) | collective-permute-done | bytes 65568 | tf_op jit(solution)/shard_map/ppermute | solution.py:405
  79.3 1.2 collective-permute-done.10.refs_1_
  80.5 0.1 sums.2.refs_1_.refs_2_.refs_3_.refs_4_
  80.6 1.7 %collective-permute-start.11 = (f32[8,1024]{1,0:T(8,128)S(1)}, f32[8,1024]{1,0:T(8,128)S(1)}, u32[]{:S(2)}, u32[]{:S(2)}) collective-permute-start(f32[8,1024]{1,0:T(8,128)S(1)} %sums.2.refs_1_.refs_2_.refs_3_.refs_4_), channel_id=1, source_target_pairs={{0,16},{16,0},{1,17},{17,1},{2,18},{18,2},{3,19},{19,3},{4,20},{20... | collective-permute-start | bytes 98312 | tf_op jit(solution)/shard_map/ppermute | solution.py:431
  82.3 2.2 %collective-permute-done.11.refs_3_.refs_2_.refs_4_.refs_5_ = f32[8,1024]{1,0:T(8,128)S(1)} collective-permute-done((f32[8,1024]{1,0:T(8,128)S(1)}, f32[8,1024]{1,0:T(8,128)S(1)}, u32[]{:S(2)}, u32[]{:S(2)}) %collective-permute-start.11) | collective-permute-done | bytes 32800 | tf_op jit(solution)/shard_map/ppermute | solution.py:431
  84.5 2.5 %scatter_own.3.grad_ref = f32[128,1024]{1,0:T(8,128)S(1)} custom-call(f32[24,1024]{1,0:T(8,128)S(1)} %add.76.refs_0_.message.refs_2_, f32[8,1024]{1,0:T(8,128)S(1)} %sums.2.refs_1_.refs_2_.refs_3_.refs_4_, f32[8,1024]{1,0:T(8,128)S(1)} %sums.2.refs_1_.refs_2_.refs_3_.refs_4_, f32[8,1024]{1,0:T(8,128)S(1)} %collective-permute-done.11.refs_3_.refs_2_.refs_4_.refs_5_), custom_call_target="tpu_custom_call" | custom-call | tf_op jit(solution)/shard_map/scatter_own/pallas_call | solution.py:201
  87.0 2.3 %scatter_near.3.gext_ref = f32[64,1024]{1,0:T(8,128)S(1)} custom-call(s32[1]{0:T(128)} %bitcast.2.refs_0_, f32[24,1024]{1,0:T(8,128)} %collective-permute-done.5.refs_1_, f32[8,1024]{1,0:T(8,128)S(1)} %collective-permute-done.11.refs_3_.refs_2_.refs_4_.refs_5_, f32[8,1024]{1,0:T(8,128)S(1)} %sums.2.refs_1_.refs_2_.refs_3_.refs_4_, ...), custom_call_target="tpu_custom_call" | custom-call | tf_op jit(solution)/shard_map/scatter_near/pallas_call | solution.py:201
  89.3 10.7 %filter_members.3 = (f32[64,1024]{1,0:T(8,128)S(1)}, f32[64,1024]{1,0:T(8,128)S(1)}) custom-call(bf16[8,128,1024]{2,1,0:T(8,128)(2,1)S(1)} %bitcast.10, bf16[8,64,1024]{2,1,0:T(8,128)(2,1)S(1)} %bitcast.12, f32[128,1024]{1,0:T(8,128)S(1)} %scatter_own.3.grad_ref, f32[64,1024]{1,0:T(8,128)S(1)} %scatter_near.3.gext_ref, f32[128,1024]{1,0:T(8,128)S(1)} %bitcast.14, ...), custom_call_target="tpu_custom_call" | custom-call | tf_op jit(solution)/shard_map/filter_members/pallas_call | solution.py:269
  100.0 1.5 %collective-permute-done.12.got_ref = f32[64,1024]{1,0:T(8,128)S(1)} collective-permute-done((f32[64,1024]{1,0:T(8,128)S(1)}, f32[64,1024]{1,0:T(8,128)S(1)}, u32[]{:S(2)}, u32[]{:S(2)}) %collective-permute-start.12) | collective-permute-done | bytes 262176 | tf_op jit(solution)/shard_map/ppermute | solution.py:405
  101.6 1.4 gather_places.3
  103.0 1.8 %collective-permute-start.13 = (f32[36,1024]{1,0:T(8,128)S(1)}, f32[36,1024]{1,0:T(8,128)S(1)}, u32[]{:S(2)}, u32[]{:S(2)}) collective-permute-start(f32[36,1024]{1,0:T(8,128)S(1)} %get-tuple-element.24), channel_id=1, source_target_pairs={{0,2},{1,3},{2,0},{3,1},{4,6},{5,7},{6,4},{7,5},{8,10},{9,11},{10,... | collective-permute-start | bytes 442376 | tf_op jit(solution)/shard_map/ppermute | solution.py:405
  104.7 4.5 %collective-permute-done.13 = f32[36,1024]{1,0:T(8,128)S(1)} collective-permute-done((f32[36,1024]{1,0:T(8,128)S(1)}, f32[36,1024]{1,0:T(8,128)S(1)}, u32[]{:S(2)}, u32[]{:S(2)}) %collective-permute-start.13) | collective-permute-done | bytes 147488 | tf_op jit(solution)/shard_map/ppermute | solution.py:405
  109.3 1.9 %collective-permute-start.14 = (f32[20,1024]{1,0:T(8,128)S(1)}, f32[20,1024]{1,0:T(8,128)S(1)}, u32[]{:S(2)}, u32[]{:S(2)}) collective-permute-start(f32[20,1024]{1,0:T(8,128)S(1)} %pad_maximum_fusion.5), channel_id=1, source_target_pairs={{0,4},{1,5},{2,6},{3,7},{4,0},{5,1},{6,2},{7,3},{8,12},{9,13},{10,... | collective-permute-start | bytes 245768 | tf_op jit(solution)/shard_map/ppermute | solution.py:405
  111.2 2.8 %collective-permute-done.14 = f32[20,1024]{1,0:T(8,128)S(1)} collective-permute-done((f32[20,1024]{1,0:T(8,128)S(1)}, f32[20,1024]{1,0:T(8,128)S(1)}, u32[]{:S(2)}, u32[]{:S(2)}) %collective-permute-start.14) | collective-permute-done | bytes 81952 | tf_op jit(solution)/shard_map/ppermute | solution.py:405
  114.1 3.0 %collective-permute-start.15 = (f32[12,1024]{1,0:T(8,128)S(1)}, f32[12,1024]{1,0:T(8,128)S(1)}, u32[]{:S(2)}, u32[]{:S(2)}) collective-permute-start(f32[12,1024]{1,0:T(8,128)S(1)} %pad_maximum_fusion.7), channel_id=1, source_target_pairs={{0,8},{1,9},{2,10},{3,11},{4,12},{5,13},{6,14},{7,15},{8,0},{9,1},... | collective-permute-start | bytes 147464 | tf_op jit(solution)/shard_map/ppermute | solution.py:405
  117.1 2.2 %collective-permute-done.15 = f32[12,1024]{1,0:T(8,128)S(1)} collective-permute-done((f32[12,1024]{1,0:T(8,128)S(1)}, f32[12,1024]{1,0:T(8,128)S(1)}, u32[]{:S(2)}, u32[]{:S(2)}) %collective-permute-start.15) | collective-permute-done | bytes 49184 | tf_op jit(solution)/shard_map/ppermute | solution.py:405
  119.4 3.0 %collective-permute-start.16 = (f32[2,8,1024]{2,1,0:T(8,128)S(1)}, f32[2,8,1024]{2,1,0:T(8,128)S(1)}, u32[]{:S(2)}, u32[]{:S(2)}) collective-permute-start(f32[2,8,1024]{2,1,0:T(8,128)S(1)} %pad_maximum_fusion.8), channel_id=1, source_target_pairs={{0,8},{1,9},{2,10},{3,11},{4,12},{5,13},{6,14},{7,15},{8,0},{9,1},... | collective-permute-start | bytes 196616 | tf_op jit(solution)/shard_map/ppermute | solution.py:405
  122.4 1.2 collective-permute-done.17.refs_1_
  123.6 0.2 sums.3.refs_3_
  123.8 1.5 %collective-permute-start.18 = (f32[8,128]{1,0:T(8,128)S(1)}, f32[8,128]{1,0:T(8,128)S(1)}, u32[]{:S(2)}, u32[]{:S(2)}) collective-permute-start(f32[8,128]{1,0:T(8,128)S(1)} %sums.3.refs_3_), channel_id=1, source_target_pairs={{0,16},{16,0},{1,17},{17,1},{2,18},{18,2},{3,19},{19,3},{4,20},{20... | collective-permute-start | bytes 12296 | tf_op jit(solution)/shard_map/ppermute | solution.py:431
  125.3 2.1 %collective-permute-done.18.refs_4_ = f32[8,128]{1,0:T(8,128)S(1)} collective-permute-done((f32[8,128]{1,0:T(8,128)S(1)}, f32[8,128]{1,0:T(8,128)S(1)}, u32[]{:S(2)}, u32[]{:S(2)}) %collective-permute-start.18) | collective-permute-done | bytes 4128 | tf_op jit(solution)/shard_map/ppermute | solution.py:431
  127.5 2.2 %collective-permute-start.19 = (f32[16,1024]{1,0:T(8,128)S(1)}, f32[16,1024]{1,0:T(8,128)S(1)}, u32[]{:S(2)}, u32[]{:S(2)}) collective-permute-start(f32[16,1024]{1,0:T(8,128)S(1)} %combine.1), channel_id=1, source_target_pairs={{0,4},{1,5},{2,6},{3,7},{4,0},{5,1},{6,2},{7,3},{8,12},{9,13},{10,... | collective-permute-start | bytes 196616 | tf_op jit(solution)/shard_map/ppermute | solution.py:405
  129.7 2.2 %collective-permute-done.19 = f32[16,1024]{1,0:T(8,128)S(1)} collective-permute-done((f32[16,1024]{1,0:T(8,128)S(1)}, f32[16,1024]{1,0:T(8,128)S(1)}, u32[]{:S(2)}, u32[]{:S(2)}) %collective-permute-start.19) | collective-permute-done | bytes 65568 | tf_op jit(solution)/shard_map/ppermute | solution.py:405
  131.9 1.5 %collective-permute-start.20 = (f32[32,1024]{1,0:T(8,128)S(1)}, f32[32,1024]{1,0:T(8,128)S(1)}, u32[]{:S(2)}, u32[]{:S(2)}) collective-permute-start(f32[32,1024]{1,0:T(8,128)S(1)} %pad_maximum_fusion.3), channel_id=1, source_target_pairs={{0,2},{1,3},{2,0},{3,1},{4,6},{5,7},{6,4},{7,5},{8,10},{9,11},{10,... | collective-permute-start | bytes 393224 | tf_op jit(solution)/shard_map/ppermute | solution.py:405
  133.5 3.5 %collective-permute-done.20 = f32[32,1024]{1,0:T(8,128)S(1)} collective-permute-done((f32[32,1024]{1,0:T(8,128)S(1)}, f32[32,1024]{1,0:T(8,128)S(1)}, u32[]{:S(2)}, u32[]{:S(2)}) %collective-permute-start.20) | collective-permute-done | bytes 131104 | tf_op jit(solution)/shard_map/ppermute | solution.py:405
  137.1 1.5 %collective-permute-done.21 = f32[64,1024]{1,0:T(8,128)S(1)} collective-permute-done((f32[64,1024]{1,0:T(8,128)S(1)}, f32[64,1024]{1,0:T(8,128)S(1)}, u32[]{:S(2)}, u32[]{:S(2)}) %collective-permute-start.21) | collective-permute-done | bytes 262176 | tf_op jit(solution)/shard_map/ppermute | solution.py:405
  138.7 0.8 pad_maximum_fusion
  (52 shorter events, 0.7 us)
Async XLA Ops:
  0.0 0.7 copy-start.9
  0.7 0.7 copy-start.10
  1.4 0.7 copy-start.11
  2.2 0.7 copy-start.12
  3.4 1.5 %collective-permute-start = (f32[24,1024]{1,0:T(8,128)S(1)}, f32[24,1024]{1,0:T(8,128)S(1)}, u32[]{:S(2)}, u32[]{:S(2)}) collective-permute-start(f32[24,1024]{1,0:T(8,128)S(1)} %prepare.1), channel_id=1, source_target_pairs={{0,1},{1,0},{2,3},{3,2},{4,5},{5,4},{6,7},{7,6},{8,9},{9,8},{10,11... | collective-permute-start | bytes 294920 | tf_op jit(solution)/shard_map/ppermute | solution.py:405
  4.9 33.8 %copy-start = (bf16[8,4,32,1024]{3,2,1,0:T(8,128)(2,1)S(1)}, bf16[8,4,32,1024]{3,2,1,0:T(8,128)(2,1)}, u32[]{:S(2)}) copy-start(bf16[8,4,32,1024]{3,2,1,0:T(8,128)(2,1)} %param.9) | copy-start | bytes 6291460
  4.9 33.8 %copy-start.3 = (bf16[512,256]{1,0:T(8,128)(2,1)S(1)}, bf16[512,256]{1,0:T(8,128)(2,1)}, u32[]{:S(2)}) copy-start(bf16[512,256]{1,0:T(8,128)(2,1)} %constant.101.clone.tile_ref) | copy-start | bytes 786436
  7.7 31.0 %collective-permute-start.1 = (bf16[8,4,16,1024]{3,2,1,0:T(8,128)(2,1)}, bf16[8,4,16,1024]{3,2,1,0:T(8,128)(2,1)S(1)}, u32[]{:S(2)}, u32[]{:S(2)}) collective-permute-start(bf16[8,4,16,1024]{3,2,1,0:T(8,128)(2,1)} %slice_select_fusion), channel_id=1, source_target_pairs={{0,16},{16,0},{1,17},{17,1},{2,18},{18,2},{3,19},{19,3},{4,20},{20... | collective-permute-start | bytes 3145736 | tf_op jit(solution)/shard_map/ppermute | solution.py:442
  10.6 4.6 %collective-permute-start.2 = (f32[24,1024]{1,0:T(8,128)S(1)}, f32[24,1024]{1,0:T(8,128)S(1)}, u32[]{:S(2)}, u32[]{:S(2)}) collective-permute-start(f32[24,1024]{1,0:T(8,128)S(1)} %add.73), channel_id=1, source_target_pairs={{0,2},{1,3},{2,0},{3,1},{4,6},{5,7},{6,4},{7,5},{8,10},{9,11},{10,... | collective-permute-start | bytes 294920 | tf_op jit(solution)/shard_map/ppermute | solution.py:405
  15.2 4.7 %collective-permute-start.3 = (f32[24,1024]{1,0:T(8,128)S(1)}, f32[24,1024]{1,0:T(8,128)S(1)}, u32[]{:S(2)}, u32[]{:S(2)}) collective-permute-start(f32[24,1024]{1,0:T(8,128)S(1)} %add.74), channel_id=1, source_target_pairs={{0,4},{1,5},{2,6},{3,7},{4,0},{5,1},{6,2},{7,3},{8,12},{9,13},{10,... | collective-permute-start | bytes 294920 | tf_op jit(solution)/shard_map/ppermute | solution.py:405
  19.9 5.6 %collective-permute-start.4 = (f32[24,1024]{1,0:T(8,128)S(1)}, f32[24,1024]{1,0:T(8,128)S(1)}, u32[]{:S(2)}, u32[]{:S(2)}) collective-permute-start(f32[24,1024]{1,0:T(8,128)S(1)} %add.75), channel_id=1, source_target_pairs={{0,8},{1,9},{2,10},{3,11},{4,12},{5,13},{6,14},{7,15},{8,0},{9,1},... | collective-permute-start | bytes 294920 | tf_op jit(solution)/shard_map/ppermute | solution.py:405
  25.5 11.0 %collective-permute-start.5 = (f32[24,1024]{1,0:T(8,128)S(1)}, f32[24,1024]{1,0:T(8,128)}, u32[]{:S(2)}, u32[]{:S(2)}) collective-permute-start(f32[24,1024]{1,0:T(8,128)S(1)} %add.76.refs_0_.message.refs_2_), channel_id=1, source_target_pairs={{0,16},{16,0},{1,17},{17,1},{2,18},{18,2},{3,19},{19,3},{4,20},{20... | collective-permute-start | bytes 294920 | tf_op jit(solution)/shard_map/ppermute | solution.py:431
  38.7 1.0 copy-start.1
  39.8 0.9 copy-start.4
  40.7 0.9 copy-start.6
  52.2 1.6 %collective-permute-start.6 = (f32[64,1024]{1,0:T(8,128)S(1)}, f32[64,1024]{1,0:T(8,128)S(1)}, u32[]{:S(2)}, u32[]{:S(2)}) collective-permute-start(f32[64,1024]{1,0:T(8,128)S(1)} %get-tuple-element.18), channel_id=1, source_target_pairs={{0,1},{1,0},{2,3},{3,2},{4,5},{5,4},{6,7},{7,6},{8,9},{9,8},{10,11... | collective-permute-start | bytes 786440 | tf_op jit(solution)/shard_map/ppermute | solution.py:405
  57.0 0.7 copy-start.8
  57.7 6.6 %collective-permute-start.7 = (f32[40,1024]{1,0:T(8,128)}, f32[40,1024]{1,0:T(8,128)}, u32[]{:S(2)}, u32[]{:S(2)}) collective-permute-start(f32[40,1024]{1,0:T(8,128)} %get-tuple-element.20), channel_id=1, source_target_pairs={{0,2},{1,3},{2,0},{3,1},{4,6},{5,7},{6,4},{7,5},{8,10},{9,11},{10,... | collective-permute-start | bytes 491528 | tf_op jit(solution)/shard_map/ppermute | solution.py:405
  65.2 0.7 copy-start.13
  67.3 4.9 %collective-permute-start.8 = (f32[24,1024]{1,0:T(8,128)}, f32[24,1024]{1,0:T(8,128)}, u32[]{:S(2)}, u32[]{:S(2)}) collective-permute-start(f32[24,1024]{1,0:T(8,128)} %pad_maximum_fusion.4), channel_id=1, source_target_pairs={{0,4},{1,5},{2,6},{3,7},{4,0},{5,1},{6,2},{7,3},{8,12},{9,13},{10,... | collective-permute-start | bytes 294920 | tf_op jit(solution)/shard_map/ppermute | solution.py:405
  69.2 20.1 %copy-start.2 = (f32[4,32,1024]{2,1,0:T(8,128)S(1)}, f32[4,32,1024]{2,1,0:T(8,128)}, u32[]{:S(2)}) copy-start(f32[4,32,1024]{2,1,0:T(8,128)} %param.10) | copy-start | bytes 1572868
  69.2 20.1 %copy-start.5 = (bf16[2,160,192]{2,1,0:T(8,128)(2,1)S(1)}, bf16[2,160,192]{2,1,0:T(8,128)(2,1)}, u32[]{:S(2)}) copy-start(bf16[2,160,192]{2,1,0:T(8,128)(2,1)} %constant.99.clone.lat1_ref) | copy-start | bytes 368644
  69.2 20.1 %copy-start.7 = (bf16[2,128,160]{2,1,0:T(8,128)(2,1)S(1)}, bf16[2,128,160]{2,1,0:T(8,128)(2,1)}, u32[]{:S(2)}) copy-start(bf16[2,128,160]{2,1,0:T(8,128)(2,1)} %constant.100.clone.lat2_ref) | copy-start | bytes 245764
  74.0 5.2 %collective-permute-start.9 = (f32[16,1024]{1,0:T(8,128)S(1)}, f32[16,1024]{1,0:T(8,128)S(1)}, u32[]{:S(2)}, u32[]{:S(2)}) collective-permute-start(f32[16,1024]{1,0:T(8,128)S(1)} %pad_maximum_fusion.6), channel_id=1, source_target_pairs={{0,8},{1,9},{2,10},{3,11},{4,12},{5,13},{6,14},{7,15},{8,0},{9,1},... | collective-permute-start | bytes 196616 | tf_op jit(solution)/shard_map/ppermute | solution.py:405
  79.2 1.3 collective-permute-start.10
  80.6 3.9 %collective-permute-start.11 = (f32[8,1024]{1,0:T(8,128)S(1)}, f32[8,1024]{1,0:T(8,128)S(1)}, u32[]{:S(2)}, u32[]{:S(2)}) collective-permute-start(f32[8,1024]{1,0:T(8,128)S(1)} %sums.2.refs_1_.refs_2_.refs_3_.refs_4_), channel_id=1, source_target_pairs={{0,16},{16,0},{1,17},{17,1},{2,18},{18,2},{3,19},{19,3},{4,20},{20... | collective-permute-start | bytes 98312 | tf_op jit(solution)/shard_map/ppermute | solution.py:431
  100.0 1.6 %collective-permute-start.12 = (f32[64,1024]{1,0:T(8,128)S(1)}, f32[64,1024]{1,0:T(8,128)S(1)}, u32[]{:S(2)}, u32[]{:S(2)}) collective-permute-start(f32[64,1024]{1,0:T(8,128)S(1)} %get-tuple-element.22), channel_id=1, source_target_pairs={{0,1},{1,0},{2,3},{3,2},{4,5},{5,4},{6,7},{7,6},{8,9},{9,8},{10,11... | collective-permute-start | bytes 786440 | tf_op jit(solution)/shard_map/ppermute | solution.py:405
  103.0 6.3 %collective-permute-start.13 = (f32[36,1024]{1,0:T(8,128)S(1)}, f32[36,1024]{1,0:T(8,128)S(1)}, u32[]{:S(2)}, u32[]{:S(2)}) collective-permute-start(f32[36,1024]{1,0:T(8,128)S(1)} %get-tuple-element.24), channel_id=1, source_target_pairs={{0,2},{1,3},{2,0},{3,1},{4,6},{5,7},{6,4},{7,5},{8,10},{9,11},{10,... | collective-permute-start | bytes 442376 | tf_op jit(solution)/shard_map/ppermute | solution.py:405
  109.3 4.7 %collective-permute-start.14 = (f32[20,1024]{1,0:T(8,128)S(1)}, f32[20,1024]{1,0:T(8,128)S(1)}, u32[]{:S(2)}, u32[]{:S(2)}) collective-permute-start(f32[20,1024]{1,0:T(8,128)S(1)} %pad_maximum_fusion.5), channel_id=1, source_target_pairs={{0,4},{1,5},{2,6},{3,7},{4,0},{5,1},{6,2},{7,3},{8,12},{9,13},{10,... | collective-permute-start | bytes 245768 | tf_op jit(solution)/shard_map/ppermute | solution.py:405
  114.1 5.3 %collective-permute-start.15 = (f32[12,1024]{1,0:T(8,128)S(1)}, f32[12,1024]{1,0:T(8,128)S(1)}, u32[]{:S(2)}, u32[]{:S(2)}) collective-permute-start(f32[12,1024]{1,0:T(8,128)S(1)} %pad_maximum_fusion.7), channel_id=1, source_target_pairs={{0,8},{1,9},{2,10},{3,11},{4,12},{5,13},{6,14},{7,15},{8,0},{9,1},... | collective-permute-start | bytes 147464 | tf_op jit(solution)/shard_map/ppermute | solution.py:405
  119.4 5.9 %collective-permute-start.16 = (f32[2,8,1024]{2,1,0:T(8,128)S(1)}, f32[2,8,1024]{2,1,0:T(8,128)S(1)}, u32[]{:S(2)}, u32[]{:S(2)}) collective-permute-start(f32[2,8,1024]{2,1,0:T(8,128)S(1)} %pad_maximum_fusion.8), channel_id=1, source_target_pairs={{0,8},{1,9},{2,10},{3,11},{4,12},{5,13},{6,14},{7,15},{8,0},{9,1},... | collective-permute-start | bytes 196616 | tf_op jit(solution)/shard_map/ppermute | solution.py:405
  122.4 1.2 collective-permute-start.17
  123.8 3.6 %collective-permute-start.18 = (f32[8,128]{1,0:T(8,128)S(1)}, f32[8,128]{1,0:T(8,128)S(1)}, u32[]{:S(2)}, u32[]{:S(2)}) collective-permute-start(f32[8,128]{1,0:T(8,128)S(1)} %sums.3.refs_3_), channel_id=1, source_target_pairs={{0,16},{16,0},{1,17},{17,1},{2,18},{18,2},{3,19},{19,3},{4,20},{20... | collective-permute-start | bytes 12296 | tf_op jit(solution)/shard_map/ppermute | solution.py:431
  127.5 4.5 %collective-permute-start.19 = (f32[16,1024]{1,0:T(8,128)S(1)}, f32[16,1024]{1,0:T(8,128)S(1)}, u32[]{:S(2)}, u32[]{:S(2)}) collective-permute-start(f32[16,1024]{1,0:T(8,128)S(1)} %combine.1), channel_id=1, source_target_pairs={{0,4},{1,5},{2,6},{3,7},{4,0},{5,1},{6,2},{7,3},{8,12},{9,13},{10,... | collective-permute-start | bytes 196616 | tf_op jit(solution)/shard_map/ppermute | solution.py:405
  131.9 5.0 %collective-permute-start.20 = (f32[32,1024]{1,0:T(8,128)S(1)}, f32[32,1024]{1,0:T(8,128)S(1)}, u32[]{:S(2)}, u32[]{:S(2)}) collective-permute-start(f32[32,1024]{1,0:T(8,128)S(1)} %pad_maximum_fusion.3), channel_id=1, source_target_pairs={{0,2},{1,3},{2,0},{3,1},{4,6},{5,7},{6,4},{7,5},{8,10},{9,11},{10,... | collective-permute-start | bytes 393224 | tf_op jit(solution)/shard_map/ppermute | solution.py:405
  137.0 1.6 %collective-permute-start.21 = (f32[64,1024]{1,0:T(8,128)S(1)}, f32[64,1024]{1,0:T(8,128)S(1)}, u32[]{:S(2)}, u32[]{:S(2)}) collective-permute-start(f32[64,1024]{1,0:T(8,128)S(1)} %pad_maximum_fusion.1), channel_id=1, source_target_pairs={{0,1},{1,0},{2,3},{3,2},{4,5},{5,4},{6,7},{7,6},{8,9},{9,8},{10,11... | collective-permute-start | bytes 786440 | tf_op jit(solution)/shard_map/ppermute | solution.py:405

commit v4 on v3

--- a/solution.py
+++ b/solution.py
@@ -17,7 +17,8 @@
 static_share = 0.25
 
 LANES = 256
-GRANT = 20 << 20
+MIB = 1 << 20
+GROUP = 4
 F32 = jnp.float32
 BF16 = jnp.bfloat16
 
@@ -87,8 +88,8 @@
     return jnp.concatenate(parts, axis=0)
 
 
-def limit():
-    return pltpu.CompilerParams(vmem_limit_bytes=GRANT)
+def limit(mebibytes):
+    return pltpu.CompilerParams(vmem_limit_bytes=mebibytes * MIB)
 
 
 def vmem():
@@ -128,7 +129,6 @@
         out_shape=jax.ShapeDtypeStruct((6 * (index.shape[1] // lon), lon), F32),
         in_specs=[smem(), vmem(), vmem(), vmem()],
         out_specs=vmem(),
-        compiler_params=limit(),
         name="prepare",
     )(roots, index, value, error)
 
@@ -204,7 +204,7 @@
         in_specs=specs,
         out_specs=vmem(),
         scratch_shapes=[pltpu.VMEM(((lon // LANES) * width, 2 * LANES), F32)],
-        compiler_params=limit(),
+        compiler_params=limit(8),
         name="scatter_own" if near is None else "scatter_near",
     )(*args)
 
@@ -227,60 +227,73 @@
     return jnp.concatenate([y[j * rows:(j + 1) * rows] for j in range(lon // LANES)], axis=1)
 
 
-def filter_kernel(share, own_ref, ext_ref, grad_ref, gext_ref, var_ref,
-                  tile_ref, lat1_ref, lat2_ref, keep_ref, send_ref, acc_ref):
-    step = pl.program_id(0)
+def filter_kernel(share, own_ref, ext_ref, grad_ref, gext_ref, tile_ref, var_hbm, lat1_hbm,
+                  lat2_hbm, keep_ref, send_ref, acc_ref, var_ref, lat1_ref, lat2_ref, arrived):
     position = lax.axis_index("member")
-    own = own_ref[0].astype(F32)
-    ext = ext_ref[0].astype(F32)
-    mixed = jnp.concatenate(
-        [(own * grad_ref[...]).astype(BF16), (ext * gext_ref[...]).astype(BF16)], axis=0
-    )
-    tile = tile_ref[...]
-    first = lon_pass(mixed, tile)
     band = lax.axis_index("band")
-    first = jnp.dot(lat1_ref[band], first, preferred_element_type=F32).astype(BF16)
-    second = lon_pass(first, tile)
-    second = jnp.dot(lat2_ref[band], second, preferred_element_type=F32)
-    product = own * second
-
-    @pl.when(step == 0)
-    def _():
-        acc_ref[...] = product
-
-    @pl.when(step > 0)
-    def _():
-        acc_ref[...] += product
-
-    @pl.when(step == pl.num_programs(0) - 1)
-    def _():
-        half = keep_ref.shape[0]
-        static = jnp.where(position == 0, static_share, 0.0)
-        bit = position % 2
-        for ref, start in ((keep_ref, bit * half), (send_ref, (1 - bit) * half)):
-            rows = pl.ds(pl.multiple_of(start, half), half)
-            ref[...] = share * acc_ref[rows, :] + static * var_ref[rows, :] * grad_ref[rows, :]
+    members = own_ref.shape[0]
+    loads = [
+        pltpu.make_async_copy(source, target, arrived.at[k])
+        for k, (source, target) in enumerate(
+            [(lat1_hbm.at[band], lat1_ref), (lat2_hbm.at[band], lat2_ref), (var_hbm, var_ref)]
+        )
+    ]
+    for load in loads:
+        load.start()
+    size = GROUP if members % GROUP == 0 else 1
+    for start in range(0, members, size):
+        group = range(start, start + size)
+        mixed = [
+            jnp.concatenate(
+                [
+                    (own_ref[m].astype(F32) * grad_ref[...]).astype(BF16),
+                    (ext_ref[m].astype(F32) * gext_ref[...]).astype(BF16),
+                ],
+                axis=0,
+            )
+            for m in group
+        ]
+        tile = tile_ref[...]
+        first = [lon_pass(x, tile) for x in mixed]
+        if start == 0:
+            loads[0].wait()
+            loads[1].wait()
+        lat1, lat2 = lat1_ref[...], lat2_ref[...]
+        first = [jnp.dot(lat1, x, preferred_element_type=F32).astype(BF16) for x in first]
+        second = [lon_pass(x, tile) for x in first]
+        second = [jnp.dot(lat2, x, preferred_element_type=F32) for x in second]
+        product = own_ref[group[0]].astype(F32) * second[0]
+        for m, x in zip(group[1:], second[1:]):
+            product += own_ref[m].astype(F32) * x
+        acc_ref[...] = product if start == 0 else acc_ref[...] + product
+    loads[2].wait()
+    half = keep_ref.shape[0]
+    static = jnp.where(position == 0, static_share, 0.0)
+    bit = position % 2
+    for ref, start in ((keep_ref, bit * half), (send_ref, (1 - bit) * half)):
+        rows = pl.ds(pl.multiple_of(start, half), half)
+        ref[...] = share * acc_ref[rows, :] + static * var_ref[rows, :] * grad_ref[rows, :]
 
 
 def filter_members(share, own, ext, grad, gext, variance, tile, lat1, lat2):
     members, rows, lon = own.shape
-    whole = lambda a: pl.BlockSpec(a.shape, lambda i: (0,) * a.ndim)
     half = jax.ShapeDtypeStruct((rows // 2, lon), F32)
+    away = pl.BlockSpec(memory_space=pltpu.HBM)
     return pl.pallas_call(
         functools.partial(filter_kernel, share),
-        grid=(members,),
         out_shape=(half, half),
-        in_specs=[
-            pl.BlockSpec((1,) + own.shape[1:], lambda i: (i, 0, 0)),
-            pl.BlockSpec((1,) + ext.shape[1:], lambda i: (i, 0, 0)),
-            whole(grad), whole(gext), whole(variance),
-            whole(tile), whole(lat1), whole(lat2),
+        in_specs=[vmem()] * 5 + [away] * 3,
+        out_specs=(vmem(), vmem()),
+        scratch_shapes=[
+            pltpu.VMEM((rows, lon), F32),
+            pltpu.VMEM((rows, lon), F32),
+            pltpu.VMEM(lat1.shape[1:], BF16),
+            pltpu.VMEM(lat2.shape[1:], BF16),
+            pltpu.SemaphoreType.DMA((3,)),
         ],
-        out_specs=(whole(half), whole(half)),
-        scratch_shapes=[pltpu.VMEM((rows, lon), F32)],
-        compiler_params=limit(),
+        compiler_params=limit(14),
         name="filter_members",
-    )(own, ext, grad, gext, variance, tile, lat1, lat2)
+    )(own, ext, grad, gext, tile, variance, lat1, lat2)
 
 
 def gather_kernel(which, keep_ref, got_ref, message, next_ref, send_ref):
@@ -325,7 +338,7 @@
         ),
         in_specs=[vmem()] * 3,
         out_specs=(vmem(), vmem()),
-        compiler_params=limit(),
+        compiler_params=limit(8),
         name="gather_places",
     )(keep, got, message)
 
@@ -363,7 +376,7 @@
         out_shape=jax.ShapeDtypeStruct((rows, LANES // 2 if second else lon), F32),
         in_specs=[vmem()] * len(args),
         out_specs=vmem(),
-        compiler_params=limit(),
+        compiler_params=limit(2),
         name="sums",
     )(*args)
 
@@ -383,7 +396,7 @@
         out_shape=jax.ShapeDtypeStruct(pair.shape[1:], F32),
         in_specs=[vmem()] * len(args),
         out_specs=vmem(),
-        compiler_params=limit(),
+        compiler_params=limit(2),
         name="combine",
     )(*args)
 
@@ -461,10 +474,9 @@
     lat1, lat2 = (jnp.asarray(m, BF16) for m in lat_operators(levels, lat_rows, n_band, HALF))
     tile = jnp.asarray(lon_tile(HALF), BF16)
 
+    halo = band_halo(ensemble, n_band, band_pos)
     message = prepare(root_ranks, obs_index, obs_value, obs_error, lon)
     message = message + swap(message, bits[0], n_member)
-    ensemble, message = lax.optimization_barrier((ensemble, message))
-    halo = band_halo(ensemble, n_band, band_pos)
     for bit in bits[1:]:
         message = message + swap(message, bit, n_member)
     around = from_bands(message, n_band)

time: 140 us -> 124 us (0.89)
  Pallas kernels: 36.1 us -> 26.2 us
  waiting for transfers between devices: 55.1 us -> 51.4 us
  local copies, waits for them, and re-layouts: 7 us -> 4.16 us
    pallas_call x2, Pallas kernels: 21.3 us -> 10.5 us  [filter_members(): pl.pallas_call(functools.partial(filter_kernel, share), out_shape=(half,...]
    ppermute x3, waiting for transfers between devices: 12.5 us -> 7.97 us  [from_bands(): return [lax.ppermute(x, 'band', [(0, 1), (1, 0)])]]
    unnamed x28 -> x20, local copies, waits for them, and re-layouts: 7 us -> 4.16 us
  transfers between devices with their start and end apart: 22 -> 22, of which waited for: 20 -> 20; matrix products, arithmetic and copies ran while one was open for 0% -> 1% of each run, Pallas kernels for 3% -> 5%
where the time goes in v4:
time: 124 us
  waiting for transfers between devices  51.4 us (41%)
  starting transfers between devices  32.5 us (26%)
  Pallas kernels  26.2 us (21%)
  other arithmetic  8.95 us (7%)
  local copies, waits for them, and re-layouts  4.16 us (3%)
    ppermute x18, waiting for transfers between devices, swap(): return lax.ppermute(x, 'member', partner(count, bit))  43.4 us
    ppermute x18, starting transfers between devices, swap(): return lax.ppermute(x, 'member', partner(count, bit))  25.9 us
    pallas_call x2, Pallas kernels, filter_members(): pl.pallas_call(functools.partial(filter_kernel, share), out_shape=(half,...  10.5 us
    pallas_call x4, Pallas kernels, scatter_obs(): pl.pallas_call(functools.partial(scatter_kernel, second, rows, lon, near)...  9.31 us
    ppermute x3, waiting for transfers between devices, from_bands(): return [lax.ppermute(x, 'band', [(0, 1), (1, 0)])]  7.97 us
    pallas_call x2, Pallas kernels, gather_places(): pl.pallas_call(functools.partial(gather_kernel, which), out_shape=(jax.Sh...  4.57 us
    unnamed x20, local copies, waits for them, and re-layouts  4.16 us
    ppermute x3, starting transfers between devices, from_bands(): return [lax.ppermute(x, 'band', [(0, 1), (1, 0)])]  3.58 us
  transfers between devices with their start and end apart: 22, of which 20 were waited for; matrix products, arithmetic and copies ran while one was open for 1% of the time, Pallas kernels for 5%

profile of v4, /device:TPU:0, one launch (start us, length us, event | category | flops | bytes accessed | tf_op | source)
XLA Modules:
  0.0 123.5 jit_solution(1358974970002094316)
XLA Ops:
  0.0 2.8 %slice_select_fusion = bf16[8,4,16,1024]{3,2,1,0:T(8,128)(2,1)} fusion(bf16[8,4,32,1024]{3,2,1,0:T(8,128)(2,1)} %param.9, pred[]{:T(512)S(6)} %eq.33), kind=kLoop, calls=%fused_computation | loop fusion | flops 524288 | bytes 3145729 | tf_op jit(solution)/shard_map/jit(_where)/select_n | solution.py:454
  2.8 3.0 %collective-permute-start = (bf16[8,4,16,1024]{3,2,1,0:T(8,128)(2,1)}, bf16[8,4,16,1024]{3,2,1,0:T(8,128)(2,1)S(1)}, u32[]{:S(2)}, u32[]{:S(2)}) collective-permute-start(bf16[8,4,16,1024]{3,2,1,0:T(8,128)(2,1)} %slice_select_fusion), channel_id=1, source_target_pairs={{0,16},{16,0},{1,17},{17,1},{2,18},{18,2},{3,19},{19,3},{4,20},{20... | collective-permute-start | bytes 3145736 | tf_op jit(solution)/shard_map/ppermute | solution.py:455
  5.8 1.5 %prepare.1 = f32[24,1024]{1,0:T(8,128)} custom-call(s32[2]{0:T(128)} %roots.1, s32[1,4096]{1,0:T(1,128)} %idx_ref.1, f32[1,4096]{1,0:T(1,128)} %value_ref.1, f32[1,4096]{1,0:T(1,128)} %error_ref.1), custom_call_target="tpu_custom_call" | custom-call | tf_op jit(solution)/shard_map/prepare/pallas_call | solution.py:127
  7.3 1.5 %collective-permute-done.1 = f32[24,1024]{1,0:T(8,128)S(1)} collective-permute-done((f32[24,1024]{1,0:T(8,128)}, f32[24,1024]{1,0:T(8,128)S(1)}, u32[]{:S(2)}, u32[]{:S(2)}) %collective-permute-start.1) | collective-permute-done | bytes 98336 | tf_op jit(solution)/shard_map/ppermute | solution.py:418
  8.8 0.9 add.73
  9.7 1.6 %collective-permute-start.2 = (f32[24,1024]{1,0:T(8,128)S(1)}, f32[24,1024]{1,0:T(8,128)S(1)}, u32[]{:S(2)}, u32[]{:S(2)}) collective-permute-start(f32[24,1024]{1,0:T(8,128)S(1)} %add.73), channel_id=1, source_target_pairs={{0,2},{1,3},{2,0},{3,1},{4,6},{5,7},{6,4},{7,5},{8,10},{9,11},{10,... | collective-permute-start | bytes 294920 | tf_op jit(solution)/shard_map/ppermute | solution.py:418
  11.2 3.4 %collective-permute-done.2 = f32[24,1024]{1,0:T(8,128)S(1)} collective-permute-done((f32[24,1024]{1,0:T(8,128)S(1)}, f32[24,1024]{1,0:T(8,128)S(1)}, u32[]{:S(2)}, u32[]{:S(2)}) %collective-permute-start.2) | collective-permute-done | bytes 98336 | tf_op jit(solution)/shard_map/ppermute | solution.py:418
  14.6 1.6 %collective-permute-start.3 = (f32[24,1024]{1,0:T(8,128)S(1)}, f32[24,1024]{1,0:T(8,128)S(1)}, u32[]{:S(2)}, u32[]{:S(2)}) collective-permute-start(f32[24,1024]{1,0:T(8,128)S(1)} %add.74), channel_id=1, source_target_pairs={{0,4},{1,5},{2,6},{3,7},{4,0},{5,1},{6,2},{7,3},{8,12},{9,13},{10,... | collective-permute-start | bytes 294920 | tf_op jit(solution)/shard_map/ppermute | solution.py:418
  16.3 3.0 %collective-permute-done.3 = f32[24,1024]{1,0:T(8,128)S(1)} collective-permute-done((f32[24,1024]{1,0:T(8,128)S(1)}, f32[24,1024]{1,0:T(8,128)S(1)}, u32[]{:S(2)}, u32[]{:S(2)}) %collective-permute-start.3) | collective-permute-done | bytes 98336 | tf_op jit(solution)/shard_map/ppermute | solution.py:418
  19.3 2.7 %collective-permute-start.4 = (f32[24,1024]{1,0:T(8,128)S(1)}, f32[24,1024]{1,0:T(8,128)S(1)}, u32[]{:S(2)}, u32[]{:S(2)}) collective-permute-start(f32[24,1024]{1,0:T(8,128)S(1)} %add.75), channel_id=1, source_target_pairs={{0,8},{1,9},{2,10},{3,11},{4,12},{5,13},{6,14},{7,15},{8,0},{9,1},... | collective-permute-start | bytes 294920 | tf_op jit(solution)/shard_map/ppermute | solution.py:418
  22.0 2.9 %collective-permute-done.4 = f32[24,1024]{1,0:T(8,128)S(1)} collective-permute-done((f32[24,1024]{1,0:T(8,128)S(1)}, f32[24,1024]{1,0:T(8,128)S(1)}, u32[]{:S(2)}, u32[]{:S(2)}) %collective-permute-start.4) | collective-permute-done | bytes 98336 | tf_op jit(solution)/shard_map/ppermute | solution.py:418
  24.9 0.3 collective-permute-start.5
  25.2 2.4 %scatter_own.2.grad_ref = f32[128,1024]{1,0:T(8,128)S(1)} custom-call(f32[24,1024]{1,0:T(8,128)S(1)} %add.76.refs_0_.message.refs_2_), custom_call_target="tpu_custom_call" | custom-call | tf_op jit(solution)/shard_map/scatter_own/pallas_call | solution.py:201
  27.6 3.7 %collective-permute-done.5.refs_1_ = f32[24,1024]{1,0:T(8,128)} collective-permute-done((f32[24,1024]{1,0:T(8,128)S(1)}, f32[24,1024]{1,0:T(8,128)}, u32[]{:S(2)}, u32[]{:S(2)}) %collective-permute-start.5) | collective-permute-done | bytes 98336 | tf_op jit(solution)/shard_map/ppermute | solution.py:444
  31.4 2.2 %scatter_near.2.gext_ref = f32[64,1024]{1,0:T(8,128)S(1)} custom-call(s32[1]{0:T(128)} %bitcast.2.refs_0_, f32[24,1024]{1,0:T(8,128)} %collective-permute-done.5.refs_1_), custom_call_target="tpu_custom_call" | custom-call | tf_op jit(solution)/shard_map/scatter_near/pallas_call | solution.py:201
  33.6 1.0 copy-done.1
  34.7 0.9 copy-done.4
  35.6 0.9 copy-done.6
  36.5 5.1 %filter_members.2 = (f32[64,1024]{1,0:T(8,128)S(1)}, f32[64,1024]{1,0:T(8,128)S(1)}) custom-call(bf16[8,128,1024]{2,1,0:T(8,128)(2,1)S(1)} %bitcast.9, bf16[8,64,1024]{2,1,0:T(8,128)(2,1)S(1)} %bitcast.11, f32[128,1024]{1,0:T(8,128)S(1)} %scatter_own.2.grad_ref, f32[64,1024]{1,0:T(8,128)S(1)} %scatter_near.2.gext_ref, bf16[512,256]{1,0:T(8,128)(2,1)S(1)} %copy-done.3, ...), custom_call_target="tpu_custom_call" | custom-call | tf_op jit(solution)/shard_map/filter_members/pallas_call | solution.py:282
  41.6 0.1 collective-permute-start.6
  41.7 1.5 %collective-permute-done.6.got_ref = f32[64,1024]{1,0:T(8,128)S(1)} collective-permute-done((f32[64,1024]{1,0:T(8,128)S(1)}, f32[64,1024]{1,0:T(8,128)S(1)}, u32[]{:S(2)}, u32[]{:S(2)}) %collective-permute-start.6) | collective-permute-done | bytes 262176 | tf_op jit(solution)/shard_map/ppermute | solution.py:418
  43.2 3.2 %gather_places.2 = (f32[32,1024]{1,0:T(8,128)S(1)}, f32[40,1024]{1,0:T(8,128)}) custom-call(f32[64,1024]{1,0:T(8,128)S(1)} %get-tuple-element.13.keep_ref, f32[64,1024]{1,0:T(8,128)S(1)} %collective-permute-done.6.got_ref, f32[24,1024]{1,0:T(8,128)S(1)} %add.76.refs_0_.message.refs_2_), custom_call_target="tpu_custom_call" | custom-call | tf_op jit(solution)/shard_map/gather_places/pallas_call | solution.py:333
  46.4 0.6 copy-done.8
  47.0 1.7 %collective-permute-start.7 = (f32[40,1024]{1,0:T(8,128)}, f32[40,1024]{1,0:T(8,128)}, u32[]{:S(2)}, u32[]{:S(2)}) collective-permute-start(f32[40,1024]{1,0:T(8,128)} %get-tuple-element.16), channel_id=1, source_target_pairs={{0,2},{1,3},{2,0},{3,1},{4,6},{5,7},{6,4},{7,5},{8,10},{9,11},{10,... | collective-permute-start | bytes 491528 | tf_op jit(solution)/shard_map/ppermute | solution.py:418
  48.7 4.8 %collective-permute-done.7 = f32[40,1024]{1,0:T(8,128)} collective-permute-done((f32[40,1024]{1,0:T(8,128)}, f32[40,1024]{1,0:T(8,128)}, u32[]{:S(2)}, u32[]{:S(2)}) %collective-permute-start.7) | collective-permute-done | bytes 163872 | tf_op jit(solution)/shard_map/ppermute | solution.py:418
  53.6 1.0 slice_add_fusion.1
  54.6 0.6 copy-done.9
  55.2 0.8 slice_add_fusion.8
  56.0 0.6 pad_maximum_fusion.4
  56.6 1.8 %collective-permute-start.8 = (f32[24,1024]{1,0:T(8,128)}, f32[24,1024]{1,0:T(8,128)}, u32[]{:S(2)}, u32[]{:S(2)}) collective-permute-start(f32[24,1024]{1,0:T(8,128)} %pad_maximum_fusion.4), channel_id=1, source_target_pairs={{0,4},{1,5},{2,6},{3,7},{4,0},{5,1},{6,2},{7,3},{8,12},{9,13},{10,... | collective-permute-start | bytes 294920 | tf_op jit(solution)/shard_map/ppermute | solution.py:418
  58.5 3.1 %collective-permute-done.8 = f32[24,1024]{1,0:T(8,128)} collective-permute-done((f32[24,1024]{1,0:T(8,128)}, f32[24,1024]{1,0:T(8,128)}, u32[]{:S(2)}, u32[]{:S(2)}) %collective-permute-start.8) | collective-permute-done | bytes 98336 | tf_op jit(solution)/shard_map/ppermute | solution.py:418
  61.6 0.9 slice_add_fusion.3
  62.5 0.8 slice_add_fusion.7
  63.3 2.9 %collective-permute-start.9 = (f32[16,1024]{1,0:T(8,128)S(1)}, f32[16,1024]{1,0:T(8,128)S(1)}, u32[]{:S(2)}, u32[]{:S(2)}) collective-permute-start(f32[16,1024]{1,0:T(8,128)S(1)} %pad_maximum_fusion.6), channel_id=1, source_target_pairs={{0,8},{1,9},{2,10},{3,11},{4,12},{5,13},{6,14},{7,15},{8,0},{9,1},... | collective-permute-start | bytes 196616 | tf_op jit(solution)/shard_map/ppermute | solution.py:418
  66.2 2.4 %collective-permute-done.9 = f32[16,1024]{1,0:T(8,128)S(1)} collective-permute-done((f32[16,1024]{1,0:T(8,128)S(1)}, f32[16,1024]{1,0:T(8,128)S(1)}, u32[]{:S(2)}, u32[]{:S(2)}) %collective-permute-start.9) | collective-permute-done | bytes 65568 | tf_op jit(solution)/shard_map/ppermute | solution.py:418
  68.5 0.1 collective-permute-start.10
  68.6 1.2 collective-permute-done.10.refs_1_
  69.8 0.1 sums.2.refs_1_.refs_2_.refs_3_.refs_4_
  69.9 1.7 %collective-permute-start.11 = (f32[8,1024]{1,0:T(8,128)S(1)}, f32[8,1024]{1,0:T(8,128)S(1)}, u32[]{:S(2)}, u32[]{:S(2)}) collective-permute-start(f32[8,1024]{1,0:T(8,128)S(1)} %sums.2.refs_1_.refs_2_.refs_3_.refs_4_), channel_id=1, source_target_pairs={{0,16},{16,0},{1,17},{17,1},{2,18},{18,2},{3,19},{19,3},{4,20},{20... | collective-permute-start | bytes 98312 | tf_op jit(solution)/shard_map/ppermute | solution.py:444
  71.6 2.2 %collective-permute-done.11.refs_3_.refs_2_.refs_4_.refs_5_ = f32[8,1024]{1,0:T(8,128)S(1)} collective-permute-done((f32[8,1024]{1,0:T(8,128)S(1)}, f32[8,1024]{1,0:T(8,128)S(1)}, u32[]{:S(2)}, u32[]{:S(2)}) %collective-permute-start.11) | collective-permute-done | bytes 32800 | tf_op jit(solution)/shard_map/ppermute | solution.py:444
  73.8 2.5 %scatter_own.3.grad_ref = f32[128,1024]{1,0:T(8,128)S(1)} custom-call(f32[24,1024]{1,0:T(8,128)S(1)} %add.76.refs_0_.message.refs_2_, f32[8,1024]{1,0:T(8,128)S(1)} %sums.2.refs_1_.refs_2_.refs_3_.refs_4_, f32[8,1024]{1,0:T(8,128)S(1)} %sums.2.refs_1_.refs_2_.refs_3_.refs_4_, f32[8,1024]{1,0:T(8,128)S(1)} %collective-permute-done.11.refs_3_.refs_2_.refs_4_.refs_5_), custom_call_target="tpu_custom_call" | custom-call | tf_op jit(solution)/shard_map/scatter_own/pallas_call | solution.py:201
  76.3 2.3 %scatter_near.3.gext_ref = f32[64,1024]{1,0:T(8,128)S(1)} custom-call(s32[1]{0:T(128)} %bitcast.2.refs_0_, f32[24,1024]{1,0:T(8,128)} %collective-permute-done.5.refs_1_, f32[8,1024]{1,0:T(8,128)S(1)} %collective-permute-done.11.refs_3_.refs_2_.refs_4_.refs_5_, f32[8,1024]{1,0:T(8,128)S(1)} %sums.2.refs_1_.refs_2_.refs_3_.refs_4_, ...), custom_call_target="tpu_custom_call" | custom-call | tf_op jit(solution)/shard_map/scatter_near/pallas_call | solution.py:201
  78.6 5.4 %filter_members.3 = (f32[64,1024]{1,0:T(8,128)S(1)}, f32[64,1024]{1,0:T(8,128)S(1)}) custom-call(bf16[8,128,1024]{2,1,0:T(8,128)(2,1)S(1)} %bitcast.10, bf16[8,64,1024]{2,1,0:T(8,128)(2,1)S(1)} %bitcast.12, f32[128,1024]{1,0:T(8,128)S(1)} %scatter_own.3.grad_ref, f32[64,1024]{1,0:T(8,128)S(1)} %scatter_near.3.gext_ref, bf16[512,256]{1,0:T(8,128)(2,1)S(1)} %copy-done.3, ...), custom_call_target="tpu_custom_call" | custom-call | tf_op jit(solution)/shard_map/filter_members/pallas_call | solution.py:282
  84.0 0.1 collective-permute-start.12
  84.1 1.5 %collective-permute-done.12.got_ref = f32[64,1024]{1,0:T(8,128)S(1)} collective-permute-done((f32[64,1024]{1,0:T(8,128)S(1)}, f32[64,1024]{1,0:T(8,128)S(1)}, u32[]{:S(2)}, u32[]{:S(2)}) %collective-permute-start.12) | collective-permute-done | bytes 262176 | tf_op jit(solution)/shard_map/ppermute | solution.py:418
  85.6 1.4 %gather_places.3 = (f32[32,1024]{1,0:T(8,128)S(1)}, f32[36,1024]{1,0:T(8,128)S(1)}) custom-call(f32[64,1024]{1,0:T(8,128)S(1)} %get-tuple-element.17.keep_ref, f32[64,1024]{1,0:T(8,128)S(1)} %collective-permute-done.12.got_ref, f32[24,1024]{1,0:T(8,128)S(1)} %add.76.refs_0_.message.refs_2_), custom_call_target="tpu_custom_call" | custom-call | tf_op jit(solution)/shard_map/gather_places/pallas_call | solution.py:333
  87.0 1.8 %collective-permute-start.13 = (f32[36,1024]{1,0:T(8,128)S(1)}, f32[36,1024]{1,0:T(8,128)S(1)}, u32[]{:S(2)}, u32[]{:S(2)}) collective-permute-start(f32[36,1024]{1,0:T(8,128)S(1)} %get-tuple-element.20), channel_id=1, source_target_pairs={{0,2},{1,3},{2,0},{3,1},{4,6},{5,7},{6,4},{7,5},{8,10},{9,11},{10,... | collective-permute-start | bytes 442376 | tf_op jit(solution)/shard_map/ppermute | solution.py:418
  88.8 4.5 %collective-permute-done.13 = f32[36,1024]{1,0:T(8,128)S(1)} collective-permute-done((f32[36,1024]{1,0:T(8,128)S(1)}, f32[36,1024]{1,0:T(8,128)S(1)}, u32[]{:S(2)}, u32[]{:S(2)}) %collective-permute-start.13) | collective-permute-done | bytes 147488 | tf_op jit(solution)/shard_map/ppermute | solution.py:418
  93.4 1.9 %collective-permute-start.14 = (f32[20,1024]{1,0:T(8,128)S(1)}, f32[20,1024]{1,0:T(8,128)S(1)}, u32[]{:S(2)}, u32[]{:S(2)}) collective-permute-start(f32[20,1024]{1,0:T(8,128)S(1)} %pad_maximum_fusion.5), channel_id=1, source_target_pairs={{0,4},{1,5},{2,6},{3,7},{4,0},{5,1},{6,2},{7,3},{8,12},{9,13},{10,... | collective-permute-start | bytes 245768 | tf_op jit(solution)/shard_map/ppermute | solution.py:418
  95.2 2.8 %collective-permute-done.14 = f32[20,1024]{1,0:T(8,128)S(1)} collective-permute-done((f32[20,1024]{1,0:T(8,128)S(1)}, f32[20,1024]{1,0:T(8,128)S(1)}, u32[]{:S(2)}, u32[]{:S(2)}) %collective-permute-start.14) | collective-permute-done | bytes 81952 | tf_op jit(solution)/shard_map/ppermute | solution.py:418
  98.1 3.0 %collective-permute-start.15 = (f32[12,1024]{1,0:T(8,128)S(1)}, f32[12,1024]{1,0:T(8,128)S(1)}, u32[]{:S(2)}, u32[]{:S(2)}) collective-permute-start(f32[12,1024]{1,0:T(8,128)S(1)} %pad_maximum_fusion.7), channel_id=1, source_target_pairs={{0,8},{1,9},{2,10},{3,11},{4,12},{5,13},{6,14},{7,15},{8,0},{9,1},... | collective-permute-start | bytes 147464 | tf_op jit(solution)/shard_map/ppermute | solution.py:418
  101.1 2.2 %collective-permute-done.15 = f32[12,1024]{1,0:T(8,128)S(1)} collective-permute-done((f32[12,1024]{1,0:T(8,128)S(1)}, f32[12,1024]{1,0:T(8,128)S(1)}, u32[]{:S(2)}, u32[]{:S(2)}) %collective-permute-start.15) | collective-permute-done | bytes 49184 | tf_op jit(solution)/shard_map/ppermute | solution.py:418
  103.4 3.0 %collective-permute-start.16 = (f32[2,8,1024]{2,1,0:T(8,128)S(1)}, f32[2,8,1024]{2,1,0:T(8,128)S(1)}, u32[]{:S(2)}, u32[]{:S(2)}) collective-permute-start(f32[2,8,1024]{2,1,0:T(8,128)S(1)} %pad_maximum_fusion.8), channel_id=1, source_target_pairs={{0,8},{1,9},{2,10},{3,11},{4,12},{5,13},{6,14},{7,15},{8,0},{9,1},... | collective-permute-start | bytes 196616 | tf_op jit(solution)/shard_map/ppermute | solution.py:418
  106.4 1.2 collective-permute-done.17.refs_1_
  107.6 0.2 sums.3.refs_3_
  107.8 1.5 %collective-permute-start.18 = (f32[8,128]{1,0:T(8,128)S(1)}, f32[8,128]{1,0:T(8,128)S(1)}, u32[]{:S(2)}, u32[]{:S(2)}) collective-permute-start(f32[8,128]{1,0:T(8,128)S(1)} %sums.3.refs_3_), channel_id=1, source_target_pairs={{0,16},{16,0},{1,17},{17,1},{2,18},{18,2},{3,19},{19,3},{4,20},{20... | collective-permute-start | bytes 12296 | tf_op jit(solution)/shard_map/ppermute | solution.py:444
  109.3 2.1 %collective-permute-done.18.refs_4_ = f32[8,128]{1,0:T(8,128)S(1)} collective-permute-done((f32[8,128]{1,0:T(8,128)S(1)}, f32[8,128]{1,0:T(8,128)S(1)}, u32[]{:S(2)}, u32[]{:S(2)}) %collective-permute-start.18) | collective-permute-done | bytes 4128 | tf_op jit(solution)/shard_map/ppermute | solution.py:444
  111.4 0.1 combine.1
  111.5 2.2 %collective-permute-start.19 = (f32[16,1024]{1,0:T(8,128)S(1)}, f32[16,1024]{1,0:T(8,128)S(1)}, u32[]{:S(2)}, u32[]{:S(2)}) collective-permute-start(f32[16,1024]{1,0:T(8,128)S(1)} %combine.1), channel_id=1, source_target_pairs={{0,4},{1,5},{2,6},{3,7},{4,0},{5,1},{6,2},{7,3},{8,12},{9,13},{10,... | collective-permute-start | bytes 196616 | tf_op jit(solution)/shard_map/ppermute | solution.py:418
  113.7 2.2 %collective-permute-done.19 = f32[16,1024]{1,0:T(8,128)S(1)} collective-permute-done((f32[16,1024]{1,0:T(8,128)S(1)}, f32[16,1024]{1,0:T(8,128)S(1)}, u32[]{:S(2)}, u32[]{:S(2)}) %collective-permute-start.19) | collective-permute-done | bytes 65568 | tf_op jit(solution)/shard_map/ppermute | solution.py:418
  116.0 1.6 %collective-permute-start.20 = (f32[32,1024]{1,0:T(8,128)S(1)}, f32[32,1024]{1,0:T(8,128)S(1)}, u32[]{:S(2)}, u32[]{:S(2)}) collective-permute-start(f32[32,1024]{1,0:T(8,128)S(1)} %pad_maximum_fusion.3), channel_id=1, source_target_pairs={{0,2},{1,3},{2,0},{3,1},{4,6},{5,7},{6,4},{7,5},{8,10},{9,11},{10,... | collective-permute-start | bytes 393224 | tf_op jit(solution)/shard_map/ppermute | solution.py:418
  117.5 3.5 %collective-permute-done.20 = f32[32,1024]{1,0:T(8,128)S(1)} collective-permute-done((f32[32,1024]{1,0:T(8,128)S(1)}, f32[32,1024]{1,0:T(8,128)S(1)}, u32[]{:S(2)}, u32[]{:S(2)}) %collective-permute-start.20) | collective-permute-done | bytes 131104 | tf_op jit(solution)/shard_map/ppermute | solution.py:418
  121.1 1.5 %collective-permute-done.21 = f32[64,1024]{1,0:T(8,128)S(1)} collective-permute-done((f32[64,1024]{1,0:T(8,128)S(1)}, f32[64,1024]{1,0:T(8,128)S(1)}, u32[]{:S(2)}, u32[]{:S(2)}) %collective-permute-start.21) | collective-permute-done | bytes 262176 | tf_op jit(solution)/shard_map/ppermute | solution.py:418
  122.7 0.8 pad_maximum_fusion
  (44 shorter events, 0.4 us)
Async XLA Ops:
  0.0 33.6 %copy-start = (bf16[8,4,32,1024]{3,2,1,0:T(8,128)(2,1)S(1)}, bf16[8,4,32,1024]{3,2,1,0:T(8,128)(2,1)}, u32[]{:S(2)}) copy-start(bf16[8,4,32,1024]{3,2,1,0:T(8,128)(2,1)} %param.9) | copy-start | bytes 6291460
  0.0 33.6 %copy-start.3 = (bf16[512,256]{1,0:T(8,128)(2,1)S(1)}, bf16[512,256]{1,0:T(8,128)(2,1)}, u32[]{:S(2)}) copy-start(bf16[512,256]{1,0:T(8,128)(2,1)} %constant.101.clone.tile_ref) | copy-start | bytes 786436
  2.8 30.8 %collective-permute-start = (bf16[8,4,16,1024]{3,2,1,0:T(8,128)(2,1)}, bf16[8,4,16,1024]{3,2,1,0:T(8,128)(2,1)S(1)}, u32[]{:S(2)}, u32[]{:S(2)}) collective-permute-start(bf16[8,4,16,1024]{3,2,1,0:T(8,128)(2,1)} %slice_select_fusion), channel_id=1, source_target_pairs={{0,16},{16,0},{1,17},{17,1},{2,18},{18,2},{3,19},{19,3},{4,20},{20... | collective-permute-start | bytes 3145736 | tf_op jit(solution)/shard_map/ppermute | solution.py:455
  7.3 1.5 %collective-permute-start.1 = (f32[24,1024]{1,0:T(8,128)}, f32[24,1024]{1,0:T(8,128)S(1)}, u32[]{:S(2)}, u32[]{:S(2)}) collective-permute-start(f32[24,1024]{1,0:T(8,128)} %prepare.1), channel_id=1, source_target_pairs={{0,1},{1,0},{2,3},{3,2},{4,5},{5,4},{6,7},{7,6},{8,9},{9,8},{10,11... | collective-permute-start | bytes 294920 | tf_op jit(solution)/shard_map/ppermute | solution.py:418
  9.7 4.9 %collective-permute-start.2 = (f32[24,1024]{1,0:T(8,128)S(1)}, f32[24,1024]{1,0:T(8,128)S(1)}, u32[]{:S(2)}, u32[]{:S(2)}) collective-permute-start(f32[24,1024]{1,0:T(8,128)S(1)} %add.73), channel_id=1, source_target_pairs={{0,2},{1,3},{2,0},{3,1},{4,6},{5,7},{6,4},{7,5},{8,10},{9,11},{10,... | collective-permute-start | bytes 294920 | tf_op jit(solution)/shard_map/ppermute | solution.py:418
  14.6 4.7 %collective-permute-start.3 = (f32[24,1024]{1,0:T(8,128)S(1)}, f32[24,1024]{1,0:T(8,128)S(1)}, u32[]{:S(2)}, u32[]{:S(2)}) collective-permute-start(f32[24,1024]{1,0:T(8,128)S(1)} %add.74), channel_id=1, source_target_pairs={{0,4},{1,5},{2,6},{3,7},{4,0},{5,1},{6,2},{7,3},{8,12},{9,13},{10,... | collective-permute-start | bytes 294920 | tf_op jit(solution)/shard_map/ppermute | solution.py:418
  19.3 5.6 %collective-permute-start.4 = (f32[24,1024]{1,0:T(8,128)S(1)}, f32[24,1024]{1,0:T(8,128)S(1)}, u32[]{:S(2)}, u32[]{:S(2)}) collective-permute-start(f32[24,1024]{1,0:T(8,128)S(1)} %add.75), channel_id=1, source_target_pairs={{0,8},{1,9},{2,10},{3,11},{4,12},{5,13},{6,14},{7,15},{8,0},{9,1},... | collective-permute-start | bytes 294920 | tf_op jit(solution)/shard_map/ppermute | solution.py:418
  24.9 6.4 %collective-permute-start.5 = (f32[24,1024]{1,0:T(8,128)S(1)}, f32[24,1024]{1,0:T(8,128)}, u32[]{:S(2)}, u32[]{:S(2)}) collective-permute-start(f32[24,1024]{1,0:T(8,128)S(1)} %add.76.refs_0_.message.refs_2_), channel_id=1, source_target_pairs={{0,16},{16,0},{1,17},{17,1},{2,18},{18,2},{3,19},{19,3},{4,20},{20... | collective-permute-start | bytes 294920 | tf_op jit(solution)/shard_map/ppermute | solution.py:444
  33.6 1.0 copy-start.1
  34.6 0.9 copy-start.4
  35.6 0.9 copy-start.6
  41.6 1.6 %collective-permute-start.6 = (f32[64,1024]{1,0:T(8,128)S(1)}, f32[64,1024]{1,0:T(8,128)S(1)}, u32[]{:S(2)}, u32[]{:S(2)}) collective-permute-start(f32[64,1024]{1,0:T(8,128)S(1)} %get-tuple-element.14), channel_id=1, source_target_pairs={{0,1},{1,0},{2,3},{3,2},{4,5},{5,4},{6,7},{7,6},{8,9},{9,8},{10,11... | collective-permute-start | bytes 786440 | tf_op jit(solution)/shard_map/ppermute | solution.py:418
  46.4 0.6 copy-start.8
  47.0 6.6 %collective-permute-start.7 = (f32[40,1024]{1,0:T(8,128)}, f32[40,1024]{1,0:T(8,128)}, u32[]{:S(2)}, u32[]{:S(2)}) collective-permute-start(f32[40,1024]{1,0:T(8,128)} %get-tuple-element.16), channel_id=1, source_target_pairs={{0,2},{1,3},{2,0},{3,1},{4,6},{5,7},{6,4},{7,5},{8,10},{9,11},{10,... | collective-permute-start | bytes 491528 | tf_op jit(solution)/shard_map/ppermute | solution.py:418
  54.6 0.6 copy-start.9
  56.6 4.9 %collective-permute-start.8 = (f32[24,1024]{1,0:T(8,128)}, f32[24,1024]{1,0:T(8,128)}, u32[]{:S(2)}, u32[]{:S(2)}) collective-permute-start(f32[24,1024]{1,0:T(8,128)} %pad_maximum_fusion.4), channel_id=1, source_target_pairs={{0,4},{1,5},{2,6},{3,7},{4,0},{5,1},{6,2},{7,3},{8,12},{9,13},{10,... | collective-permute-start | bytes 294920 | tf_op jit(solution)/shard_map/ppermute | solution.py:418
  58.4 20.1 %copy-start.2 = (f32[4,32,1024]{2,1,0:T(8,128)S(1)}, f32[4,32,1024]{2,1,0:T(8,128)}, u32[]{:S(2)}) copy-start(f32[4,32,1024]{2,1,0:T(8,128)} %param.10) | copy-start | bytes 1572868
  58.4 20.1 %copy-start.5 = (bf16[2,160,192]{2,1,0:T(8,128)(2,1)S(1)}, bf16[2,160,192]{2,1,0:T(8,128)(2,1)}, u32[]{:S(2)}) copy-start(bf16[2,160,192]{2,1,0:T(8,128)(2,1)} %constant.99.clone.lat1_hbm) | copy-start | bytes 368644
  58.5 20.1 %copy-start.7 = (bf16[2,128,160]{2,1,0:T(8,128)(2,1)S(1)}, bf16[2,128,160]{2,1,0:T(8,128)(2,1)}, u32[]{:S(2)}) copy-start(bf16[2,128,160]{2,1,0:T(8,128)(2,1)} %constant.100.clone.lat2_hbm) | copy-start | bytes 245764
  63.3 5.2 %collective-permute-start.9 = (f32[16,1024]{1,0:T(8,128)S(1)}, f32[16,1024]{1,0:T(8,128)S(1)}, u32[]{:S(2)}, u32[]{:S(2)}) collective-permute-start(f32[16,1024]{1,0:T(8,128)S(1)} %pad_maximum_fusion.6), channel_id=1, source_target_pairs={{0,8},{1,9},{2,10},{3,11},{4,12},{5,13},{6,14},{7,15},{8,0},{9,1},... | collective-permute-start | bytes 196616 | tf_op jit(solution)/shard_map/ppermute | solution.py:418
  68.5 1.3 %collective-permute-start.10 = (f32[8,1024]{1,0:T(8,128)S(1)}, f32[8,1024]{1,0:T(8,128)S(1)}, u32[]{:S(2)}, u32[]{:S(2)}) collective-permute-start(f32[8,1024]{1,0:T(8,128)S(1)} %get-tuple-element.30.refs_0_), channel_id=1, source_target_pairs={{0,1},{1,0},{2,3},{3,2},{4,5},{5,4},{6,7},{7,6},{8,9},{9,8},{10,11... | collective-permute-start | bytes 98312 | tf_op jit(solution)/shard_map/ppermute | solution.py:418
  69.9 3.9 %collective-permute-start.11 = (f32[8,1024]{1,0:T(8,128)S(1)}, f32[8,1024]{1,0:T(8,128)S(1)}, u32[]{:S(2)}, u32[]{:S(2)}) collective-permute-start(f32[8,1024]{1,0:T(8,128)S(1)} %sums.2.refs_1_.refs_2_.refs_3_.refs_4_), channel_id=1, source_target_pairs={{0,16},{16,0},{1,17},{17,1},{2,18},{18,2},{3,19},{19,3},{4,20},{20... | collective-permute-start | bytes 98312 | tf_op jit(solution)/shard_map/ppermute | solution.py:444
  84.0 1.6 %collective-permute-start.12 = (f32[64,1024]{1,0:T(8,128)S(1)}, f32[64,1024]{1,0:T(8,128)S(1)}, u32[]{:S(2)}, u32[]{:S(2)}) collective-permute-start(f32[64,1024]{1,0:T(8,128)S(1)} %get-tuple-element.18), channel_id=1, source_target_pairs={{0,1},{1,0},{2,3},{3,2},{4,5},{5,4},{6,7},{7,6},{8,9},{9,8},{10,11... | collective-permute-start | bytes 786440 | tf_op jit(solution)/shard_map/ppermute | solution.py:418
  87.0 6.3 %collective-permute-start.13 = (f32[36,1024]{1,0:T(8,128)S(1)}, f32[36,1024]{1,0:T(8,128)S(1)}, u32[]{:S(2)}, u32[]{:S(2)}) collective-permute-start(f32[36,1024]{1,0:T(8,128)S(1)} %get-tuple-element.20), channel_id=1, source_target_pairs={{0,2},{1,3},{2,0},{3,1},{4,6},{5,7},{6,4},{7,5},{8,10},{9,11},{10,... | collective-permute-start | bytes 442376 | tf_op jit(solution)/shard_map/ppermute | solution.py:418
  93.4 4.7 %collective-permute-start.14 = (f32[20,1024]{1,0:T(8,128)S(1)}, f32[20,1024]{1,0:T(8,128)S(1)}, u32[]{:S(2)}, u32[]{:S(2)}) collective-permute-start(f32[20,1024]{1,0:T(8,128)S(1)} %pad_maximum_fusion.5), channel_id=1, source_target_pairs={{0,4},{1,5},{2,6},{3,7},{4,0},{5,1},{6,2},{7,3},{8,12},{9,13},{10,... | collective-permute-start | bytes 245768 | tf_op jit(solution)/shard_map/ppermute | solution.py:418
  98.1 5.3 %collective-permute-start.15 = (f32[12,1024]{1,0:T(8,128)S(1)}, f32[12,1024]{1,0:T(8,128)S(1)}, u32[]{:S(2)}, u32[]{:S(2)}) collective-permute-start(f32[12,1024]{1,0:T(8,128)S(1)} %pad_maximum_fusion.7), channel_id=1, source_target_pairs={{0,8},{1,9},{2,10},{3,11},{4,12},{5,13},{6,14},{7,15},{8,0},{9,1},... | collective-permute-start | bytes 147464 | tf_op jit(solution)/shard_map/ppermute | solution.py:418
  103.4 5.9 %collective-permute-start.16 = (f32[2,8,1024]{2,1,0:T(8,128)S(1)}, f32[2,8,1024]{2,1,0:T(8,128)S(1)}, u32[]{:S(2)}, u32[]{:S(2)}) collective-permute-start(f32[2,8,1024]{2,1,0:T(8,128)S(1)} %pad_maximum_fusion.8), channel_id=1, source_target_pairs={{0,8},{1,9},{2,10},{3,11},{4,12},{5,13},{6,14},{7,15},{8,0},{9,1},... | collective-permute-start | bytes 196616 | tf_op jit(solution)/shard_map/ppermute | solution.py:418
  106.4 1.2 collective-permute-start.17
  107.8 3.6 %collective-permute-start.18 = (f32[8,128]{1,0:T(8,128)S(1)}, f32[8,128]{1,0:T(8,128)S(1)}, u32[]{:S(2)}, u32[]{:S(2)}) collective-permute-start(f32[8,128]{1,0:T(8,128)S(1)} %sums.3.refs_3_), channel_id=1, source_target_pairs={{0,16},{16,0},{1,17},{17,1},{2,18},{18,2},{3,19},{19,3},{4,20},{20... | collective-permute-start | bytes 12296 | tf_op jit(solution)/shard_map/ppermute | solution.py:444
  111.5 4.5 %collective-permute-start.19 = (f32[16,1024]{1,0:T(8,128)S(1)}, f32[16,1024]{1,0:T(8,128)S(1)}, u32[]{:S(2)}, u32[]{:S(2)}) collective-permute-start(f32[16,1024]{1,0:T(8,128)S(1)} %combine.1), channel_id=1, source_target_pairs={{0,4},{1,5},{2,6},{3,7},{4,0},{5,1},{6,2},{7,3},{8,12},{9,13},{10,... | collective-permute-start | bytes 196616 | tf_op jit(solution)/shard_map/ppermute | solution.py:418
  116.0 5.0 %collective-permute-start.20 = (f32[32,1024]{1,0:T(8,128)S(1)}, f32[32,1024]{1,0:T(8,128)S(1)}, u32[]{:S(2)}, u32[]{:S(2)}) collective-permute-start(f32[32,1024]{1,0:T(8,128)S(1)} %pad_maximum_fusion.3), channel_id=1, source_target_pairs={{0,2},{1,3},{2,0},{3,1},{4,6},{5,7},{6,4},{7,5},{8,10},{9,11},{10,... | collective-permute-start | bytes 393224 | tf_op jit(solution)/shard_map/ppermute | solution.py:418
  121.0 1.6 %collective-permute-start.21 = (f32[64,1024]{1,0:T(8,128)S(1)}, f32[64,1024]{1,0:T(8,128)S(1)}, u32[]{:S(2)}, u32[]{:S(2)}) collective-permute-start(f32[64,1024]{1,0:T(8,128)S(1)} %pad_maximum_fusion.1), channel_id=1, source_target_pairs={{0,1},{1,0},{2,3},{3,2},{4,5},{5,4},{6,7},{7,6},{8,9},{9,8},{10,11... | collective-permute-start | bytes 786440 | tf_op jit(solution)/shard_map/ppermute | solution.py:418

commit v5 on v4

--- a/solution.py
+++ b/solution.py
@@ -96,10 +96,6 @@
     return pl.BlockSpec(memory_space=pltpu.VMEM)
 
 
-def smem():
-    return pl.BlockSpec(memory_space=pltpu.SMEM)
-
-
 def weigh(at_place, value, error):
     departure = value - at_place
     weight = huber_edge / jnp.maximum(jnp.abs(departure / error), huber_edge)
@@ -107,9 +103,30 @@
     return share * departure, share
 
 
-def prepare_kernel(roots, idx_ref, value_ref, error_ref, out_ref):
+def prepare_kernel(bands, bits, root_hbm, ens_hbm, idx_hbm, value_hbm, error_hbm, out_ref,
+                   flag_ref, *refs):
+    edges, (roots, idx_ref, value_ref, error_ref, arrived) = refs[:-5], refs[-5:]
+    rows = ens_hbm.shape[2]
     chunks, lon = out_ref.shape[0] // 6, out_ref.shape[1]
+    if bands == 2:
+        starts = [jnp.where(lax.axis_index("band") == 0, rows - REACH, 0)]
+    else:
+        starts = [rows - REACH, 0]
+    pairs = [(idx_hbm, idx_ref), (value_hbm, value_ref), (error_hbm, error_ref)]
+    pairs.append((root_hbm, roots))
+    for start, edge in zip(starts, edges):
+        pairs.append((ens_hbm.at[:, :, pl.ds(pl.multiple_of(start, REACH), REACH), :], edge))
+    loads = [pltpu.make_async_copy(x, y, arrived.at[k]) for k, (x, y) in enumerate(pairs)]
+    for load in loads:
+        load.start()
     position = lax.axis_index("member")
+    for k in range(flag_ref.shape[0]):
+        value = jnp.where(position == 0, static_share, 0.0)
+        if k < len(bits):
+            value = ((position // bits[k]) % 2).astype(F32)
+        flag_ref[k:k + 1, :] = jnp.full((1, flag_ref.shape[1]), value, F32)
+    for load in loads[:4]:
+        load.wait()
     first, second = position == roots[0], position == roots[1]
     for c in range(chunks):
         lanes = slice(c * lon, (c + 1) * lon)
@@ -121,21 +138,42 @@
         for k, x in enumerate((idx, value, error)):
             k += 3
             out_ref[k * chunks + c:k * chunks + c + 1, :] = jnp.where(second, x, 0.0)
-
-
-def prepare(roots, index, value, error, lon):
+    for load in loads[4:]:
+        load.wait()
+
+
+def prepare(bands, bits, roots, ensemble, index, value, error, lon):
+    count = 1 if bands == 2 else 2
+    away = pl.BlockSpec(memory_space=pl.ANY)
+    assert len(bits) < 8
+    inputs = [roots, ensemble, index, value, error]
+    inputs = [pltpu.with_memory_space_constraint(x, pltpu.HBM) for x in inputs]
+    edge = jax.ShapeDtypeStruct(ensemble.shape[:2] + (REACH, lon), BF16)
     return pl.pallas_call(
-        prepare_kernel,
-        out_shape=jax.ShapeDtypeStruct((6 * (index.shape[1] // lon), lon), F32),
-        in_specs=[smem(), vmem(), vmem(), vmem()],
-        out_specs=vmem(),
+        functools.partial(prepare_kernel, bands, bits),
+        out_shape=(
+            jax.ShapeDtypeStruct((6 * (index.shape[1] // lon), lon), F32),
+            jax.ShapeDtypeStruct((8, lon), F32),
+            *[edge] * count,
+        ),
+        in_specs=[away] * 5,
+        out_specs=[vmem()] * (2 + count),
+        scratch_shapes=[
+            pltpu.SMEM(roots.shape, roots.dtype),
+            pltpu.VMEM(index.shape, index.dtype),
+            pltpu.VMEM(index.shape, F32),
+            pltpu.VMEM(index.shape, F32),
+            pltpu.SemaphoreType.DMA((4 + count,)),
+        ],
+        compiler_params=limit(8),
         name="prepare",
-    )(roots, index, value, error)
-
-
-def add_onehot(idx, coef, blk, row, acc, blocks):
-    lane = (idx % LANES).astype(F32).astype(BF16)
-    spot = counter(LANES, idx.shape[1]) == lane
+    )(*inputs)
+
+
+def add_onehot(idx, coef, row, acc, blocks, lanes):
+    blk = (idx % (blocks * lanes)) // lanes
+    lane = (idx % lanes).astype(F32).astype(BF16)
+    spot = counter(lanes, idx.shape[1]) == lane
     zero = jnp.zeros((), BF16)
     side = jnp.concatenate([jnp.where(spot, x, zero) for x in split_bf16(coef)], axis=0)
     hot = onehot(blk, row, acc.shape[0] // blocks, blocks)
@@ -166,44 +204,44 @@
     return row(message, 3), coef
 
 
-def scatter_kernel(second, rows, lon, near, *refs):
-    refs = list(refs)
-    start_ref = refs.pop(0) if near is not None else None
+def scatter_kernel(second, rows, lon, bands, near, *refs):
+    if near is not None:
+        start = [rows - REACH, 0][near]
+        if bands == 2:
+            start = jnp.where(lax.axis_index("band") == 0, 0, rows - REACH)
     out_ref, acc = refs[-2:]
     message = refs[0]
     text, totals = (refs[1], refs[2:-2]) if second else (None, None)
     chunks = message.shape[0] // 6
     width = out_ref.shape[0]
     acc[...] = jnp.zeros_like(acc)
+    lanes = acc.shape[1] // 2
     for c in range(chunks):
         place, coef = coefficients(second, message, chunks, text, totals, c)
         idx = place.astype(jnp.int32)
-        blk = (idx % lon) // LANES
         if near is None:
             row = idx // lon
         else:
-            row = (idx // lon) % rows - start_ref[near]
+            row = (idx // lon) % rows - start
             inside = (row >= 0) & (row < REACH)
             row = jnp.where(inside, (idx // (lon * rows)) * REACH + row, -1)
-        add_onehot(idx, coef, blk, row, acc, lon // LANES)
-    for b in range(lon // LANES):
+        add_onehot(idx, coef, row, acc, lon // lanes, lanes)
+    for b in range(lon // lanes):
         part = acc[b * width:(b + 1) * width, :]
-        out_ref[:, b * LANES:(b + 1) * LANES] = part[:, :LANES] + part[:, LANES:]
-
-
-def scatter_obs(levels, rows, lon, message, text, totals, near=None, starts=None):
+        out_ref[:, b * lanes:(b + 1) * lanes] = part[:, :lanes] + part[:, lanes:]
+
+
+def scatter_obs(levels, rows, lon, bands, message, text, totals, near=None):
     second = text is not None
     width = levels * (rows if near is None else REACH)
+    lanes = LANES if near is None else LANES // 2
     args = [message] + ([text, *totals] if second else [])
-    specs = [vmem()] * len(args)
-    if near is not None:
-        args, specs = [starts] + args, [smem()] + specs
     return pl.pallas_call(
-        functools.partial(scatter_kernel, second, rows, lon, near),
+        functools.partial(scatter_kernel, second, rows, lon, bands, near),
         out_shape=jax.ShapeDtypeStruct((width, lon), F32),
-        in_specs=specs,
+        in_specs=[vmem()] * len(args),
         out_specs=vmem(),
-        scratch_shapes=[pltpu.VMEM(((lon // LANES) * width, 2 * LANES), F32)],
+        scratch_shapes=[pltpu.VMEM(((lon // lanes) * width, 2 * lanes), F32)],
         compiler_params=limit(8),
         name="scatter_own" if near is None else "scatter_near",
     )(*args)
@@ -227,19 +265,17 @@
     return jnp.concatenate([y[j * rows:(j + 1) * rows] for j in range(lon // LANES)], axis=1)
 
 
-def filter_kernel(share, own_ref, ext_ref, grad_ref, gext_ref, tile_ref, var_hbm, lat1_hbm,
-                  lat2_hbm, keep_ref, send_ref, acc_ref, var_ref, lat1_ref, lat2_ref, arrived):
+def filter_kernel(share, shapes, own_ref, ext_ref, grad_ref, gext_ref, var_ref, table_ref,
+                  keep_ref, send_ref, acc_ref):
     position = lax.axis_index("member")
     band = lax.axis_index("band")
     members = own_ref.shape[0]
-    loads = [
-        pltpu.make_async_copy(source, target, arrived.at[k])
-        for k, (source, target) in enumerate(
-            [(lat1_hbm.at[band], lat1_ref), (lat2_hbm.at[band], lat2_ref), (var_hbm, var_ref)]
-        )
-    ]
-    for load in loads:
-        load.start()
+    (rows_1, cols_1), (rows_2, cols_2), bands = shapes
+    tile = table_ref[:2 * LANES, :LANES]
+    start_1 = pl.multiple_of(2 * LANES + band * rows_1, 16)
+    start_2 = pl.multiple_of(2 * LANES + bands * rows_1 + band * rows_2, 16)
+    lat1 = table_ref[pl.ds(start_1, rows_1), :cols_1]
+    lat2 = table_ref[pl.ds(start_2, rows_2), :cols_2]
     size = GROUP if members % GROUP == 0 else 1
     for start in range(0, members, size):
         group = range(start, start + size)
@@ -253,12 +289,7 @@
             )
             for m in group
         ]
-        tile = tile_ref[...]
         first = [lon_pass(x, tile) for x in mixed]
-        if start == 0:
-            loads[0].wait()
-            loads[1].wait()
-        lat1, lat2 = lat1_ref[...], lat2_ref[...]
         first = [jnp.dot(lat1, x, preferred_element_type=F32).astype(BF16) for x in first]
         second = [lon_pass(x, tile) for x in first]
         second = [jnp.dot(lat2, x, preferred_element_type=F32) for x in second]
@@ -266,46 +297,32 @@
         for m, x in zip(group[1:], second[1:]):
             product += own_ref[m].astype(F32) * x
         acc_ref[...] = product if start == 0 else acc_ref[...] + product
-    loads[2].wait()
     half = keep_ref.shape[0]
-    static = jnp.where(position == 0, static_share, 0.0)
     bit = position % 2
     for ref, start in ((keep_ref, bit * half), (send_ref, (1 - bit) * half)):
         rows = pl.ds(pl.multiple_of(start, half), half)
-        ref[...] = share * acc_ref[rows, :] + static * var_ref[rows, :] * grad_ref[rows, :]
-
-
-def filter_members(share, own, ext, grad, gext, variance, tile, lat1, lat2):
+        ref[...] = share * acc_ref[rows, :] + var_ref[rows, :] * grad_ref[rows, :]
+
+
+def filter_members(share, shapes, own, ext, grad, gext, static, table):
     members, rows, lon = own.shape
     half = jax.ShapeDtypeStruct((rows // 2, lon), F32)
-    away = pl.BlockSpec(memory_space=pltpu.HBM)
     return pl.pallas_call(
-        functools.partial(filter_kernel, share),
+        functools.partial(filter_kernel, share, shapes),
         out_shape=(half, half),
-        in_specs=[vmem()] * 5 + [away] * 3,
+        in_specs=[vmem()] * 6,
         out_specs=(vmem(), vmem()),
-        scratch_shapes=[
-            pltpu.VMEM((rows, lon), F32),
-            pltpu.VMEM((rows, lon), F32),
-            pltpu.VMEM(lat1.shape[1:], BF16),
-            pltpu.VMEM(lat2.shape[1:], BF16),
-            pltpu.SemaphoreType.DMA((3,)),
-        ],
+        scratch_shapes=[pltpu.VMEM((rows, lon), F32)],
         compiler_params=limit(14),
         name="filter_members",
-    )(own, ext, grad, gext, tile, variance, lat1, lat2)
-
-
-def gather_kernel(which, keep_ref, got_ref, message, next_ref, send_ref):
-    position = lax.axis_index("member")
-    rows, lon = keep_ref.shape
+    )(own, ext, grad, gext, static, table)
+
+
+def gather_kernel(which, field_ref, message, out_ref):
+    rows, lon = field_ref.shape
     chunks = message.shape[0] // 6
-    start = (position % 2) * rows
-    field = keep_ref[...] + got_ref[...]
-    low, high = field[:rows // 2], field[rows // 2:]
-    upper = (position // 2) % 2 == 1
-    next_ref[...] = jnp.where(upper, high, low)
-    send_ref[:rows // 2, :] = jnp.where(upper, low, high)
+    start = (lax.axis_index("member") % 2) * rows
+    field = field_ref[...]
     blocks = lon // LANES
     stacked = jnp.concatenate(
         [field[:, b * LANES:(b + 1) * LANES] for b in range(blocks)], axis=0
@@ -323,24 +340,19 @@
             found = found[:LANES] + found[LANES:]
             spot = lax.broadcasted_iota(jnp.int32, found.shape, 0) == idx % LANES
             value = jnp.sum(jnp.where(spot, found, 0.0), axis=0, keepdims=True)
-            at = rows // 2 + n * chunks + c
-            send_ref[at:at + 1, :] = value
-
-
-def gather_places(which, keep, got, message):
-    rows, lon = keep.shape
+            out_ref[n * chunks + c:n * chunks + c + 1, :] = value
+
+
+def gather_places(which, field, message):
     tail = len(which) * (message.shape[0] // 6)
     return pl.pallas_call(
         functools.partial(gather_kernel, which),
-        out_shape=(
-            jax.ShapeDtypeStruct((rows // 2, lon), F32),
-            jax.ShapeDtypeStruct((rows // 2 + tail, lon), F32),
-        ),
-        in_specs=[vmem()] * 3,
-        out_specs=(vmem(), vmem()),
+        out_shape=jax.ShapeDtypeStruct((tail, field.shape[1]), F32),
+        in_specs=[vmem()] * 2,
+        out_specs=vmem(),
         compiler_params=limit(8),
         name="gather_places",
-    )(keep, got, message)
+    )(field, message)
 
 
 def sums_kernel(second, *refs):
@@ -418,23 +430,23 @@
     return lax.ppermute(x, "member", partner(count, bit))
 
 
-def reduce_with_tail(keep, send, bits, count, position):
-    rows = keep.shape[0]
-    for n, bit in enumerate(bits):
-        got = swap(send, bit, count)
+def halves(x, upper):
+    half = x.shape[0] // 2
+    return jnp.where(upper, x[half:], x[:half]), jnp.where(upper, x[:half], x[half:])
+
+
+def reduce_with_tail(x, tail, bits, count, uppers):
+    for bit in bits:
+        keep, send = halves(x, uppers[bit])
+        rows = keep.shape[0]
+        got = swap(jnp.concatenate([send, tail], axis=0), bit, count)
         x = keep + got[:rows]
-        tail = send[rows:] + got[rows:]
-        if n + 1 < len(bits):
-            rows //= 2
-            upper = (position // bits[n + 1]) % 2 == 1
-            keep = jnp.where(upper, x[rows:], x[:rows])
-            send = jnp.concatenate([jnp.where(upper, x[:rows], x[rows:]), tail], axis=0)
+        tail = tail + got[rows:]
     return x, tail
 
 
-def gather_rows(x, bit, count, position):
+def gather_rows(x, bit, count, upper):
     other = swap(x, bit, count)
-    upper = (position // bit) % 2 == 1
     axis = x.ndim - 2
     return jnp.concatenate([jnp.where(upper, other, x), jnp.where(upper, x, other)], axis=axis)
 
@@ -447,35 +459,32 @@
     return [lax.ppermute(x, "band", up), lax.ppermute(x, "band", down)]
 
 
-def band_halo(ens, count, position):
-    rows = ens.shape[2]
-    first, last = ens[:, :, :REACH], ens[:, :, rows - REACH:]
+def band_halo(edges, count):
     if count == 2:
-        edge = jnp.where(position == 0, last, first)
-        return [lax.ppermute(edge, "band", [(0, 1), (1, 0)])]
+        return [lax.ppermute(edges[0], "band", [(0, 1), (1, 0)])]
     up = [(i, i + 1) for i in range(count - 1)]
     down = [(j, i) for i, j in up]
-    return [lax.ppermute(last, "band", up), lax.ppermute(first, "band", down)]
+    return [lax.ppermute(e, "band", pairs) for e, pairs in zip(edges, (up, down))]
 
 
 def local(ensemble, variance, obs_index, obs_value, obs_error, root_ranks):
     members_here, levels, lat_rows, lon = ensemble.shape
     n_member, n_band = lax.axis_size("member"), lax.axis_size("band")
-    member_pos, band_pos = lax.axis_index("member"), lax.axis_index("band")
     members = members_here * n_member
     chunks = obs_index.shape[1] // lon
     bits = member_bits(n_member)
 
-    if n_band == 2:
-        starts = jnp.where(band_pos == 0, 0, lat_rows - REACH).reshape(1)
-    else:
-        starts = jnp.array([lat_rows - REACH, 0])
-    starts = starts.astype(jnp.int32)
-    lat1, lat2 = (jnp.asarray(m, BF16) for m in lat_operators(levels, lat_rows, n_band, HALF))
-    tile = jnp.asarray(lon_tile(HALF), BF16)
-
-    halo = band_halo(ensemble, n_band, band_pos)
-    message = prepare(root_ranks, obs_index, obs_value, obs_error, lon)
+    lat1, lat2 = lat_operators(levels, lat_rows, n_band, HALF)
+    shapes = (lat1.shape[1:], lat2.shape[1:], n_band)
+    wide = max(LANES, lat1.shape[2])
+    parts = [lon_tile(HALF), *lat1, *lat2]
+    parts = [np.pad(p, ((0, 0), (0, wide - p.shape[1]))) for p in parts]
+    table = jnp.asarray(np.concatenate(parts, axis=0), BF16)
+
+    message, flags, *edges = prepare(
+        n_band, bits, root_ranks, ensemble, obs_index, obs_value, obs_error, lon
+    )
+    halo = band_halo(edges, n_band)
     message = message + swap(message, bits[0], n_member)
     for bit in bits[1:]:
         message = message + swap(message, bit, n_member)
@@ -483,22 +492,26 @@
 
     own = ensemble.reshape(members_here, levels * lat_rows, lon)
     ext = jnp.concatenate([h.reshape(members_here, levels * REACH, lon) for h in halo], axis=1)
-    variance = variance.reshape(levels * lat_rows, lon)
+    uppers = {bit: flags[k:k + 1] > 0 for k, bit in enumerate(bits)}
+    static = flags[-1] * variance
+    static = static.reshape(levels * lat_rows, lon)
     share = ensemble_share / (members - 1)
 
     def direction_parts(text=None, totals=(), texts=()):
-        scatter = functools.partial(scatter_obs, levels, lat_rows, lon)
+        scatter = functools.partial(scatter_obs, levels, lat_rows, lon, n_band)
         grad = scatter(message, text, totals)
         gext = [
-            scatter(a, texts[s] if texts else None, totals, s, starts)
+            scatter(a, texts[s] if texts else None, totals, s)
             for s, a in enumerate(around)
         ]
         gext = jnp.concatenate(gext, axis=0)
-        keep, send = filter_members(share, own, ext, grad, gext, variance, tile, lat1, lat2)
-        got = swap(send, bits[0], n_member)
-        which = (3,) if texts else (0, 3)
-        keep, send = gather_places(which, keep, got, message)
-        piece, tail = reduce_with_tail(keep, send, bits[1:], n_member, member_pos)
+        keep, send = filter_members(share, shapes, own, ext, grad, gext, static, table)
+        field = keep + swap(send, bits[0], n_member)
+        keep, send = halves(field, uppers[bits[1]])
+        piece = keep + swap(send, bits[1], n_member)
+        tail = gather_places((3,) if texts else (0, 3), field, message)
+        tail = tail + swap(tail, bits[1], n_member)
+        piece, tail = reduce_with_tail(piece, tail, bits[2:], n_member, uppers)
         return piece, (tail, swap(tail, bits[0], n_member))
 
     def band_totals(text):
@@ -513,10 +526,10 @@
 
     piece_1, tail = direction_parts(text, totals_0, texts)
     totals_1, _ = band_totals(sums(tail, message, text, totals_0))
-    pair = gather_rows(jnp.stack([piece_0, piece_1]), bits[-1], n_member, member_pos)
+    pair = gather_rows(jnp.stack([piece_0, piece_1]), bits[-1], n_member, uppers[bits[-1]])
     out = combine(pair, totals_0, totals_1, chunks)
     for bit in reversed(bits[:-1]):
-        out = gather_rows(out, bit, n_member, member_pos)
+        out = gather_rows(out, bit, n_member, uppers[bit])
     return out.reshape(levels, lat_rows, lon)
 
 

time: 124 us -> 108 us (0.87)
  other arithmetic: 8.95 us -> 1.45 us
  local copies, waits for them, and re-layouts: 4.16 us -> 0.02 us
  Pallas kernels: 26.2 us -> 23 us
    unnamed x20 -> x6, local copies, waits for them, and re-layouts: 4.16 us -> 0.02 us
    pallas_call x9, Pallas kernels: 25.8 us -> 22.6 us  [the longest x2 9.57 us: filter_members(): pl.pallas_call(functools.partial(filter_kernel, share, shapes), out_shape...]
    ppermute x18 -> x20, waiting for transfers between devices: 43.4 us -> 40.5 us  [swap(): return lax.ppermute(x, 'member', partner(count, bit))]
    select_n x4 -> x5, other arithmetic: 2.82 us -> 0.07 us  [halves(): jnp.where(upper, x[:half], x[half:])]
    ppermute x3, waiting for transfers between devices: 7.97 us -> 10.4 us  [from_bands(): return [lax.ppermute(x, 'band', [(0, 1), (1, 0)])]]
    add x4 -> x2, other arithmetic: 1.93 us -> 0.03 us  [reduce_with_tail(): x = keep + got[:rows]]
    add x5 -> x9, other arithmetic: 1.58 us -> 0.16 us  [the longest x2 0.06 us: direction_parts(): piece = keep + swap(send, bits[1], n_member)]
    ppermute x18 -> x20, starting transfers between devices: 25.9 us -> 25.6 us  [swap(): return lax.ppermute(x, 'member', partner(count, bit))]
  transfers between devices with their start and end apart: 22 -> 24, of which waited for: 20 -> 20; matrix products, arithmetic and copies ran while one was open for 1% -> 0% of each run, Pallas kernels for 5% -> 7%
where the time goes in v5:
time: 108 us
  waiting for transfers between devices  50.9 us (47%)
  starting transfers between devices  32 us (30%)
  Pallas kernels  23 us (21%)
  other arithmetic  1.45 us (1%)
    ppermute x20, waiting for transfers between devices, swap(): return lax.ppermute(x, 'member', partner(count, bit))  40.5 us
    ppermute x20, starting transfers between devices, swap(): return lax.ppermute(x, 'member', partner(count, bit))  25.6 us
    ppermute x3, waiting for transfers between devices, from_bands(): return [lax.ppermute(x, 'band', [(0, 1), (1, 0)])]  10.4 us
    pallas_call x2, Pallas kernels, filter_members(): pl.pallas_call(functools.partial(filter_kernel, share, shapes), out_shape...  9.57 us
    pallas_call x4, Pallas kernels, scatter_obs(): pl.pallas_call(functools.partial(scatter_kernel, second, rows, lon, bands...  7.73 us
    pallas_call x2, Pallas kernels, gather_places(): pl.pallas_call(functools.partial(gather_kernel, which), out_shape=jax.Sha...  3.93 us
    ppermute x3, starting transfers between devices, from_bands(): return [lax.ppermute(x, 'band', [(0, 1), (1, 0)])]  3.35 us
    ppermute x1, starting transfers between devices, band_halo(): return [lax.ppermute(edges[0], 'band', [(0, 1), (1, 0)])]  3.06 us
  transfers between devices with their start and end apart: 24, of which 20 were waited for; matrix products, arithmetic and copies ran while one was open for 0% of the time, Pallas kernels for 7%

profile of v5, /device:TPU:0, one launch (start us, length us, event | category | flops | bytes accessed | tf_op | source)
XLA Modules:
  0.0 107.7 jit_solution(6642375159545542969)
XLA Ops:
  0.0 1.4 %prepare.1 = (f32[24,1024]{1,0:T(8,128)S(1)}, f32[8,1024]{1,0:T(8,128)S(1)}, bf16[8,4,16,1024]{3,2,1,0:T(8,128)(2,1)S(1)}) custom-call(s32[2]{0:T(128)} %root_hbm.1, bf16[8,4,32,1024]{3,2,1,0:T(8,128)(2,1)} %ens_hbm.1, s32[1,4096]{1,0:T(1,128)} %idx_hbm.1, f32[1,4096]{1,0:T(1,128)} %value_hbm.1, f32[1,4096]{1,0:T(1,128)} %error_hbm.1), custom_call_target="tpu_custom_call" | custom-call | tf_op jit(solution)/shard_map/prepare/pallas_call | solution.py:152
  1.4 0.0 copy-start
  1.4 0.0 copy-start.1
  1.4 3.1 %collective-permute-start = (bf16[8,4,16,1024]{3,2,1,0:T(8,128)(2,1)S(1)}, bf16[8,4,16,1024]{3,2,1,0:T(8,128)(2,1)S(1)}, u32[]{:S(2)}, u32[]{:S(2)}) collective-permute-start(bf16[8,4,16,1024]{3,2,1,0:T(8,128)(2,1)S(1)} %get-tuple-element.13), channel_id=1, source_target_pairs={{0,16},{16,0},{1,17},{17,1},{2,18},{18,2},{3,19},{19,3},{4,20},{20... | collective-permute-start | bytes 3145736 | tf_op jit(solution)/shard_map/ppermute | solution.py:464
  4.5 0.0 collective-permute-start.1
  4.5 1.3 %collective-permute-done.1 = f32[24,1024]{1,0:T(8,128)S(1)} collective-permute-done((f32[24,1024]{1,0:T(8,128)S(1)}, f32[24,1024]{1,0:T(8,128)S(1)}, u32[]{:S(2)}, u32[]{:S(2)}) %collective-permute-start.1) | collective-permute-done | bytes 98336 | tf_op jit(solution)/shard_map/ppermute | solution.py:430
  5.8 1.6 %collective-permute-start.2 = (f32[24,1024]{1,0:T(8,128)S(1)}, f32[24,1024]{1,0:T(8,128)S(1)}, u32[]{:S(2)}, u32[]{:S(2)}) collective-permute-start(f32[24,1024]{1,0:T(8,128)S(1)} %add.54), channel_id=1, source_target_pairs={{0,2},{1,3},{2,0},{3,1},{4,6},{5,7},{6,4},{7,5},{8,10},{9,11},{10,... | collective-permute-start | bytes 294920 | tf_op jit(solution)/shard_map/ppermute | solution.py:430
  7.3 3.4 %collective-permute-done.2 = f32[24,1024]{1,0:T(8,128)S(1)} collective-permute-done((f32[24,1024]{1,0:T(8,128)S(1)}, f32[24,1024]{1,0:T(8,128)S(1)}, u32[]{:S(2)}, u32[]{:S(2)}) %collective-permute-start.2) | collective-permute-done | bytes 98336 | tf_op jit(solution)/shard_map/ppermute | solution.py:430
  10.7 1.6 %collective-permute-start.3 = (f32[24,1024]{1,0:T(8,128)S(1)}, f32[24,1024]{1,0:T(8,128)S(1)}, u32[]{:S(2)}, u32[]{:S(2)}) collective-permute-start(f32[24,1024]{1,0:T(8,128)S(1)} %add.55), channel_id=1, source_target_pairs={{0,4},{1,5},{2,6},{3,7},{4,0},{5,1},{6,2},{7,3},{8,12},{9,13},{10,... | collective-permute-start | bytes 294920 | tf_op jit(solution)/shard_map/ppermute | solution.py:430
  12.4 3.0 %collective-permute-done.3 = f32[24,1024]{1,0:T(8,128)S(1)} collective-permute-done((f32[24,1024]{1,0:T(8,128)S(1)}, f32[24,1024]{1,0:T(8,128)S(1)}, u32[]{:S(2)}, u32[]{:S(2)}) %collective-permute-start.3) | collective-permute-done | bytes 98336 | tf_op jit(solution)/shard_map/ppermute | solution.py:430
  15.4 2.7 %collective-permute-start.4 = (f32[24,1024]{1,0:T(8,128)S(1)}, f32[24,1024]{1,0:T(8,128)S(1)}, u32[]{:S(2)}, u32[]{:S(2)}) collective-permute-start(f32[24,1024]{1,0:T(8,128)S(1)} %add.56), channel_id=1, source_target_pairs={{0,8},{1,9},{2,10},{3,11},{4,12},{5,13},{6,14},{7,15},{8,0},{9,1},... | collective-permute-start | bytes 294920 | tf_op jit(solution)/shard_map/ppermute | solution.py:430
  18.1 2.9 %collective-permute-done.4 = f32[24,1024]{1,0:T(8,128)S(1)} collective-permute-done((f32[24,1024]{1,0:T(8,128)S(1)}, f32[24,1024]{1,0:T(8,128)S(1)}, u32[]{:S(2)}, u32[]{:S(2)}) %collective-permute-start.4) | collective-permute-done | bytes 98336 | tf_op jit(solution)/shard_map/ppermute | solution.py:430
  21.0 0.3 collective-permute-start.5
  21.4 2.4 %scatter_own.2.grad_ref = f32[128,1024]{1,0:T(8,128)S(1)} custom-call(f32[24,1024]{1,0:T(8,128)S(1)} %add.57.refs_0_.message.refs_2_), custom_call_target="tpu_custom_call" | custom-call | tf_op jit(solution)/shard_map/scatter_own/pallas_call | solution.py:239
  23.8 5.9 %collective-permute-done.5.refs_0_ = f32[24,1024]{1,0:T(8,128)S(1)} collective-permute-done((f32[24,1024]{1,0:T(8,128)S(1)}, f32[24,1024]{1,0:T(8,128)S(1)}, u32[]{:S(2)}, u32[]{:S(2)}) %collective-permute-start.5) | collective-permute-done | bytes 98336 | tf_op jit(solution)/shard_map/ppermute | solution.py:456
  29.7 1.3 %scatter_near.2.gext_ref = f32[64,1024]{1,0:T(8,128)S(1)} custom-call(f32[24,1024]{1,0:T(8,128)S(1)} %collective-permute-done.5.refs_0_), custom_call_target="tpu_custom_call" | custom-call | tf_op jit(solution)/shard_map/scatter_near/pallas_call | solution.py:239
  31.1 0.0 collective-permute-done
  31.1 4.8 %filter_members.2 = (f32[64,1024]{1,0:T(8,128)S(1)}, f32[64,1024]{1,0:T(8,128)S(1)}) custom-call(bf16[8,128,1024]{2,1,0:T(8,128)(2,1)S(1)} %bitcast.9, bf16[8,64,1024]{2,1,0:T(8,128)(2,1)S(1)} %bitcast.13, f32[128,1024]{1,0:T(8,128)S(1)} %scatter_own.2.grad_ref, f32[64,1024]{1,0:T(8,128)S(1)} %scatter_near.2.gext_ref, f32[128,1024]{1,0:T(8,128)S(1)} %bitcast.11, ...), custom_call_target="tpu_custom_call" | custom-call | tf_op jit(solution)/shard_map/filter_members/pallas_call | solution.py:310
  35.9 0.1 collective-permute-start.6
  36.0 0.1 compare_reduce_fusion.3
  36.0 1.5 %collective-permute-done.6 = f32[64,1024]{1,0:T(8,128)S(1)} collective-permute-done((f32[64,1024]{1,0:T(8,128)S(1)}, f32[64,1024]{1,0:T(8,128)S(1)}, u32[]{:S(2)}, u32[]{:S(2)}) %collective-permute-start.6) | collective-permute-done | bytes 262176 | tf_op jit(solution)/shard_map/ppermute | solution.py:430
  37.5 1.8 %collective-permute-start.7 = (f32[32,1024]{1,0:T(8,128)S(1)}, f32[32,1024]{1,0:T(8,128)S(1)}, u32[]{:S(2)}, u32[]{:S(2)}) collective-permute-start(f32[32,1024]{1,0:T(8,128)S(1)} %slice_select_fusion.1), channel_id=1, source_target_pairs={{0,2},{1,3},{2,0},{3,1},{4,6},{5,7},{6,4},{7,5},{8,10},{9,11},{10,... | collective-permute-start | bytes 393224 | tf_op jit(solution)/shard_map/ppermute | solution.py:430
  39.3 2.6 %gather_places.2 = f32[8,1024]{1,0:T(8,128)S(1)} custom-call(f32[64,1024]{1,0:T(8,128)S(1)} %add.58.field_ref, f32[24,1024]{1,0:T(8,128)S(1)} %add.57.refs_0_.message.refs_2_), custom_call_target="tpu_custom_call" | custom-call | tf_op jit(solution)/shard_map/gather_places/pallas_call | solution.py:348
  41.9 0.4 collective-permute-start.8
  42.3 3.6 %collective-permute-done.8 = f32[8,1024]{1,0:T(8,128)S(1)} collective-permute-done((f32[8,1024]{1,0:T(8,128)S(1)}, f32[8,1024]{1,0:T(8,128)S(1)}, u32[]{:S(2)}, u32[]{:S(2)}) %collective-permute-start.8) | collective-permute-done | bytes 32800 | tf_op jit(solution)/shard_map/ppermute | solution.py:430
  45.9 0.0 collective-permute-done.7
  45.9 1.6 %collective-permute-start.9 = (f32[24,1024]{1,0:T(8,128)S(1)}, f32[24,1024]{1,0:T(8,128)S(1)}, u32[]{:S(2)}, u32[]{:S(2)}) collective-permute-start(f32[24,1024]{1,0:T(8,128)S(1)} %pad_maximum_fusion.4), channel_id=1, source_target_pairs={{0,4},{1,5},{2,6},{3,7},{4,0},{5,1},{6,2},{7,3},{8,12},{9,13},{10,... | collective-permute-start | bytes 294920 | tf_op jit(solution)/shard_map/ppermute | solution.py:430
  47.6 3.0 %collective-permute-done.9 = f32[24,1024]{1,0:T(8,128)S(1)} collective-permute-done((f32[24,1024]{1,0:T(8,128)S(1)}, f32[24,1024]{1,0:T(8,128)S(1)}, u32[]{:S(2)}, u32[]{:S(2)}) %collective-permute-start.9) | collective-permute-done | bytes 98336 | tf_op jit(solution)/shard_map/ppermute | solution.py:430
  50.7 2.7 %collective-permute-start.10 = (f32[16,1024]{1,0:T(8,128)S(1)}, f32[16,1024]{1,0:T(8,128)S(1)}, u32[]{:S(2)}, u32[]{:S(2)}) collective-permute-start(f32[16,1024]{1,0:T(8,128)S(1)} %pad_maximum_fusion.6), channel_id=1, source_target_pairs={{0,8},{1,9},{2,10},{3,11},{4,12},{5,13},{6,14},{7,15},{8,0},{9,1},... | collective-permute-start | bytes 196616 | tf_op jit(solution)/shard_map/ppermute | solution.py:430
  53.3 2.6 %collective-permute-done.10 = f32[16,1024]{1,0:T(8,128)S(1)} collective-permute-done((f32[16,1024]{1,0:T(8,128)S(1)}, f32[16,1024]{1,0:T(8,128)S(1)}, u32[]{:S(2)}, u32[]{:S(2)}) %collective-permute-start.10) | collective-permute-done | bytes 65568 | tf_op jit(solution)/shard_map/ppermute | solution.py:430
  55.9 0.1 collective-permute-start.11
  56.0 1.2 %collective-permute-done.11.refs_1_ = f32[8,1024]{1,0:T(8,128)S(1)} collective-permute-done((f32[8,1024]{1,0:T(8,128)S(1)}, f32[8,1024]{1,0:T(8,128)S(1)}, u32[]{:S(2)}, u32[]{:S(2)}) %collective-permute-start.11) | collective-permute-done | bytes 32800 | tf_op jit(solution)/shard_map/ppermute | solution.py:430
  57.2 0.1 sums.2.refs_1_.refs_2_.refs_3_.refs_4_
  57.3 1.5 %collective-permute-start.12 = (f32[8,1024]{1,0:T(8,128)S(1)}, f32[8,1024]{1,0:T(8,128)S(1)}, u32[]{:S(2)}, u32[]{:S(2)}) collective-permute-start(f32[8,1024]{1,0:T(8,128)S(1)} %sums.2.refs_1_.refs_2_.refs_3_.refs_4_), channel_id=1, source_target_pairs={{0,16},{16,0},{1,17},{17,1},{2,18},{18,2},{3,19},{19,3},{4,20},{20... | collective-permute-start | bytes 98312 | tf_op jit(solution)/shard_map/ppermute | solution.py:456
  58.8 2.4 %collective-permute-done.12.refs_3_.refs_1_.refs_5_.refs_2_ = f32[8,1024]{1,0:T(8,128)S(1)} collective-permute-done((f32[8,1024]{1,0:T(8,128)S(1)}, f32[8,1024]{1,0:T(8,128)S(1)}, u32[]{:S(2)}, u32[]{:S(2)}) %collective-permute-start.12) | collective-permute-done | bytes 32800 | tf_op jit(solution)/shard_map/ppermute | solution.py:456
  61.2 2.6 %scatter_own.3.grad_ref = f32[128,1024]{1,0:T(8,128)S(1)} custom-call(f32[24,1024]{1,0:T(8,128)S(1)} %add.57.refs_0_.message.refs_2_, f32[8,1024]{1,0:T(8,128)S(1)} %sums.2.refs_1_.refs_2_.refs_3_.refs_4_, f32[8,1024]{1,0:T(8,128)S(1)} %sums.2.refs_1_.refs_2_.refs_3_.refs_4_, f32[8,1024]{1,0:T(8,128)S(1)} %collective-permute-done.12.refs_3_.refs_1_.refs_5_.refs_2_), custom_call_target="tpu_custom_call" | custom-call | tf_op jit(solution)/shard_map/scatter_own/pallas_call | solution.py:239
  63.9 1.4 %scatter_near.3.gext_ref = f32[64,1024]{1,0:T(8,128)S(1)} custom-call(f32[24,1024]{1,0:T(8,128)S(1)} %collective-permute-done.5.refs_0_, f32[8,1024]{1,0:T(8,128)S(1)} %collective-permute-done.12.refs_3_.refs_1_.refs_5_.refs_2_, f32[8,1024]{1,0:T(8,128)S(1)} %sums.2.refs_1_.refs_2_.refs_3_.refs_4_, ...), custom_call_target="tpu_custom_call" | custom-call | tf_op jit(solution)/shard_map/scatter_near/pallas_call | solution.py:239
  65.3 4.8 %filter_members.3 = (f32[64,1024]{1,0:T(8,128)S(1)}, f32[64,1024]{1,0:T(8,128)S(1)}) custom-call(bf16[8,128,1024]{2,1,0:T(8,128)(2,1)S(1)} %bitcast.10, bf16[8,64,1024]{2,1,0:T(8,128)(2,1)S(1)} %bitcast.14, f32[128,1024]{1,0:T(8,128)S(1)} %scatter_own.3.grad_ref, f32[64,1024]{1,0:T(8,128)S(1)} %scatter_near.3.gext_ref, f32[128,1024]{1,0:T(8,128)S(1)} %bitcast.12, ...), custom_call_target="tpu_custom_call" | custom-call | tf_op jit(solution)/shard_map/filter_members/pallas_call | solution.py:310
  70.1 0.1 collective-permute-start.13
  70.1 1.5 %collective-permute-done.13 = f32[64,1024]{1,0:T(8,128)S(1)} collective-permute-done((f32[64,1024]{1,0:T(8,128)S(1)}, f32[64,1024]{1,0:T(8,128)S(1)}, u32[]{:S(2)}, u32[]{:S(2)}) %collective-permute-start.13) | collective-permute-done | bytes 262176 | tf_op jit(solution)/shard_map/ppermute | solution.py:430
  71.7 0.4 collective-permute-start.14
  72.1 1.4 %gather_places.3 = f32[4,1024]{1,0:T(4,128)S(1)} custom-call(f32[64,1024]{1,0:T(8,128)S(1)} %add.65.field_ref, f32[24,1024]{1,0:T(8,128)S(1)} %add.57.refs_0_.message.refs_2_), custom_call_target="tpu_custom_call" | custom-call | tf_op jit(solution)/shard_map/gather_places/pallas_call | solution.py:348
  73.5 1.8 %collective-permute-start.15 = (f32[4,1024]{1,0:T(4,128)S(1)}, f32[4,1024]{1,0:T(4,128)S(1)}, u32[]{:S(2)}, u32[]{:S(2)}) collective-permute-start(f32[4,1024]{1,0:T(4,128)S(1)} %gather_places.3), channel_id=1, source_target_pairs={{0,2},{1,3},{2,0},{3,1},{4,6},{5,7},{6,4},{7,5},{8,10},{9,11},{10,... | collective-permute-start | bytes 49160 | tf_op jit(solution)/shard_map/ppermute | solution.py:430
  75.2 2.4 %collective-permute-done.15 = f32[4,1024]{1,0:T(4,128)S(1)} collective-permute-done((f32[4,1024]{1,0:T(4,128)S(1)}, f32[4,1024]{1,0:T(4,128)S(1)}, u32[]{:S(2)}, u32[]{:S(2)}) %collective-permute-start.15) | collective-permute-done | bytes 16416 | tf_op jit(solution)/shard_map/ppermute | solution.py:430
  77.7 0.0 collective-permute-done.14
  77.8 1.6 %collective-permute-start.16 = (f32[20,1024]{1,0:T(8,128)S(1)}, f32[20,1024]{1,0:T(8,128)S(1)}, u32[]{:S(2)}, u32[]{:S(2)}) collective-permute-start(f32[20,1024]{1,0:T(8,128)S(1)} %pad_maximum_fusion.5), channel_id=1, source_target_pairs={{0,4},{1,5},{2,6},{3,7},{4,0},{5,1},{6,2},{7,3},{8,12},{9,13},{10,... | collective-permute-start | bytes 245768 | tf_op jit(solution)/shard_map/ppermute | solution.py:430
  79.4 3.0 %collective-permute-done.16 = f32[20,1024]{1,0:T(8,128)S(1)} collective-permute-done((f32[20,1024]{1,0:T(8,128)S(1)}, f32[20,1024]{1,0:T(8,128)S(1)}, u32[]{:S(2)}, u32[]{:S(2)}) %collective-permute-start.16) | collective-permute-done | bytes 81952 | tf_op jit(solution)/shard_map/ppermute | solution.py:430
  82.5 2.8 %collective-permute-start.17 = (f32[12,1024]{1,0:T(8,128)S(1)}, f32[12,1024]{1,0:T(8,128)S(1)}, u32[]{:S(2)}, u32[]{:S(2)}) collective-permute-start(f32[12,1024]{1,0:T(8,128)S(1)} %pad_maximum_fusion.7), channel_id=1, source_target_pairs={{0,8},{1,9},{2,10},{3,11},{4,12},{5,13},{6,14},{7,15},{8,0},{9,1},... | collective-permute-start | bytes 147464 | tf_op jit(solution)/shard_map/ppermute | solution.py:430
  85.3 2.4 %collective-permute-done.17 = f32[12,1024]{1,0:T(8,128)S(1)} collective-permute-done((f32[12,1024]{1,0:T(8,128)S(1)}, f32[12,1024]{1,0:T(8,128)S(1)}, u32[]{:S(2)}, u32[]{:S(2)}) %collective-permute-start.17) | collective-permute-done | bytes 49184 | tf_op jit(solution)/shard_map/ppermute | solution.py:430
  87.8 2.8 %collective-permute-start.18 = (f32[2,8,1024]{2,1,0:T(8,128)S(1)}, f32[2,8,1024]{2,1,0:T(8,128)S(1)}, u32[]{:S(2)}, u32[]{:S(2)}) collective-permute-start(f32[2,8,1024]{2,1,0:T(8,128)S(1)} %pad_maximum_fusion.8), channel_id=1, source_target_pairs={{0,8},{1,9},{2,10},{3,11},{4,12},{5,13},{6,14},{7,15},{8,0},{9,1},... | collective-permute-start | bytes 196616 | tf_op jit(solution)/shard_map/ppermute | solution.py:430
  90.6 0.0 collective-permute-start.19
  90.6 1.2 %collective-permute-done.19.refs_1_ = f32[4,1024]{1,0:T(4,128)S(1)} collective-permute-done((f32[4,1024]{1,0:T(4,128)S(1)}, f32[4,1024]{1,0:T(4,128)S(1)}, u32[]{:S(2)}, u32[]{:S(2)}) %collective-permute-start.19) | collective-permute-done | bytes 16416 | tf_op jit(solution)/shard_map/ppermute | solution.py:430
  91.8 0.2 sums.3.refs_3_
  92.0 1.5 %collective-permute-start.20 = (f32[8,128]{1,0:T(8,128)S(1)}, f32[8,128]{1,0:T(8,128)S(1)}, u32[]{:S(2)}, u32[]{:S(2)}) collective-permute-start(f32[8,128]{1,0:T(8,128)S(1)} %sums.3.refs_3_), channel_id=1, source_target_pairs={{0,16},{16,0},{1,17},{17,1},{2,18},{18,2},{3,19},{19,3},{4,20},{20... | collective-permute-start | bytes 12296 | tf_op jit(solution)/shard_map/ppermute | solution.py:456
  93.5 0.0 collective-permute-done.18
  93.5 2.1 %collective-permute-done.20.refs_4_ = f32[8,128]{1,0:T(8,128)S(1)} collective-permute-done((f32[8,128]{1,0:T(8,128)S(1)}, f32[8,128]{1,0:T(8,128)S(1)}, u32[]{:S(2)}, u32[]{:S(2)}) %collective-permute-start.20) | collective-permute-done | bytes 4128 | tf_op jit(solution)/shard_map/ppermute | solution.py:456
  95.6 0.1 combine.1
  95.7 2.2 %collective-permute-start.21 = (f32[16,1024]{1,0:T(8,128)S(1)}, f32[16,1024]{1,0:T(8,128)S(1)}, u32[]{:S(2)}, u32[]{:S(2)}) collective-permute-start(f32[16,1024]{1,0:T(8,128)S(1)} %combine.1), channel_id=1, source_target_pairs={{0,4},{1,5},{2,6},{3,7},{4,0},{5,1},{6,2},{7,3},{8,12},{9,13},{10,... | collective-permute-start | bytes 196616 | tf_op jit(solution)/shard_map/ppermute | solution.py:430
  97.9 2.2 %collective-permute-done.21 = f32[16,1024]{1,0:T(8,128)S(1)} collective-permute-done((f32[16,1024]{1,0:T(8,128)S(1)}, f32[16,1024]{1,0:T(8,128)S(1)}, u32[]{:S(2)}, u32[]{:S(2)}) %collective-permute-start.21) | collective-permute-done | bytes 65568 | tf_op jit(solution)/shard_map/ppermute | solution.py:430
  100.2 1.4 %collective-permute-start.22 = (f32[32,1024]{1,0:T(8,128)S(1)}, f32[32,1024]{1,0:T(8,128)S(1)}, u32[]{:S(2)}, u32[]{:S(2)}) collective-permute-start(f32[32,1024]{1,0:T(8,128)S(1)} %pad_maximum_fusion.3), channel_id=1, source_target_pairs={{0,2},{1,3},{2,0},{3,1},{4,6},{5,7},{6,4},{7,5},{8,10},{9,11},{10,... | collective-permute-start | bytes 393224 | tf_op jit(solution)/shard_map/ppermute | solution.py:430
  101.5 3.7 %collective-permute-done.22 = f32[32,1024]{1,0:T(8,128)S(1)} collective-permute-done((f32[32,1024]{1,0:T(8,128)S(1)}, f32[32,1024]{1,0:T(8,128)S(1)}, u32[]{:S(2)}, u32[]{:S(2)}) %collective-permute-start.22) | collective-permute-done | bytes 131104 | tf_op jit(solution)/shard_map/ppermute | solution.py:430
  105.2 0.1 collective-permute-start.23
  105.3 1.5 %collective-permute-done.23 = f32[64,1024]{1,0:T(8,128)S(1)} collective-permute-done((f32[64,1024]{1,0:T(8,128)S(1)}, f32[64,1024]{1,0:T(8,128)S(1)}, u32[]{:S(2)}, u32[]{:S(2)}) %collective-permute-start.23) | collective-permute-done | bytes 262176 | tf_op jit(solution)/shard_map/ppermute | solution.py:430
  106.9 0.8 pad_maximum_fusion
  (40 shorter events, 0.6 us)
Async XLA Ops:
  0.0 21.3 %copy-start.2 = (f32[4,32,1024]{2,1,0:T(8,128)S(1)}, f32[4,32,1024]{2,1,0:T(8,128)}, u32[]{:S(2)}) copy-start(f32[4,32,1024]{2,1,0:T(8,128)} %param.8) | copy-start | bytes 1572868
  1.4 29.7 %copy-start = (bf16[8,4,32,1024]{3,2,1,0:T(8,128)(2,1)S(1)}, bf16[8,4,32,1024]{3,2,1,0:T(8,128)(2,1)}, u32[]{:S(2)}) copy-start(bf16[8,4,32,1024]{3,2,1,0:T(8,128)(2,1)} %ens_hbm.1) | copy-start | bytes 6291460
  1.4 29.7 %copy-start.1 = (bf16[1088,256]{1,0:T(8,128)(2,1)S(1)}, bf16[1088,256]{1,0:T(8,128)(2,1)}, u32[]{:S(2)}) copy-start(bf16[1088,256]{1,0:T(8,128)(2,1)} %constant.4.clone.table_ref) | copy-start | bytes 1671172
  1.4 29.6 %collective-permute-start = (bf16[8,4,16,1024]{3,2,1,0:T(8,128)(2,1)S(1)}, bf16[8,4,16,1024]{3,2,1,0:T(8,128)(2,1)S(1)}, u32[]{:S(2)}, u32[]{:S(2)}) collective-permute-start(bf16[8,4,16,1024]{3,2,1,0:T(8,128)(2,1)S(1)} %get-tuple-element.13), channel_id=1, source_target_pairs={{0,16},{16,0},{1,17},{17,1},{2,18},{18,2},{3,19},{19,3},{4,20},{20... | collective-permute-start | bytes 3145736 | tf_op jit(solution)/shard_map/ppermute | solution.py:464
  4.5 1.3 %collective-permute-start.1 = (f32[24,1024]{1,0:T(8,128)S(1)}, f32[24,1024]{1,0:T(8,128)S(1)}, u32[]{:S(2)}, u32[]{:S(2)}) collective-permute-start(f32[24,1024]{1,0:T(8,128)S(1)} %get-tuple-element.14), channel_id=1, source_target_pairs={{0,1},{1,0},{2,3},{3,2},{4,5},{5,4},{6,7},{7,6},{8,9},{9,8},{10,11... | collective-permute-start | bytes 294920 | tf_op jit(solution)/shard_map/ppermute | solution.py:430
  5.8 4.9 %collective-permute-start.2 = (f32[24,1024]{1,0:T(8,128)S(1)}, f32[24,1024]{1,0:T(8,128)S(1)}, u32[]{:S(2)}, u32[]{:S(2)}) collective-permute-start(f32[24,1024]{1,0:T(8,128)S(1)} %add.54), channel_id=1, source_target_pairs={{0,2},{1,3},{2,0},{3,1},{4,6},{5,7},{6,4},{7,5},{8,10},{9,11},{10,... | collective-permute-start | bytes 294920 | tf_op jit(solution)/shard_map/ppermute | solution.py:430
  10.7 4.7 %collective-permute-start.3 = (f32[24,1024]{1,0:T(8,128)S(1)}, f32[24,1024]{1,0:T(8,128)S(1)}, u32[]{:S(2)}, u32[]{:S(2)}) collective-permute-start(f32[24,1024]{1,0:T(8,128)S(1)} %add.55), channel_id=1, source_target_pairs={{0,4},{1,5},{2,6},{3,7},{4,0},{5,1},{6,2},{7,3},{8,12},{9,13},{10,... | collective-permute-start | bytes 294920 | tf_op jit(solution)/shard_map/ppermute | solution.py:430
  15.4 5.6 %collective-permute-start.4 = (f32[24,1024]{1,0:T(8,128)S(1)}, f32[24,1024]{1,0:T(8,128)S(1)}, u32[]{:S(2)}, u32[]{:S(2)}) collective-permute-start(f32[24,1024]{1,0:T(8,128)S(1)} %add.56), channel_id=1, source_target_pairs={{0,8},{1,9},{2,10},{3,11},{4,12},{5,13},{6,14},{7,15},{8,0},{9,1},... | collective-permute-start | bytes 294920 | tf_op jit(solution)/shard_map/ppermute | solution.py:430
  21.0 8.7 %collective-permute-start.5 = (f32[24,1024]{1,0:T(8,128)S(1)}, f32[24,1024]{1,0:T(8,128)S(1)}, u32[]{:S(2)}, u32[]{:S(2)}) collective-permute-start(f32[24,1024]{1,0:T(8,128)S(1)} %add.57.refs_0_.message.refs_2_), channel_id=1, source_target_pairs={{0,16},{16,0},{1,17},{17,1},{2,18},{18,2},{3,19},{19,3},{4,20},{20... | collective-permute-start | bytes 294920 | tf_op jit(solution)/shard_map/ppermute | solution.py:456
  35.9 1.6 %collective-permute-start.6 = (f32[64,1024]{1,0:T(8,128)S(1)}, f32[64,1024]{1,0:T(8,128)S(1)}, u32[]{:S(2)}, u32[]{:S(2)}) collective-permute-start(f32[64,1024]{1,0:T(8,128)S(1)} %get-tuple-element.16), channel_id=1, source_target_pairs={{0,1},{1,0},{2,3},{3,2},{4,5},{5,4},{6,7},{7,6},{8,9},{9,8},{10,11... | collective-permute-start | bytes 786440 | tf_op jit(solution)/shard_map/ppermute | solution.py:430
  37.5 8.3 %collective-permute-start.7 = (f32[32,1024]{1,0:T(8,128)S(1)}, f32[32,1024]{1,0:T(8,128)S(1)}, u32[]{:S(2)}, u32[]{:S(2)}) collective-permute-start(f32[32,1024]{1,0:T(8,128)S(1)} %slice_select_fusion.1), channel_id=1, source_target_pairs={{0,2},{1,3},{2,0},{3,1},{4,6},{5,7},{6,4},{7,5},{8,10},{9,11},{10,... | collective-permute-start | bytes 393224 | tf_op jit(solution)/shard_map/ppermute | solution.py:430
  41.9 4.0 %collective-permute-start.8 = (f32[8,1024]{1,0:T(8,128)S(1)}, f32[8,1024]{1,0:T(8,128)S(1)}, u32[]{:S(2)}, u32[]{:S(2)}) collective-permute-start(f32[8,1024]{1,0:T(8,128)S(1)} %gather_places.2), channel_id=1, source_target_pairs={{0,2},{1,3},{2,0},{3,1},{4,6},{5,7},{6,4},{7,5},{8,10},{9,11},{10,... | collective-permute-start | bytes 98312 | tf_op jit(solution)/shard_map/ppermute | solution.py:430
  45.9 4.7 %collective-permute-start.9 = (f32[24,1024]{1,0:T(8,128)S(1)}, f32[24,1024]{1,0:T(8,128)S(1)}, u32[]{:S(2)}, u32[]{:S(2)}) collective-permute-start(f32[24,1024]{1,0:T(8,128)S(1)} %pad_maximum_fusion.4), channel_id=1, source_target_pairs={{0,4},{1,5},{2,6},{3,7},{4,0},{5,1},{6,2},{7,3},{8,12},{9,13},{10,... | collective-permute-start | bytes 294920 | tf_op jit(solution)/shard_map/ppermute | solution.py:430
  50.7 5.2 %collective-permute-start.10 = (f32[16,1024]{1,0:T(8,128)S(1)}, f32[16,1024]{1,0:T(8,128)S(1)}, u32[]{:S(2)}, u32[]{:S(2)}) collective-permute-start(f32[16,1024]{1,0:T(8,128)S(1)} %pad_maximum_fusion.6), channel_id=1, source_target_pairs={{0,8},{1,9},{2,10},{3,11},{4,12},{5,13},{6,14},{7,15},{8,0},{9,1},... | collective-permute-start | bytes 196616 | tf_op jit(solution)/shard_map/ppermute | solution.py:430
  55.9 1.3 %collective-permute-start.11 = (f32[8,1024]{1,0:T(8,128)S(1)}, f32[8,1024]{1,0:T(8,128)S(1)}, u32[]{:S(2)}, u32[]{:S(2)}) collective-permute-start(f32[8,1024]{1,0:T(8,128)S(1)} %get-tuple-element.32.refs_0_), channel_id=1, source_target_pairs={{0,1},{1,0},{2,3},{3,2},{4,5},{5,4},{6,7},{7,6},{8,9},{9,8},{10,11... | collective-permute-start | bytes 98312 | tf_op jit(solution)/shard_map/ppermute | solution.py:430
  57.3 3.9 %collective-permute-start.12 = (f32[8,1024]{1,0:T(8,128)S(1)}, f32[8,1024]{1,0:T(8,128)S(1)}, u32[]{:S(2)}, u32[]{:S(2)}) collective-permute-start(f32[8,1024]{1,0:T(8,128)S(1)} %sums.2.refs_1_.refs_2_.refs_3_.refs_4_), channel_id=1, source_target_pairs={{0,16},{16,0},{1,17},{17,1},{2,18},{18,2},{3,19},{19,3},{4,20},{20... | collective-permute-start | bytes 98312 | tf_op jit(solution)/shard_map/ppermute | solution.py:456
  70.1 1.6 %collective-permute-start.13 = (f32[64,1024]{1,0:T(8,128)S(1)}, f32[64,1024]{1,0:T(8,128)S(1)}, u32[]{:S(2)}, u32[]{:S(2)}) collective-permute-start(f32[64,1024]{1,0:T(8,128)S(1)} %get-tuple-element.18), channel_id=1, source_target_pairs={{0,1},{1,0},{2,3},{3,2},{4,5},{5,4},{6,7},{7,6},{8,9},{9,8},{10,11... | collective-permute-start | bytes 786440 | tf_op jit(solution)/shard_map/ppermute | solution.py:430
  71.7 6.0 %collective-permute-start.14 = (f32[32,1024]{1,0:T(8,128)S(1)}, f32[32,1024]{1,0:T(8,128)S(1)}, u32[]{:S(2)}, u32[]{:S(2)}) collective-permute-start(f32[32,1024]{1,0:T(8,128)S(1)} %slice_select_fusion), channel_id=1, source_target_pairs={{0,2},{1,3},{2,0},{3,1},{4,6},{5,7},{6,4},{7,5},{8,10},{9,11},{10,... | collective-permute-start | bytes 393224 | tf_op jit(solution)/shard_map/ppermute | solution.py:430
  73.5 4.2 %collective-permute-start.15 = (f32[4,1024]{1,0:T(4,128)S(1)}, f32[4,1024]{1,0:T(4,128)S(1)}, u32[]{:S(2)}, u32[]{:S(2)}) collective-permute-start(f32[4,1024]{1,0:T(4,128)S(1)} %gather_places.3), channel_id=1, source_target_pairs={{0,2},{1,3},{2,0},{3,1},{4,6},{5,7},{6,4},{7,5},{8,10},{9,11},{10,... | collective-permute-start | bytes 49160 | tf_op jit(solution)/shard_map/ppermute | solution.py:430
  77.8 4.7 %collective-permute-start.16 = (f32[20,1024]{1,0:T(8,128)S(1)}, f32[20,1024]{1,0:T(8,128)S(1)}, u32[]{:S(2)}, u32[]{:S(2)}) collective-permute-start(f32[20,1024]{1,0:T(8,128)S(1)} %pad_maximum_fusion.5), channel_id=1, source_target_pairs={{0,4},{1,5},{2,6},{3,7},{4,0},{5,1},{6,2},{7,3},{8,12},{9,13},{10,... | collective-permute-start | bytes 245768 | tf_op jit(solution)/shard_map/ppermute | solution.py:430
  82.5 5.2 %collective-permute-start.17 = (f32[12,1024]{1,0:T(8,128)S(1)}, f32[12,1024]{1,0:T(8,128)S(1)}, u32[]{:S(2)}, u32[]{:S(2)}) collective-permute-start(f32[12,1024]{1,0:T(8,128)S(1)} %pad_maximum_fusion.7), channel_id=1, source_target_pairs={{0,8},{1,9},{2,10},{3,11},{4,12},{5,13},{6,14},{7,15},{8,0},{9,1},... | collective-permute-start | bytes 147464 | tf_op jit(solution)/shard_map/ppermute | solution.py:430
  87.8 5.7 %collective-permute-start.18 = (f32[2,8,1024]{2,1,0:T(8,128)S(1)}, f32[2,8,1024]{2,1,0:T(8,128)S(1)}, u32[]{:S(2)}, u32[]{:S(2)}) collective-permute-start(f32[2,8,1024]{2,1,0:T(8,128)S(1)} %pad_maximum_fusion.8), channel_id=1, source_target_pairs={{0,8},{1,9},{2,10},{3,11},{4,12},{5,13},{6,14},{7,15},{8,0},{9,1},... | collective-permute-start | bytes 196616 | tf_op jit(solution)/shard_map/ppermute | solution.py:430
  90.6 1.2 %collective-permute-start.19 = (f32[4,1024]{1,0:T(4,128)S(1)}, f32[4,1024]{1,0:T(4,128)S(1)}, u32[]{:S(2)}, u32[]{:S(2)}) collective-permute-start(f32[4,1024]{1,0:T(4,128)S(1)} %slice_add_fusion.6.refs_0_), channel_id=1, source_target_pairs={{0,1},{1,0},{2,3},{3,2},{4,5},{5,4},{6,7},{7,6},{8,9},{9,8},{10,11... | collective-permute-start | bytes 49160 | tf_op jit(solution)/shard_map/ppermute | solution.py:430
  92.0 3.6 %collective-permute-start.20 = (f32[8,128]{1,0:T(8,128)S(1)}, f32[8,128]{1,0:T(8,128)S(1)}, u32[]{:S(2)}, u32[]{:S(2)}) collective-permute-start(f32[8,128]{1,0:T(8,128)S(1)} %sums.3.refs_3_), channel_id=1, source_target_pairs={{0,16},{16,0},{1,17},{17,1},{2,18},{18,2},{3,19},{19,3},{4,20},{20... | collective-permute-start | bytes 12296 | tf_op jit(solution)/shard_map/ppermute | solution.py:456
  95.7 4.5 %collective-permute-start.21 = (f32[16,1024]{1,0:T(8,128)S(1)}, f32[16,1024]{1,0:T(8,128)S(1)}, u32[]{:S(2)}, u32[]{:S(2)}) collective-permute-start(f32[16,1024]{1,0:T(8,128)S(1)} %combine.1), channel_id=1, source_target_pairs={{0,4},{1,5},{2,6},{3,7},{4,0},{5,1},{6,2},{7,3},{8,12},{9,13},{10,... | collective-permute-start | bytes 196616 | tf_op jit(solution)/shard_map/ppermute | solution.py:430
  100.2 5.0 %collective-permute-start.22 = (f32[32,1024]{1,0:T(8,128)S(1)}, f32[32,1024]{1,0:T(8,128)S(1)}, u32[]{:S(2)}, u32[]{:S(2)}) collective-permute-start(f32[32,1024]{1,0:T(8,128)S(1)} %pad_maximum_fusion.3), channel_id=1, source_target_pairs={{0,2},{1,3},{2,0},{3,1},{4,6},{5,7},{6,4},{7,5},{8,10},{9,11},{10,... | collective-permute-start | bytes 393224 | tf_op jit(solution)/shard_map/ppermute | solution.py:430
  105.2 1.6 %collective-permute-start.23 = (f32[64,1024]{1,0:T(8,128)S(1)}, f32[64,1024]{1,0:T(8,128)S(1)}, u32[]{:S(2)}, u32[]{:S(2)}) collective-permute-start(f32[64,1024]{1,0:T(8,128)S(1)} %pad_maximum_fusion.1), channel_id=1, source_target_pairs={{0,1},{1,0},{2,3},{3,2},{4,5},{5,4},{6,7},{7,6},{8,9},{9,8},{10,11... | collective-permute-start | bytes 786440 | tf_op jit(solution)/shard_map/ppermute | solution.py:430

commit v6 on v5

--- a/solution.py
+++ b/solution.py
@@ -8,8 +8,8 @@
 from jax.experimental.pallas import tpu as pltpu
 from jax.sharding import PartitionSpec as P
 
+
 HALF = 8
-ITERS = 2
 REACH = 2 * HALF
 
 huber_edge = 1.5
@@ -18,7 +18,7 @@
 
 LANES = 256
 MIB = 1 << 20
-GROUP = 4
+GROUP = 8
 F32 = jnp.float32
 BF16 = jnp.bfloat16
 
@@ -101,6 +101,11 @@
     weight = huber_edge / jnp.maximum(jnp.abs(departure / error), huber_edge)
     share = weight / (error * error)
     return share * departure, share
+
+
+def halo_groups(members):
+    late = members // 4
+    return [members - late, late] if late else [members]
 
 
 def prepare_kernel(bands, bits, root_hbm, ens_hbm, idx_hbm, value_hbm, error_hbm, out_ref,
@@ -114,8 +119,13 @@
         starts = [rows - REACH, 0]
     pairs = [(idx_hbm, idx_ref), (value_hbm, value_ref), (error_hbm, error_ref)]
     pairs.append((root_hbm, roots))
-    for start, edge in zip(starts, edges):
-        pairs.append((ens_hbm.at[:, :, pl.ds(pl.multiple_of(start, REACH), REACH), :], edge))
+    member = 0
+    for k, edge in enumerate(edges):
+        side = k % len(starts)
+        some = pl.ds(member, edge.shape[0])
+        row = pl.ds(pl.multiple_of(starts[side], REACH), REACH)
+        pairs.append((ens_hbm.at[some, :, row, :], edge))
+        member += edge.shape[0] if side == len(starts) - 1 else 0
     loads = [pltpu.make_async_copy(x, y, arrived.at[k]) for k, (x, y) in enumerate(pairs)]
     for load in loads:
         load.start()
@@ -143,18 +153,24 @@
 
 
 def prepare(bands, bits, roots, ensemble, index, value, error, lon):
-    count = 1 if bands == 2 else 2
+    sides = 1 if bands == 2 else 2
+    groups = halo_groups(ensemble.shape[0])
+    count = sides * len(groups)
     away = pl.BlockSpec(memory_space=pl.ANY)
     assert len(bits) < 8
     inputs = [roots, ensemble, index, value, error]
     inputs = [pltpu.with_memory_space_constraint(x, pltpu.HBM) for x in inputs]
-    edge = jax.ShapeDtypeStruct(ensemble.shape[:2] + (REACH, lon), BF16)
+    edges = [
+        jax.ShapeDtypeStruct((n, ensemble.shape[1], REACH, lon), BF16)
+        for n in groups
+        for _ in range(sides)
+    ]
     return pl.pallas_call(
         functools.partial(prepare_kernel, bands, bits),
         out_shape=(
             jax.ShapeDtypeStruct((6 * (index.shape[1] // lon), lon), F32),
             jax.ShapeDtypeStruct((8, lon), F32),
-            *[edge] * count,
+            *edges,
         ),
         in_specs=[away] * 5,
         out_specs=[vmem()] * (2 + count),
@@ -265,57 +281,72 @@
     return jnp.concatenate([y[j * rows:(j + 1) * rows] for j in range(lon // LANES)], axis=1)
 
 
-def filter_kernel(share, shapes, own_ref, ext_ref, grad_ref, gext_ref, var_ref, table_ref,
-                  keep_ref, send_ref, acc_ref):
-    position = lax.axis_index("member")
+def filter_kernel(share, shapes, kept, first_member, resume, finish, *refs):
+    own_ref, grad_ref, gext_ref, static_ref, table_ref = refs[:5]
+    ext_refs, out_ref = refs[5:-1], refs[-1]
+    sum_ref = None
+    if resume:
+        ext_refs, sum_ref = ext_refs[:-1], ext_refs[-1]
+    bit = lax.axis_index("member") % 2
+    bit = bit if kept else 1 - bit
     band = lax.axis_index("band")
-    members = own_ref.shape[0]
+    near_of = [(ref, k) for ref in ext_refs for k in range(ref.shape[1])]
+    members = len(near_of)
     (rows_1, cols_1), (rows_2, cols_2), bands = shapes
+    sources = ext_refs[0].shape[0]
     tile = table_ref[:2 * LANES, :LANES]
     start_1 = pl.multiple_of(2 * LANES + band * rows_1, 16)
     start_2 = pl.multiple_of(2 * LANES + bands * rows_1 + band * rows_2, 16)
     lat1 = table_ref[pl.ds(start_1, rows_1), :cols_1]
     lat2 = table_ref[pl.ds(start_2, rows_2), :cols_2]
-    size = GROUP if members % GROUP == 0 else 1
+    rows = own_ref.shape[1] // 2
+    near = ext_refs[0].shape[2] // 2
+    own_part = pl.ds(pl.multiple_of(bit * rows, rows), rows)
+    ext_part = pl.ds(pl.multiple_of(bit * near, near), near)
+    grad = grad_ref[own_part, :]
+    size = min(GROUP, members)
     for start in range(0, members, size):
-        group = range(start, start + size)
-        mixed = [
-            jnp.concatenate(
-                [
-                    (own_ref[m].astype(F32) * grad_ref[...]).astype(BF16),
-                    (ext_ref[m].astype(F32) * gext_ref[...]).astype(BF16),
-                ],
-                axis=0,
-            )
-            for m in group
-        ]
+        group = range(start, min(start + size, members))
+        mixed = []
+        for m in group:
+            parts = [(own_ref[first_member + m, own_part, :].astype(F32) * grad).astype(BF16)]
+            ext_ref, k = near_of[m]
+            for s in range(sources):
+                ext = ext_ref[s, k, ext_part, :].astype(F32)
+                parts.append((ext * gext_ref[s, ext_part, :]).astype(BF16))
+            mixed.append(jnp.concatenate(parts, axis=0))
         first = [lon_pass(x, tile) for x in mixed]
         first = [jnp.dot(lat1, x, preferred_element_type=F32).astype(BF16) for x in first]
         second = [lon_pass(x, tile) for x in first]
         second = [jnp.dot(lat2, x, preferred_element_type=F32) for x in second]
-        product = own_ref[group[0]].astype(F32) * second[0]
+        product = own_ref[first_member + group[0], own_part, :].astype(F32) * second[0]
         for m, x in zip(group[1:], second[1:]):
-            product += own_ref[m].astype(F32) * x
-        acc_ref[...] = product if start == 0 else acc_ref[...] + product
-    half = keep_ref.shape[0]
-    bit = position % 2
-    for ref, start in ((keep_ref, bit * half), (send_ref, (1 - bit) * half)):
-        rows = pl.ds(pl.multiple_of(start, half), half)
-        ref[...] = share * acc_ref[rows, :] + var_ref[rows, :] * grad_ref[rows, :]
-
-
-def filter_members(share, shapes, own, ext, grad, gext, static, table):
-    members, rows, lon = own.shape
-    half = jax.ShapeDtypeStruct((rows // 2, lon), F32)
+            product += own_ref[first_member + m, own_part, :].astype(F32) * x
+        if start > 0:
+            product += out_ref[...]
+        elif resume:
+            product += sum_ref[...]
+        if finish and start + size >= members:
+            product = share * product + static_ref[own_part, :] * grad
+        out_ref[...] = product
+
+
+def filter_members(share, shapes, kept, first_member, total, own, ext, grad, gext, static, table):
+    _, rows, lon = own.shape
+    resume = total is not None
+    finish = first_member + sum(e.shape[1] for e in ext) == own.shape[0]
+    args = [own, grad, gext, static, table, *ext] + ([total] if resume else [])
+    kernel = functools.partial(
+        filter_kernel, share, shapes, kept, first_member, resume, finish
+    )
     return pl.pallas_call(
-        functools.partial(filter_kernel, share, shapes),
-        out_shape=(half, half),
-        in_specs=[vmem()] * 6,
-        out_specs=(vmem(), vmem()),
-        scratch_shapes=[pltpu.VMEM((rows, lon), F32)],
+        kernel,
+        out_shape=jax.ShapeDtypeStruct((rows // 2, lon), F32),
+        in_specs=[vmem()] * len(args),
+        out_specs=vmem(),
         compiler_params=limit(14),
-        name="filter_members",
-    )(own, ext, grad, gext, static, table)
+        name="filter_keep" if kept else "filter_send",
+    )(*args)
 
 
 def gather_kernel(which, field_ref, message, out_ref):
@@ -359,7 +390,6 @@
     tail = refs[0][...] + refs[1][...]
     message, out_ref = refs[2], refs[-1]
     chunks = message.shape[0] // 6
-    lon = message.shape[1]
     part = lambda ref, k: ref[k * chunks:(k + 1) * chunks, :]
     total = lambda x: jnp.sum(jnp.sum(x, axis=0, keepdims=True), axis=1, keepdims=True)
     out_ref[...] = jnp.zeros_like(out_ref)
@@ -398,14 +428,14 @@
     first, second = refs[1:1 + count], refs[1 + count:-1]
     scale_0 = scale_of(first, chunks)
     scale_1 = scale_of(second, chunks)
-    out_ref[...] = scale_0 * pair[0] + scale_1 * pair[1]
+    out_ref[...] = (scale_0 * pair[0] + scale_1 * pair[1]).astype(out_ref.dtype)
 
 
 def combine(pair, first, second, chunks):
     args = [pair, *first, *second]
     return pl.pallas_call(
         functools.partial(combine_kernel, chunks, len(first)),
-        out_shape=jax.ShapeDtypeStruct(pair.shape[1:], F32),
+        out_shape=jax.ShapeDtypeStruct(pair.shape[1:], BF16),
         in_specs=[vmem()] * len(args),
         out_specs=vmem(),
         compiler_params=limit(2),
@@ -445,10 +475,32 @@
     return x, tail
 
 
+def reduce_square(x, tail, high, low, count, uppers):
+    keep, send = halves(x, uppers[high])
+    near, far = halves(keep, uppers[low]), halves(send, uppers[low])
+    rows = near[0].shape[0]
+    total = jnp.concatenate([near[0], tail], axis=0)
+    for part, bit in ((near[1], low), (far[0], high), (far[1], high | low)):
+        total = total + swap(jnp.concatenate([part, tail], axis=0), bit, count)
+    return total[:rows], total[rows:]
+
+
 def gather_rows(x, bit, count, upper):
     other = swap(x, bit, count)
     axis = x.ndim - 2
     return jnp.concatenate([jnp.where(upper, other, x), jnp.where(upper, x, other)], axis=axis)
+
+
+def join_rows(x, other, upper):
+    axis = x.ndim - 2
+    return jnp.concatenate([jnp.where(upper, other, x), jnp.where(upper, x, other)], axis=axis)
+
+
+def gather_square(x, high, low, count, uppers):
+    across, along, both = (swap(x, bit, count) for bit in (high, low, high | low))
+    mine = join_rows(x, along, uppers[low])
+    other = join_rows(across, both, uppers[low])
+    return join_rows(mine, other, uppers[high])
 
 
 def from_bands(x, count):
@@ -474,7 +526,7 @@
     chunks = obs_index.shape[1] // lon
     bits = member_bits(n_member)
 
-    lat1, lat2 = lat_operators(levels, lat_rows, n_band, HALF)
+    lat1, lat2 = lat_operators(levels // 2, lat_rows, n_band, HALF)
     shapes = (lat1.shape[1:], lat2.shape[1:], n_band)
     wide = max(LANES, lat1.shape[2])
     parts = [lon_tile(HALF), *lat1, *lat2]
@@ -484,34 +536,49 @@
     message, flags, *edges = prepare(
         n_band, bits, root_ranks, ensemble, obs_index, obs_value, obs_error, lon
     )
-    halo = band_halo(edges, n_band)
+    sides = 1 if n_band == 2 else 2
+    halo = band_halo(edges[:sides], n_band)
     message = message + swap(message, bits[0], n_member)
     for bit in bits[1:]:
         message = message + swap(message, bit, n_member)
     around = from_bands(message, n_band)
 
     own = ensemble.reshape(members_here, levels * lat_rows, lon)
-    ext = jnp.concatenate([h.reshape(members_here, levels * REACH, lon) for h in halo], axis=1)
+    near_rows = lambda part: jnp.stack(
+        [h.reshape(h.shape[0], levels * REACH, lon) for h in part]
+    )
+    ext = [near_rows(halo)]
     uppers = {bit: flags[k:k + 1] > 0 for k, bit in enumerate(bits)}
     static = flags[-1] * variance
     static = static.reshape(levels * lat_rows, lon)
     share = ensemble_share / (members - 1)
 
-    def direction_parts(text=None, totals=(), texts=()):
+    def direction_parts(rest, text=None, totals=(), texts=()):
         scatter = functools.partial(scatter_obs, levels, lat_rows, lon, n_band)
         grad = scatter(message, text, totals)
         gext = [
             scatter(a, texts[s] if texts else None, totals, s)
             for s, a in enumerate(around)
         ]
-        gext = jnp.concatenate(gext, axis=0)
-        keep, send = filter_members(share, shapes, own, ext, grad, gext, static, table)
-        field = keep + swap(send, bits[0], n_member)
+        filters = functools.partial(filter_members, share, shapes)
+        parts = (grad, jnp.stack(gext), static, table)
+        if rest:
+            early = [filters(kept, 0, None, own, ext, *parts) for kept in (False, True)]
+            first = ext[0].shape[1]
+            late = band_halo(rest, n_band)
+            ext.append(near_rows(late))
+            send = filters(False, first, early[0], own, ext[1:], *parts)
+            got = swap(send, bits[0], n_member)
+            field = filters(True, first, early[1], own, ext[1:], *parts) + got
+        else:
+            got = swap(filters(False, 0, None, own, ext, *parts), bits[0], n_member)
+            field = filters(True, 0, None, own, ext, *parts) + got
         keep, send = halves(field, uppers[bits[1]])
         piece = keep + swap(send, bits[1], n_member)
         tail = gather_places((3,) if texts else (0, 3), field, message)
         tail = tail + swap(tail, bits[1], n_member)
-        piece, tail = reduce_with_tail(piece, tail, bits[2:], n_member, uppers)
+        piece, tail = reduce_square(piece, tail, bits[2], bits[3], n_member, uppers)
+        piece, tail = reduce_with_tail(piece, tail, bits[4:], n_member, uppers)
         return piece, (tail, swap(tail, bits[0], n_member))
 
     def band_totals(text):
@@ -520,17 +587,20 @@
             return [text, *texts], texts
         return [lax.psum(text, "band")], texts
 
-    piece_0, tail = direction_parts()
+    piece_0, tail = direction_parts(edges[sides:])
     text = sums(tail, message)
     totals_0, texts = band_totals(text)
 
-    piece_1, tail = direction_parts(text, totals_0, texts)
+    piece_1, tail = direction_parts([], text, totals_0, texts)
     totals_1, _ = band_totals(sums(tail, message, text, totals_0))
-    pair = gather_rows(jnp.stack([piece_0, piece_1]), bits[-1], n_member, uppers[bits[-1]])
+    pair = jnp.stack([piece_0, piece_1])
+    for bit in bits[:3:-1]:
+        pair = gather_rows(pair, bit, n_member, uppers[bit])
+    pair = gather_square(pair, bits[2], bits[3], n_member, uppers)
     out = combine(pair, totals_0, totals_1, chunks)
-    for bit in reversed(bits[:-1]):
+    for bit in (bits[1], bits[0]):
         out = gather_rows(out, bit, n_member, uppers[bit])
-    return out.reshape(levels, lat_rows, lon)
+    return out.astype(F32).reshape(levels, lat_rows, lon)
 
 
 def solution(mesh):

time: 108 us -> 101 us (0.935)
  waiting for transfers between devices: 50.9 us -> 43 us
    ppermute x20 -> x23, waiting for transfers between devices: 40.5 us -> 34.7 us  [swap(): return lax.ppermute(x, 'member', partner(count, bit))]
    ppermute x3, waiting for transfers between devices: 10.4 us -> 8.31 us  [from_bands(): return [lax.ppermute(x, 'band', [(0, 1), (1, 0)])]]
    pallas_call x2 -> x6, Pallas kernels: 9.57 us -> 10.4 us  [filter_members(): pl.pallas_call(kernel, out_shape=jax.ShapeDtypeStruct((rows // 2, lon), F...]
    ppermute x20 -> x23, starting transfers between devices: 25.6 us -> 24.8 us  [swap(): return lax.ppermute(x, 'member', partner(count, bit))]
    ppermute x1 -> x2, starting transfers between devices: 3.06 us -> 3.57 us  [band_halo(): return [lax.ppermute(edges[0], 'band', [(0, 1), (1, 0)])]]
  transfers between devices with their start and end apart: 24 -> 28, of which waited for: 20 -> 18; matrix products, arithmetic and copies ran while one was open for 0% -> 0% of each run, Pallas kernels for 7% -> 15%
where the time goes in v6:
time: 101 us
  waiting for transfers between devices  43 us (43%)
  starting transfers between devices  31.8 us (31%)
  Pallas kernels  23.8 us (24%)
  other arithmetic  1.45 us (1%)
    ppermute x23, waiting for transfers between devices, swap(): return lax.ppermute(x, 'member', partner(count, bit))  34.7 us
    ppermute x23, starting transfers between devices, swap(): return lax.ppermute(x, 'member', partner(count, bit))  24.8 us
    pallas_call x6, Pallas kernels, filter_members(): pl.pallas_call(kernel, out_shape=jax.ShapeDtypeStruct((rows // 2, lon), F...  10.4 us
    ppermute x3, waiting for transfers between devices, from_bands(): return [lax.ppermute(x, 'band', [(0, 1), (1, 0)])]  8.31 us
    pallas_call x4, Pallas kernels, scatter_obs(): pl.pallas_call(functools.partial(scatter_kernel, second, rows, lon, bands...  7.76 us
    pallas_call x2, Pallas kernels, gather_places(): pl.pallas_call(functools.partial(gather_kernel, which), out_shape=jax.Sha...  3.92 us
    ppermute x2, starting transfers between devices, band_halo(): return [lax.ppermute(edges[0], 'band', [(0, 1), (1, 0)])]  3.57 us
    ppermute x3, starting transfers between devices, from_bands(): return [lax.ppermute(x, 'band', [(0, 1), (1, 0)])]  3.42 us
  transfers between devices with their start and end apart: 28, of which 18 were waited for; matrix products, arithmetic and copies ran while one was open for 0% of the time, Pallas kernels for 15%

profile of v6, /device:TPU:0, one launch (start us, length us, event | category | flops | bytes accessed | tf_op | source)
XLA Modules:
  0.0 100.6 jit_solution(9197991110455837677)
XLA Ops:
  0.0 1.3 %prepare.1 = (f32[24,1024]{1,0:T(8,128)S(1)}, f32[8,1024]{1,0:T(8,128)S(1)}, bf16[6,4,16,1024]{3,2,1,0:T(8,128)(2,1)S(1)}, bf16[2,4,16,1024]{3,2,1,0:T(8,128)(2,1)S(1)}) custom-call(s32[2]{0:T(128)} %root_hbm.1, bf16[8,4,32,1024]{3,2,1,0:T(8,128)(2,1)} %ens_hbm.1, s32[1,4096]{1,0:T(1,128)} %idx_hbm.1, f32[1,4096]{1,0:T(1,128)} %value_hbm.1, f32[1,4096]{1,0:T(1,128)} %error_hbm.1), custom_call_target="tpu_custom_call" | custom-call | tf_op jit(solution)/shard_map/prepare/pallas_call | solution.py:168
  1.4 0.0 copy-start.1
  1.4 3.1 %collective-permute-start.6 = (bf16[6,4,16,1024]{3,2,1,0:T(8,128)(2,1)S(1)}, bf16[6,4,16,1024]{3,2,1,0:T(8,128)(2,1)S(1)}, u32[]{:S(2)}, u32[]{:S(2)}) collective-permute-start(bf16[6,4,16,1024]{3,2,1,0:T(8,128)(2,1)S(1)} %get-tuple-element.12), channel_id=1, source_target_pairs={{0,16},{16,0},{1,17},{17,1},{2,18},{18,2},{3,19},{19,3},{4,20},{20... | collective-permute-start | bytes 2359304 | tf_op jit(solution)/shard_map/ppermute | solution.py:516
  4.4 1.3 %collective-permute-done = f32[24,1024]{1,0:T(8,128)S(1)} collective-permute-done((f32[24,1024]{1,0:T(8,128)S(1)}, f32[24,1024]{1,0:T(8,128)S(1)}, u32[]{:S(2)}, u32[]{:S(2)}) %collective-permute-start) | collective-permute-done | bytes 98336 | tf_op jit(solution)/shard_map/ppermute | solution.py:460
  5.8 1.6 %collective-permute-start.1 = (f32[24,1024]{1,0:T(8,128)S(1)}, f32[24,1024]{1,0:T(8,128)S(1)}, u32[]{:S(2)}, u32[]{:S(2)}) collective-permute-start(f32[24,1024]{1,0:T(8,128)S(1)} %add.48), channel_id=1, source_target_pairs={{0,2},{1,3},{2,0},{3,1},{4,6},{5,7},{6,4},{7,5},{8,10},{9,11},{10,... | collective-permute-start | bytes 294920 | tf_op jit(solution)/shard_map/ppermute | solution.py:460
  7.3 3.4 %collective-permute-done.1 = f32[24,1024]{1,0:T(8,128)S(1)} collective-permute-done((f32[24,1024]{1,0:T(8,128)S(1)}, f32[24,1024]{1,0:T(8,128)S(1)}, u32[]{:S(2)}, u32[]{:S(2)}) %collective-permute-start.1) | collective-permute-done | bytes 98336 | tf_op jit(solution)/shard_map/ppermute | solution.py:460
  10.7 1.6 %collective-permute-start.2 = (f32[24,1024]{1,0:T(8,128)S(1)}, f32[24,1024]{1,0:T(8,128)S(1)}, u32[]{:S(2)}, u32[]{:S(2)}) collective-permute-start(f32[24,1024]{1,0:T(8,128)S(1)} %add.49), channel_id=1, source_target_pairs={{0,4},{1,5},{2,6},{3,7},{4,0},{5,1},{6,2},{7,3},{8,12},{9,13},{10,... | collective-permute-start | bytes 294920 | tf_op jit(solution)/shard_map/ppermute | solution.py:460
  12.3 3.0 %collective-permute-done.2 = f32[24,1024]{1,0:T(8,128)S(1)} collective-permute-done((f32[24,1024]{1,0:T(8,128)S(1)}, f32[24,1024]{1,0:T(8,128)S(1)}, u32[]{:S(2)}, u32[]{:S(2)}) %collective-permute-start.2) | collective-permute-done | bytes 98336 | tf_op jit(solution)/shard_map/ppermute | solution.py:460
  15.4 2.7 %collective-permute-start.3 = (f32[24,1024]{1,0:T(8,128)S(1)}, f32[24,1024]{1,0:T(8,128)S(1)}, u32[]{:S(2)}, u32[]{:S(2)}) collective-permute-start(f32[24,1024]{1,0:T(8,128)S(1)} %add.50), channel_id=1, source_target_pairs={{0,8},{1,9},{2,10},{3,11},{4,12},{5,13},{6,14},{7,15},{8,0},{9,1},... | collective-permute-start | bytes 294920 | tf_op jit(solution)/shard_map/ppermute | solution.py:460
  18.0 0.5 collective-permute-start.5
  18.6 2.4 %collective-permute-done.3 = f32[24,1024]{1,0:T(8,128)S(1)} collective-permute-done((f32[24,1024]{1,0:T(8,128)S(1)}, f32[24,1024]{1,0:T(8,128)S(1)}, u32[]{:S(2)}, u32[]{:S(2)}) %collective-permute-start.3) | collective-permute-done | bytes 98336 | tf_op jit(solution)/shard_map/ppermute | solution.py:460
  21.0 0.3 collective-permute-start.4
  21.4 2.4 %scatter_own.2.refs_1_ = f32[128,1024]{1,0:T(8,128)S(1)} custom-call(f32[24,1024]{1,0:T(8,128)S(1)} %add.51.refs_0_.message.refs_2_), custom_call_target="tpu_custom_call" | custom-call | tf_op jit(solution)/shard_map/scatter_own/pallas_call | solution.py:255
  23.8 5.9 %collective-permute-done.4.refs_0_ = f32[24,1024]{1,0:T(8,128)S(1)} collective-permute-done((f32[24,1024]{1,0:T(8,128)S(1)}, f32[24,1024]{1,0:T(8,128)S(1)}, u32[]{:S(2)}, u32[]{:S(2)}) %collective-permute-start.4) | collective-permute-done | bytes 98336 | tf_op jit(solution)/shard_map/ppermute | solution.py:508
  29.7 1.3 %scatter_near.2 = f32[64,1024]{1,0:T(8,128)S(1)} custom-call(f32[24,1024]{1,0:T(8,128)S(1)} %collective-permute-done.4.refs_0_), custom_call_target="tpu_custom_call" | custom-call | tf_op jit(solution)/shard_map/scatter_near/pallas_call | solution.py:255
  31.0 1.8 %filter_send.3.refs_6_ = f32[64,1024]{1,0:T(8,128)S(1)} custom-call(bf16[8,128,1024]{2,1,0:T(8,128)(2,1)S(1)} %bitcast.13, f32[128,1024]{1,0:T(8,128)S(1)} %scatter_own.2.refs_1_, f32[1,64,1024]{2,1,0:T(8,128)S(1)} %bitcast.29, f32[128,1024]{1,0:T(8,128)S(1)} %bitcast.19, bf16[800,256]{1,0:T(8,128)(2,1)S(1)} %copy-done.1, bf16[1,6,64,1024]{3,2,1,0:T(8,128)(2,1)S(1)} %bitcast.25), custom_call_target="tpu_custom_call" | custom-call | tf_op jit(solution)/shard_map/filter_send/pallas_call | solution.py:342
  32.9 1.0 filter_send.4
  33.9 0.1 collective-permute-start.7
  34.0 0.1 compare_reduce_fusion.3
  34.0 1.8 %filter_keep.3.refs_6_ = f32[64,1024]{1,0:T(8,128)S(1)} custom-call(bf16[8,128,1024]{2,1,0:T(8,128)(2,1)S(1)} %bitcast.15, f32[128,1024]{1,0:T(8,128)S(1)} %scatter_own.2.refs_1_, f32[1,64,1024]{2,1,0:T(8,128)S(1)} %bitcast.31, f32[128,1024]{1,0:T(8,128)S(1)} %bitcast.21, bf16[800,256]{1,0:T(8,128)(2,1)S(1)} %copy-done.1, bf16[1,6,64,1024]{3,2,1,0:T(8,128)(2,1)S(1)} %bitcast.26), custom_call_target="tpu_custom_call" | custom-call | tf_op jit(solution)/shard_map/filter_keep/pallas_call | solution.py:342
  35.8 1.0 filter_keep.4
  36.9 1.8 %collective-permute-start.8 = (f32[32,1024]{1,0:T(8,128)S(1)}, f32[32,1024]{1,0:T(8,128)S(1)}, u32[]{:S(2)}, u32[]{:S(2)}) collective-permute-start(f32[32,1024]{1,0:T(8,128)S(1)} %slice_select_fusion.1), channel_id=1, source_target_pairs={{0,2},{1,3},{2,0},{3,1},{4,6},{5,7},{6,4},{7,5},{8,10},{9,11},{10,... | collective-permute-start | bytes 393224 | tf_op jit(solution)/shard_map/ppermute | solution.py:460
  38.7 2.6 %gather_places.2 = f32[8,1024]{1,0:T(8,128)S(1)} custom-call(f32[64,1024]{1,0:T(8,128)S(1)} %add.52.field_ref, f32[24,1024]{1,0:T(8,128)S(1)} %add.51.refs_0_.message.refs_2_), custom_call_target="tpu_custom_call" | custom-call | tf_op jit(solution)/shard_map/gather_places/pallas_call | solution.py:379
  41.3 0.4 collective-permute-start.9
  41.6 3.6 %collective-permute-done.9 = f32[8,1024]{1,0:T(8,128)S(1)} collective-permute-done((f32[8,1024]{1,0:T(8,128)S(1)}, f32[8,1024]{1,0:T(8,128)S(1)}, u32[]{:S(2)}, u32[]{:S(2)}) %collective-permute-start.9) | collective-permute-done | bytes 32800 | tf_op jit(solution)/shard_map/ppermute | solution.py:460
  45.3 2.6 %collective-permute-start.10 = (f32[16,1024]{1,0:T(8,128)S(1)}, f32[16,1024]{1,0:T(8,128)S(1)}, u32[]{:S(2)}, u32[]{:S(2)}) collective-permute-start(f32[16,1024]{1,0:T(8,128)S(1)} %get-tuple-element.41), channel_id=1, source_target_pairs={{0,8},{1,9},{2,10},{3,11},{4,12},{5,13},{6,14},{7,15},{8,0},{9,1},... | collective-permute-start | bytes 196616 | tf_op jit(solution)/shard_map/ppermute | solution.py:460
  48.0 1.6 %collective-permute-start.11 = (f32[16,1024]{1,0:T(8,128)S(1)}, f32[16,1024]{1,0:T(8,128)S(1)}, u32[]{:S(2)}, u32[]{:S(2)}) collective-permute-start(f32[16,1024]{1,0:T(8,128)S(1)} %get-tuple-element.42), channel_id=1, source_target_pairs={{0,4},{1,5},{2,6},{3,7},{4,0},{5,1},{6,2},{7,3},{8,12},{9,13},{10,... | collective-permute-start | bytes 196616 | tf_op jit(solution)/shard_map/ppermute | solution.py:460
  49.6 0.2 collective-permute-start.12
  49.8 0.9 collective-permute-done.10
  50.7 1.6 %collective-permute-done.11 = f32[16,1024]{1,0:T(8,128)S(1)} collective-permute-done((f32[16,1024]{1,0:T(8,128)S(1)}, f32[16,1024]{1,0:T(8,128)S(1)}, u32[]{:S(2)}, u32[]{:S(2)}) %collective-permute-start.11) | collective-permute-done | bytes 65568 | tf_op jit(solution)/shard_map/ppermute | solution.py:460
  52.2 3.4 %collective-permute-done.12 = f32[16,1024]{1,0:T(8,128)S(1)} collective-permute-done((f32[16,1024]{1,0:T(8,128)S(1)}, f32[16,1024]{1,0:T(8,128)S(1)}, u32[]{:S(2)}, u32[]{:S(2)}) %collective-permute-start.12) | collective-permute-done | bytes 65568 | tf_op jit(solution)/shard_map/ppermute | solution.py:460
  55.7 0.1 collective-permute-start.13
  55.7 1.2 %collective-permute-done.13.refs_1_ = f32[8,1024]{1,0:T(8,128)S(1)} collective-permute-done((f32[8,1024]{1,0:T(8,128)S(1)}, f32[8,1024]{1,0:T(8,128)S(1)}, u32[]{:S(2)}, u32[]{:S(2)}) %collective-permute-start.13) | collective-permute-done | bytes 32800 | tf_op jit(solution)/shard_map/ppermute | solution.py:460
  56.9 0.1 sums.2.refs_1_.refs_2_.refs_3_.refs_4_
  57.0 1.6 %collective-permute-start.14 = (f32[8,1024]{1,0:T(8,128)S(1)}, f32[8,1024]{1,0:T(8,128)S(1)}, u32[]{:S(2)}, u32[]{:S(2)}) collective-permute-start(f32[8,1024]{1,0:T(8,128)S(1)} %sums.2.refs_1_.refs_2_.refs_3_.refs_4_), channel_id=1, source_target_pairs={{0,16},{16,0},{1,17},{17,1},{2,18},{18,2},{3,19},{19,3},{4,20},{20... | collective-permute-start | bytes 98312 | tf_op jit(solution)/shard_map/ppermute | solution.py:508
  58.6 2.4 %collective-permute-done.14.refs_3_.refs_1_.refs_5_.refs_2_ = f32[8,1024]{1,0:T(8,128)S(1)} collective-permute-done((f32[8,1024]{1,0:T(8,128)S(1)}, f32[8,1024]{1,0:T(8,128)S(1)}, u32[]{:S(2)}, u32[]{:S(2)}) %collective-permute-start.14) | collective-permute-done | bytes 32800 | tf_op jit(solution)/shard_map/ppermute | solution.py:508
  61.0 1.6 %scatter_near.3 = f32[64,1024]{1,0:T(8,128)S(1)} custom-call(f32[24,1024]{1,0:T(8,128)S(1)} %collective-permute-done.4.refs_0_, f32[8,1024]{1,0:T(8,128)S(1)} %collective-permute-done.14.refs_3_.refs_1_.refs_5_.refs_2_, f32[8,1024]{1,0:T(8,128)S(1)} %sums.2.refs_1_.refs_2_.refs_3_.refs_4_, f32[8,1024]{1,0:T(8,128)S(1)} %collective-permute-done.14.refs_3_.refs_1_.refs_5_.refs_2_), custom_call_target="tpu_custom_call" | custom-call | tf_op jit(solution)/shard_map/scatter_near/pallas_call | solution.py:255
  62.6 2.5 %scatter_own.3.refs_1_ = f32[128,1024]{1,0:T(8,128)S(1)} custom-call(f32[24,1024]{1,0:T(8,128)S(1)} %add.51.refs_0_.message.refs_2_, f32[8,1024]{1,0:T(8,128)S(1)} %sums.2.refs_1_.refs_2_.refs_3_.refs_4_, f32[8,1024]{1,0:T(8,128)S(1)} %sums.2.refs_1_.refs_2_.refs_3_.refs_4_, f32[8,1024]{1,0:T(8,128)S(1)} %collective-permute-done.14.refs_3_.refs_1_.refs_5_.refs_2_), custom_call_target="tpu_custom_call" | custom-call | tf_op jit(solution)/shard_map/scatter_own/pallas_call | solution.py:255
  65.0 2.4 %filter_send.5 = f32[64,1024]{1,0:T(8,128)S(1)} custom-call(bf16[8,128,1024]{2,1,0:T(8,128)(2,1)S(1)} %bitcast.17, f32[128,1024]{1,0:T(8,128)S(1)} %scatter_own.3.refs_1_, f32[1,64,1024]{2,1,0:T(8,128)S(1)} %bitcast.37, f32[128,1024]{1,0:T(8,128)S(1)} %bitcast.23, bf16[800,256]{1,0:T(8,128)(2,1)S(1)} %copy-done.1, bf16[1,6,64,1024]{3,2,1,0:T(8,128)(2,1)S(1)} %bitcast.27, ...), custom_call_target="tpu_custom_call" | custom-call | tf_op jit(solution)/shard_map/filter_send/pallas_call | solution.py:342
  67.4 0.1 collective-permute-start.15
  67.5 2.4 %filter_keep.5 = f32[64,1024]{1,0:T(8,128)S(1)} custom-call(bf16[8,128,1024]{2,1,0:T(8,128)(2,1)S(1)} %bitcast.18, f32[128,1024]{1,0:T(8,128)S(1)} %scatter_own.3.refs_1_, f32[1,64,1024]{2,1,0:T(8,128)S(1)} %bitcast.38, f32[128,1024]{1,0:T(8,128)S(1)} %bitcast.24, bf16[800,256]{1,0:T(8,128)(2,1)S(1)} %copy-done.1, bf16[1,6,64,1024]{3,2,1,0:T(8,128)(2,1)S(1)} %bitcast.28, ...), custom_call_target="tpu_custom_call" | custom-call | tf_op jit(solution)/shard_map/filter_keep/pallas_call | solution.py:342
  70.0 0.6 collective-permute-start.16
  70.6 1.4 %gather_places.3 = f32[4,1024]{1,0:T(4,128)S(1)} custom-call(f32[64,1024]{1,0:T(8,128)S(1)} %add.58.field_ref, f32[24,1024]{1,0:T(8,128)S(1)} %add.51.refs_0_.message.refs_2_), custom_call_target="tpu_custom_call" | custom-call | tf_op jit(solution)/shard_map/gather_places/pallas_call | solution.py:379
  71.9 1.6 %collective-permute-start.17 = (f32[4,1024]{1,0:T(4,128)S(1)}, f32[4,1024]{1,0:T(4,128)S(1)}, u32[]{:S(2)}, u32[]{:S(2)}) collective-permute-start(f32[4,1024]{1,0:T(4,128)S(1)} %gather_places.3), channel_id=1, source_target_pairs={{0,2},{1,3},{2,0},{3,1},{4,6},{5,7},{6,4},{7,5},{8,10},{9,11},{10,... | collective-permute-start | bytes 49160 | tf_op jit(solution)/shard_map/ppermute | solution.py:460
  73.5 2.8 %collective-permute-done.17 = f32[4,1024]{1,0:T(4,128)S(1)} collective-permute-done((f32[4,1024]{1,0:T(4,128)S(1)}, f32[4,1024]{1,0:T(4,128)S(1)}, u32[]{:S(2)}, u32[]{:S(2)}) %collective-permute-start.17) | collective-permute-done | bytes 16416 | tf_op jit(solution)/shard_map/ppermute | solution.py:460
  76.4 0.6 collective-permute-start.18
  77.0 0.8 collective-permute-start.19
  77.8 3.0 %collective-permute-start.20 = (f32[12,1024]{1,0:T(8,128)S(1)}, f32[12,1024]{1,0:T(8,128)S(1)}, u32[]{:S(2)}, u32[]{:S(2)}) collective-permute-start(f32[12,1024]{1,0:T(8,128)S(1)} %get-tuple-element.46), channel_id=1, source_target_pairs={{0,12},{1,13},{2,14},{3,15},{4,8},{5,9},{6,10},{7,11},{8,4},{9,5},... | collective-permute-start | bytes 147464 | tf_op jit(solution)/shard_map/ppermute | solution.py:460
  80.8 1.8 %collective-permute-done.18 = f32[12,1024]{1,0:T(8,128)S(1)} collective-permute-done((f32[12,1024]{1,0:T(8,128)S(1)}, f32[12,1024]{1,0:T(8,128)S(1)}, u32[]{:S(2)}, u32[]{:S(2)}) %collective-permute-start.18) | collective-permute-done | bytes 49184 | tf_op jit(solution)/shard_map/ppermute | solution.py:460
  82.7 1.3 %collective-permute-done.20 = f32[12,1024]{1,0:T(8,128)S(1)} collective-permute-done((f32[12,1024]{1,0:T(8,128)S(1)}, f32[12,1024]{1,0:T(8,128)S(1)}, u32[]{:S(2)}, u32[]{:S(2)}) %collective-permute-start.20) | collective-permute-done | bytes 49184 | tf_op jit(solution)/shard_map/ppermute | solution.py:460
  84.0 0.5 collective-permute-start.23
  84.5 3.1 %collective-permute-start.22 = (f32[2,8,1024]{2,1,0:T(8,128)S(1)}, f32[2,8,1024]{2,1,0:T(8,128)S(1)}, u32[]{:S(2)}, u32[]{:S(2)}) collective-permute-start(f32[2,8,1024]{2,1,0:T(8,128)S(1)} %pad_maximum_fusion.13), channel_id=1, source_target_pairs={{0,4},{1,5},{2,6},{3,7},{4,0},{5,1},{6,2},{7,3},{8,12},{9,13},{10,... | collective-permute-start | bytes 196616 | tf_op jit(solution)/shard_map/ppermute | solution.py:460
  87.6 0.9 collective-permute-start.21
  88.5 1.2 %collective-permute-done.24.refs_1_ = f32[4,1024]{1,0:T(4,128)S(1)} collective-permute-done((f32[4,1024]{1,0:T(4,128)S(1)}, f32[4,1024]{1,0:T(4,128)S(1)}, u32[]{:S(2)}, u32[]{:S(2)}) %collective-permute-start.24) | collective-permute-done | bytes 16416 | tf_op jit(solution)/shard_map/ppermute | solution.py:460
  89.7 0.2 sums.3.refs_3_
  89.9 1.6 %collective-permute-start.25 = (f32[8,128]{1,0:T(8,128)S(1)}, f32[8,128]{1,0:T(8,128)S(1)}, u32[]{:S(2)}, u32[]{:S(2)}) collective-permute-start(f32[8,128]{1,0:T(8,128)S(1)} %sums.3.refs_3_), channel_id=1, source_target_pairs={{0,16},{16,0},{1,17},{17,1},{2,18},{18,2},{3,19},{19,3},{4,20},{20... | collective-permute-start | bytes 12296 | tf_op jit(solution)/shard_map/ppermute | solution.py:508
  91.4 2.2 %collective-permute-done.21 = f32[2,8,1024]{2,1,0:T(8,128)S(1)} collective-permute-done((f32[2,8,1024]{2,1,0:T(8,128)S(1)}, f32[2,8,1024]{2,1,0:T(8,128)S(1)}, u32[]{:S(2)}, u32[]{:S(2)}) %collective-permute-start.21) | collective-permute-done | bytes 65568 | tf_op jit(solution)/shard_map/ppermute | solution.py:460
  93.7 0.1 combine.1
  93.8 1.0 %collective-permute-start.26 = (bf16[32,1024]{1,0:T(8,128)(2,1)S(1)}, bf16[32,1024]{1,0:T(8,128)(2,1)S(1)}, u32[]{:S(2)}, u32[]{:S(2)}) collective-permute-start(bf16[32,1024]{1,0:T(8,128)(2,1)S(1)} %combine.1), channel_id=1, source_target_pairs={{0,2},{1,3},{2,0},{3,1},{4,6},{5,7},{6,4},{7,5},{8,10},{9,11},{10,... | collective-permute-start | bytes 196616 | tf_op jit(solution)/shard_map/ppermute | solution.py:460
  94.9 3.3 %collective-permute-done.26 = bf16[32,1024]{1,0:T(8,128)(2,1)S(1)} collective-permute-done((bf16[32,1024]{1,0:T(8,128)(2,1)S(1)}, bf16[32,1024]{1,0:T(8,128)(2,1)S(1)}, u32[]{:S(2)}, u32[]{:S(2)}) %collective-permute-start.26) | collective-permute-done | bytes 65568 | tf_op jit(solution)/shard_map/ppermute | solution.py:460
  98.2 0.1 collective-permute-start.27
  98.3 1.3 %collective-permute-done.27 = bf16[64,1024]{1,0:T(8,128)(2,1)S(1)} collective-permute-done((bf16[64,1024]{1,0:T(8,128)(2,1)S(1)}, bf16[64,1024]{1,0:T(8,128)(2,1)S(1)}, u32[]{:S(2)}, u32[]{:S(2)}) %collective-permute-start.27) | collective-permute-done | bytes 131104 | tf_op jit(solution)/shard_map/ppermute | solution.py:460
  99.6 0.1 broadcast_select_fusion.1
  99.7 0.8 convert.1
  (49 shorter events, 0.6 us)
Async XLA Ops:
  0.0 21.3 %copy-start.2 = (f32[4,32,1024]{2,1,0:T(8,128)S(1)}, f32[4,32,1024]{2,1,0:T(8,128)}, u32[]{:S(2)}) copy-start(f32[4,32,1024]{2,1,0:T(8,128)} %param.8) | copy-start | bytes 1572868
  1.4 29.7 %copy-start = (bf16[8,4,32,1024]{3,2,1,0:T(8,128)(2,1)S(1)}, bf16[8,4,32,1024]{3,2,1,0:T(8,128)(2,1)}, u32[]{:S(2)}) copy-start(bf16[8,4,32,1024]{3,2,1,0:T(8,128)(2,1)} %ens_hbm.1) | copy-start | bytes 6291460
  1.4 29.7 %copy-start.1 = (bf16[800,256]{1,0:T(8,128)(2,1)S(1)}, bf16[800,256]{1,0:T(8,128)(2,1)}, u32[]{:S(2)}) copy-start(bf16[800,256]{1,0:T(8,128)(2,1)} %constant.4.clone.refs_4_) | copy-start | bytes 1228804
  1.4 29.6 %collective-permute-start.6 = (bf16[6,4,16,1024]{3,2,1,0:T(8,128)(2,1)S(1)}, bf16[6,4,16,1024]{3,2,1,0:T(8,128)(2,1)S(1)}, u32[]{:S(2)}, u32[]{:S(2)}) collective-permute-start(bf16[6,4,16,1024]{3,2,1,0:T(8,128)(2,1)S(1)} %get-tuple-element.12), channel_id=1, source_target_pairs={{0,16},{16,0},{1,17},{17,1},{2,18},{18,2},{3,19},{19,3},{4,20},{20... | collective-permute-start | bytes 2359304 | tf_op jit(solution)/shard_map/ppermute | solution.py:516
  4.4 1.3 %collective-permute-start = (f32[24,1024]{1,0:T(8,128)S(1)}, f32[24,1024]{1,0:T(8,128)S(1)}, u32[]{:S(2)}, u32[]{:S(2)}) collective-permute-start(f32[24,1024]{1,0:T(8,128)S(1)} %get-tuple-element.10), channel_id=1, source_target_pairs={{0,1},{1,0},{2,3},{3,2},{4,5},{5,4},{6,7},{7,6},{8,9},{9,8},{10,11... | collective-permute-start | bytes 294920 | tf_op jit(solution)/shard_map/ppermute | solution.py:460
  5.8 4.9 %collective-permute-start.1 = (f32[24,1024]{1,0:T(8,128)S(1)}, f32[24,1024]{1,0:T(8,128)S(1)}, u32[]{:S(2)}, u32[]{:S(2)}) collective-permute-start(f32[24,1024]{1,0:T(8,128)S(1)} %add.48), channel_id=1, source_target_pairs={{0,2},{1,3},{2,0},{3,1},{4,6},{5,7},{6,4},{7,5},{8,10},{9,11},{10,... | collective-permute-start | bytes 294920 | tf_op jit(solution)/shard_map/ppermute | solution.py:460
  10.7 4.7 %collective-permute-start.2 = (f32[24,1024]{1,0:T(8,128)S(1)}, f32[24,1024]{1,0:T(8,128)S(1)}, u32[]{:S(2)}, u32[]{:S(2)}) collective-permute-start(f32[24,1024]{1,0:T(8,128)S(1)} %add.49), channel_id=1, source_target_pairs={{0,4},{1,5},{2,6},{3,7},{4,0},{5,1},{6,2},{7,3},{8,12},{9,13},{10,... | collective-permute-start | bytes 294920 | tf_op jit(solution)/shard_map/ppermute | solution.py:460
  15.4 5.6 %collective-permute-start.3 = (f32[24,1024]{1,0:T(8,128)S(1)}, f32[24,1024]{1,0:T(8,128)S(1)}, u32[]{:S(2)}, u32[]{:S(2)}) collective-permute-start(f32[24,1024]{1,0:T(8,128)S(1)} %add.50), channel_id=1, source_target_pairs={{0,8},{1,9},{2,10},{3,11},{4,12},{5,13},{6,14},{7,15},{8,0},{9,1},... | collective-permute-start | bytes 294920 | tf_op jit(solution)/shard_map/ppermute | solution.py:460
  18.0 14.8 %collective-permute-start.5 = (bf16[2,4,16,1024]{3,2,1,0:T(8,128)(2,1)S(1)}, bf16[2,4,16,1024]{3,2,1,0:T(8,128)(2,1)S(1)}, u32[]{:S(2)}, u32[]{:S(2)}) collective-permute-start(bf16[2,4,16,1024]{3,2,1,0:T(8,128)(2,1)S(1)} %get-tuple-element.11), channel_id=1, source_target_pairs={{0,16},{16,0},{1,17},{17,1},{2,18},{18,2},{3,19},{19,3},{4,20},{20... | collective-permute-start | bytes 786440 | tf_op jit(solution)/shard_map/ppermute | solution.py:516
  21.0 8.7 %collective-permute-start.4 = (f32[24,1024]{1,0:T(8,128)S(1)}, f32[24,1024]{1,0:T(8,128)S(1)}, u32[]{:S(2)}, u32[]{:S(2)}) collective-permute-start(f32[24,1024]{1,0:T(8,128)S(1)} %add.51.refs_0_.message.refs_2_), channel_id=1, source_target_pairs={{0,16},{16,0},{1,17},{17,1},{2,18},{18,2},{3,19},{19,3},{4,20},{20... | collective-permute-start | bytes 294920 | tf_op jit(solution)/shard_map/ppermute | solution.py:508
  33.9 3.0 %collective-permute-start.7 = (f32[64,1024]{1,0:T(8,128)S(1)}, f32[64,1024]{1,0:T(8,128)S(1)}, u32[]{:S(2)}, u32[]{:S(2)}) collective-permute-start(f32[64,1024]{1,0:T(8,128)S(1)} %filter_send.4), channel_id=1, source_target_pairs={{0,1},{1,0},{2,3},{3,2},{4,5},{5,4},{6,7},{7,6},{8,9},{9,8},{10,11... | collective-permute-start | bytes 786440 | tf_op jit(solution)/shard_map/ppermute | solution.py:460
  36.9 8.3 %collective-permute-start.8 = (f32[32,1024]{1,0:T(8,128)S(1)}, f32[32,1024]{1,0:T(8,128)S(1)}, u32[]{:S(2)}, u32[]{:S(2)}) collective-permute-start(f32[32,1024]{1,0:T(8,128)S(1)} %slice_select_fusion.1), channel_id=1, source_target_pairs={{0,2},{1,3},{2,0},{3,1},{4,6},{5,7},{6,4},{7,5},{8,10},{9,11},{10,... | collective-permute-start | bytes 393224 | tf_op jit(solution)/shard_map/ppermute | solution.py:460
  41.3 4.0 %collective-permute-start.9 = (f32[8,1024]{1,0:T(8,128)S(1)}, f32[8,1024]{1,0:T(8,128)S(1)}, u32[]{:S(2)}, u32[]{:S(2)}) collective-permute-start(f32[8,1024]{1,0:T(8,128)S(1)} %gather_places.2), channel_id=1, source_target_pairs={{0,2},{1,3},{2,0},{3,1},{4,6},{5,7},{6,4},{7,5},{8,10},{9,11},{10,... | collective-permute-start | bytes 98312 | tf_op jit(solution)/shard_map/ppermute | solution.py:460
  45.3 5.3 %collective-permute-start.10 = (f32[16,1024]{1,0:T(8,128)S(1)}, f32[16,1024]{1,0:T(8,128)S(1)}, u32[]{:S(2)}, u32[]{:S(2)}) collective-permute-start(f32[16,1024]{1,0:T(8,128)S(1)} %get-tuple-element.41), channel_id=1, source_target_pairs={{0,8},{1,9},{2,10},{3,11},{4,12},{5,13},{6,14},{7,15},{8,0},{9,1},... | collective-permute-start | bytes 196616 | tf_op jit(solution)/shard_map/ppermute | solution.py:460
  48.0 4.3 %collective-permute-start.11 = (f32[16,1024]{1,0:T(8,128)S(1)}, f32[16,1024]{1,0:T(8,128)S(1)}, u32[]{:S(2)}, u32[]{:S(2)}) collective-permute-start(f32[16,1024]{1,0:T(8,128)S(1)} %get-tuple-element.42), channel_id=1, source_target_pairs={{0,4},{1,5},{2,6},{3,7},{4,0},{5,1},{6,2},{7,3},{8,12},{9,13},{10,... | collective-permute-start | bytes 196616 | tf_op jit(solution)/shard_map/ppermute | solution.py:460
  49.6 6.1 %collective-permute-start.12 = (f32[16,1024]{1,0:T(8,128)S(1)}, f32[16,1024]{1,0:T(8,128)S(1)}, u32[]{:S(2)}, u32[]{:S(2)}) collective-permute-start(f32[16,1024]{1,0:T(8,128)S(1)} %get-tuple-element.43), channel_id=1, source_target_pairs={{0,12},{1,13},{2,14},{3,15},{4,8},{5,9},{6,10},{7,11},{8,4},{9,5},... | collective-permute-start | bytes 196616 | tf_op jit(solution)/shard_map/ppermute | solution.py:460
  55.7 1.3 %collective-permute-start.13 = (f32[8,1024]{1,0:T(8,128)S(1)}, f32[8,1024]{1,0:T(8,128)S(1)}, u32[]{:S(2)}, u32[]{:S(2)}) collective-permute-start(f32[8,1024]{1,0:T(8,128)S(1)} %get-tuple-element.40.refs_0_), channel_id=1, source_target_pairs={{0,1},{1,0},{2,3},{3,2},{4,5},{5,4},{6,7},{7,6},{8,9},{9,8},{10,11... | collective-permute-start | bytes 98312 | tf_op jit(solution)/shard_map/ppermute | solution.py:460
  57.0 3.9 %collective-permute-start.14 = (f32[8,1024]{1,0:T(8,128)S(1)}, f32[8,1024]{1,0:T(8,128)S(1)}, u32[]{:S(2)}, u32[]{:S(2)}) collective-permute-start(f32[8,1024]{1,0:T(8,128)S(1)} %sums.2.refs_1_.refs_2_.refs_3_.refs_4_), channel_id=1, source_target_pairs={{0,16},{16,0},{1,17},{17,1},{2,18},{18,2},{3,19},{19,3},{4,20},{20... | collective-permute-start | bytes 98312 | tf_op jit(solution)/shard_map/ppermute | solution.py:508
  67.4 2.5 %collective-permute-start.15 = (f32[64,1024]{1,0:T(8,128)S(1)}, f32[64,1024]{1,0:T(8,128)S(1)}, u32[]{:S(2)}, u32[]{:S(2)}) collective-permute-start(f32[64,1024]{1,0:T(8,128)S(1)} %filter_send.5), channel_id=1, source_target_pairs={{0,1},{1,0},{2,3},{3,2},{4,5},{5,4},{6,7},{7,6},{8,9},{9,8},{10,11... | collective-permute-start | bytes 786440 | tf_op jit(solution)/shard_map/ppermute | solution.py:460
  70.0 6.3 %collective-permute-start.16 = (f32[32,1024]{1,0:T(8,128)S(1)}, f32[32,1024]{1,0:T(8,128)S(1)}, u32[]{:S(2)}, u32[]{:S(2)}) collective-permute-start(f32[32,1024]{1,0:T(8,128)S(1)} %slice_select_fusion), channel_id=1, source_target_pairs={{0,2},{1,3},{2,0},{3,1},{4,6},{5,7},{6,4},{7,5},{8,10},{9,11},{10,... | collective-permute-start | bytes 393224 | tf_op jit(solution)/shard_map/ppermute | solution.py:460
  71.9 4.3 %collective-permute-start.17 = (f32[4,1024]{1,0:T(4,128)S(1)}, f32[4,1024]{1,0:T(4,128)S(1)}, u32[]{:S(2)}, u32[]{:S(2)}) collective-permute-start(f32[4,1024]{1,0:T(4,128)S(1)} %gather_places.3), channel_id=1, source_target_pairs={{0,2},{1,3},{2,0},{3,1},{4,6},{5,7},{6,4},{7,5},{8,10},{9,11},{10,... | collective-permute-start | bytes 49160 | tf_op jit(solution)/shard_map/ppermute | solution.py:460
  76.4 6.3 %collective-permute-start.18 = (f32[12,1024]{1,0:T(8,128)S(1)}, f32[12,1024]{1,0:T(8,128)S(1)}, u32[]{:S(2)}, u32[]{:S(2)}) collective-permute-start(f32[12,1024]{1,0:T(8,128)S(1)} %get-tuple-element.44), channel_id=1, source_target_pairs={{0,8},{1,9},{2,10},{3,11},{4,12},{5,13},{6,14},{7,15},{8,0},{9,1},... | collective-permute-start | bytes 147464 | tf_op jit(solution)/shard_map/ppermute | solution.py:460
  77.0 5.7 %collective-permute-start.19 = (f32[12,1024]{1,0:T(8,128)S(1)}, f32[12,1024]{1,0:T(8,128)S(1)}, u32[]{:S(2)}, u32[]{:S(2)}) collective-permute-start(f32[12,1024]{1,0:T(8,128)S(1)} %get-tuple-element.45), channel_id=1, source_target_pairs={{0,4},{1,5},{2,6},{3,7},{4,0},{5,1},{6,2},{7,3},{8,12},{9,13},{10,... | collective-permute-start | bytes 147464 | tf_op jit(solution)/shard_map/ppermute | solution.py:460
  77.8 6.2 %collective-permute-start.20 = (f32[12,1024]{1,0:T(8,128)S(1)}, f32[12,1024]{1,0:T(8,128)S(1)}, u32[]{:S(2)}, u32[]{:S(2)}) collective-permute-start(f32[12,1024]{1,0:T(8,128)S(1)} %get-tuple-element.46), channel_id=1, source_target_pairs={{0,12},{1,13},{2,14},{3,15},{4,8},{5,9},{6,10},{7,11},{8,4},{9,5},... | collective-permute-start | bytes 147464 | tf_op jit(solution)/shard_map/ppermute | solution.py:460
  84.0 7.4 %collective-permute-start.23 = (f32[2,8,1024]{2,1,0:T(8,128)S(1)}, f32[2,8,1024]{2,1,0:T(8,128)S(1)}, u32[]{:S(2)}, u32[]{:S(2)}) collective-permute-start(f32[2,8,1024]{2,1,0:T(8,128)S(1)} %pad_maximum_fusion.13), channel_id=1, source_target_pairs={{0,8},{1,9},{2,10},{3,11},{4,12},{5,13},{6,14},{7,15},{8,0},{9,1},... | collective-permute-start | bytes 196616 | tf_op jit(solution)/shard_map/ppermute | solution.py:460
  84.5 6.9 %collective-permute-start.22 = (f32[2,8,1024]{2,1,0:T(8,128)S(1)}, f32[2,8,1024]{2,1,0:T(8,128)S(1)}, u32[]{:S(2)}, u32[]{:S(2)}) collective-permute-start(f32[2,8,1024]{2,1,0:T(8,128)S(1)} %pad_maximum_fusion.13), channel_id=1, source_target_pairs={{0,4},{1,5},{2,6},{3,7},{4,0},{5,1},{6,2},{7,3},{8,12},{9,13},{10,... | collective-permute-start | bytes 196616 | tf_op jit(solution)/shard_map/ppermute | solution.py:460
  87.6 6.1 %collective-permute-start.21 = (f32[2,8,1024]{2,1,0:T(8,128)S(1)}, f32[2,8,1024]{2,1,0:T(8,128)S(1)}, u32[]{:S(2)}, u32[]{:S(2)}) collective-permute-start(f32[2,8,1024]{2,1,0:T(8,128)S(1)} %pad_maximum_fusion.13), channel_id=1, source_target_pairs={{0,12},{1,13},{2,14},{3,15},{4,8},{5,9},{6,10},{7,11},{8,4},{9,5},... | collective-permute-start | bytes 196616 | tf_op jit(solution)/shard_map/ppermute | solution.py:460
  88.5 1.2 %collective-permute-start.24 = (f32[4,1024]{1,0:T(4,128)S(1)}, f32[4,1024]{1,0:T(4,128)S(1)}, u32[]{:S(2)}, u32[]{:S(2)}) collective-permute-start(f32[4,1024]{1,0:T(4,128)S(1)} %slice.135.refs_0_), channel_id=1, source_target_pairs={{0,1},{1,0},{2,3},{3,2},{4,5},{5,4},{6,7},{7,6},{8,9},{9,8},{10,11... | collective-permute-start | bytes 49160 | tf_op jit(solution)/shard_map/ppermute | solution.py:460
  89.9 3.9 %collective-permute-start.25 = (f32[8,128]{1,0:T(8,128)S(1)}, f32[8,128]{1,0:T(8,128)S(1)}, u32[]{:S(2)}, u32[]{:S(2)}) collective-permute-start(f32[8,128]{1,0:T(8,128)S(1)} %sums.3.refs_3_), channel_id=1, source_target_pairs={{0,16},{16,0},{1,17},{17,1},{2,18},{18,2},{3,19},{19,3},{4,20},{20... | collective-permute-start | bytes 12296 | tf_op jit(solution)/shard_map/ppermute | solution.py:508
  93.8 4.3 %collective-permute-start.26 = (bf16[32,1024]{1,0:T(8,128)(2,1)S(1)}, bf16[32,1024]{1,0:T(8,128)(2,1)S(1)}, u32[]{:S(2)}, u32[]{:S(2)}) collective-permute-start(bf16[32,1024]{1,0:T(8,128)(2,1)S(1)} %combine.1), channel_id=1, source_target_pairs={{0,2},{1,3},{2,0},{3,1},{4,6},{5,7},{6,4},{7,5},{8,10},{9,11},{10,... | collective-permute-start | bytes 196616 | tf_op jit(solution)/shard_map/ppermute | solution.py:460
  98.2 1.4 %collective-permute-start.27 = (bf16[64,1024]{1,0:T(8,128)(2,1)S(1)}, bf16[64,1024]{1,0:T(8,128)(2,1)S(1)}, u32[]{:S(2)}, u32[]{:S(2)}) collective-permute-start(bf16[64,1024]{1,0:T(8,128)(2,1)S(1)} %pad_maximum_fusion.4), channel_id=1, source_target_pairs={{0,1},{1,0},{2,3},{3,2},{4,5},{5,4},{6,7},{7,6},{8,9},{9,8},{10,11... | collective-permute-start | bytes 393224 | tf_op jit(solution)/shard_map/ppermute | solution.py:460

commit v7 on v6

--- a/solution.py
+++ b/solution.py
@@ -538,9 +538,14 @@
     )
     sides = 1 if n_band == 2 else 2
     halo = band_halo(edges[:sides], n_band)
-    message = message + swap(message, bits[0], n_member)
-    for bit in bits[1:]:
+    keep, send = halves(message, flags[:1] > 0)
+    message = keep + swap(send, bits[0], n_member)
+    message = message + swap(message, bits[1], n_member)
+    square = (bits[2], bits[3], bits[2] | bits[3])
+    message = message + sum(swap(message, bit, n_member) for bit in square)
+    for bit in bits[4:]:
         message = message + swap(message, bit, n_member)
+    message = gather_rows(message, bits[0], n_member, flags[:1] > 0)
     around = from_bands(message, n_band)
 
     own = ensemble.reshape(members_here, levels * lat_rows, lon)
@@ -566,6 +571,7 @@
             early = [filters(kept, 0, None, own, ext, *parts) for kept in (False, True)]
             first = ext[0].shape[1]
             late = band_halo(rest, n_band)
+            late, early = lax.optimization_barrier((late, early))
             ext.append(near_rows(late))
             send = filters(False, first, early[0], own, ext[1:], *parts)
             got = swap(send, bits[0], n_member)

time: 101 us -> 110 us (1.089)
  waiting for transfers between devices: 43 us -> 49.1 us
  starting transfers between devices: 31.8 us -> 34.7 us
    ppermute x3, waiting for transfers between devices: 8.31 us -> 17.9 us  [from_bands(): return [lax.ppermute(x, 'band', [(0, 1), (1, 0)])]]
    ppermute x23 -> x25, waiting for transfers between devices: 34.7 us -> 31.1 us  [swap(): return lax.ppermute(x, 'member', partner(count, bit))]
    ppermute x23 -> x25, starting transfers between devices: 24.8 us -> 27.2 us  [swap(): return lax.ppermute(x, 'member', partner(count, bit))]
  transfers between devices with their start and end apart: 28 -> 30, of which waited for: 18 -> 19; matrix products, arithmetic and copies ran while one was open for 0% -> 0% of each run, Pallas kernels for 15% -> 14%
where the time goes in v7:
time: 110 us
  waiting for transfers between devices  49.1 us (45%)
  starting transfers between devices  34.7 us (32%)
  Pallas kernels  23.8 us (22%)
  other arithmetic  1.48 us (1%)
    ppermute x25, waiting for transfers between devices, swap(): return lax.ppermute(x, 'member', partner(count, bit))  31.1 us
    ppermute x25, starting transfers between devices, swap(): return lax.ppermute(x, 'member', partner(count, bit))  27.2 us
    ppermute x3, waiting for transfers between devices, from_bands(): return [lax.ppermute(x, 'band', [(0, 1), (1, 0)])]  17.9 us
    pallas_call x6, Pallas kernels, filter_members(): pl.pallas_call(kernel, out_shape=jax.ShapeDtypeStruct((rows // 2, lon), F...  10.4 us
    pallas_call x4, Pallas kernels, scatter_obs(): pl.pallas_call(functools.partial(scatter_kernel, second, rows, lon, bands...  7.75 us
    ppermute x3, starting transfers between devices, from_bands(): return [lax.ppermute(x, 'band', [(0, 1), (1, 0)])]  4.3 us
    pallas_call x2, Pallas kernels, gather_places(): pl.pallas_call(functools.partial(gather_kernel, which), out_shape=jax.Sha...  3.92 us
    ppermute x2, starting transfers between devices, band_halo(): return [lax.ppermute(edges[0], 'band', [(0, 1), (1, 0)])]  3.25 us
  transfers between devices with their start and end apart: 30, of which 19 were waited for; matrix products, arithmetic and copies ran while one was open for 0% of the time, Pallas kernels for 14%

profile of v7, /device:TPU:0, one launch (start us, length us, event | category | flops | bytes accessed | tf_op | source)
XLA Modules:
  0.0 109.5 jit_solution(5566061183905067694)
XLA Ops:
  0.0 1.3 %prepare.1 = (f32[24,1024]{1,0:T(8,128)S(1)}, f32[8,1024]{1,0:T(8,128)S(1)}, bf16[6,4,16,1024]{3,2,1,0:T(8,128)(2,1)S(1)}, bf16[2,4,16,1024]{3,2,1,0:T(8,128)(2,1)S(1)}) custom-call(s32[2]{0:T(128)} %root_hbm.1, bf16[8,4,32,1024]{3,2,1,0:T(8,128)(2,1)} %ens_hbm.1, s32[1,4096]{1,0:T(1,128)} %idx_hbm.1, f32[1,4096]{1,0:T(1,128)} %value_hbm.1, f32[1,4096]{1,0:T(1,128)} %error_hbm.1), custom_call_target="tpu_custom_call" | custom-call | tf_op jit(solution)/shard_map/prepare/pallas_call | solution.py:168
  1.5 0.6 collective-permute-start
  2.0 0.9 collective-permute-done
  2.9 2.9 %collective-permute-start.1 = (f32[12,1024]{1,0:T(8,128)S(1)}, f32[12,1024]{1,0:T(8,128)S(1)}, u32[]{:S(2)}, u32[]{:S(2)}) collective-permute-start(f32[12,1024]{1,0:T(8,128)S(1)} %select_add_fusion.2), channel_id=1, source_target_pairs={{0,2},{1,3},{2,0},{3,1},{4,6},{5,7},{6,4},{7,5},{8,10},{9,11},{10,... | collective-permute-start | bytes 147464 | tf_op jit(solution)/shard_map/ppermute | solution.py:460
  5.8 2.4 %collective-permute-done.1 = f32[12,1024]{1,0:T(8,128)S(1)} collective-permute-done((f32[12,1024]{1,0:T(8,128)S(1)}, f32[12,1024]{1,0:T(8,128)S(1)}, u32[]{:S(2)}, u32[]{:S(2)}) %collective-permute-start.1) | collective-permute-done | bytes 49184 | tf_op jit(solution)/shard_map/ppermute | solution.py:460
  8.3 4.0 %collective-permute-start.4 = (f32[12,1024]{1,0:T(8,128)S(1)}, f32[12,1024]{1,0:T(8,128)S(1)}, u32[]{:S(2)}, u32[]{:S(2)}) collective-permute-start(f32[12,1024]{1,0:T(8,128)S(1)} %add.52), channel_id=1, source_target_pairs={{0,12},{1,13},{2,14},{3,15},{4,8},{5,9},{6,10},{7,11},{8,4},{9,5},... | collective-permute-start | bytes 147464 | tf_op jit(solution)/shard_map/ppermute | solution.py:460
  12.3 0.6 collective-permute-start.2
  12.9 1.7 %collective-permute-start.8 = (bf16[6,4,16,1024]{3,2,1,0:T(8,128)(2,1)S(1)}, bf16[6,4,16,1024]{3,2,1,0:T(8,128)(2,1)S(1)}, u32[]{:S(2)}, u32[]{:S(2)}) collective-permute-start(bf16[6,4,16,1024]{3,2,1,0:T(8,128)(2,1)S(1)} %get-tuple-element.15), channel_id=1, source_target_pairs={{0,16},{16,0},{1,17},{17,1},{2,18},{18,2},{3,19},{19,3},{4,20},{20... | collective-permute-start | bytes 2359304 | tf_op jit(solution)/shard_map/ppermute | solution.py:516
  14.6 0.4 collective-permute-done.4
  15.0 2.6 %collective-permute-done.3 = f32[12,1024]{1,0:T(8,128)S(1)} collective-permute-done((f32[12,1024]{1,0:T(8,128)S(1)}, f32[12,1024]{1,0:T(8,128)S(1)}, u32[]{:S(2)}, u32[]{:S(2)}) %collective-permute-start.3) | collective-permute-done | bytes 49184 | tf_op jit(solution)/shard_map/ppermute | solution.py:460
  17.7 0.1 collective-permute-start.5
  17.8 1.6 %collective-permute-start.7 = (bf16[2,4,16,1024]{3,2,1,0:T(8,128)(2,1)S(1)}, bf16[2,4,16,1024]{3,2,1,0:T(8,128)(2,1)S(1)}, u32[]{:S(2)}, u32[]{:S(2)}) collective-permute-start(bf16[2,4,16,1024]{3,2,1,0:T(8,128)(2,1)S(1)} %get-tuple-element.14), channel_id=1, source_target_pairs={{0,16},{16,0},{1,17},{17,1},{2,18},{18,2},{3,19},{19,3},{4,20},{20... | collective-permute-start | bytes 786440 | tf_op jit(solution)/shard_map/ppermute | solution.py:516
  19.4 1.2 %collective-permute-start.6 = (f32[24,1024]{1,0:T(8,128)S(1)}, f32[24,1024]{1,0:T(8,128)S(1)}, u32[]{:S(2)}, u32[]{:S(2)}) collective-permute-start(f32[24,1024]{1,0:T(8,128)S(1)} %pad_maximum_fusion.13.refs_0_.message.refs_2_), channel_id=1, source_target_pairs={{0,16},{16,0},{1,17},{17,1},{2,18},{18,2},{3,19},{19,3},{4,20},{20... | collective-permute-start | bytes 294920 | tf_op jit(solution)/shard_map/ppermute | solution.py:508
  20.7 2.4 %scatter_own.2.refs_1_ = f32[128,1024]{1,0:T(8,128)S(1)} custom-call(f32[24,1024]{1,0:T(8,128)S(1)} %pad_maximum_fusion.13.refs_0_.message.refs_2_), custom_call_target="tpu_custom_call" | custom-call | tf_op jit(solution)/shard_map/scatter_own/pallas_call | solution.py:255
  23.1 15.6 %collective-permute-done.6.refs_0_ = f32[24,1024]{1,0:T(8,128)S(1)} collective-permute-done((f32[24,1024]{1,0:T(8,128)S(1)}, f32[24,1024]{1,0:T(8,128)S(1)}, u32[]{:S(2)}, u32[]{:S(2)}) %collective-permute-start.6) | collective-permute-done | bytes 98336 | tf_op jit(solution)/shard_map/ppermute | solution.py:508
  38.6 1.3 %scatter_near.2 = f32[64,1024]{1,0:T(8,128)S(1)} custom-call(f32[24,1024]{1,0:T(8,128)S(1)} %collective-permute-done.6.refs_0_), custom_call_target="tpu_custom_call" | custom-call | tf_op jit(solution)/shard_map/scatter_near/pallas_call | solution.py:255
  40.0 1.8 %filter_keep.3.refs_6_ = f32[64,1024]{1,0:T(8,128)S(1)} custom-call(bf16[8,128,1024]{2,1,0:T(8,128)(2,1)S(1)} %bitcast.13, f32[128,1024]{1,0:T(8,128)S(1)} %scatter_own.2.refs_1_, f32[1,64,1024]{2,1,0:T(8,128)S(1)} %bitcast.29, f32[128,1024]{1,0:T(8,128)S(1)} %bitcast.19, bf16[800,256]{1,0:T(8,128)(2,1)S(1)} %copy-done.1, bf16[1,6,64,1024]{3,2,1,0:T(8,128)(2,1)S(1)} %bitcast.25), custom_call_target="tpu_custom_call" | custom-call | tf_op jit(solution)/shard_map/filter_keep/pallas_call | solution.py:342
  41.8 1.8 %filter_send.3.refs_6_ = f32[64,1024]{1,0:T(8,128)S(1)} custom-call(bf16[8,128,1024]{2,1,0:T(8,128)(2,1)S(1)} %bitcast.14, f32[128,1024]{1,0:T(8,128)S(1)} %scatter_own.2.refs_1_, f32[1,64,1024]{2,1,0:T(8,128)S(1)} %bitcast.30, f32[128,1024]{1,0:T(8,128)S(1)} %bitcast.20, bf16[800,256]{1,0:T(8,128)(2,1)S(1)} %copy-done.1, bf16[1,6,64,1024]{3,2,1,0:T(8,128)(2,1)S(1)} %bitcast.26), custom_call_target="tpu_custom_call" | custom-call | tf_op jit(solution)/shard_map/filter_send/pallas_call | solution.py:342
  43.6 1.0 filter_send.4
  44.6 0.1 collective-permute-start.9
  44.7 1.0 filter_keep.4
  45.7 0.5 collective-permute-done.9
  46.3 1.5 %collective-permute-start.10 = (f32[32,1024]{1,0:T(8,128)S(1)}, f32[32,1024]{1,0:T(8,128)S(1)}, u32[]{:S(2)}, u32[]{:S(2)}) collective-permute-start(f32[32,1024]{1,0:T(8,128)S(1)} %slice_select_fusion.1), channel_id=1, source_target_pairs={{0,2},{1,3},{2,0},{3,1},{4,6},{5,7},{6,4},{7,5},{8,10},{9,11},{10,... | collective-permute-start | bytes 393224 | tf_op jit(solution)/shard_map/ppermute | solution.py:460
  47.8 2.6 %gather_places.2 = f32[8,1024]{1,0:T(8,128)S(1)} custom-call(f32[64,1024]{1,0:T(8,128)S(1)} %add.56.field_ref, f32[24,1024]{1,0:T(8,128)S(1)} %pad_maximum_fusion.13.refs_0_.message.refs_2_), custom_call_target="tpu_custom_call" | custom-call | tf_op jit(solution)/shard_map/gather_places/pallas_call | solution.py:379
  50.3 0.7 collective-permute-start.11
  51.0 3.3 %collective-permute-done.11 = f32[8,1024]{1,0:T(8,128)S(1)} collective-permute-done((f32[8,1024]{1,0:T(8,128)S(1)}, f32[8,1024]{1,0:T(8,128)S(1)}, u32[]{:S(2)}, u32[]{:S(2)}) %collective-permute-start.11) | collective-permute-done | bytes 32800 | tf_op jit(solution)/shard_map/ppermute | solution.py:460
  54.4 2.3 %collective-permute-start.12 = (f32[16,1024]{1,0:T(8,128)S(1)}, f32[16,1024]{1,0:T(8,128)S(1)}, u32[]{:S(2)}, u32[]{:S(2)}) collective-permute-start(f32[16,1024]{1,0:T(8,128)S(1)} %get-tuple-element.49), channel_id=1, source_target_pairs={{0,8},{1,9},{2,10},{3,11},{4,12},{5,13},{6,14},{7,15},{8,0},{9,1},... | collective-permute-start | bytes 196616 | tf_op jit(solution)/shard_map/ppermute | solution.py:460
  56.8 1.8 %collective-permute-start.13 = (f32[16,1024]{1,0:T(8,128)S(1)}, f32[16,1024]{1,0:T(8,128)S(1)}, u32[]{:S(2)}, u32[]{:S(2)}) collective-permute-start(f32[16,1024]{1,0:T(8,128)S(1)} %get-tuple-element.50), channel_id=1, source_target_pairs={{0,4},{1,5},{2,6},{3,7},{4,0},{5,1},{6,2},{7,3},{8,12},{9,13},{10,... | collective-permute-start | bytes 196616 | tf_op jit(solution)/shard_map/ppermute | solution.py:460
  58.5 0.3 collective-permute-start.14
  58.9 2.1 %collective-permute-done.12 = f32[16,1024]{1,0:T(8,128)S(1)} collective-permute-done((f32[16,1024]{1,0:T(8,128)S(1)}, f32[16,1024]{1,0:T(8,128)S(1)}, u32[]{:S(2)}, u32[]{:S(2)}) %collective-permute-start.12) | collective-permute-done | bytes 65568 | tf_op jit(solution)/shard_map/ppermute | solution.py:460
  61.0 0.4 collective-permute-done.13
  61.4 3.2 %collective-permute-done.14 = f32[16,1024]{1,0:T(8,128)S(1)} collective-permute-done((f32[16,1024]{1,0:T(8,128)S(1)}, f32[16,1024]{1,0:T(8,128)S(1)}, u32[]{:S(2)}, u32[]{:S(2)}) %collective-permute-start.14) | collective-permute-done | bytes 65568 | tf_op jit(solution)/shard_map/ppermute | solution.py:460
  64.6 0.1 collective-permute-start.15
  64.7 1.2 %collective-permute-done.15.refs_1_ = f32[8,1024]{1,0:T(8,128)S(1)} collective-permute-done((f32[8,1024]{1,0:T(8,128)S(1)}, f32[8,1024]{1,0:T(8,128)S(1)}, u32[]{:S(2)}, u32[]{:S(2)}) %collective-permute-start.15) | collective-permute-done | bytes 32800 | tf_op jit(solution)/shard_map/ppermute | solution.py:460
  65.9 0.1 sums.2.refs_1_.refs_2_.refs_3_.refs_4_
  66.0 1.5 %collective-permute-start.16 = (f32[8,1024]{1,0:T(8,128)S(1)}, f32[8,1024]{1,0:T(8,128)S(1)}, u32[]{:S(2)}, u32[]{:S(2)}) collective-permute-start(f32[8,1024]{1,0:T(8,128)S(1)} %sums.2.refs_1_.refs_2_.refs_3_.refs_4_), channel_id=1, source_target_pairs={{0,16},{16,0},{1,17},{17,1},{2,18},{18,2},{3,19},{19,3},{4,20},{20... | collective-permute-start | bytes 98312 | tf_op jit(solution)/shard_map/ppermute | solution.py:508
  67.5 2.4 %collective-permute-done.16.refs_3_.refs_1_.refs_5_.refs_2_ = f32[8,1024]{1,0:T(8,128)S(1)} collective-permute-done((f32[8,1024]{1,0:T(8,128)S(1)}, f32[8,1024]{1,0:T(8,128)S(1)}, u32[]{:S(2)}, u32[]{:S(2)}) %collective-permute-start.16) | collective-permute-done | bytes 32800 | tf_op jit(solution)/shard_map/ppermute | solution.py:508
  69.9 1.6 %scatter_near.3 = f32[64,1024]{1,0:T(8,128)S(1)} custom-call(f32[24,1024]{1,0:T(8,128)S(1)} %collective-permute-done.6.refs_0_, f32[8,1024]{1,0:T(8,128)S(1)} %collective-permute-done.16.refs_3_.refs_1_.refs_5_.refs_2_, f32[8,1024]{1,0:T(8,128)S(1)} %sums.2.refs_1_.refs_2_.refs_3_.refs_4_, f32[8,1024]{1,0:T(8,128)S(1)} %collective-permute-done.16.refs_3_.refs_1_.refs_5_.refs_2_), custom_call_target="tpu_custom_call" | custom-call | tf_op jit(solution)/shard_map/scatter_near/pallas_call | solution.py:255
  71.5 2.5 %scatter_own.3.refs_1_ = f32[128,1024]{1,0:T(8,128)S(1)} custom-call(f32[24,1024]{1,0:T(8,128)S(1)} %pad_maximum_fusion.13.refs_0_.message.refs_2_, f32[8,1024]{1,0:T(8,128)S(1)} %sums.2.refs_1_.refs_2_.refs_3_.refs_4_, f32[8,1024]{1,0:T(8,128)S(1)} %sums.2.refs_1_.refs_2_.refs_3_.refs_4_, f32[8,1024]{1,0:T(8,128)S(1)} %collective-permute-done.16.refs_3_.refs_1_.refs_5_.refs_2_), custom_call_target="tpu_custom_call" | custom-call | tf_op jit(solution)/shard_map/scatter_own/pallas_call | solution.py:255
  74.0 2.4 %filter_send.5 = f32[64,1024]{1,0:T(8,128)S(1)} custom-call(bf16[8,128,1024]{2,1,0:T(8,128)(2,1)S(1)} %bitcast.17, f32[128,1024]{1,0:T(8,128)S(1)} %scatter_own.3.refs_1_, f32[1,64,1024]{2,1,0:T(8,128)S(1)} %bitcast.37, f32[128,1024]{1,0:T(8,128)S(1)} %bitcast.23, bf16[800,256]{1,0:T(8,128)(2,1)S(1)} %copy-done.1, bf16[1,6,64,1024]{3,2,1,0:T(8,128)(2,1)S(1)} %bitcast.27, ...), custom_call_target="tpu_custom_call" | custom-call | tf_op jit(solution)/shard_map/filter_send/pallas_call | solution.py:342
  76.4 0.1 collective-permute-start.17
  76.4 2.4 %filter_keep.5 = f32[64,1024]{1,0:T(8,128)S(1)} custom-call(bf16[8,128,1024]{2,1,0:T(8,128)(2,1)S(1)} %bitcast.18, f32[128,1024]{1,0:T(8,128)S(1)} %scatter_own.3.refs_1_, f32[1,64,1024]{2,1,0:T(8,128)S(1)} %bitcast.38, f32[128,1024]{1,0:T(8,128)S(1)} %bitcast.24, bf16[800,256]{1,0:T(8,128)(2,1)S(1)} %copy-done.1, bf16[1,6,64,1024]{3,2,1,0:T(8,128)(2,1)S(1)} %bitcast.28, ...), custom_call_target="tpu_custom_call" | custom-call | tf_op jit(solution)/shard_map/filter_keep/pallas_call | solution.py:342
  78.9 0.6 collective-permute-start.18
  79.5 1.4 %gather_places.3 = f32[4,1024]{1,0:T(4,128)S(1)} custom-call(f32[64,1024]{1,0:T(8,128)S(1)} %add.62.field_ref, f32[24,1024]{1,0:T(8,128)S(1)} %pad_maximum_fusion.13.refs_0_.message.refs_2_), custom_call_target="tpu_custom_call" | custom-call | tf_op jit(solution)/shard_map/gather_places/pallas_call | solution.py:379
  80.9 1.6 %collective-permute-start.19 = (f32[4,1024]{1,0:T(4,128)S(1)}, f32[4,1024]{1,0:T(4,128)S(1)}, u32[]{:S(2)}, u32[]{:S(2)}) collective-permute-start(f32[4,1024]{1,0:T(4,128)S(1)} %gather_places.3), channel_id=1, source_target_pairs={{0,2},{1,3},{2,0},{3,1},{4,6},{5,7},{6,4},{7,5},{8,10},{9,11},{10,... | collective-permute-start | bytes 49160 | tf_op jit(solution)/shard_map/ppermute | solution.py:460
  82.4 2.8 %collective-permute-done.19 = f32[4,1024]{1,0:T(4,128)S(1)} collective-permute-done((f32[4,1024]{1,0:T(4,128)S(1)}, f32[4,1024]{1,0:T(4,128)S(1)}, u32[]{:S(2)}, u32[]{:S(2)}) %collective-permute-start.19) | collective-permute-done | bytes 16416 | tf_op jit(solution)/shard_map/ppermute | solution.py:460
  85.3 0.1 collective-permute-start.20
  85.5 1.3 %collective-permute-start.21 = (f32[12,1024]{1,0:T(8,128)S(1)}, f32[12,1024]{1,0:T(8,128)S(1)}, u32[]{:S(2)}, u32[]{:S(2)}) collective-permute-start(f32[12,1024]{1,0:T(8,128)S(1)} %get-tuple-element.53), channel_id=1, source_target_pairs={{0,4},{1,5},{2,6},{3,7},{4,0},{5,1},{6,2},{7,3},{8,12},{9,13},{10,... | collective-permute-start | bytes 147464 | tf_op jit(solution)/shard_map/ppermute | solution.py:460
  86.8 3.0 %collective-permute-start.22 = (f32[12,1024]{1,0:T(8,128)S(1)}, f32[12,1024]{1,0:T(8,128)S(1)}, u32[]{:S(2)}, u32[]{:S(2)}) collective-permute-start(f32[12,1024]{1,0:T(8,128)S(1)} %get-tuple-element.54), channel_id=1, source_target_pairs={{0,12},{1,13},{2,14},{3,15},{4,8},{5,9},{6,10},{7,11},{8,4},{9,5},... | collective-permute-start | bytes 147464 | tf_op jit(solution)/shard_map/ppermute | solution.py:460
  89.8 1.6 %collective-permute-done.20 = f32[12,1024]{1,0:T(8,128)S(1)} collective-permute-done((f32[12,1024]{1,0:T(8,128)S(1)}, f32[12,1024]{1,0:T(8,128)S(1)}, u32[]{:S(2)}, u32[]{:S(2)}) %collective-permute-start.20) | collective-permute-done | bytes 49184 | tf_op jit(solution)/shard_map/ppermute | solution.py:460
  91.4 1.5 %collective-permute-done.22 = f32[12,1024]{1,0:T(8,128)S(1)} collective-permute-done((f32[12,1024]{1,0:T(8,128)S(1)}, f32[12,1024]{1,0:T(8,128)S(1)}, u32[]{:S(2)}, u32[]{:S(2)}) %collective-permute-start.22) | collective-permute-done | bytes 49184 | tf_op jit(solution)/shard_map/ppermute | solution.py:460
  92.9 0.6 collective-permute-start.25
  93.5 3.1 %collective-permute-start.24 = (f32[2,8,1024]{2,1,0:T(8,128)S(1)}, f32[2,8,1024]{2,1,0:T(8,128)S(1)}, u32[]{:S(2)}, u32[]{:S(2)}) collective-permute-start(f32[2,8,1024]{2,1,0:T(8,128)S(1)} %pad_maximum_fusion.14), channel_id=1, source_target_pairs={{0,4},{1,5},{2,6},{3,7},{4,0},{5,1},{6,2},{7,3},{8,12},{9,13},{10,... | collective-permute-start | bytes 196616 | tf_op jit(solution)/shard_map/ppermute | solution.py:460
  96.5 0.8 collective-permute-start.23
  97.3 1.2 %collective-permute-done.26.refs_1_ = f32[4,1024]{1,0:T(4,128)S(1)} collective-permute-done((f32[4,1024]{1,0:T(4,128)S(1)}, f32[4,1024]{1,0:T(4,128)S(1)}, u32[]{:S(2)}, u32[]{:S(2)}) %collective-permute-start.26) | collective-permute-done | bytes 16416 | tf_op jit(solution)/shard_map/ppermute | solution.py:460
  98.5 0.2 sums.3.refs_3_
  98.7 1.5 %collective-permute-start.27 = (f32[8,128]{1,0:T(8,128)S(1)}, f32[8,128]{1,0:T(8,128)S(1)}, u32[]{:S(2)}, u32[]{:S(2)}) collective-permute-start(f32[8,128]{1,0:T(8,128)S(1)} %sums.3.refs_3_), channel_id=1, source_target_pairs={{0,16},{16,0},{1,17},{17,1},{2,18},{18,2},{3,19},{19,3},{4,20},{20... | collective-permute-start | bytes 12296 | tf_op jit(solution)/shard_map/ppermute | solution.py:508
  100.3 2.3 %collective-permute-done.23 = f32[2,8,1024]{2,1,0:T(8,128)S(1)} collective-permute-done((f32[2,8,1024]{2,1,0:T(8,128)S(1)}, f32[2,8,1024]{2,1,0:T(8,128)S(1)}, u32[]{:S(2)}, u32[]{:S(2)}) %collective-permute-start.23) | collective-permute-done | bytes 65568 | tf_op jit(solution)/shard_map/ppermute | solution.py:460
  102.7 0.1 combine.1
  102.8 1.0 collective-permute-start.28
  103.8 3.3 %collective-permute-done.28 = bf16[32,1024]{1,0:T(8,128)(2,1)S(1)} collective-permute-done((bf16[32,1024]{1,0:T(8,128)(2,1)S(1)}, bf16[32,1024]{1,0:T(8,128)(2,1)S(1)}, u32[]{:S(2)}, u32[]{:S(2)}) %collective-permute-start.28) | collective-permute-done | bytes 65568 | tf_op jit(solution)/shard_map/ppermute | solution.py:460
  107.2 0.1 collective-permute-start.29
  107.2 1.3 %collective-permute-done.29 = bf16[64,1024]{1,0:T(8,128)(2,1)S(1)} collective-permute-done((bf16[64,1024]{1,0:T(8,128)(2,1)S(1)}, bf16[64,1024]{1,0:T(8,128)(2,1)S(1)}, u32[]{:S(2)}, u32[]{:S(2)}) %collective-permute-start.29) | collective-permute-done | bytes 131104 | tf_op jit(solution)/shard_map/ppermute | solution.py:460
  108.7 0.8 convert.1
  (55 shorter events, 0.7 us)
Async XLA Ops:
  0.0 20.6 %copy-start.2 = (f32[4,32,1024]{2,1,0:T(8,128)S(1)}, f32[4,32,1024]{2,1,0:T(8,128)}, u32[]{:S(2)}) copy-start(f32[4,32,1024]{2,1,0:T(8,128)} %param.8) | copy-start | bytes 1572868
  1.4 38.6 %copy-start = (bf16[8,4,32,1024]{3,2,1,0:T(8,128)(2,1)S(1)}, bf16[8,4,32,1024]{3,2,1,0:T(8,128)(2,1)}, u32[]{:S(2)}) copy-start(bf16[8,4,32,1024]{3,2,1,0:T(8,128)(2,1)} %ens_hbm.1) | copy-start | bytes 6291460
  1.4 38.6 %copy-start.1 = (bf16[800,256]{1,0:T(8,128)(2,1)S(1)}, bf16[800,256]{1,0:T(8,128)(2,1)}, u32[]{:S(2)}) copy-start(bf16[800,256]{1,0:T(8,128)(2,1)} %constant.4.clone.refs_4_) | copy-start | bytes 1228804
  1.5 1.5 %collective-permute-start = (f32[12,1024]{1,0:T(8,128)S(1)}, f32[12,1024]{1,0:T(8,128)S(1)}, u32[]{:S(2)}, u32[]{:S(2)}) collective-permute-start(f32[12,1024]{1,0:T(8,128)S(1)} %slice_select_fusion.6), channel_id=1, source_target_pairs={{0,1},{1,0},{2,3},{3,2},{4,5},{5,4},{6,7},{7,6},{8,9},{9,8},{10,11... | collective-permute-start | bytes 147464 | tf_op jit(solution)/shard_map/ppermute | solution.py:460
  2.9 5.3 %collective-permute-start.1 = (f32[12,1024]{1,0:T(8,128)S(1)}, f32[12,1024]{1,0:T(8,128)S(1)}, u32[]{:S(2)}, u32[]{:S(2)}) collective-permute-start(f32[12,1024]{1,0:T(8,128)S(1)} %select_add_fusion.2), channel_id=1, source_target_pairs={{0,2},{1,3},{2,0},{3,1},{4,6},{5,7},{6,4},{7,5},{8,10},{9,11},{10,... | collective-permute-start | bytes 147464 | tf_op jit(solution)/shard_map/ppermute | solution.py:460
  8.3 6.8 %collective-permute-start.4 = (f32[12,1024]{1,0:T(8,128)S(1)}, f32[12,1024]{1,0:T(8,128)S(1)}, u32[]{:S(2)}, u32[]{:S(2)}) collective-permute-start(f32[12,1024]{1,0:T(8,128)S(1)} %add.52), channel_id=1, source_target_pairs={{0,12},{1,13},{2,14},{3,15},{4,8},{5,9},{6,10},{7,11},{8,4},{9,5},... | collective-permute-start | bytes 147464 | tf_op jit(solution)/shard_map/ppermute | solution.py:460
  12.3 5.4 %collective-permute-start.3 = (f32[12,1024]{1,0:T(8,128)S(1)}, f32[12,1024]{1,0:T(8,128)S(1)}, u32[]{:S(2)}, u32[]{:S(2)}) collective-permute-start(f32[12,1024]{1,0:T(8,128)S(1)} %add.52), channel_id=1, source_target_pairs={{0,8},{1,9},{2,10},{3,11},{4,12},{5,13},{6,14},{7,15},{8,0},{9,1},... | collective-permute-start | bytes 147464 | tf_op jit(solution)/shard_map/ppermute | solution.py:460
  12.3 5.4 %collective-permute-start.2 = (f32[12,1024]{1,0:T(8,128)S(1)}, f32[12,1024]{1,0:T(8,128)S(1)}, u32[]{:S(2)}, u32[]{:S(2)}) collective-permute-start(f32[12,1024]{1,0:T(8,128)S(1)} %add.52), channel_id=1, source_target_pairs={{0,4},{1,5},{2,6},{3,7},{4,0},{5,1},{6,2},{7,3},{8,12},{9,13},{10,... | collective-permute-start | bytes 147464 | tf_op jit(solution)/shard_map/ppermute | solution.py:460
  12.9 27.0 %collective-permute-start.8 = (bf16[6,4,16,1024]{3,2,1,0:T(8,128)(2,1)S(1)}, bf16[6,4,16,1024]{3,2,1,0:T(8,128)(2,1)S(1)}, u32[]{:S(2)}, u32[]{:S(2)}) collective-permute-start(bf16[6,4,16,1024]{3,2,1,0:T(8,128)(2,1)S(1)} %get-tuple-element.15), channel_id=1, source_target_pairs={{0,16},{16,0},{1,17},{17,1},{2,18},{18,2},{3,19},{19,3},{4,20},{20... | collective-permute-start | bytes 2359304 | tf_op jit(solution)/shard_map/ppermute | solution.py:516
  17.7 1.7 %collective-permute-start.5 = (f32[12,1024]{1,0:T(8,128)S(1)}, f32[12,1024]{1,0:T(8,128)S(1)}, u32[]{:S(2)}, u32[]{:S(2)}) collective-permute-start(f32[12,1024]{1,0:T(8,128)S(1)} %add_add_fusion), channel_id=1, source_target_pairs={{0,1},{1,0},{2,3},{3,2},{4,5},{5,4},{6,7},{7,6},{8,9},{9,8},{10,11... | collective-permute-start | bytes 147464 | tf_op jit(solution)/shard_map/ppermute | solution.py:460
  17.8 25.9 %collective-permute-start.7 = (bf16[2,4,16,1024]{3,2,1,0:T(8,128)(2,1)S(1)}, bf16[2,4,16,1024]{3,2,1,0:T(8,128)(2,1)S(1)}, u32[]{:S(2)}, u32[]{:S(2)}) collective-permute-start(bf16[2,4,16,1024]{3,2,1,0:T(8,128)(2,1)S(1)} %get-tuple-element.14), channel_id=1, source_target_pairs={{0,16},{16,0},{1,17},{17,1},{2,18},{18,2},{3,19},{19,3},{4,20},{20... | collective-permute-start | bytes 786440 | tf_op jit(solution)/shard_map/ppermute | solution.py:516
  19.4 19.2 %collective-permute-start.6 = (f32[24,1024]{1,0:T(8,128)S(1)}, f32[24,1024]{1,0:T(8,128)S(1)}, u32[]{:S(2)}, u32[]{:S(2)}) collective-permute-start(f32[24,1024]{1,0:T(8,128)S(1)} %pad_maximum_fusion.13.refs_0_.message.refs_2_), channel_id=1, source_target_pairs={{0,16},{16,0},{1,17},{17,1},{2,18},{18,2},{3,19},{19,3},{4,20},{20... | collective-permute-start | bytes 294920 | tf_op jit(solution)/shard_map/ppermute | solution.py:508
  44.6 1.6 %collective-permute-start.9 = (f32[64,1024]{1,0:T(8,128)S(1)}, f32[64,1024]{1,0:T(8,128)S(1)}, u32[]{:S(2)}, u32[]{:S(2)}) collective-permute-start(f32[64,1024]{1,0:T(8,128)S(1)} %filter_send.4), channel_id=1, source_target_pairs={{0,1},{1,0},{2,3},{3,2},{4,5},{5,4},{6,7},{7,6},{8,9},{9,8},{10,11... | collective-permute-start | bytes 786440 | tf_op jit(solution)/shard_map/ppermute | solution.py:460
  46.3 8.0 %collective-permute-start.10 = (f32[32,1024]{1,0:T(8,128)S(1)}, f32[32,1024]{1,0:T(8,128)S(1)}, u32[]{:S(2)}, u32[]{:S(2)}) collective-permute-start(f32[32,1024]{1,0:T(8,128)S(1)} %slice_select_fusion.1), channel_id=1, source_target_pairs={{0,2},{1,3},{2,0},{3,1},{4,6},{5,7},{6,4},{7,5},{8,10},{9,11},{10,... | collective-permute-start | bytes 393224 | tf_op jit(solution)/shard_map/ppermute | solution.py:460
  50.3 4.0 %collective-permute-start.11 = (f32[8,1024]{1,0:T(8,128)S(1)}, f32[8,1024]{1,0:T(8,128)S(1)}, u32[]{:S(2)}, u32[]{:S(2)}) collective-permute-start(f32[8,1024]{1,0:T(8,128)S(1)} %gather_places.2), channel_id=1, source_target_pairs={{0,2},{1,3},{2,0},{3,1},{4,6},{5,7},{6,4},{7,5},{8,10},{9,11},{10,... | collective-permute-start | bytes 98312 | tf_op jit(solution)/shard_map/ppermute | solution.py:460
  54.4 6.6 %collective-permute-start.12 = (f32[16,1024]{1,0:T(8,128)S(1)}, f32[16,1024]{1,0:T(8,128)S(1)}, u32[]{:S(2)}, u32[]{:S(2)}) collective-permute-start(f32[16,1024]{1,0:T(8,128)S(1)} %get-tuple-element.49), channel_id=1, source_target_pairs={{0,8},{1,9},{2,10},{3,11},{4,12},{5,13},{6,14},{7,15},{8,0},{9,1},... | collective-permute-start | bytes 196616 | tf_op jit(solution)/shard_map/ppermute | solution.py:460
  56.8 4.6 %collective-permute-start.13 = (f32[16,1024]{1,0:T(8,128)S(1)}, f32[16,1024]{1,0:T(8,128)S(1)}, u32[]{:S(2)}, u32[]{:S(2)}) collective-permute-start(f32[16,1024]{1,0:T(8,128)S(1)} %get-tuple-element.50), channel_id=1, source_target_pairs={{0,4},{1,5},{2,6},{3,7},{4,0},{5,1},{6,2},{7,3},{8,12},{9,13},{10,... | collective-permute-start | bytes 196616 | tf_op jit(solution)/shard_map/ppermute | solution.py:460
  58.5 6.1 %collective-permute-start.14 = (f32[16,1024]{1,0:T(8,128)S(1)}, f32[16,1024]{1,0:T(8,128)S(1)}, u32[]{:S(2)}, u32[]{:S(2)}) collective-permute-start(f32[16,1024]{1,0:T(8,128)S(1)} %get-tuple-element.51), channel_id=1, source_target_pairs={{0,12},{1,13},{2,14},{3,15},{4,8},{5,9},{6,10},{7,11},{8,4},{9,5},... | collective-permute-start | bytes 196616 | tf_op jit(solution)/shard_map/ppermute | solution.py:460
  64.6 1.3 %collective-permute-start.15 = (f32[8,1024]{1,0:T(8,128)S(1)}, f32[8,1024]{1,0:T(8,128)S(1)}, u32[]{:S(2)}, u32[]{:S(2)}) collective-permute-start(f32[8,1024]{1,0:T(8,128)S(1)} %get-tuple-element.48.refs_0_), channel_id=1, source_target_pairs={{0,1},{1,0},{2,3},{3,2},{4,5},{5,4},{6,7},{7,6},{8,9},{9,8},{10,11... | collective-permute-start | bytes 98312 | tf_op jit(solution)/shard_map/ppermute | solution.py:460
  66.0 3.9 %collective-permute-start.16 = (f32[8,1024]{1,0:T(8,128)S(1)}, f32[8,1024]{1,0:T(8,128)S(1)}, u32[]{:S(2)}, u32[]{:S(2)}) collective-permute-start(f32[8,1024]{1,0:T(8,128)S(1)} %sums.2.refs_1_.refs_2_.refs_3_.refs_4_), channel_id=1, source_target_pairs={{0,16},{16,0},{1,17},{17,1},{2,18},{18,2},{3,19},{19,3},{4,20},{20... | collective-permute-start | bytes 98312 | tf_op jit(solution)/shard_map/ppermute | solution.py:508
  76.4 2.5 %collective-permute-start.17 = (f32[64,1024]{1,0:T(8,128)S(1)}, f32[64,1024]{1,0:T(8,128)S(1)}, u32[]{:S(2)}, u32[]{:S(2)}) collective-permute-start(f32[64,1024]{1,0:T(8,128)S(1)} %filter_send.5), channel_id=1, source_target_pairs={{0,1},{1,0},{2,3},{3,2},{4,5},{5,4},{6,7},{7,6},{8,9},{9,8},{10,11... | collective-permute-start | bytes 786440 | tf_op jit(solution)/shard_map/ppermute | solution.py:460
  78.9 6.3 %collective-permute-start.18 = (f32[32,1024]{1,0:T(8,128)S(1)}, f32[32,1024]{1,0:T(8,128)S(1)}, u32[]{:S(2)}, u32[]{:S(2)}) collective-permute-start(f32[32,1024]{1,0:T(8,128)S(1)} %slice_select_fusion), channel_id=1, source_target_pairs={{0,2},{1,3},{2,0},{3,1},{4,6},{5,7},{6,4},{7,5},{8,10},{9,11},{10,... | collective-permute-start | bytes 393224 | tf_op jit(solution)/shard_map/ppermute | solution.py:460
  80.9 4.4 %collective-permute-start.19 = (f32[4,1024]{1,0:T(4,128)S(1)}, f32[4,1024]{1,0:T(4,128)S(1)}, u32[]{:S(2)}, u32[]{:S(2)}) collective-permute-start(f32[4,1024]{1,0:T(4,128)S(1)} %gather_places.3), channel_id=1, source_target_pairs={{0,2},{1,3},{2,0},{3,1},{4,6},{5,7},{6,4},{7,5},{8,10},{9,11},{10,... | collective-permute-start | bytes 49160 | tf_op jit(solution)/shard_map/ppermute | solution.py:460
  85.3 6.0 %collective-permute-start.20 = (f32[12,1024]{1,0:T(8,128)S(1)}, f32[12,1024]{1,0:T(8,128)S(1)}, u32[]{:S(2)}, u32[]{:S(2)}) collective-permute-start(f32[12,1024]{1,0:T(8,128)S(1)} %get-tuple-element.52), channel_id=1, source_target_pairs={{0,8},{1,9},{2,10},{3,11},{4,12},{5,13},{6,14},{7,15},{8,0},{9,1},... | collective-permute-start | bytes 147464 | tf_op jit(solution)/shard_map/ppermute | solution.py:460
  85.5 5.9 %collective-permute-start.21 = (f32[12,1024]{1,0:T(8,128)S(1)}, f32[12,1024]{1,0:T(8,128)S(1)}, u32[]{:S(2)}, u32[]{:S(2)}) collective-permute-start(f32[12,1024]{1,0:T(8,128)S(1)} %get-tuple-element.53), channel_id=1, source_target_pairs={{0,4},{1,5},{2,6},{3,7},{4,0},{5,1},{6,2},{7,3},{8,12},{9,13},{10,... | collective-permute-start | bytes 147464 | tf_op jit(solution)/shard_map/ppermute | solution.py:460
  86.8 6.1 %collective-permute-start.22 = (f32[12,1024]{1,0:T(8,128)S(1)}, f32[12,1024]{1,0:T(8,128)S(1)}, u32[]{:S(2)}, u32[]{:S(2)}) collective-permute-start(f32[12,1024]{1,0:T(8,128)S(1)} %get-tuple-element.54), channel_id=1, source_target_pairs={{0,12},{1,13},{2,14},{3,15},{4,8},{5,9},{6,10},{7,11},{8,4},{9,5},... | collective-permute-start | bytes 147464 | tf_op jit(solution)/shard_map/ppermute | solution.py:460
  92.9 7.4 %collective-permute-start.25 = (f32[2,8,1024]{2,1,0:T(8,128)S(1)}, f32[2,8,1024]{2,1,0:T(8,128)S(1)}, u32[]{:S(2)}, u32[]{:S(2)}) collective-permute-start(f32[2,8,1024]{2,1,0:T(8,128)S(1)} %pad_maximum_fusion.14), channel_id=1, source_target_pairs={{0,8},{1,9},{2,10},{3,11},{4,12},{5,13},{6,14},{7,15},{8,0},{9,1},... | collective-permute-start | bytes 196616 | tf_op jit(solution)/shard_map/ppermute | solution.py:460
  93.5 6.8 %collective-permute-start.24 = (f32[2,8,1024]{2,1,0:T(8,128)S(1)}, f32[2,8,1024]{2,1,0:T(8,128)S(1)}, u32[]{:S(2)}, u32[]{:S(2)}) collective-permute-start(f32[2,8,1024]{2,1,0:T(8,128)S(1)} %pad_maximum_fusion.14), channel_id=1, source_target_pairs={{0,4},{1,5},{2,6},{3,7},{4,0},{5,1},{6,2},{7,3},{8,12},{9,13},{10,... | collective-permute-start | bytes 196616 | tf_op jit(solution)/shard_map/ppermute | solution.py:460
  96.5 6.1 %collective-permute-start.23 = (f32[2,8,1024]{2,1,0:T(8,128)S(1)}, f32[2,8,1024]{2,1,0:T(8,128)S(1)}, u32[]{:S(2)}, u32[]{:S(2)}) collective-permute-start(f32[2,8,1024]{2,1,0:T(8,128)S(1)} %pad_maximum_fusion.14), channel_id=1, source_target_pairs={{0,12},{1,13},{2,14},{3,15},{4,8},{5,9},{6,10},{7,11},{8,4},{9,5},... | collective-permute-start | bytes 196616 | tf_op jit(solution)/shard_map/ppermute | solution.py:460
  97.3 1.2 %collective-permute-start.26 = (f32[4,1024]{1,0:T(4,128)S(1)}, f32[4,1024]{1,0:T(4,128)S(1)}, u32[]{:S(2)}, u32[]{:S(2)}) collective-permute-start(f32[4,1024]{1,0:T(4,128)S(1)} %slice.147.refs_0_), channel_id=1, source_target_pairs={{0,1},{1,0},{2,3},{3,2},{4,5},{5,4},{6,7},{7,6},{8,9},{9,8},{10,11... | collective-permute-start | bytes 49160 | tf_op jit(solution)/shard_map/ppermute | solution.py:460
  98.7 4.0 %collective-permute-start.27 = (f32[8,128]{1,0:T(8,128)S(1)}, f32[8,128]{1,0:T(8,128)S(1)}, u32[]{:S(2)}, u32[]{:S(2)}) collective-permute-start(f32[8,128]{1,0:T(8,128)S(1)} %sums.3.refs_3_), channel_id=1, source_target_pairs={{0,16},{16,0},{1,17},{17,1},{2,18},{18,2},{3,19},{19,3},{4,20},{20... | collective-permute-start | bytes 12296 | tf_op jit(solution)/shard_map/ppermute | solution.py:508
  102.8 4.3 %collective-permute-start.28 = (bf16[32,1024]{1,0:T(8,128)(2,1)S(1)}, bf16[32,1024]{1,0:T(8,128)(2,1)S(1)}, u32[]{:S(2)}, u32[]{:S(2)}) collective-permute-start(bf16[32,1024]{1,0:T(8,128)(2,1)S(1)} %combine.1), channel_id=1, source_target_pairs={{0,2},{1,3},{2,0},{3,1},{4,6},{5,7},{6,4},{7,5},{8,10},{9,11},{10,... | collective-permute-start | bytes 196616 | tf_op jit(solution)/shard_map/ppermute | solution.py:460
  107.2 1.4 %collective-permute-start.29 = (bf16[64,1024]{1,0:T(8,128)(2,1)S(1)}, bf16[64,1024]{1,0:T(8,128)(2,1)S(1)}, u32[]{:S(2)}, u32[]{:S(2)}) collective-permute-start(bf16[64,1024]{1,0:T(8,128)(2,1)S(1)} %pad_maximum_fusion.4), channel_id=1, source_target_pairs={{0,1},{1,0},{2,3},{3,2},{4,5},{5,4},{6,7},{7,6},{8,9},{9,8},{10,11... | collective-permute-start | bytes 393224 | tf_op jit(solution)/shard_map/ppermute | solution.py:460

commit v8 on v7

--- a/solution.py
+++ b/solution.py
@@ -143,10 +143,9 @@
         idx = idx_ref[:, lanes].astype(F32)
         value, error = value_ref[:, lanes], error_ref[:, lanes]
         coef, share = weigh(0.0, value, error)
-        for k, x in enumerate((idx, coef, share)):
+        for k, x in ((0, idx), (1, coef), (5, share)):
             out_ref[k * chunks + c:k * chunks + c + 1, :] = jnp.where(first, x, 0.0)
-        for k, x in enumerate((idx, value, error)):
-            k += 3
+        for k, x in ((2, idx), (3, value), (4, error)):
             out_ref[k * chunks + c:k * chunks + c + 1, :] = jnp.where(second, x, 0.0)
     for load in loads[4:]:
         load.wait()
@@ -215,9 +214,9 @@
     if not second:
         return row(message, 0), row(message, 1)
     at_place = scale_of(totals, chunks) * row(text, 0)
-    error = row(message, 5)
-    coef, _ = weigh(at_place, row(message, 4), jnp.where(error > 0, error, 1.0))
-    return row(message, 3), coef
+    error = row(message, 4)
+    coef, _ = weigh(at_place, row(message, 3), jnp.where(error > 0, error, 1.0))
+    return row(message, 2), coef
 
 
 def scatter_kernel(second, rows, lon, bands, near, *refs):
@@ -228,7 +227,7 @@
     out_ref, acc = refs[-2:]
     message = refs[0]
     text, totals = (refs[1], refs[2:-2]) if second else (None, None)
-    chunks = message.shape[0] // 6
+    chunks = message.shape[0] // (6 if near is None else 5)
     width = out_ref.shape[0]
     acc[...] = jnp.zeros_like(acc)
     lanes = acc.shape[1] // 2
@@ -397,13 +396,13 @@
     if second:
         text, totals = refs[3], refs[4:-1]
         at_place = scale_of(totals, chunks) * part(text, 0)
-        coef, share = weigh(at_place, part(message, 4), part(message, 5))
+        coef, share = weigh(at_place, part(message, 3), part(message, 4))
         along = total(coef * (reached - at_place))
         curve = total(coef * at_place) + total(share * reached * reached)
     else:
         out_ref[:chunks, :] = part(tail, 1)
         along = total(part(message, 1) * reached)
-        curve = total(part(message, 2) * reached * reached)
+        curve = total(part(message, 5) * reached * reached)
     out_ref[chunks:chunks + 1, :] = jnp.broadcast_to(along, (1, out_ref.shape[1]))
     out_ref[chunks + 1:chunks + 2, :] = jnp.broadcast_to(curve, (1, out_ref.shape[1]))
 
@@ -480,7 +479,7 @@
     near, far = halves(keep, uppers[low]), halves(send, uppers[low])
     rows = near[0].shape[0]
     total = jnp.concatenate([near[0], tail], axis=0)
-    for part, bit in ((near[1], low), (far[0], high), (far[1], high | low)):
+    for part, bit in zip((near[1], far[0], far[1]), (low, high, high | low)):
         total = total + swap(jnp.concatenate([part, tail], axis=0), bit, count)
     return total[:rows], total[rows:]
 
@@ -497,7 +496,10 @@
 
 
 def gather_square(x, high, low, count, uppers):
-    across, along, both = (swap(x, bit, count) for bit in (high, low, high | low))
+    got = []
+    for bit in (low, high, high | low):
+        got.append(swap(x, bit, count))
+    along, across, both = got
     mine = join_rows(x, along, uppers[low])
     other = join_rows(across, both, uppers[low])
     return join_rows(mine, other, uppers[high])
@@ -546,7 +548,7 @@
     for bit in bits[4:]:
         message = message + swap(message, bit, n_member)
     message = gather_rows(message, bits[0], n_member, flags[:1] > 0)
-    around = from_bands(message, n_band)
+    around = from_bands(message[:5 * chunks], n_band)
 
     own = ensemble.reshape(members_here, levels * lat_rows, lon)
     near_rows = lambda part: jnp.stack(
@@ -581,7 +583,7 @@
             field = filters(True, 0, None, own, ext, *parts) + got
         keep, send = halves(field, uppers[bits[1]])
         piece = keep + swap(send, bits[1], n_member)
-        tail = gather_places((3,) if texts else (0, 3), field, message)
+        tail = gather_places((2,) if texts else (0, 2), field, message)
         tail = tail + swap(tail, bits[1], n_member)
         piece, tail = reduce_square(piece, tail, bits[2], bits[3], n_member, uppers)
         piece, tail = reduce_with_tail(piece, tail, bits[4:], n_member, uppers)
@@ -604,8 +606,7 @@
         pair = gather_rows(pair, bit, n_member, uppers[bit])
     pair = gather_square(pair, bits[2], bits[3], n_member, uppers)
     out = combine(pair, totals_0, totals_1, chunks)
-    for bit in (bits[1], bits[0]):
-        out = gather_rows(out, bit, n_member, uppers[bit])
+    out = gather_square(out, bits[0], bits[1], n_member, uppers)
     return out.astype(F32).reshape(levels, lat_rows, lon)
 
 

time: 110 us -> 109 us (level)
    ppermute x2, starting transfers between devices: 3.25 us -> 2.03 us  [band_halo(): return [lax.ppermute(edges[0], 'band', [(0, 1), (1, 0)])]]
    ppermute x25 -> x26, starting transfers between devices: 27.2 us -> 28.3 us  [swap(): return lax.ppermute(x, 'member', partner(count, bit))]
    ppermute x25 -> x26, waiting for transfers between devices: 31.1 us -> 30.4 us  [swap(): return lax.ppermute(x, 'member', partner(count, bit))]
  transfers between devices with their start and end apart: 30 -> 31, of which waited for: 19 -> 20; matrix products, arithmetic and copies ran while one was open for 0% -> 0% of each run, Pallas kernels for 14% -> 14%
where the time goes in v8:
time: 109 us
  waiting for transfers between devices  48.4 us (44%)
  starting transfers between devices  35 us (32%)
  Pallas kernels  23.8 us (22%)
  other arithmetic  1.5 us (1%)
    ppermute x26, waiting for transfers between devices, swap(): return lax.ppermute(x, 'member', partner(count, bit))  30.4 us
    ppermute x26, starting transfers between devices, swap(): return lax.ppermute(x, 'member', partner(count, bit))  28.3 us
    ppermute x3, waiting for transfers between devices, from_bands(): return [lax.ppermute(x, 'band', [(0, 1), (1, 0)])]  18 us
    pallas_call x6, Pallas kernels, filter_members(): pl.pallas_call(kernel, out_shape=jax.ShapeDtypeStruct((rows // 2, lon), F...  10.4 us
    pallas_call x4, Pallas kernels, scatter_obs(): pl.pallas_call(functools.partial(scatter_kernel, second, rows, lon, bands...  7.74 us
    ppermute x3, starting transfers between devices, from_bands(): return [lax.ppermute(x, 'band', [(0, 1), (1, 0)])]  4.65 us
    pallas_call x2, Pallas kernels, gather_places(): pl.pallas_call(functools.partial(gather_kernel, which), out_shape=jax.Sha...  3.92 us
  transfers between devices with their start and end apart: 31, of which 20 were waited for; matrix products, arithmetic and copies ran while one was open for 0% of the time, Pallas kernels for 14%

profile of v8, /device:TPU:0, one launch (start us, length us, event | category | flops | bytes accessed | tf_op | source)
XLA Modules:
  0.0 109.1 jit_solution(17342163521978581069)
XLA Ops:
  0.0 1.3 %prepare.1 = (f32[24,1024]{1,0:T(8,128)S(1)}, f32[8,1024]{1,0:T(8,128)S(1)}, bf16[6,4,16,1024]{3,2,1,0:T(8,128)(2,1)S(1)}, bf16[2,4,16,1024]{3,2,1,0:T(8,128)(2,1)S(1)}) custom-call(s32[2]{0:T(128)} %root_hbm.1, bf16[8,4,32,1024]{3,2,1,0:T(8,128)(2,1)} %ens_hbm.1, s32[1,4096]{1,0:T(1,128)} %idx_hbm.1, f32[1,4096]{1,0:T(1,128)} %value_hbm.1, f32[1,4096]{1,0:T(1,128)} %error_hbm.1), custom_call_target="tpu_custom_call" | custom-call | tf_op jit(solution)/shard_map/prepare/pallas_call | solution.py:167
  1.5 0.6 collective-permute-start
  2.0 0.9 collective-permute-done
  2.9 2.9 %collective-permute-start.1 = (f32[12,1024]{1,0:T(8,128)S(1)}, f32[12,1024]{1,0:T(8,128)S(1)}, u32[]{:S(2)}, u32[]{:S(2)}) collective-permute-start(f32[12,1024]{1,0:T(8,128)S(1)} %select_add_fusion.2), channel_id=1, source_target_pairs={{0,2},{1,3},{2,0},{3,1},{4,6},{5,7},{6,4},{7,5},{8,10},{9,11},{10,... | collective-permute-start | bytes 147464 | tf_op jit(solution)/shard_map/ppermute | solution.py:459
  5.8 2.4 %collective-permute-done.1 = f32[12,1024]{1,0:T(8,128)S(1)} collective-permute-done((f32[12,1024]{1,0:T(8,128)S(1)}, f32[12,1024]{1,0:T(8,128)S(1)}, u32[]{:S(2)}, u32[]{:S(2)}) %collective-permute-start.1) | collective-permute-done | bytes 49184 | tf_op jit(solution)/shard_map/ppermute | solution.py:459
  8.3 4.0 %collective-permute-start.4 = (f32[12,1024]{1,0:T(8,128)S(1)}, f32[12,1024]{1,0:T(8,128)S(1)}, u32[]{:S(2)}, u32[]{:S(2)}) collective-permute-start(f32[12,1024]{1,0:T(8,128)S(1)} %add.52), channel_id=1, source_target_pairs={{0,12},{1,13},{2,14},{3,15},{4,8},{5,9},{6,10},{7,11},{8,4},{9,5},... | collective-permute-start | bytes 147464 | tf_op jit(solution)/shard_map/ppermute | solution.py:459
  12.3 0.6 collective-permute-start.2
  12.9 1.7 %collective-permute-start.7 = (bf16[2,4,16,1024]{3,2,1,0:T(8,128)(2,1)S(1)}, bf16[2,4,16,1024]{3,2,1,0:T(8,128)(2,1)S(1)}, u32[]{:S(2)}, u32[]{:S(2)}) collective-permute-start(bf16[2,4,16,1024]{3,2,1,0:T(8,128)(2,1)S(1)} %get-tuple-element.14), channel_id=1, source_target_pairs={{0,16},{16,0},{1,17},{17,1},{2,18},{18,2},{3,19},{19,3},{4,20},{20... | collective-permute-start | bytes 786440 | tf_op jit(solution)/shard_map/ppermute | solution.py:518
  14.6 0.4 collective-permute-start.8
  15.0 2.6 %collective-permute-done.3 = f32[12,1024]{1,0:T(8,128)S(1)} collective-permute-done((f32[12,1024]{1,0:T(8,128)S(1)}, f32[12,1024]{1,0:T(8,128)S(1)}, u32[]{:S(2)}, u32[]{:S(2)}) %collective-permute-start.3) | collective-permute-done | bytes 49184 | tf_op jit(solution)/shard_map/ppermute | solution.py:459
  17.7 0.1 collective-permute-start.5
  17.8 1.2 %collective-permute-done.5 = f32[12,1024]{1,0:T(8,128)S(1)} collective-permute-done((f32[12,1024]{1,0:T(8,128)S(1)}, f32[12,1024]{1,0:T(8,128)S(1)}, u32[]{:S(2)}, u32[]{:S(2)}) %collective-permute-start.5) | collective-permute-done | bytes 49184 | tf_op jit(solution)/shard_map/ppermute | solution.py:459
  19.0 1.6 %collective-permute-start.6 = (f32[20,1024]{1,0:T(8,128)S(1)}, f32[20,1024]{1,0:T(8,128)S(1)}, u32[]{:S(2)}, u32[]{:S(2)}) collective-permute-start(f32[20,1024]{1,0:T(8,128)S(1)} %fusion.2), channel_id=1, source_target_pairs={{0,16},{16,0},{1,17},{17,1},{2,18},{18,2},{3,19},{19,3},{4,20},{20... | collective-permute-start | bytes 245768 | tf_op jit(solution)/shard_map/ppermute | solution.py:510
  20.6 2.4 %scatter_own.2.refs_1_ = f32[128,1024]{1,0:T(8,128)S(1)} custom-call(f32[24,1024]{1,0:T(8,128)S(1)} %pad_maximum_fusion.10.refs_0_.message.refs_2_), custom_call_target="tpu_custom_call" | custom-call | tf_op jit(solution)/shard_map/scatter_own/pallas_call | solution.py:254
  23.0 15.6 %collective-permute-done.6.refs_0_ = f32[20,1024]{1,0:T(8,128)S(1)} collective-permute-done((f32[20,1024]{1,0:T(8,128)S(1)}, f32[20,1024]{1,0:T(8,128)S(1)}, u32[]{:S(2)}, u32[]{:S(2)}) %collective-permute-start.6) | collective-permute-done | bytes 81952 | tf_op jit(solution)/shard_map/ppermute | solution.py:510
  38.6 1.3 %scatter_near.2 = f32[64,1024]{1,0:T(8,128)S(1)} custom-call(f32[20,1024]{1,0:T(8,128)S(1)} %collective-permute-done.6.refs_0_), custom_call_target="tpu_custom_call" | custom-call | tf_op jit(solution)/shard_map/scatter_near/pallas_call | solution.py:254
  40.0 1.8 %filter_keep.3.refs_6_ = f32[64,1024]{1,0:T(8,128)S(1)} custom-call(bf16[8,128,1024]{2,1,0:T(8,128)(2,1)S(1)} %bitcast.13, f32[128,1024]{1,0:T(8,128)S(1)} %scatter_own.2.refs_1_, f32[1,64,1024]{2,1,0:T(8,128)S(1)} %bitcast.29, f32[128,1024]{1,0:T(8,128)S(1)} %bitcast.19, bf16[800,256]{1,0:T(8,128)(2,1)S(1)} %copy-done.1, bf16[1,6,64,1024]{3,2,1,0:T(8,128)(2,1)S(1)} %bitcast.25), custom_call_target="tpu_custom_call" | custom-call | tf_op jit(solution)/shard_map/filter_keep/pallas_call | solution.py:341
  41.8 1.8 %filter_send.3.refs_6_ = f32[64,1024]{1,0:T(8,128)S(1)} custom-call(bf16[8,128,1024]{2,1,0:T(8,128)(2,1)S(1)} %bitcast.14, f32[128,1024]{1,0:T(8,128)S(1)} %scatter_own.2.refs_1_, f32[1,64,1024]{2,1,0:T(8,128)S(1)} %bitcast.30, f32[128,1024]{1,0:T(8,128)S(1)} %bitcast.20, bf16[800,256]{1,0:T(8,128)(2,1)S(1)} %copy-done.1, bf16[1,6,64,1024]{3,2,1,0:T(8,128)(2,1)S(1)} %bitcast.26), custom_call_target="tpu_custom_call" | custom-call | tf_op jit(solution)/shard_map/filter_send/pallas_call | solution.py:341
  43.6 1.0 filter_send.4
  44.6 0.1 collective-permute-start.9
  44.7 1.0 filter_keep.4
  45.7 0.5 collective-permute-done.9
  46.3 1.5 %collective-permute-start.10 = (f32[32,1024]{1,0:T(8,128)S(1)}, f32[32,1024]{1,0:T(8,128)S(1)}, u32[]{:S(2)}, u32[]{:S(2)}) collective-permute-start(f32[32,1024]{1,0:T(8,128)S(1)} %slice_select_fusion.1), channel_id=1, source_target_pairs={{0,2},{1,3},{2,0},{3,1},{4,6},{5,7},{6,4},{7,5},{8,10},{9,11},{10,... | collective-permute-start | bytes 393224 | tf_op jit(solution)/shard_map/ppermute | solution.py:459
  47.8 2.6 %gather_places.2 = f32[8,1024]{1,0:T(8,128)S(1)} custom-call(f32[64,1024]{1,0:T(8,128)S(1)} %add.56.field_ref, f32[24,1024]{1,0:T(8,128)S(1)} %pad_maximum_fusion.10.refs_0_.message.refs_2_), custom_call_target="tpu_custom_call" | custom-call | tf_op jit(solution)/shard_map/gather_places/pallas_call | solution.py:378
  50.3 0.7 collective-permute-start.11
  51.0 3.3 %collective-permute-done.11 = f32[8,1024]{1,0:T(8,128)S(1)} collective-permute-done((f32[8,1024]{1,0:T(8,128)S(1)}, f32[8,1024]{1,0:T(8,128)S(1)}, u32[]{:S(2)}, u32[]{:S(2)}) %collective-permute-start.11) | collective-permute-done | bytes 32800 | tf_op jit(solution)/shard_map/ppermute | solution.py:459
  54.4 2.3 %collective-permute-start.12 = (f32[16,1024]{1,0:T(8,128)S(1)}, f32[16,1024]{1,0:T(8,128)S(1)}, u32[]{:S(2)}, u32[]{:S(2)}) collective-permute-start(f32[16,1024]{1,0:T(8,128)S(1)} %get-tuple-element.51), channel_id=1, source_target_pairs={{0,8},{1,9},{2,10},{3,11},{4,12},{5,13},{6,14},{7,15},{8,0},{9,1},... | collective-permute-start | bytes 196616 | tf_op jit(solution)/shard_map/ppermute | solution.py:459
  56.8 1.8 %collective-permute-start.13 = (f32[16,1024]{1,0:T(8,128)S(1)}, f32[16,1024]{1,0:T(8,128)S(1)}, u32[]{:S(2)}, u32[]{:S(2)}) collective-permute-start(f32[16,1024]{1,0:T(8,128)S(1)} %get-tuple-element.52), channel_id=1, source_target_pairs={{0,4},{1,5},{2,6},{3,7},{4,0},{5,1},{6,2},{7,3},{8,12},{9,13},{10,... | collective-permute-start | bytes 196616 | tf_op jit(solution)/shard_map/ppermute | solution.py:459
  58.5 0.3 collective-permute-start.14
  58.9 2.1 %collective-permute-done.12 = f32[16,1024]{1,0:T(8,128)S(1)} collective-permute-done((f32[16,1024]{1,0:T(8,128)S(1)}, f32[16,1024]{1,0:T(8,128)S(1)}, u32[]{:S(2)}, u32[]{:S(2)}) %collective-permute-start.12) | collective-permute-done | bytes 65568 | tf_op jit(solution)/shard_map/ppermute | solution.py:459
  61.0 0.4 collective-permute-done.13
  61.4 3.2 %collective-permute-done.14 = f32[16,1024]{1,0:T(8,128)S(1)} collective-permute-done((f32[16,1024]{1,0:T(8,128)S(1)}, f32[16,1024]{1,0:T(8,128)S(1)}, u32[]{:S(2)}, u32[]{:S(2)}) %collective-permute-start.14) | collective-permute-done | bytes 65568 | tf_op jit(solution)/shard_map/ppermute | solution.py:459
  64.6 0.1 collective-permute-start.15
  64.7 1.2 %collective-permute-done.15.refs_1_ = f32[8,1024]{1,0:T(8,128)S(1)} collective-permute-done((f32[8,1024]{1,0:T(8,128)S(1)}, f32[8,1024]{1,0:T(8,128)S(1)}, u32[]{:S(2)}, u32[]{:S(2)}) %collective-permute-start.15) | collective-permute-done | bytes 32800 | tf_op jit(solution)/shard_map/ppermute | solution.py:459
  65.9 0.1 sums.2.refs_1_.refs_2_.refs_3_.refs_4_
  66.0 1.5 %collective-permute-start.16 = (f32[8,1024]{1,0:T(8,128)S(1)}, f32[8,1024]{1,0:T(8,128)S(1)}, u32[]{:S(2)}, u32[]{:S(2)}) collective-permute-start(f32[8,1024]{1,0:T(8,128)S(1)} %sums.2.refs_1_.refs_2_.refs_3_.refs_4_), channel_id=1, source_target_pairs={{0,16},{16,0},{1,17},{17,1},{2,18},{18,2},{3,19},{19,3},{4,20},{20... | collective-permute-start | bytes 98312 | tf_op jit(solution)/shard_map/ppermute | solution.py:510
  67.5 2.4 %collective-permute-done.16.refs_3_.refs_1_.refs_5_.refs_2_ = f32[8,1024]{1,0:T(8,128)S(1)} collective-permute-done((f32[8,1024]{1,0:T(8,128)S(1)}, f32[8,1024]{1,0:T(8,128)S(1)}, u32[]{:S(2)}, u32[]{:S(2)}) %collective-permute-start.16) | collective-permute-done | bytes 32800 | tf_op jit(solution)/shard_map/ppermute | solution.py:510
  69.9 1.6 %scatter_near.3 = f32[64,1024]{1,0:T(8,128)S(1)} custom-call(f32[20,1024]{1,0:T(8,128)S(1)} %collective-permute-done.6.refs_0_, f32[8,1024]{1,0:T(8,128)S(1)} %collective-permute-done.16.refs_3_.refs_1_.refs_5_.refs_2_, f32[8,1024]{1,0:T(8,128)S(1)} %sums.2.refs_1_.refs_2_.refs_3_.refs_4_, f32[8,1024]{1,0:T(8,128)S(1)} %collective-permute-done.16.refs_3_.refs_1_.refs_5_.refs_2_), custom_call_target="tpu_custom_call" | custom-call | tf_op jit(solution)/shard_map/scatter_near/pallas_call | solution.py:254
  71.5 2.5 %scatter_own.3.refs_1_ = f32[128,1024]{1,0:T(8,128)S(1)} custom-call(f32[24,1024]{1,0:T(8,128)S(1)} %pad_maximum_fusion.10.refs_0_.message.refs_2_, f32[8,1024]{1,0:T(8,128)S(1)} %sums.2.refs_1_.refs_2_.refs_3_.refs_4_, f32[8,1024]{1,0:T(8,128)S(1)} %sums.2.refs_1_.refs_2_.refs_3_.refs_4_, f32[8,1024]{1,0:T(8,128)S(1)} %collective-permute-done.16.refs_3_.refs_1_.refs_5_.refs_2_), custom_call_target="tpu_custom_call" | custom-call | tf_op jit(solution)/shard_map/scatter_own/pallas_call | solution.py:254
  74.0 2.4 %filter_send.5 = f32[64,1024]{1,0:T(8,128)S(1)} custom-call(bf16[8,128,1024]{2,1,0:T(8,128)(2,1)S(1)} %bitcast.17, f32[128,1024]{1,0:T(8,128)S(1)} %scatter_own.3.refs_1_, f32[1,64,1024]{2,1,0:T(8,128)S(1)} %bitcast.37, f32[128,1024]{1,0:T(8,128)S(1)} %bitcast.23, bf16[800,256]{1,0:T(8,128)(2,1)S(1)} %copy-done.1, bf16[1,6,64,1024]{3,2,1,0:T(8,128)(2,1)S(1)} %bitcast.27, ...), custom_call_target="tpu_custom_call" | custom-call | tf_op jit(solution)/shard_map/filter_send/pallas_call | solution.py:341
  76.4 0.1 collective-permute-start.17
  76.5 2.4 %filter_keep.5 = f32[64,1024]{1,0:T(8,128)S(1)} custom-call(bf16[8,128,1024]{2,1,0:T(8,128)(2,1)S(1)} %bitcast.18, f32[128,1024]{1,0:T(8,128)S(1)} %scatter_own.3.refs_1_, f32[1,64,1024]{2,1,0:T(8,128)S(1)} %bitcast.38, f32[128,1024]{1,0:T(8,128)S(1)} %bitcast.24, bf16[800,256]{1,0:T(8,128)(2,1)S(1)} %copy-done.1, bf16[1,6,64,1024]{3,2,1,0:T(8,128)(2,1)S(1)} %bitcast.28, ...), custom_call_target="tpu_custom_call" | custom-call | tf_op jit(solution)/shard_map/filter_keep/pallas_call | solution.py:341
  78.9 0.6 collective-permute-start.18
  79.5 1.4 %gather_places.3 = f32[4,1024]{1,0:T(4,128)S(1)} custom-call(f32[64,1024]{1,0:T(8,128)S(1)} %add.62.field_ref, f32[24,1024]{1,0:T(8,128)S(1)} %pad_maximum_fusion.10.refs_0_.message.refs_2_), custom_call_target="tpu_custom_call" | custom-call | tf_op jit(solution)/shard_map/gather_places/pallas_call | solution.py:378
  80.9 1.6 %collective-permute-start.19 = (f32[4,1024]{1,0:T(4,128)S(1)}, f32[4,1024]{1,0:T(4,128)S(1)}, u32[]{:S(2)}, u32[]{:S(2)}) collective-permute-start(f32[4,1024]{1,0:T(4,128)S(1)} %gather_places.3), channel_id=1, source_target_pairs={{0,2},{1,3},{2,0},{3,1},{4,6},{5,7},{6,4},{7,5},{8,10},{9,11},{10,... | collective-permute-start | bytes 49160 | tf_op jit(solution)/shard_map/ppermute | solution.py:459
  82.4 2.8 %collective-permute-done.19 = f32[4,1024]{1,0:T(4,128)S(1)} collective-permute-done((f32[4,1024]{1,0:T(4,128)S(1)}, f32[4,1024]{1,0:T(4,128)S(1)}, u32[]{:S(2)}, u32[]{:S(2)}) %collective-permute-start.19) | collective-permute-done | bytes 16416 | tf_op jit(solution)/shard_map/ppermute | solution.py:459
  85.3 0.1 collective-permute-start.20
  85.5 1.3 %collective-permute-start.21 = (f32[12,1024]{1,0:T(8,128)S(1)}, f32[12,1024]{1,0:T(8,128)S(1)}, u32[]{:S(2)}, u32[]{:S(2)}) collective-permute-start(f32[12,1024]{1,0:T(8,128)S(1)} %get-tuple-element.55), channel_id=1, source_target_pairs={{0,4},{1,5},{2,6},{3,7},{4,0},{5,1},{6,2},{7,3},{8,12},{9,13},{10,... | collective-permute-start | bytes 147464 | tf_op jit(solution)/shard_map/ppermute | solution.py:459
  86.8 3.0 %collective-permute-start.22 = (f32[12,1024]{1,0:T(8,128)S(1)}, f32[12,1024]{1,0:T(8,128)S(1)}, u32[]{:S(2)}, u32[]{:S(2)}) collective-permute-start(f32[12,1024]{1,0:T(8,128)S(1)} %get-tuple-element.56), channel_id=1, source_target_pairs={{0,12},{1,13},{2,14},{3,15},{4,8},{5,9},{6,10},{7,11},{8,4},{9,5},... | collective-permute-start | bytes 147464 | tf_op jit(solution)/shard_map/ppermute | solution.py:459
  89.8 1.6 %collective-permute-done.20 = f32[12,1024]{1,0:T(8,128)S(1)} collective-permute-done((f32[12,1024]{1,0:T(8,128)S(1)}, f32[12,1024]{1,0:T(8,128)S(1)}, u32[]{:S(2)}, u32[]{:S(2)}) %collective-permute-start.20) | collective-permute-done | bytes 49184 | tf_op jit(solution)/shard_map/ppermute | solution.py:459
  91.4 1.5 %collective-permute-done.22 = f32[12,1024]{1,0:T(8,128)S(1)} collective-permute-done((f32[12,1024]{1,0:T(8,128)S(1)}, f32[12,1024]{1,0:T(8,128)S(1)}, u32[]{:S(2)}, u32[]{:S(2)}) %collective-permute-start.22) | collective-permute-done | bytes 49184 | tf_op jit(solution)/shard_map/ppermute | solution.py:459
  92.9 0.6 collective-permute-start.25
  93.5 3.1 %collective-permute-start.24 = (f32[2,8,1024]{2,1,0:T(8,128)S(1)}, f32[2,8,1024]{2,1,0:T(8,128)S(1)}, u32[]{:S(2)}, u32[]{:S(2)}) collective-permute-start(f32[2,8,1024]{2,1,0:T(8,128)S(1)} %pad_maximum_fusion.15), channel_id=1, source_target_pairs={{0,4},{1,5},{2,6},{3,7},{4,0},{5,1},{6,2},{7,3},{8,12},{9,13},{10,... | collective-permute-start | bytes 196616 | tf_op jit(solution)/shard_map/ppermute | solution.py:459
  96.5 0.8 collective-permute-start.23
  97.3 1.2 %collective-permute-done.26.refs_1_ = f32[4,1024]{1,0:T(4,128)S(1)} collective-permute-done((f32[4,1024]{1,0:T(4,128)S(1)}, f32[4,1024]{1,0:T(4,128)S(1)}, u32[]{:S(2)}, u32[]{:S(2)}) %collective-permute-start.26) | collective-permute-done | bytes 16416 | tf_op jit(solution)/shard_map/ppermute | solution.py:459
  98.5 0.2 sums.3.refs_3_
  98.7 1.5 %collective-permute-start.27 = (f32[8,128]{1,0:T(8,128)S(1)}, f32[8,128]{1,0:T(8,128)S(1)}, u32[]{:S(2)}, u32[]{:S(2)}) collective-permute-start(f32[8,128]{1,0:T(8,128)S(1)} %sums.3.refs_3_), channel_id=1, source_target_pairs={{0,16},{16,0},{1,17},{17,1},{2,18},{18,2},{3,19},{19,3},{4,20},{20... | collective-permute-start | bytes 12296 | tf_op jit(solution)/shard_map/ppermute | solution.py:510
  100.3 2.3 %collective-permute-done.23 = f32[2,8,1024]{2,1,0:T(8,128)S(1)} collective-permute-done((f32[2,8,1024]{2,1,0:T(8,128)S(1)}, f32[2,8,1024]{2,1,0:T(8,128)S(1)}, u32[]{:S(2)}, u32[]{:S(2)}) %collective-permute-start.23) | collective-permute-done | bytes 65568 | tf_op jit(solution)/shard_map/ppermute | solution.py:459
  102.7 0.1 combine.1
  102.8 1.0 collective-permute-start.30
  103.8 1.2 %collective-permute-start.28 = (bf16[32,1024]{1,0:T(8,128)(2,1)S(1)}, bf16[32,1024]{1,0:T(8,128)(2,1)S(1)}, u32[]{:S(2)}, u32[]{:S(2)}) collective-permute-start(bf16[32,1024]{1,0:T(8,128)(2,1)S(1)} %combine.1), channel_id=1, source_target_pairs={{0,3},{1,2},{2,1},{3,0},{4,7},{5,6},{6,5},{7,4},{8,11},{9,10},{10,... | collective-permute-start | bytes 196616 | tf_op jit(solution)/shard_map/ppermute | solution.py:459
  105.0 2.4 %collective-permute-done.30 = bf16[32,1024]{1,0:T(8,128)(2,1)S(1)} collective-permute-done((bf16[32,1024]{1,0:T(8,128)(2,1)S(1)}, bf16[32,1024]{1,0:T(8,128)(2,1)S(1)}, u32[]{:S(2)}, u32[]{:S(2)}) %collective-permute-start.30) | collective-permute-done | bytes 65568 | tf_op jit(solution)/shard_map/ppermute | solution.py:459
  107.5 0.7 collective-permute-done.28
  108.3 0.8 convert.1
  (57 shorter events, 0.8 us)
Async XLA Ops:
  0.0 17.8 %copy-start.2 = (f32[4,32,1024]{2,1,0:T(8,128)S(1)}, f32[4,32,1024]{2,1,0:T(8,128)}, u32[]{:S(2)}) copy-start(f32[4,32,1024]{2,1,0:T(8,128)} %param.8) | copy-start | bytes 1572868
  1.4 38.6 %copy-start = (bf16[8,4,32,1024]{3,2,1,0:T(8,128)(2,1)S(1)}, bf16[8,4,32,1024]{3,2,1,0:T(8,128)(2,1)}, u32[]{:S(2)}) copy-start(bf16[8,4,32,1024]{3,2,1,0:T(8,128)(2,1)} %ens_hbm.1) | copy-start | bytes 6291460
  1.4 38.6 %copy-start.1 = (bf16[800,256]{1,0:T(8,128)(2,1)S(1)}, bf16[800,256]{1,0:T(8,128)(2,1)}, u32[]{:S(2)}) copy-start(bf16[800,256]{1,0:T(8,128)(2,1)} %constant.4.clone.refs_4_) | copy-start | bytes 1228804
  1.5 1.5 %collective-permute-start = (f32[12,1024]{1,0:T(8,128)S(1)}, f32[12,1024]{1,0:T(8,128)S(1)}, u32[]{:S(2)}, u32[]{:S(2)}) collective-permute-start(f32[12,1024]{1,0:T(8,128)S(1)} %slice_select_fusion.6), channel_id=1, source_target_pairs={{0,1},{1,0},{2,3},{3,2},{4,5},{5,4},{6,7},{7,6},{8,9},{9,8},{10,11... | collective-permute-start | bytes 147464 | tf_op jit(solution)/shard_map/ppermute | solution.py:459
  2.9 5.3 %collective-permute-start.1 = (f32[12,1024]{1,0:T(8,128)S(1)}, f32[12,1024]{1,0:T(8,128)S(1)}, u32[]{:S(2)}, u32[]{:S(2)}) collective-permute-start(f32[12,1024]{1,0:T(8,128)S(1)} %select_add_fusion.2), channel_id=1, source_target_pairs={{0,2},{1,3},{2,0},{3,1},{4,6},{5,7},{6,4},{7,5},{8,10},{9,11},{10,... | collective-permute-start | bytes 147464 | tf_op jit(solution)/shard_map/ppermute | solution.py:459
  8.3 6.8 %collective-permute-start.4 = (f32[12,1024]{1,0:T(8,128)S(1)}, f32[12,1024]{1,0:T(8,128)S(1)}, u32[]{:S(2)}, u32[]{:S(2)}) collective-permute-start(f32[12,1024]{1,0:T(8,128)S(1)} %add.52), channel_id=1, source_target_pairs={{0,12},{1,13},{2,14},{3,15},{4,8},{5,9},{6,10},{7,11},{8,4},{9,5},... | collective-permute-start | bytes 147464 | tf_op jit(solution)/shard_map/ppermute | solution.py:459
  12.3 5.4 %collective-permute-start.3 = (f32[12,1024]{1,0:T(8,128)S(1)}, f32[12,1024]{1,0:T(8,128)S(1)}, u32[]{:S(2)}, u32[]{:S(2)}) collective-permute-start(f32[12,1024]{1,0:T(8,128)S(1)} %add.52), channel_id=1, source_target_pairs={{0,8},{1,9},{2,10},{3,11},{4,12},{5,13},{6,14},{7,15},{8,0},{9,1},... | collective-permute-start | bytes 147464 | tf_op jit(solution)/shard_map/ppermute | solution.py:459
  12.3 5.4 %collective-permute-start.2 = (f32[12,1024]{1,0:T(8,128)S(1)}, f32[12,1024]{1,0:T(8,128)S(1)}, u32[]{:S(2)}, u32[]{:S(2)}) collective-permute-start(f32[12,1024]{1,0:T(8,128)S(1)} %add.52), channel_id=1, source_target_pairs={{0,4},{1,5},{2,6},{3,7},{4,0},{5,1},{6,2},{7,3},{8,12},{9,13},{10,... | collective-permute-start | bytes 147464 | tf_op jit(solution)/shard_map/ppermute | solution.py:459
  12.9 30.7 %collective-permute-start.7 = (bf16[2,4,16,1024]{3,2,1,0:T(8,128)(2,1)S(1)}, bf16[2,4,16,1024]{3,2,1,0:T(8,128)(2,1)S(1)}, u32[]{:S(2)}, u32[]{:S(2)}) collective-permute-start(bf16[2,4,16,1024]{3,2,1,0:T(8,128)(2,1)S(1)} %get-tuple-element.14), channel_id=1, source_target_pairs={{0,16},{16,0},{1,17},{17,1},{2,18},{18,2},{3,19},{19,3},{4,20},{20... | collective-permute-start | bytes 786440 | tf_op jit(solution)/shard_map/ppermute | solution.py:518
  14.6 25.3 %collective-permute-start.8 = (bf16[6,4,16,1024]{3,2,1,0:T(8,128)(2,1)S(1)}, bf16[6,4,16,1024]{3,2,1,0:T(8,128)(2,1)S(1)}, u32[]{:S(2)}, u32[]{:S(2)}) collective-permute-start(bf16[6,4,16,1024]{3,2,1,0:T(8,128)(2,1)S(1)} %get-tuple-element.15), channel_id=1, source_target_pairs={{0,16},{16,0},{1,17},{17,1},{2,18},{18,2},{3,19},{19,3},{4,20},{20... | collective-permute-start | bytes 2359304 | tf_op jit(solution)/shard_map/ppermute | solution.py:518
  17.7 1.3 %collective-permute-start.5 = (f32[12,1024]{1,0:T(8,128)S(1)}, f32[12,1024]{1,0:T(8,128)S(1)}, u32[]{:S(2)}, u32[]{:S(2)}) collective-permute-start(f32[12,1024]{1,0:T(8,128)S(1)} %add_add_fusion), channel_id=1, source_target_pairs={{0,1},{1,0},{2,3},{3,2},{4,5},{5,4},{6,7},{7,6},{8,9},{9,8},{10,11... | collective-permute-start | bytes 147464 | tf_op jit(solution)/shard_map/ppermute | solution.py:459
  19.0 19.6 %collective-permute-start.6 = (f32[20,1024]{1,0:T(8,128)S(1)}, f32[20,1024]{1,0:T(8,128)S(1)}, u32[]{:S(2)}, u32[]{:S(2)}) collective-permute-start(f32[20,1024]{1,0:T(8,128)S(1)} %fusion.2), channel_id=1, source_target_pairs={{0,16},{16,0},{1,17},{17,1},{2,18},{18,2},{3,19},{19,3},{4,20},{20... | collective-permute-start | bytes 245768 | tf_op jit(solution)/shard_map/ppermute | solution.py:510
  44.6 1.6 %collective-permute-start.9 = (f32[64,1024]{1,0:T(8,128)S(1)}, f32[64,1024]{1,0:T(8,128)S(1)}, u32[]{:S(2)}, u32[]{:S(2)}) collective-permute-start(f32[64,1024]{1,0:T(8,128)S(1)} %filter_send.4), channel_id=1, source_target_pairs={{0,1},{1,0},{2,3},{3,2},{4,5},{5,4},{6,7},{7,6},{8,9},{9,8},{10,11... | collective-permute-start | bytes 786440 | tf_op jit(solution)/shard_map/ppermute | solution.py:459
  46.3 8.0 %collective-permute-start.10 = (f32[32,1024]{1,0:T(8,128)S(1)}, f32[32,1024]{1,0:T(8,128)S(1)}, u32[]{:S(2)}, u32[]{:S(2)}) collective-permute-start(f32[32,1024]{1,0:T(8,128)S(1)} %slice_select_fusion.1), channel_id=1, source_target_pairs={{0,2},{1,3},{2,0},{3,1},{4,6},{5,7},{6,4},{7,5},{8,10},{9,11},{10,... | collective-permute-start | bytes 393224 | tf_op jit(solution)/shard_map/ppermute | solution.py:459
  50.3 4.0 %collective-permute-start.11 = (f32[8,1024]{1,0:T(8,128)S(1)}, f32[8,1024]{1,0:T(8,128)S(1)}, u32[]{:S(2)}, u32[]{:S(2)}) collective-permute-start(f32[8,1024]{1,0:T(8,128)S(1)} %gather_places.2), channel_id=1, source_target_pairs={{0,2},{1,3},{2,0},{3,1},{4,6},{5,7},{6,4},{7,5},{8,10},{9,11},{10,... | collective-permute-start | bytes 98312 | tf_op jit(solution)/shard_map/ppermute | solution.py:459
  54.4 6.6 %collective-permute-start.12 = (f32[16,1024]{1,0:T(8,128)S(1)}, f32[16,1024]{1,0:T(8,128)S(1)}, u32[]{:S(2)}, u32[]{:S(2)}) collective-permute-start(f32[16,1024]{1,0:T(8,128)S(1)} %get-tuple-element.51), channel_id=1, source_target_pairs={{0,8},{1,9},{2,10},{3,11},{4,12},{5,13},{6,14},{7,15},{8,0},{9,1},... | collective-permute-start | bytes 196616 | tf_op jit(solution)/shard_map/ppermute | solution.py:459
  56.8 4.6 %collective-permute-start.13 = (f32[16,1024]{1,0:T(8,128)S(1)}, f32[16,1024]{1,0:T(8,128)S(1)}, u32[]{:S(2)}, u32[]{:S(2)}) collective-permute-start(f32[16,1024]{1,0:T(8,128)S(1)} %get-tuple-element.52), channel_id=1, source_target_pairs={{0,4},{1,5},{2,6},{3,7},{4,0},{5,1},{6,2},{7,3},{8,12},{9,13},{10,... | collective-permute-start | bytes 196616 | tf_op jit(solution)/shard_map/ppermute | solution.py:459
  58.5 6.1 %collective-permute-start.14 = (f32[16,1024]{1,0:T(8,128)S(1)}, f32[16,1024]{1,0:T(8,128)S(1)}, u32[]{:S(2)}, u32[]{:S(2)}) collective-permute-start(f32[16,1024]{1,0:T(8,128)S(1)} %get-tuple-element.53), channel_id=1, source_target_pairs={{0,12},{1,13},{2,14},{3,15},{4,8},{5,9},{6,10},{7,11},{8,4},{9,5},... | collective-permute-start | bytes 196616 | tf_op jit(solution)/shard_map/ppermute | solution.py:459
  64.6 1.3 %collective-permute-start.15 = (f32[8,1024]{1,0:T(8,128)S(1)}, f32[8,1024]{1,0:T(8,128)S(1)}, u32[]{:S(2)}, u32[]{:S(2)}) collective-permute-start(f32[8,1024]{1,0:T(8,128)S(1)} %get-tuple-element.50.refs_0_), channel_id=1, source_target_pairs={{0,1},{1,0},{2,3},{3,2},{4,5},{5,4},{6,7},{7,6},{8,9},{9,8},{10,11... | collective-permute-start | bytes 98312 | tf_op jit(solution)/shard_map/ppermute | solution.py:459
  66.0 3.9 %collective-permute-start.16 = (f32[8,1024]{1,0:T(8,128)S(1)}, f32[8,1024]{1,0:T(8,128)S(1)}, u32[]{:S(2)}, u32[]{:S(2)}) collective-permute-start(f32[8,1024]{1,0:T(8,128)S(1)} %sums.2.refs_1_.refs_2_.refs_3_.refs_4_), channel_id=1, source_target_pairs={{0,16},{16,0},{1,17},{17,1},{2,18},{18,2},{3,19},{19,3},{4,20},{20... | collective-permute-start | bytes 98312 | tf_op jit(solution)/shard_map/ppermute | solution.py:510
  76.4 2.5 %collective-permute-start.17 = (f32[64,1024]{1,0:T(8,128)S(1)}, f32[64,1024]{1,0:T(8,128)S(1)}, u32[]{:S(2)}, u32[]{:S(2)}) collective-permute-start(f32[64,1024]{1,0:T(8,128)S(1)} %filter_send.5), channel_id=1, source_target_pairs={{0,1},{1,0},{2,3},{3,2},{4,5},{5,4},{6,7},{7,6},{8,9},{9,8},{10,11... | collective-permute-start | bytes 786440 | tf_op jit(solution)/shard_map/ppermute | solution.py:459
  78.9 6.3 %collective-permute-start.18 = (f32[32,1024]{1,0:T(8,128)S(1)}, f32[32,1024]{1,0:T(8,128)S(1)}, u32[]{:S(2)}, u32[]{:S(2)}) collective-permute-start(f32[32,1024]{1,0:T(8,128)S(1)} %slice_select_fusion), channel_id=1, source_target_pairs={{0,2},{1,3},{2,0},{3,1},{4,6},{5,7},{6,4},{7,5},{8,10},{9,11},{10,... | collective-permute-start | bytes 393224 | tf_op jit(solution)/shard_map/ppermute | solution.py:459
  80.9 4.4 %collective-permute-start.19 = (f32[4,1024]{1,0:T(4,128)S(1)}, f32[4,1024]{1,0:T(4,128)S(1)}, u32[]{:S(2)}, u32[]{:S(2)}) collective-permute-start(f32[4,1024]{1,0:T(4,128)S(1)} %gather_places.3), channel_id=1, source_target_pairs={{0,2},{1,3},{2,0},{3,1},{4,6},{5,7},{6,4},{7,5},{8,10},{9,11},{10,... | collective-permute-start | bytes 49160 | tf_op jit(solution)/shard_map/ppermute | solution.py:459
  85.3 6.0 %collective-permute-start.20 = (f32[12,1024]{1,0:T(8,128)S(1)}, f32[12,1024]{1,0:T(8,128)S(1)}, u32[]{:S(2)}, u32[]{:S(2)}) collective-permute-start(f32[12,1024]{1,0:T(8,128)S(1)} %get-tuple-element.54), channel_id=1, source_target_pairs={{0,8},{1,9},{2,10},{3,11},{4,12},{5,13},{6,14},{7,15},{8,0},{9,1},... | collective-permute-start | bytes 147464 | tf_op jit(solution)/shard_map/ppermute | solution.py:459
  85.5 5.9 %collective-permute-start.21 = (f32[12,1024]{1,0:T(8,128)S(1)}, f32[12,1024]{1,0:T(8,128)S(1)}, u32[]{:S(2)}, u32[]{:S(2)}) collective-permute-start(f32[12,1024]{1,0:T(8,128)S(1)} %get-tuple-element.55), channel_id=1, source_target_pairs={{0,4},{1,5},{2,6},{3,7},{4,0},{5,1},{6,2},{7,3},{8,12},{9,13},{10,... | collective-permute-start | bytes 147464 | tf_op jit(solution)/shard_map/ppermute | solution.py:459
  86.8 6.1 %collective-permute-start.22 = (f32[12,1024]{1,0:T(8,128)S(1)}, f32[12,1024]{1,0:T(8,128)S(1)}, u32[]{:S(2)}, u32[]{:S(2)}) collective-permute-start(f32[12,1024]{1,0:T(8,128)S(1)} %get-tuple-element.56), channel_id=1, source_target_pairs={{0,12},{1,13},{2,14},{3,15},{4,8},{5,9},{6,10},{7,11},{8,4},{9,5},... | collective-permute-start | bytes 147464 | tf_op jit(solution)/shard_map/ppermute | solution.py:459
  92.9 7.4 %collective-permute-start.25 = (f32[2,8,1024]{2,1,0:T(8,128)S(1)}, f32[2,8,1024]{2,1,0:T(8,128)S(1)}, u32[]{:S(2)}, u32[]{:S(2)}) collective-permute-start(f32[2,8,1024]{2,1,0:T(8,128)S(1)} %pad_maximum_fusion.15), channel_id=1, source_target_pairs={{0,8},{1,9},{2,10},{3,11},{4,12},{5,13},{6,14},{7,15},{8,0},{9,1},... | collective-permute-start | bytes 196616 | tf_op jit(solution)/shard_map/ppermute | solution.py:459
  93.5 6.8 %collective-permute-start.24 = (f32[2,8,1024]{2,1,0:T(8,128)S(1)}, f32[2,8,1024]{2,1,0:T(8,128)S(1)}, u32[]{:S(2)}, u32[]{:S(2)}) collective-permute-start(f32[2,8,1024]{2,1,0:T(8,128)S(1)} %pad_maximum_fusion.15), channel_id=1, source_target_pairs={{0,4},{1,5},{2,6},{3,7},{4,0},{5,1},{6,2},{7,3},{8,12},{9,13},{10,... | collective-permute-start | bytes 196616 | tf_op jit(solution)/shard_map/ppermute | solution.py:459
  96.5 6.1 %collective-permute-start.23 = (f32[2,8,1024]{2,1,0:T(8,128)S(1)}, f32[2,8,1024]{2,1,0:T(8,128)S(1)}, u32[]{:S(2)}, u32[]{:S(2)}) collective-permute-start(f32[2,8,1024]{2,1,0:T(8,128)S(1)} %pad_maximum_fusion.15), channel_id=1, source_target_pairs={{0,12},{1,13},{2,14},{3,15},{4,8},{5,9},{6,10},{7,11},{8,4},{9,5},... | collective-permute-start | bytes 196616 | tf_op jit(solution)/shard_map/ppermute | solution.py:459
  97.3 1.2 %collective-permute-start.26 = (f32[4,1024]{1,0:T(4,128)S(1)}, f32[4,1024]{1,0:T(4,128)S(1)}, u32[]{:S(2)}, u32[]{:S(2)}) collective-permute-start(f32[4,1024]{1,0:T(4,128)S(1)} %slice.153.refs_0_), channel_id=1, source_target_pairs={{0,1},{1,0},{2,3},{3,2},{4,5},{5,4},{6,7},{7,6},{8,9},{9,8},{10,11... | collective-permute-start | bytes 49160 | tf_op jit(solution)/shard_map/ppermute | solution.py:459
  98.7 4.0 %collective-permute-start.27 = (f32[8,128]{1,0:T(8,128)S(1)}, f32[8,128]{1,0:T(8,128)S(1)}, u32[]{:S(2)}, u32[]{:S(2)}) collective-permute-start(f32[8,128]{1,0:T(8,128)S(1)} %sums.3.refs_3_), channel_id=1, source_target_pairs={{0,16},{16,0},{1,17},{17,1},{2,18},{18,2},{3,19},{19,3},{4,20},{20... | collective-permute-start | bytes 12296 | tf_op jit(solution)/shard_map/ppermute | solution.py:510
  102.8 4.6 %collective-permute-start.30 = (bf16[32,1024]{1,0:T(8,128)(2,1)S(1)}, bf16[32,1024]{1,0:T(8,128)(2,1)S(1)}, u32[]{:S(2)}, u32[]{:S(2)}) collective-permute-start(bf16[32,1024]{1,0:T(8,128)(2,1)S(1)} %combine.1), channel_id=1, source_target_pairs={{0,2},{1,3},{2,0},{3,1},{4,6},{5,7},{6,4},{7,5},{8,10},{9,11},{10,... | collective-permute-start | bytes 196616 | tf_op jit(solution)/shard_map/ppermute | solution.py:459
  103.8 3.6 %collective-permute-start.29 = (bf16[32,1024]{1,0:T(8,128)(2,1)S(1)}, bf16[32,1024]{1,0:T(8,128)(2,1)S(1)}, u32[]{:S(2)}, u32[]{:S(2)}) collective-permute-start(bf16[32,1024]{1,0:T(8,128)(2,1)S(1)} %combine.1), channel_id=1, source_target_pairs={{0,1},{1,0},{2,3},{3,2},{4,5},{5,4},{6,7},{7,6},{8,9},{9,8},{10,11... | collective-permute-start | bytes 196616 | tf_op jit(solution)/shard_map/ppermute | solution.py:459
  103.8 4.3 %collective-permute-start.28 = (bf16[32,1024]{1,0:T(8,128)(2,1)S(1)}, bf16[32,1024]{1,0:T(8,128)(2,1)S(1)}, u32[]{:S(2)}, u32[]{:S(2)}) collective-permute-start(bf16[32,1024]{1,0:T(8,128)(2,1)S(1)} %combine.1), channel_id=1, source_target_pairs={{0,3},{1,2},{2,1},{3,0},{4,7},{5,6},{6,5},{7,4},{8,11},{9,10},{10,... | collective-permute-start | bytes 196616 | tf_op jit(solution)/shard_map/ppermute | solution.py:459
